TPU v7x, 32 devices: a whole 2x2x4 slice. The times are simulated.
32 devices in a mesh: groups: 2 (over y), rows: 4 (over x, core), cols: 4 (over z).
Axes of the slice: x: 2, y: 2, z: 4, core: 2. Of those that a mesh axis runs over, the one named last changes fastest.
Arguments:
- q_fresh: bfloat16 [64, 128, 1536], P(('groups', 'rows'), 'cols'), parts along dimension 0, may hold values from -33 to 33
- k_fresh: bfloat16 [64, 128, 1536], P(('groups', 'rows'), 'cols'), parts along dimension 0, may hold values from -6.5 to 6.5
- v_fresh: bfloat16 [64, 128, 1536], P(('groups', 'rows'), 'cols'), parts along dimension 0, may hold values from -6 to 6
- k_stale: bfloat16 [64, 128, 1536], P(('groups', 'rows'), 'cols'), parts along dimension 0, may hold values from -6.375 to 6.375
- v_stale: bfloat16 [64, 128, 1536], P(('groups', 'rows'), 'cols'), parts along dimension 0, may hold values from -6 to 6
- text_k: bfloat16 [1024, 1536], P(('groups', 'rows', 'cols')), parts along dimension 0, may hold values from -6.375 to 6.375
- text_v: bfloat16 [1024, 1536], P(('groups', 'rows', 'cols')), parts along dimension 0, may hold values from -6 to 6
- conv_w: float32 [3, 3, 1536], replicated, may hold values from -0.8 to 0.8
- reads: int32 [8, 4, 2], P(('groups', 'rows'), 'cols'), parts along dimension 0, may hold values from 0 to 7, as said below
- pattern: int32 [16, 4, 2], P(('groups', 'rows'), 'cols'), parts along dimension 0, may hold values from 0 to 3, as said below
- text_blocks: int32 [16, 4, 2], P(('groups', 'rows'), 'cols'), parts along dimension 0, may hold values from 0 to 3, all different within a row
Outputs:
- attended: float32 [64, 128, 1536], P(('groups', 'rows'), 'cols'), parts along dimension 0
There are 2 independent parts, one for each index of `groups`. A program takes and returns all parts, laid end to end along the dimension named above; an argument that names none is the same for every part. Nothing has to cross between parts.
Inputs may be any that keep to these rules, and one draw needn't show every extreme that they name: `reads`: entry f of device (r, c) names a block row of column strip c; the device row of that block row (the entry // 2) differs from r and from those of the device's other entries. `pattern`: each row lists 2 distinct slots; the row of block row i always lists slot i % 2, and every slot from 2 up is listed by some block of its device.
All inputs are finite; a program needn't handle non-finite values.
Results may differ from a plain program's by a relative error of at most 0.00075.
Values may be sent and summed in bfloat16 or wider, within the bound.
No kernel may reach another device: no remote copies, remote signals or barrier semaphores. Data moves between devices by JAX's collectives and lax.ppermute only.
A program may use at most 192 MiB of HBM per device.

v0:
```python
import math

import jax
import jax.numpy as jnp
from jax import lax
from jax.sharding import PartitionSpec as P

HEAD_DIM = 128
BLOCK_ROWS = 4
BLOCK_COLS = 32


def extended(cells, sides, width):
    for axis, dim in sides:
        count = lax.axis_size(axis)
        ends = count - 1
        head = lax.slice_in_dim(cells, 0, width, axis=dim)
        tail = lax.slice_in_dim(cells, cells.shape[dim] - width, cells.shape[dim], axis=dim)
        cells = jnp.concatenate(
            [
                lax.ppermute(tail, axis, [(i, (i + 1) % count) for i in range(ends)]),
                cells,
                lax.ppermute(head, axis, [((i + 1) % count, i) for i in range(ends)]),
            ],
            axis=dim,
        )
    return cells


def split_heads(flat_rows):
    return flat_rows.reshape(flat_rows.shape[:-1] + (flat_rows.shape[-1] // HEAD_DIM, HEAD_DIM))


def attend(softmax_state, queries, key_blocks, value_blocks, allowed):
    old_peak, old_total, old_summed = softmax_state
    scores = jnp.einsum(
        "bqhd,nkhd->bhqnk", queries, key_blocks, preferred_element_type=jnp.float32
    ) * (1.0 / math.sqrt(HEAD_DIM))
    scores = jnp.where(allowed[:, None, None, :, None], scores, -1e30)
    new_peak = jnp.maximum(old_peak, jnp.max(scores, axis=(3, 4)))
    weights = jnp.exp(scores - new_peak[:, :, :, None, None]).astype(jnp.bfloat16)
    factor = jnp.exp(old_peak - new_peak)
    new_total = old_total * factor + jnp.sum(weights.astype(jnp.float32), axis=(3, 4))
    product = jnp.einsum(
        "bhqnk,nkhd->bqhd", weights, value_blocks, preferred_element_type=jnp.float32
    )
    new_summed = old_summed * jnp.transpose(factor, (0, 2, 1))[:, :, :, None] + product
    return (new_peak, new_total, new_summed)


def body(
    q_fresh, k_fresh, v_fresh, k_stale, v_stale, text_k, text_v, conv_w, reads, pattern, text_blocks
):
    rows_here, cols_here, feature_width = q_fresh.shape
    per_block = BLOCK_ROWS * BLOCK_COLS
    blocks_here = rows_here // BLOCK_ROWS
    head_count = feature_width // HEAD_DIM

    def as_blocks(grid_values):
        return split_heads(grid_values.reshape(blocks_here, per_block, feature_width))

    queries = as_blocks(q_fresh)
    own_keys = as_blocks(k_fresh)
    own_values = as_blocks(v_fresh)
    text_keys, text_values = (
        lax.all_gather(text_k, ("rows", "cols"), axis=0, tiled=True),
        lax.all_gather(text_v, ("rows", "cols"), axis=0, tiled=True),
    )
    text_count = text_keys.shape[0] // per_block
    text_keys = split_heads(text_keys.reshape(text_count, per_block, feature_width))
    text_values = split_heads(text_values.reshape(text_count, per_block, feature_width))
    wanted = pattern[:, 0, :]
    fetch_rows = reads[0, 0, :]
    fetch_count = fetch_rows.shape[0]
    slot_count = blocks_here + fetch_count
    slot_mask = jnp.any(
        wanted[:, :, None] == jnp.arange(slot_count, dtype=jnp.int32)[None, None, :], axis=1
    )
    text_mask = jnp.any(
        text_blocks[:, 0, :, None] == jnp.arange(text_count, dtype=jnp.int32)[None, None, :], axis=1
    )
    start_state = (
        jnp.full((blocks_here, head_count, per_block), -1e30, jnp.float32),
        jnp.zeros((blocks_here, head_count, per_block), jnp.float32),
        jnp.zeros((blocks_here, per_block, head_count, HEAD_DIM), jnp.float32),
    )
    softmax_state = attend(
        start_state,
        queries,
        jnp.concatenate([own_keys, text_keys], axis=0),
        jnp.concatenate([own_values, text_values], axis=0),
        jnp.concatenate([slot_mask[:, :blocks_here], text_mask], axis=1),
    )
    chosen = jnp.where(
        wanted >= blocks_here, fetch_rows[jnp.clip(wanted - blocks_here, 0, fetch_count - 1)], -1
    )
    piece_keys = lax.all_gather(as_blocks(k_stale), "rows", axis=0, tiled=True)
    piece_values = lax.all_gather(as_blocks(v_stale), "rows", axis=0, tiled=True)
    piece_count = piece_keys.shape[0]
    block_rows = jnp.arange(piece_count, dtype=jnp.int32)
    piece_mask = jnp.any(chosen[:, :, None] == block_rows[None, None, :], axis=1)
    softmax_state = attend(softmax_state, queries, piece_keys, piece_values, piece_mask)
    final_peak, final_total, final_summed = softmax_state
    mixed_rows = final_summed / jnp.transpose(final_total, (0, 2, 1))[:, :, :, None]
    attention = mixed_rows.reshape(rows_here, cols_here, feature_width)
    rims = extended(v_fresh, (("rows", 0), ("cols", 1)), 1)
    position_term = jnp.zeros((rows_here, cols_here, feature_width), jnp.float32)
    for row_tap in range(3):
        for col_tap in range(3):
            position_term = position_term + conv_w[row_tap, col_tap] * rims[
                row_tap : row_tap + rows_here, col_tap : col_tap + cols_here
            ].astype(jnp.float32)
    return attention + position_term


def solution(mesh):
    in_specs = (
        P(("groups", "rows"), "cols", None),
        P(("groups", "rows"), "cols", None),
        P(("groups", "rows"), "cols", None),
        P(("groups", "rows"), "cols", None),
        P(("groups", "rows"), "cols", None),
        P(("groups", "rows", "cols"), None),
        P(("groups", "rows", "cols"), None),
        P(),
        P(("groups", "rows"), "cols", None),
        P(("groups", "rows"), "cols", None),
        P(("groups", "rows"), "cols", None),
    )
    out_specs = P(("groups", "rows"), "cols", None)
    return jax.shard_map(body, mesh=mesh, in_specs=in_specs, out_specs=out_specs, check_vma=False)
```

profile of v0, /device:TPU:0, one launch (start us, length us, event | category | flops | bytes accessed | tf_op | source)
XLA Modules:
  0.0 184.2 jit_solution(10982115010975947880)
XLA Ops:
  8.1 1.6 reshape_reshape.26
  10.9 2.4 %collective-permute-start = (bf16[1,32,1536]{2,1,0:T(8,128)(2,1)S(1)}, bf16[1,32,1536]{2,1,0:T(8,128)(2,1)S(1)}, u32[]{:S(2)}, u32[]{:S(2)}) collective-permute-start(bf16[1,32,1536]{2,1,0:T(8,128)(2,1)S(1)} %get-tuple-element.19), channel_id=1, source_target_pairs={{0,4},{4,8},{8,12},{1,5},{5,9},{9,13},{2,6},{6,10},{10,14},{3,7},{... | collective-permute-start | bytes 294920 | tf_op jit(solution)/shard_map/ppermute | solution.py:21
  17.4 1.5 reshape_reshape.23
  19.0 1.6 reshape_reshape.21
  22.8 1.5 copy.37
  26.3 4.3 %collective-permute-start.2 = (bf16[10,1,1536]{2,1,0:T(2,128)(2,1)S(1)}, bf16[10,1,1536]{2,1,0:T(2,128)(2,1)S(1)}, u32[]{:S(2)}, u32[]{:S(2)}) collective-permute-start(bf16[10,1,1536]{2,1,0:T(2,128)(2,1)S(1)} %get-tuple-element.16), channel_id=1, source_target_pairs={{0,1},{1,2},{2,3},{4,5},{5,6},{6,7},{8,9},{9,10},{10,11},{12,13},{... | collective-permute-start | bytes 92168 | tf_op jit(solution)/shard_map/ppermute | solution.py:21
  30.6 1.5 collective-permute-start.3
  32.1 20.0 %all-gather.5.cloned.1.call-done = bf16[512,1536]{1,0:T(8,128)(2,1)} async-done(((bf16[32,1536]{1,0:T(8,128)(2,1)}), bf16[512,1536]{1,0:T(8,128)(2,1)}) %all-gather.5.cloned.1.call-update) | async-done | bytes 1572880 | tf_op jit(solution)/shard_map/all_gather | solution.py:66
  52.1 2.9 %reshape.71 = bf16[4,128,12,128]{3,2,1,0:T(8,128)(2,1)S(1)} reshape(bf16[512,1536]{1,0:T(8,128)(2,1)} %all-gather.5.cloned.1.call-done) | data formatting | bytes 3145728 | tf_op jit(solution)/shard_map/reshape;reshape | solution.py:31
  55.0 1.6 copy.34
  56.5 36.5 %all-gather.7.cloned.1.call-done = bf16[512,1536]{1,0:T(8,128)(2,1)} async-done(((bf16[32,1536]{1,0:T(8,128)(2,1)}), bf16[512,1536]{1,0:T(8,128)(2,1)}) %all-gather.7.cloned.1.call-update) | async-done | bytes 1572880 | tf_op jit(solution)/shard_map/all_gather | solution.py:67
  93.0 2.9 %reshape.72 = bf16[4,128,12,128]{3,2,1,0:T(8,128)(2,1)S(1)} reshape(bf16[512,1536]{1,0:T(8,128)(2,1)} %all-gather.7.cloned.1.call-done) | data formatting | bytes 3145728 | tf_op jit(solution)/shard_map/reshape;reshape | solution.py:31
  95.9 2.8 %copy.38 = bf16[4,128,12,128]{1,3,0,2:T(8,128)(2,1)} copy(bf16[4,128,12,128]{3,2,1,0:T(8,128)(2,1)S(1)} %reshape.72) | data formatting | bytes 3145728 | tf_op jit(solution)/shard_map/reshape;reshape | solution.py:31
  98.6 7.3 %fusion.1 = (f32[2,12,128]{2,0,1:T(2,128)S(1)}, f32[12,6,128,2,128]{4,2,3,1,0:T(8,128)}) fusion(pred[2,6]{0,1:T(8,128)(4,1)S(1)} %copy.31, bf16[2,128,12,128,1]{3,2,1,0,4:T(8,128)(2,1)} %bitcast.98, bf16[4,128,12,128]{3,1,0,2:T(8,128)(2,1)} %copy.34, bf16[2,128,12,128]{3,1,0,2:T(8,128)(2,1)} %copy.33), kind=kOutput, calls=%fused_computation.8 | convolution fusion | flops 615773184 | bytes 12595212 | tf_op jit(solution)/shard_map/bqhd,nkhd->bhqnk/dot_general | solution.py:36
  106.0 16.1 %all-gather.9.cloned.1.call-done = bf16[8,128,12,128]{3,1,0,2:T(8,128)(2,1)} async-done(((bf16[2,128,12,128]{3,1,0,2:T(8,128)(2,1)}), bf16[8,128,12,128]{3,1,0,2:T(8,128)(2,1)}) %all-gather.9.cloned.1.call-update) | async-done | bytes 3145744 | tf_op jit(solution)/shard_map/all_gather | solution.py:97
  122.0 3.6 %fusion = (f32[2,12,128]{2,0,1:T(2,128)S(1)}, f32[12,8,128,2,128]{4,2,3,1,0:T(8,128)S(1)}) fusion(pred[2,8]{0,1:T(8,128)(4,1)S(1)} %copy.40, bf16[2,128,12,128,1]{3,2,1,0,4:T(8,128)(2,1)S(1)} %bitcast.99, bf16[8,128,12,128]{3,1,0,2:T(8,128)(2,1)} %all-gather.9.cloned.1.call-done), kind=kOutput, calls=%fused_computation.4 | convolution fusion | flops 814740480 | bytes 16527376 | tf_op jit(solution)/shard_map/bqhd,nkhd->bhqnk/dot_general | solution.py:36
  125.6 10.4 %convert_reduce_fusion.1 = f32[2,12,128]{2,0,1:T(2,128)S(1)} fusion(f32[2,12,128]{2,0,1:T(2,128)S(1)} %get-tuple-element.21, f32[12,6,128,2,128]{4,2,3,1,0:T(8,128)} %get-tuple-element.24, pred[2,6]{0,1:T(8,128)(4,1)S(1)} %copy.31), kind=kLoop, calls=%fused_computation.6 | loop fusion | flops 14152704 | bytes 9461772 | tf_op jit(solution)/shard_map/reduce_sum | solution.py:43
  136.0 2.6 %convert_reduce_fusion = f32[2,12,128]{2,0,1:T(2,128)S(1)} fusion(f32[2,12,128]{2,0,1:T(2,128)S(1)} %get-tuple-element.22, f32[12,8,128,2,128]{4,2,3,1,0:T(8,128)S(1)} %get-tuple-element.26, pred[2,8]{0,1:T(8,128)(4,1)S(1)} %copy.40), kind=kLoop, calls=%fused_computation.2 | loop fusion | flops 18871296 | bytes 12607504 | tf_op jit(solution)/shard_map/reduce_sum | solution.py:43
  139.3 12.7 %all-gather.11.cloned.1.call-done = bf16[8,128,12,128]{3,1,0,2:T(8,128)(2,1)} async-done(((bf16[2,128,12,128]{3,1,0,2:T(8,128)(2,1)}), bf16[8,128,12,128]{3,1,0,2:T(8,128)(2,1)}) %all-gather.11.cloned.1.call-update) | async-done | bytes 3145744 | tf_op jit(solution)/shard_map/all_gather | solution.py:98
  152.0 8.5 %fusion.2 = f32[12,2,128,128,1]{2,3,1,4,0:T(8,128)S(1)} fusion(bf16[8,128,12,128]{3,1,0,2:T(8,128)(2,1)} %all-gather.11.cloned.1.call-done, f32[12,8,128,2,128]{4,2,3,1,0:T(8,128)} %copy-done.1, f32[2,12,128]{2,0,1:T(2,128)S(1)} %get-tuple-element.22, pred[2,8]{0,1:T(8,128)(4,1)} %copy-done.22), kind=kOutput, calls=%fused_computation.9 | convolution fusion | flops 817889280 | bytes 17313808 | tf_op jit(solution)/shard_map/bhqnk,nkhd->bqhd/dot_general | solution.py:44
  160.5 7.3 %fusion.14 = f32[2,128,12,128]{1,3,0,2:T(8,128)} fusion(f32[12,2,128,128,1]{2,3,1,4,0:T(8,128)S(1)} %fusion.2, bf16[4,128,12,128]{1,3,0,2:T(8,128)(2,1)S(1)} %copy-done.4, bf16[2,128,12,128]{1,3,0,2:T(8,128)(2,1)S(1)} %copy-done.8, f32[2,128,12]{1,0,2:T(2,128)S(1)} %copy-done.19, f32[2,128,12]{1,0,2:T(2,128)S(1)} %copy-done.20, ...), kind=kOutput, calls=%fused_computation.27 | convolution fusion | flops 619708416 | bytes 14991372 | tf_op jit(solution)/shard_map/bhqnk,nkhd->bqhd/dot_general | solution.py:44
  167.9 2.2 %copy.46 = f32[2,128,12,128]{3,2,1,0:T(8,128)S(1)} copy(f32[2,128,12,128]{1,3,0,2:T(8,128)} %fusion.14) | data formatting | bytes 3145728 | tf_op jit(solution)/shard_map/div | solution.py:104
  170.1 1.4 reshape.53
  171.6 6.0 %add_add_fusion = f32[8,32,1536]{2,1,0:T(8,128)} fusion(f32[8,32,1536]{2,1,0:T(8,128)} %reshape.53, bf16[8,32,1536]{2,1,0:T(8,128)(2,1)S(1)} %copy-done.2, bf16[10,32,1536]{2,1,0:T(8,128)(2,1)} %copy-done.5, bf16[10,1,1536]{2,1,0:T(2,128)(2,1)} %collective-permute-done.3, bf16[10,1,1536]{2,1,0:T(2,128)(2,1)S(1)} %collective-permute-done.2, ...), kind=kLoop, calls=%fused_computation.30 | loop fusion | flops 20054016 | bytes 5228544 | tf_op jit(solution)/shard_map/add | solution.py:113
  (93 shorter events, 11.5 us)
Async XLA Ops:
  6.5 15.3 %copy-start = (s32[1,1,2]{2,1,0:T(1,128)S(1)}, s32[1,1,2]{2,1,0:T(1,128)}, u32[]{:S(2)}) copy-start(s32[1,1,2]{2,1,0:T(1,128)} %param.19) | copy-start | bytes 28
  6.5 45.5 %all-gather.5.cloned.1.call-start = ((), (), s32[]{:S(2)}) async-start(), calls=%async_computation | async-start | bytes 1671168 | tf_op jit(solution)/shard_map/all_gather | solution.py:66
  7.3 85.7 %all-gather.7.cloned.1.call-start = ((), (), s32[]{:S(2)}) async-start(), calls=%async_computation.1 | async-start | bytes 1671168 | tf_op jit(solution)/shard_map/all_gather | solution.py:67
  8.0 114.0 %all-gather.9.cloned.1.call-start = ((), (), s32[]{:S(2)}) async-start(), calls=%async_computation.2 | async-start | bytes 3932160 | tf_op jit(solution)/shard_map/all_gather | solution.py:97
  9.7 4.9 %copy-start.6 = (bf16[8,32,1536]{2,1,0:T(8,128)(2,1)S(1)}, bf16[8,32,1536]{2,1,0:T(8,128)(2,1)}, u32[]{:S(2)}) copy-start(bf16[8,32,1536]{2,1,0:T(8,128)(2,1)} %param.15) | copy-start | bytes 2359300
  10.8 141.2 %all-gather.11.cloned.1.call-start = ((), (), s32[]{:S(2)}) async-start(), calls=%async_computation.3 | async-start | bytes 3932160 | tf_op jit(solution)/shard_map/all_gather | solution.py:98
  10.9 14.2 %collective-permute-start = (bf16[1,32,1536]{2,1,0:T(8,128)(2,1)S(1)}, bf16[1,32,1536]{2,1,0:T(8,128)(2,1)S(1)}, u32[]{:S(2)}, u32[]{:S(2)}) collective-permute-start(bf16[1,32,1536]{2,1,0:T(8,128)(2,1)S(1)} %get-tuple-element.19), channel_id=1, source_target_pairs={{0,4},{4,8},{8,12},{1,5},{5,9},{9,13},{2,6},{6,10},{10,14},{3,7},{... | collective-permute-start | bytes 294920 | tf_op jit(solution)/shard_map/ppermute | solution.py:21
  13.3 11.9 %collective-permute-start.1 = (bf16[1,32,1536]{2,1,0:T(8,128)(2,1)S(1)}, bf16[1,32,1536]{2,1,0:T(8,128)(2,1)S(1)}, u32[]{:S(2)}, u32[]{:S(2)}) collective-permute-start(bf16[1,32,1536]{2,1,0:T(8,128)(2,1)S(1)} %get-tuple-element.18), channel_id=1, source_target_pairs={{4,0},{8,4},{12,8},{5,1},{9,5},{13,9},{6,2},{10,6},{14,10},{7,3},{... | collective-permute-start | bytes 294920 | tf_op jit(solution)/shard_map/ppermute | solution.py:23
  17.4 108.2 %copy-start.24 = (pred[2,6]{0,1:T(8,128)(4,1)}, pred[2,6]{0,1:T(8,128)(4,1)S(1)}, u32[]{:S(2)}) copy-start(pred[2,6]{0,1:T(8,128)(4,1)S(1)} %copy.31) | copy-start | bytes 40
  21.8 2.6 %copy-start.9 = (f32[3,3,1536]{2,1,0:T(4,128)S(1)}, f32[3,3,1536]{2,1,0:T(4,128)}, u32[]{:S(2)}) copy-start(f32[3,3,1536]{2,1,0:T(4,128)} %param.18) | copy-start | bytes 165892
  22.8 113.2 %copy-start.22 = (pred[2,8]{0,1:T(8,128)(4,1)}, pred[2,8]{0,1:T(8,128)(4,1)S(1)}, u32[]{:S(2)}) copy-start(pred[2,8]{0,1:T(8,128)(4,1)S(1)} %copy.40) | copy-start | bytes 52
  26.3 145.3 %collective-permute-start.2 = (bf16[10,1,1536]{2,1,0:T(2,128)(2,1)S(1)}, bf16[10,1,1536]{2,1,0:T(2,128)(2,1)S(1)}, u32[]{:S(2)}, u32[]{:S(2)}) collective-permute-start(bf16[10,1,1536]{2,1,0:T(2,128)(2,1)S(1)} %get-tuple-element.16), channel_id=1, source_target_pairs={{0,1},{1,2},{2,3},{4,5},{5,6},{6,7},{8,9},{9,10},{10,11},{12,13},{... | collective-permute-start | bytes 92168 | tf_op jit(solution)/shard_map/ppermute | solution.py:21
  30.6 140.9 %collective-permute-start.3 = (bf16[10,1,1536]{2,1,0:T(2,128)(2,1)S(1)}, bf16[10,1,1536]{2,1,0:T(2,128)(2,1)}, u32[]{:S(2)}, u32[]{:S(2)}) collective-permute-start(bf16[10,1,1536]{2,1,0:T(2,128)(2,1)S(1)} %get-tuple-element.17), channel_id=1, source_target_pairs={{1,0},{2,1},{3,2},{5,4},{6,5},{7,6},{9,8},{10,9},{11,10},{13,12},{... | collective-permute-start | bytes 92168 | tf_op jit(solution)/shard_map/ppermute | solution.py:23
  98.6 23.4 %copy-start.3 = (bf16[2,128,12,128]{3,2,1,0:T(8,128)(2,1)S(1)}, bf16[2,128,12,128]{3,2,1,0:T(8,128)(2,1)}, u32[]{:S(2)}) copy-start(bf16[2,128,12,128]{3,2,1,0:T(8,128)(2,1)} %reshape_reshape.23) | copy-start | bytes 2359300
  125.6 10.4 %copy-start.1 = (f32[12,8,128,2,128]{4,2,3,1,0:T(8,128)}, f32[12,8,128,2,128]{4,2,3,1,0:T(8,128)S(1)}, u32[]{:S(2)}) copy-start(f32[12,8,128,2,128]{4,2,3,1,0:T(8,128)S(1)} %get-tuple-element.26) | copy-start | bytes 37748740
  139.3 21.2 %copy-start.4 = (bf16[4,128,12,128]{1,3,0,2:T(8,128)(2,1)S(1)}, bf16[4,128,12,128]{1,3,0,2:T(8,128)(2,1)}, u32[]{:S(2)}) copy-start(bf16[4,128,12,128]{1,3,0,2:T(8,128)(2,1)} %copy.38) | copy-start | bytes 4718596
  139.3 21.2 %copy-start.8 = (bf16[2,128,12,128]{1,3,0,2:T(8,128)(2,1)S(1)}, bf16[2,128,12,128]{1,3,0,2:T(8,128)(2,1)}, u32[]{:S(2)}) copy-start(bf16[2,128,12,128]{1,3,0,2:T(8,128)(2,1)} %copy.37) | copy-start | bytes 2359300
  152.0 8.5 %copy-start.19 = (f32[2,128,12]{1,0,2:T(2,128)S(1)}, f32[2,128,12]{1,0,2:T(2,128)}, u32[]{:S(2)}) copy-start(f32[2,128,12]{1,0,2:T(2,128)} %get-tuple-element.14) | copy-start | bytes 36868
  152.0 8.5 %copy-start.20 = (f32[2,128,12]{1,0,2:T(2,128)S(1)}, f32[2,128,12]{1,0,2:T(2,128)}, u32[]{:S(2)}) copy-start(f32[2,128,12]{1,0,2:T(2,128)} %get-tuple-element.15) | copy-start | bytes 36868
  152.0 8.5 %copy-start.21 = (f32[2,128,12]{1,0,2:T(2,128)S(1)}, f32[2,128,12]{1,0,2:T(2,128)}, u32[]{:S(2)}) copy-start(f32[2,128,12]{1,0,2:T(2,128)} %get-tuple-element.20) | copy-start | bytes 36868
  152.0 8.5 %copy-start.25 = (pred[2,6]{0,1:T(8,128)(4,1)S(1)}, pred[2,6]{0,1:T(8,128)(4,1)}, u32[]{:S(2)}) copy-start(pred[2,6]{0,1:T(8,128)(4,1)} %copy-done.24) | copy-start | bytes 40
  170.1 1.5 copy-start.10
  170.1 1.5 copy-start.11
  170.1 1.5 copy-start.12
  (11 other events, 13.6 us)
Sparse Core Ops, SparseCore 0:
  9.7 42.3 all-gather.4
  54.4 38.5 all-gather.6
  94.5 27.4 all-gather.8
  123.4 28.5 all-gather.10
where the time goes:
time: 185 us; the launch traced here: 184 us
  waiting for transfers between devices  86.7 us (47%)
  local copies, waits for them, and re-layouts  27.6 us (15%)
  matrix products  26.7 us (14%)
  other arithmetic  20 us (11%)
  between operations  13.6 us (7%)
  starting transfers between devices  9.56 us (5%)
    all_gather x1, waiting for transfers between devices, body(): lax.all_gather(text_v, ('rows', 'cols'), axis=0, tiled=True)  36.5 us
    another operation x13, local copies, waits for them, and re-layouts, split_heads(): flat_rows.reshape(flat_rows.shape[:-1] + (flat_rows.shape[-1] // HEAD_DIM...  20.9 us
    all_gather x1, waiting for transfers between devices, body(): lax.all_gather(text_k, ('rows', 'cols'), axis=0, tiled=True)  20 us
    all_gather x1, waiting for transfers between devices, body(): piece_keys = lax.all_gather(as_blocks(k_stale), 'rows', axis=0, tiled=True)  16.1 us
    dot_general x2, matrix products, attend(): jnp.einsum('bhqnk,nkhd->bqhd', weights, value_blocks, preferred_element_t...  15.8 us
    reduce_sum x2, other arithmetic, attend(): jnp.sum(weights.astype(jnp.float32), axis=(3, 4))  13 us
    all_gather x1, waiting for transfers between devices, body(): lax.all_gather(as_blocks(v_stale), 'rows', axis=0, tiled=True)  12.7 us
    dot_general x2, matrix products, attend(): jnp.einsum('bqhd,nkhd->bhqnk', queries, key_blocks, preferred_element_typ...  10.9 us
  transfers between devices with their start and end apart: 8, of which 4 were waited for; matrix products, arithmetic and copies ran while one was open for 36% of the time, Pallas kernels for 0%

commit v1 on v0

v1 whole, which is shorter than its diff:
```python
import functools
import math

import jax
import jax.numpy as jnp
from jax import lax
from jax.experimental import pallas as pl
from jax.experimental.pallas import tpu as pltpu
from jax.sharding import PartitionSpec as P

HEAD_DIM = 128
BLOCK_ROWS = 4
BLOCK_COLS = 32
PER_BLOCK = BLOCK_ROWS * BLOCK_COLS
SCORE_SCALE = 1.0 / math.sqrt(HEAD_DIM)
EXP2_SCALE = SCORE_SCALE * math.log2(math.e)
CHUNKS = 3
VMEM_LIMIT = 48 * 1024 * 1024


def extended(cells, sides, width):
    for axis, dim in sides:
        count = lax.axis_size(axis)
        ends = count - 1
        head = lax.slice_in_dim(cells, 0, width, axis=dim)
        tail = lax.slice_in_dim(cells, cells.shape[dim] - width, cells.shape[dim], axis=dim)
        cells = jnp.concatenate(
            [
                lax.ppermute(tail, axis, [(i, (i + 1) % count) for i in range(ends)]),
                cells,
                lax.ppermute(head, axis, [((i + 1) % count, i) for i in range(ends)]),
            ],
            axis=dim,
        )
    return cells


def position(v_fresh, conv_w):
    rows_here, cols_here, feature_width = v_fresh.shape
    rims = extended(v_fresh, (("rows", 0), ("cols", 1)), 1)
    position_term = jnp.zeros((rows_here, cols_here, feature_width), jnp.float32)
    for row_tap in range(3):
        for col_tap in range(3):
            position_term = position_term + conv_w[row_tap, col_tap] * rims[
                row_tap : row_tap + rows_here, col_tap : col_tap + cols_here
            ].astype(jnp.float32)
    return position_term


def split_heads(flat_rows):
    return flat_rows.reshape(flat_rows.shape[:-1] + (flat_rows.shape[-1] // HEAD_DIM, HEAD_DIM))


def attend(softmax_state, queries, key_blocks, value_blocks, allowed):
    old_peak, old_total, old_summed = softmax_state
    scores = (
        jnp.einsum(
            "bqhd,nkhd->bhqnk", queries, key_blocks, preferred_element_type=jnp.float32
        )
        * SCORE_SCALE
    )
    scores = jnp.where(allowed[:, None, None, :, None], scores, -1e30)
    new_peak = jnp.maximum(old_peak, jnp.max(scores, axis=(3, 4)))
    weights = jnp.exp(scores - new_peak[:, :, :, None, None]).astype(jnp.bfloat16)
    factor = jnp.exp(old_peak - new_peak)
    new_total = old_total * factor + jnp.sum(weights.astype(jnp.float32), axis=(3, 4))
    product = jnp.einsum(
        "bhqnk,nkhd->bqhd", weights, value_blocks, preferred_element_type=jnp.float32
    )
    new_summed = old_summed * jnp.transpose(factor, (0, 2, 1))[:, :, :, None] + product
    return (new_peak, new_total, new_summed)


def general_body(
    q_fresh, k_fresh, v_fresh, k_stale, v_stale, text_k, text_v, conv_w, reads, pattern, text_blocks
):
    rows_here, cols_here, feature_width = q_fresh.shape
    blocks_here = rows_here // BLOCK_ROWS
    head_count = feature_width // HEAD_DIM

    def as_blocks(grid_values):
        return split_heads(grid_values.reshape(blocks_here, PER_BLOCK, feature_width))

    queries = as_blocks(q_fresh)
    text_keys, text_values = (
        lax.all_gather(text_k, ("rows", "cols"), axis=0, tiled=True),
        lax.all_gather(text_v, ("rows", "cols"), axis=0, tiled=True),
    )
    text_count = text_keys.shape[0] // PER_BLOCK
    text_keys = split_heads(text_keys.reshape(text_count, PER_BLOCK, feature_width))
    text_values = split_heads(text_values.reshape(text_count, PER_BLOCK, feature_width))
    wanted = pattern[:, 0, :]
    fetch_rows = reads[0, 0, :]
    fetch_count = fetch_rows.shape[0]
    slot_count = blocks_here + fetch_count
    slot_mask = jnp.any(
        wanted[:, :, None] == jnp.arange(slot_count, dtype=jnp.int32)[None, None, :], axis=1
    )
    text_mask = jnp.any(
        text_blocks[:, 0, :, None] == jnp.arange(text_count, dtype=jnp.int32)[None, None, :], axis=1
    )
    softmax_state = (
        jnp.full((blocks_here, head_count, PER_BLOCK), -1e30, jnp.float32),
        jnp.zeros((blocks_here, head_count, PER_BLOCK), jnp.float32),
        jnp.zeros((blocks_here, PER_BLOCK, head_count, HEAD_DIM), jnp.float32),
    )
    softmax_state = attend(
        softmax_state,
        queries,
        jnp.concatenate([as_blocks(k_fresh), text_keys], axis=0),
        jnp.concatenate([as_blocks(v_fresh), text_values], axis=0),
        jnp.concatenate([slot_mask[:, :blocks_here], text_mask], axis=1),
    )
    chosen = jnp.where(
        wanted >= blocks_here, fetch_rows[jnp.clip(wanted - blocks_here, 0, fetch_count - 1)], -1
    )
    piece_keys = lax.all_gather(as_blocks(k_stale), "rows", axis=0, tiled=True)
    piece_values = lax.all_gather(as_blocks(v_stale), "rows", axis=0, tiled=True)
    block_rows = jnp.arange(piece_keys.shape[0], dtype=jnp.int32)
    piece_mask = jnp.any(chosen[:, :, None] == block_rows[None, None, :], axis=1)
    softmax_state = attend(softmax_state, queries, piece_keys, piece_values, piece_mask)
    _, final_total, final_summed = softmax_state
    mixed_rows = final_summed / jnp.transpose(final_total, (0, 2, 1))[:, :, :, None]
    attention = mixed_rows.reshape(rows_here, cols_here, feature_width)
    return attention + position(v_fresh, conv_w)


def head_scores(queries, keys):
    return lax.dot_general(
        queries, keys, (((1,), (1,)), ((), ())), preferred_element_type=jnp.float32
    )


def near_kernel(
    text_ref,
    q_ref,
    k_hbm,
    v_hbm,
    *rest,
):
    pieces = rest[:10]
    sum_ref, stat_ref, keys, values, sems = rest[10:]
    heads = q_ref.shape[1] // HEAD_DIM
    row = lax.axis_index("rows")
    col = lax.axis_index("cols")
    across, core = row // 2, row % 2
    shard = pieces[0].shape[0] // 4

    def start(source, first, target, block, at, count, which):
        pltpu.make_async_copy(
            source.at[pl.ds(first, count)], target.at[block, pl.ds(at, count)], sems.at[which, block]
        ).start()

    for block in range(2):
        start(k_hbm, block * PER_BLOCK, keys, block, 0, PER_BLOCK, 0)
        start(v_hbm, block * PER_BLOCK, values, block, 0, PER_BLOCK, 1)
        for turn in range(2):
            chosen = text_ref[block, 0, turn]
            first = pl.multiple_of(jnp.where(chosen // 2 == across, 0, 2 * shard), 2 * shard)
            at = PER_BLOCK * (1 + turn)

            def fetch(group):
                def one(source, step):
                    start(source, first, keys, block, at + step * shard, shard, 0)
                    start(source, first + shard, values, block, at + step * shard, shard, 1)

                for step in range(3):
                    one(group[step], step)

                @pl.when(col >= 2)
                def _():
                    one(group[3], 3)

                @pl.when(col < 2)
                def _():
                    one(group[4], 3)

            @pl.when(chosen % 2 == core)
            def _():
                fetch(pieces[:5])

            @pl.when(chosen % 2 != core)
            def _():
                fetch(pieces[5:])

    lane = lax.broadcasted_iota(jnp.int32, (PER_BLOCK, 128), 1)
    for block in range(2):
        rows = pl.ds(block * PER_BLOCK, PER_BLOCK)
        pltpu.make_async_copy(keys.at[block], keys.at[block], sems.at[0, block]).wait()
        pltpu.make_async_copy(values.at[block], values.at[block], sems.at[1, block]).wait()
        stats = jnp.zeros((PER_BLOCK, 128), jnp.float32)
        for head in range(heads):
            part = pl.ds(head * HEAD_DIM, HEAD_DIM)
            scores = head_scores(q_ref[rows, part], keys[block, :, part])
            peak = jnp.max(scores, axis=1, keepdims=True) * EXP2_SCALE
            weights = jnp.exp2(scores * EXP2_SCALE - peak).astype(jnp.bfloat16)
            total = jnp.sum(weights.astype(jnp.float32), axis=1, keepdims=True)
            sum_ref[rows, part] = jnp.dot(
                weights, values[block, :, part], preferred_element_type=jnp.float32
            )
            stats = jnp.where(lane == head, peak, stats)
            stats = jnp.where(lane == head + heads, total, stats)
        stat_ref[rows, :] = stats


def far_kernel(
    chunk, heads, reads_ref, pattern_ref, q_ref, sum_ref, stat_ref, term_ref, mate, across_, both, _, out_ref,
    keys, values, sems,
):
    row = lax.axis_index("rows")
    across, core = row // 2, row % 2
    half = mate.shape[0] // 2
    for block in range(2):
        slot = pattern_ref[block, 0, 0] + pattern_ref[block, 0, 1] - block - 2
        wanted = reads_ref[0, 0, slot]
        owner = wanted // 2
        first = pl.multiple_of((wanted % 2) * PER_BLOCK, PER_BLOCK)

        def fetch(source):
            pltpu.make_async_copy(
                source.at[pl.ds(first, PER_BLOCK)], keys.at[block], sems.at[0, block]
            ).start()
            pltpu.make_async_copy(
                source.at[pl.ds(half + first, PER_BLOCK)], values.at[block], sems.at[1, block]
            ).start()

        @pl.when(owner // 2 == across)
        def _():
            fetch(mate)

        @pl.when((owner // 2 != across) & (owner % 2 == core))
        def _():
            fetch(across_)

        @pl.when((owner // 2 != across) & (owner % 2 != core))
        def _():
            fetch(both)

    here = q_ref.shape[1] // HEAD_DIM
    for block in range(2):
        rows = pl.ds(block * PER_BLOCK, PER_BLOCK)
        pltpu.make_async_copy(keys.at[block], keys.at[block], sems.at[0, block]).wait()
        pltpu.make_async_copy(values.at[block], values.at[block], sems.at[1, block]).wait()
        for head in range(here):
            part = pl.ds(head * HEAD_DIM, HEAD_DIM)
            at = chunk * here + head
            old_peak = stat_ref[rows, at : at + 1]
            old_total = stat_ref[rows, at + heads : at + heads + 1]
            scores = head_scores(q_ref[rows, part], keys[block, :, part])
            peak = jnp.maximum(old_peak, jnp.max(scores, axis=1, keepdims=True) * EXP2_SCALE)
            weights = jnp.exp2(scores * EXP2_SCALE - peak).astype(jnp.bfloat16)
            factor = jnp.exp2(old_peak - peak)
            total = old_total * factor + jnp.sum(
                weights.astype(jnp.float32), axis=1, keepdims=True
            )
            product = jnp.dot(weights, values[block, :, part], preferred_element_type=jnp.float32)
            out_ref[rows, part] = (sum_ref[rows, part] * factor + product) / total + term_ref[
                rows, part
            ]


def body(
    q_fresh, k_fresh, v_fresh, k_stale, v_stale, text_k, text_v, conv_w, reads, pattern, text_blocks
):
    rows_here, cols_here, width = q_fresh.shape
    tokens = rows_here * cols_here
    heads = width // HEAD_DIM
    shard = text_k.shape[0]
    swap = [(r, (r + 2) % 4) for r in range(4)]
    mates = [(r, r ^ 1) for r in range(4)]

    def flat(grid_values):
        return grid_values.reshape(tokens, width)

    def to_mate(values):
        return lax.ppermute(values, "rows", mates)

    q, k, v = flat(q_fresh), flat(k_fresh), flat(v_fresh)
    k_old, v_old = flat(k_stale), flat(v_stale)

    across_k = lax.ppermute(text_k, "rows", swap)
    across_v = lax.ppermute(text_v, "rows", swap)
    step = width // CHUNKS
    packed = [
        jnp.concatenate(
            [k_old[:, i * step : (i + 1) * step], v_old[:, i * step : (i + 1) * step]], axis=0
        )
        for i in range(CHUNKS)
    ]
    far = [lax.ppermute(p, "rows", swap) for p in packed]

    text = jnp.concatenate([text_k, text_v, across_k, across_v], axis=0)
    left = lax.ppermute(text, "cols", [(i, (i + 1) % 4) for i in range(4)])
    right = lax.ppermute(text, "cols", [((i + 1) % 4, i) for i in range(4)])
    upper = lax.ppermute(left, "cols", [(1, 2), (2, 3)])
    lower = lax.ppermute(right, "cols", [(1, 0), (2, 1)])
    pieces = [text, left, right, upper, lower]
    pieces = pieces + [to_mate(p) for p in pieces]
    term = position(v_fresh, conv_w).reshape(tokens, width)

    any_space = pl.BlockSpec(memory_space=pl.ANY)
    params = pltpu.CompilerParams(vmem_limit_bytes=VMEM_LIMIT)
    key_count = PER_BLOCK * 3
    summed, stats = pl.pallas_call(
        near_kernel,
        out_shape=(
            jax.ShapeDtypeStruct((tokens, width), jnp.float32),
            jax.ShapeDtypeStruct((tokens, 128), jnp.float32),
        ),
        grid_spec=pltpu.PrefetchScalarGridSpec(
            num_scalar_prefetch=1,
            grid=(1,),
            in_specs=[pl.BlockSpec((tokens, width), lambda i, *_: (0, 0))] + [any_space] * 12,
            out_specs=(
                pl.BlockSpec((tokens, width), lambda i, *_: (0, 0)),
                pl.BlockSpec((tokens, 128), lambda i, *_: (0, 0)),
            ),
            scratch_shapes=[
                pltpu.VMEM((2, key_count, width), jnp.bfloat16),
                pltpu.VMEM((2, key_count, width), jnp.bfloat16),
                pltpu.SemaphoreType.DMA((2, 2)),
            ],
        ),
        compiler_params=params,
        name="near",
    )(text_blocks, q, k, v, *pieces)

    out = None
    for chunk in range(CHUNKS):
        arrived = [to_mate(packed[chunk]), far[chunk], to_mate(far[chunk])]
        part = pl.BlockSpec((tokens, step), lambda i, *_, chunk=chunk: (0, chunk))
        out = pl.pallas_call(
            functools.partial(far_kernel, chunk, heads)
            if out is not None
            else lambda *refs: far_kernel(0, heads, *refs[:9], None, *refs[9:]),
            out_shape=jax.ShapeDtypeStruct((tokens, width), jnp.float32),
            grid_spec=pltpu.PrefetchScalarGridSpec(
                num_scalar_prefetch=2,
                grid=(1,),
                in_specs=[
                    part,
                    part,
                    pl.BlockSpec((tokens, 128), lambda i, *_: (0, 0)),
                    part,
                    any_space,
                    any_space,
                    any_space,
                ]
                + ([any_space] if out is not None else []),
                out_specs=part,
                scratch_shapes=[
                    pltpu.VMEM((2, PER_BLOCK, step), jnp.bfloat16),
                    pltpu.VMEM((2, PER_BLOCK, step), jnp.bfloat16),
                    pltpu.SemaphoreType.DMA((2, 2)),
                ],
            ),
            input_output_aliases={9: 0} if out is not None else {},
            compiler_params=params,
            name=f"far{chunk}",
        )(reads, pattern, q, summed, stats, term, *arrived, *([out] if out is not None else []))
    return out.reshape(rows_here, cols_here, width)


def fits(mesh, reads, pattern, text_k):
    sizes = dict(mesh.shape)
    return (
        sizes["rows"] == 4
        and sizes["cols"] == 4
        and reads.shape[-1] == 2
        and pattern.shape[-1] == 2
        and pattern.shape[0] == 2 * sizes["groups"] * 4
        and text_k.shape[0] == sizes["groups"] * 4 * PER_BLOCK
    )


def solution(mesh):
    grid = P(("groups", "rows"), "cols", None)
    text = P(("groups", "rows", "cols"), None)
    in_specs = (grid, grid, grid, grid, grid, text, text, P(), grid, grid, grid)

    def program(*args):
        chosen = body if fits(mesh, args[8], args[9], args[5]) else general_body
        return jax.shard_map(
            chosen, mesh=mesh, in_specs=in_specs, out_specs=grid, check_vma=False
        )(*args)

    return program
```

time: 185 us -> 103 us (0.56)
  waiting for transfers between devices: 86.7 us -> 44.7 us
  Pallas kernels: 0 us -> 27.8 us
  matrix products: 26.7 us -> 0 us
  local copies, waits for them, and re-layouts: 27.6 us -> 5.18 us
  other arithmetic: 20 us -> 3.07 us
  between operations: 13.6 us -> 0.36 us
  starting transfers between devices: 9.56 us -> 21.3 us
    all_gather x4 -> x0, waiting for transfers between devices: 85.3 us -> none  [the longest x1 36.5 us: body(): lax.all_gather(text_v, ('rows', 'cols'), axis=0, tiled=True)]
    pallas_call x0 -> x4, Pallas kernels: none -> 27.8 us  [the longest x3 15.1 us: body(): pl.pallas_call(functools.partial(far_kernel, chunk, heads) if out is not...]
    dot_general x4 -> x0, matrix products: 26.7 us -> none  [the longest x2 15.8 us: attend(): jnp.einsum('bhqnk,nkhd->bqhd', weights, value_blocks, preferred_element_t...]
    ppermute x0 -> x20, waiting for transfers between devices: none -> 24.6 us  [the longest x3 20.7 us: body(): far = [lax.ppermute(p, 'rows', swap) for p in packed]]
    another operation x13 -> x0, local copies, waits for them, and re-layouts: 20.9 us -> none  [split_heads(): flat_rows.reshape(flat_rows.shape[:-1] + (flat_rows.shape[-1] // HEAD_DIM...]
    ppermute x2, waiting for transfers between devices: 0.01 us -> 14.8 us  [extended(): lax.ppermute(tail, axis, [(i, (i + 1) % count) for i in range(ends)])]
    ppermute x0 -> x20, starting transfers between devices: none -> 14.4 us  [the longest x1 4.91 us: body(): across_k = lax.ppermute(text_k, 'rows', swap)]
    reduce_sum x2 -> x0, other arithmetic: 13 us -> none  [attend(): jnp.sum(weights.astype(jnp.float32), axis=(3, 4))]
  transfers between devices with their start and end apart: 8 -> 24, of which waited for: 4 -> 6; matrix products, arithmetic and copies ran while one was open for 36% -> 6% of each run, Pallas kernels for 0% -> 22%
where the time goes in v1:
time: 103 us; the launch traced here: 102 us
  waiting for transfers between devices  44.7 us (43%)
  Pallas kernels  27.8 us (27%)
  starting transfers between devices  21.3 us (21%)
  local copies, waits for them, and re-layouts  5.18 us (5%)
  other arithmetic  3.07 us (3%)
    ppermute x3, waiting for transfers between devices, body(): far = [lax.ppermute(p, 'rows', swap) for p in packed]  20.7 us
    pallas_call x3, Pallas kernels, body(): pl.pallas_call(functools.partial(far_kernel, chunk, heads) if out is not...  15.1 us
    ppermute x2, waiting for transfers between devices, extended(): lax.ppermute(tail, axis, [(i, (i + 1) % count) for i in range(ends)])  14.8 us
    pallas_call x1, Pallas kernels, body(): pl.pallas_call(near_kernel, out_shape=(jax.ShapeDtypeStruct((tokens, widt...  12.7 us
    ppermute x2, waiting for transfers between devices, extended(): lax.ppermute(head, axis, [((i + 1) % count, i) for i in range(ends)])  5.24 us
    ppermute x1, starting transfers between devices, body(): across_k = lax.ppermute(text_k, 'rows', swap)  4.91 us
    ppermute x2, starting transfers between devices, extended(): lax.ppermute(tail, axis, [(i, (i + 1) % count) for i in range(ends)])  4.26 us
    ppermute x1, starting transfers between devices, body(): right = lax.ppermute(text, 'cols', [((i + 1) % 4, i) for i in range(4)])  3.65 us
  transfers between devices with their start and end apart: 24, of which 6 were waited for; matrix products, arithmetic and copies ran while one was open for 6% of the time, Pallas kernels for 22%

profile of v1, /device:TPU:0, one launch (start us, length us, event | category | flops | bytes accessed | tf_op | source)
XLA Modules:
  0.0 102.4 jit_solution(7357799338281501875)
XLA Ops:
  0.0 1.0 fusion.7
  1.0 2.4 %collective-permute-start.11 = (bf16[1,32,1536]{2,1,0:T(8,128)(2,1)S(1)}, bf16[1,32,1536]{2,1,0:T(8,128)(2,1)S(1)}, u32[]{:S(2)}, u32[]{:S(2)}) collective-permute-start(bf16[1,32,1536]{2,1,0:T(8,128)(2,1)S(1)} %get-tuple-element.27), channel_id=1, source_target_pairs={{0,4},{4,8},{8,12},{1,5},{5,9},{9,13},{2,6},{6,10},{10,14},{3,7},{... | collective-permute-start | bytes 294920 | tf_op jit(solution)/shard_map/ppermute | solution.py:29
  3.3 1.3 %collective-permute-start.12 = (bf16[1,32,1536]{2,1,0:T(8,128)(2,1)S(1)}, bf16[1,32,1536]{2,1,0:T(8,128)(2,1)S(1)}, u32[]{:S(2)}, u32[]{:S(2)}) collective-permute-start(bf16[1,32,1536]{2,1,0:T(8,128)(2,1)S(1)} %get-tuple-element.26), channel_id=1, source_target_pairs={{4,0},{8,4},{12,8},{5,1},{9,5},{13,9},{6,2},{10,6},{14,10},{7,3},{... | collective-permute-start | bytes 294920 | tf_op jit(solution)/shard_map/ppermute | solution.py:31
  4.6 4.9 %collective-permute-start = (bf16[32,1536]{1,0:T(8,128)(2,1)}, bf16[32,1536]{1,0:T(8,128)(2,1)S(1)}, u32[]{:S(2)}, u32[]{:S(2)}) collective-permute-start(bf16[32,1536]{1,0:T(8,128)(2,1)} %param.16), channel_id=1, source_target_pairs={{0,8},{4,12},{8,0},{12,4},{1,9},{5,13},{9,1},{13,5},{2,10},{6,14},... | collective-permute-start | bytes 294920 | tf_op jit(solution)/shard_map/ppermute | solution.py:281
  9.6 0.9 constant_dynamic-update-slice_fusion.3
  10.5 1.5 %fusion.5 = (bf16[256,512]{1,0:T(8,128)(2,1)S(1)}, bf16[256,512]{1,0:T(8,128)(2,1)S(1)}, bf16[256,512]{1,0:T(8,128)(2,1)S(1)}, bf16[256,512]{1,0:T(8,128)(2,1)S(...) fusion(bf16[256,1536]{1,0:T(8,128)(2,1)} %bitcast.16, bf16[256,1536]{1,0:T(8,128)(2,1)} %bitcast.17), kind=kLoop, calls=%fused_computation.37 | loop fusion | bytes 3145728 | tf_op jit(solution)/shard_map/slice | solution.py:286
  12.1 2.8 %collective-permute-done = bf16[32,1536]{1,0:T(8,128)(2,1)S(1)} collective-permute-done((bf16[32,1536]{1,0:T(8,128)(2,1)}, bf16[32,1536]{1,0:T(8,128)(2,1)S(1)}, u32[]{:S(2)}, u32[]{:S(2)}) %collective-permute-start) | collective-permute-done | bytes 98336 | tf_op jit(solution)/shard_map/ppermute | solution.py:281
  14.9 1.0 %collective-permute-done.1 = bf16[32,1536]{1,0:T(8,128)(2,1)S(1)} collective-permute-done((bf16[32,1536]{1,0:T(8,128)(2,1)}, bf16[32,1536]{1,0:T(8,128)(2,1)S(1)}, u32[]{:S(2)}, u32[]{:S(2)}) %collective-permute-start.1) | collective-permute-done | bytes 98336 | tf_op jit(solution)/shard_map/ppermute | solution.py:282
  16.0 3.7 %collective-permute-start.3 = (bf16[128,1536]{1,0:T(8,128)(2,1)S(1)}, bf16[128,1536]{1,0:T(8,128)(2,1)S(1)}, u32[]{:S(2)}, u32[]{:S(2)}) collective-permute-start(bf16[128,1536]{1,0:T(8,128)(2,1)S(1)} %constant_dynamic-update-slice_fusion.rest_0_), channel_id=1, source_target_pairs={{1,0},{2,1},{3,2},{0,3},{5,4},{6,5},{7,6},{4,7},{9,8},{10,9},{11,1... | collective-permute-start | bytes 1179656 | tf_op jit(solution)/shard_map/ppermute | solution.py:294
  19.9 1.9 %collective-permute-start.13 = (bf16[10,1,1536]{2,1,0:T(2,128)(2,1)S(1)}, bf16[10,1,1536]{2,1,0:T(2,128)(2,1)S(1)}, u32[]{:S(2)}, u32[]{:S(2)}) collective-permute-start(bf16[10,1,1536]{2,1,0:T(2,128)(2,1)S(1)} %get-tuple-element.18), channel_id=1, source_target_pairs={{0,1},{1,2},{2,3},{4,5},{5,6},{6,7},{8,9},{9,10},{10,11},{12,13},{... | collective-permute-start | bytes 92168 | tf_op jit(solution)/shard_map/ppermute | solution.py:29
  21.9 14.8 %collective-permute-done.13 = bf16[10,1,1536]{2,1,0:T(2,128)(2,1)S(1)} collective-permute-done((bf16[10,1,1536]{2,1,0:T(2,128)(2,1)S(1)}, bf16[10,1,1536]{2,1,0:T(2,128)(2,1)S(1)}, u32[]{:S(2)}, u32[]{:S(2)}) %collective-permute-start.13) | collective-permute-done | bytes 30752 | tf_op jit(solution)/shard_map/ppermute | solution.py:29
  36.8 1.3 %collective-permute-start.14 = (bf16[10,1,1536]{2,1,0:T(2,128)(2,1)S(1)}, bf16[10,1,1536]{2,1,0:T(2,128)(2,1)S(1)}, u32[]{:S(2)}, u32[]{:S(2)}) collective-permute-start(bf16[10,1,1536]{2,1,0:T(2,128)(2,1)S(1)} %get-tuple-element.19), channel_id=1, source_target_pairs={{1,0},{2,1},{3,2},{5,4},{6,5},{7,6},{9,8},{10,9},{11,10},{13,12},{... | collective-permute-start | bytes 92168 | tf_op jit(solution)/shard_map/ppermute | solution.py:31
  38.1 5.2 %collective-permute-done.14 = bf16[10,1,1536]{2,1,0:T(2,128)(2,1)S(1)} collective-permute-done((bf16[10,1,1536]{2,1,0:T(2,128)(2,1)S(1)}, bf16[10,1,1536]{2,1,0:T(2,128)(2,1)S(1)}, u32[]{:S(2)}, u32[]{:S(2)}) %collective-permute-start.14) | collective-permute-done | bytes 30752 | tf_op jit(solution)/shard_map/ppermute | solution.py:31
  43.4 1.3 %collective-permute-start.5 = (bf16[128,1536]{1,0:T(8,128)(2,1)S(1)}, bf16[128,1536]{1,0:T(8,128)(2,1)S(1)}, u32[]{:S(2)}, u32[]{:S(2)}) collective-permute-start(bf16[128,1536]{1,0:T(8,128)(2,1)S(1)} %collective-permute-done.3.rest_2_), channel_id=1, source_target_pairs={{1,0},{2,1},{5,4},{6,5},{9,8},{10,9},{13,12},{14,13},{17,16},{18,1... | collective-permute-start | bytes 1179656 | tf_op jit(solution)/shard_map/ppermute | solution.py:296
  44.7 0.7 collective-permute-start.4
  45.4 2.1 %collective-permute-start.16 = (bf16[512,512]{1,0:T(8,128)(2,1)S(1)}, bf16[512,512]{1,0:T(8,128)(2,1)S(1)}, u32[]{:S(2)}, u32[]{:S(2)}) collective-permute-start(bf16[512,512]{1,0:T(8,128)(2,1)S(1)} %pad_maximum_fusion.4), channel_id=1, source_target_pairs={{0,8},{4,12},{8,0},{12,4},{1,9},{5,13},{9,1},{13,5},{2,10},{6,14},... | collective-permute-start | bytes 1572872 | tf_op jit(solution)/shard_map/ppermute | solution.py:290
  47.5 10.6 %collective-permute-done.19.across_ = bf16[512,512]{1,0:T(8,128)(2,1)S(1)} collective-permute-done((bf16[512,512]{1,0:T(8,128)(2,1)S(1)}, bf16[512,512]{1,0:T(8,128)(2,1)S(1)}, u32[]{:S(2)}, u32[]{:S(2)}) %collective-permute-start.19) | collective-permute-done | bytes 524320 | tf_op jit(solution)/shard_map/ppermute | solution.py:290
  58.8 10.1 %collective-permute-done.16.across_ = bf16[512,512]{1,0:T(8,128)(2,1)S(1)} collective-permute-done((bf16[512,512]{1,0:T(8,128)(2,1)S(1)}, bf16[512,512]{1,0:T(8,128)(2,1)S(1)}, u32[]{:S(2)}, u32[]{:S(2)}) %collective-permute-start.16) | collective-permute-done | bytes 524320 | tf_op jit(solution)/shard_map/ppermute | solution.py:290
  70.0 3.0 %multiply_add_fusion = f32[8,32,1536]{2,1,0:T(8,128)S(1)} fusion(bf16[8,32,1536]{2,1,0:T(8,128)(2,1)S(1)} %copy-done.6, bf16[10,32,1536]{2,1,0:T(8,128)(2,1)S(1)} %constant_dynamic-update-slice_fusion.4, bf16[10,1,1536]{2,1,0:T(2,128)(2,1)S(1)} %collective-permute-done.14, bf16[10,1,1536]{2,1,0:T(2,128)(2,1)S(1)} %collective-permute-done.13, ...), kind=kLoop, calls=%fused_computation.4 | loop fusion | flops 19660800 | bytes 3655680 | tf_op jit(solution)/shard_map/add | solution.py:44
  73.1 12.7 %near.1 = (f32[256,1536]{1,0:T(8,128)}, f32[256,128]{1,0:T(8,128)S(1)}) custom-call(s32[2,1,2]{2,1,0:T(1,128)S(1)} %copy-done.5, bf16[256,1536]{1,0:T(8,128)(2,1)S(1)} %bitcast.10, bf16[256,1536]{1,0:T(8,128)(2,1)S(1)} %bitcast.14, bf16[256,1536]{1,0:T(8,128)(2,1)} %bitcast.15, bf16[128,1536]{1,0:T(8,128)(2,1)S(1)} %constant_dynamic-update-slice_fusion.rest_0_, ...), custom_call_target="tpu_custom_call" | custom-call | tf_op jit(solution)/shard_map/near/pallas_call | solution.py:304
  85.9 1.4 %copy-done = f32[256,1536]{1,0:T(8,128)S(1)} copy-done((f32[256,1536]{1,0:T(8,128)S(1)}, f32[256,1536]{1,0:T(8,128)}, u32[]{:S(2)}) %copy-start) | copy-done | bytes 1572888
  87.3 5.0 %far0.1._ = f32[256,1536]{1,0:T(8,128)} custom-call(s32[1,1,2]{2,1,0:T(1,128)S(1)} %copy-done.4, s32[2,1,2]{2,1,0:T(1,128)S(1)} %copy-done.3, bf16[256,1536]{1,0:T(8,128)(2,1)S(1)} %bitcast.11, f32[256,1536]{1,0:T(8,128)S(1)} %copy-done, f32[256,128]{1,0:T(8,128)S(1)} %get-tuple-element.8.refs_4_.stat_ref, f32[256,1536]{1,0:T(8,128)S(1)} %bitcast.7, ...), custom_call_target="tpu_custom_call" | custom-call | tf_op jit(solution)/shard_map/far0/pallas_call | solution.py:332
  92.3 5.0 %far1.1._ = f32[256,1536]{1,0:T(8,128)} custom-call(s32[1,1,2]{2,1,0:T(1,128)S(1)} %copy-done.4, s32[2,1,2]{2,1,0:T(1,128)S(1)} %copy-done.3, bf16[256,1536]{1,0:T(8,128)(2,1)S(1)} %bitcast.12, f32[256,1536]{1,0:T(8,128)S(1)} %copy-done, f32[256,128]{1,0:T(8,128)S(1)} %get-tuple-element.8.refs_4_.stat_ref, ...), custom_call_target="tpu_custom_call", output_to_operand_aliasing={{}: (9, {})} | custom-call | tf_op jit(solution)/shard_map/far1/pallas_call | solution.py:332
  97.4 5.0 %far2.1 = f32[256,1536]{1,0:T(8,128)} custom-call(s32[1,1,2]{2,1,0:T(1,128)S(1)} %copy-done.4, s32[2,1,2]{2,1,0:T(1,128)S(1)} %copy-done.3, bf16[256,1536]{1,0:T(8,128)(2,1)S(1)} %bitcast.13, f32[256,1536]{1,0:T(8,128)S(1)} %copy-done, f32[256,128]{1,0:T(8,128)S(1)} %get-tuple-element.8.refs_4_.stat_ref, ...), custom_call_target="tpu_custom_call", output_to_operand_aliasing={{}: (9, {})} | custom-call | tf_op jit(solution)/shard_map/far2/pallas_call | solution.py:332
  (61 shorter events, 2.4 us)
Async XLA Ops:
  1.0 18.7 %collective-permute-start.11 = (bf16[1,32,1536]{2,1,0:T(8,128)(2,1)S(1)}, bf16[1,32,1536]{2,1,0:T(8,128)(2,1)S(1)}, u32[]{:S(2)}, u32[]{:S(2)}) collective-permute-start(bf16[1,32,1536]{2,1,0:T(8,128)(2,1)S(1)} %get-tuple-element.27), channel_id=1, source_target_pairs={{0,4},{4,8},{8,12},{1,5},{5,9},{9,13},{2,6},{6,10},{10,14},{3,7},{... | collective-permute-start | bytes 294920 | tf_op jit(solution)/shard_map/ppermute | solution.py:29
  3.3 16.4 %collective-permute-start.12 = (bf16[1,32,1536]{2,1,0:T(8,128)(2,1)S(1)}, bf16[1,32,1536]{2,1,0:T(8,128)(2,1)S(1)}, u32[]{:S(2)}, u32[]{:S(2)}) collective-permute-start(bf16[1,32,1536]{2,1,0:T(8,128)(2,1)S(1)} %get-tuple-element.26), channel_id=1, source_target_pairs={{4,0},{8,4},{12,8},{5,1},{9,5},{13,9},{6,2},{10,6},{14,10},{7,3},{... | collective-permute-start | bytes 294920 | tf_op jit(solution)/shard_map/ppermute | solution.py:31
  4.6 10.3 %collective-permute-start = (bf16[32,1536]{1,0:T(8,128)(2,1)}, bf16[32,1536]{1,0:T(8,128)(2,1)S(1)}, u32[]{:S(2)}, u32[]{:S(2)}) collective-permute-start(bf16[32,1536]{1,0:T(8,128)(2,1)} %param.16), channel_id=1, source_target_pairs={{0,8},{4,12},{8,0},{12,4},{1,9},{5,13},{9,1},{13,5},{2,10},{6,14},... | collective-permute-start | bytes 294920 | tf_op jit(solution)/shard_map/ppermute | solution.py:281
  9.5 6.5 %collective-permute-start.1 = (bf16[32,1536]{1,0:T(8,128)(2,1)}, bf16[32,1536]{1,0:T(8,128)(2,1)S(1)}, u32[]{:S(2)}, u32[]{:S(2)}) collective-permute-start(bf16[32,1536]{1,0:T(8,128)(2,1)} %param.17), channel_id=1, source_target_pairs={{0,8},{4,12},{8,0},{12,4},{1,9},{5,13},{9,1},{13,5},{2,10},{6,14},... | collective-permute-start | bytes 294920 | tf_op jit(solution)/shard_map/ppermute | solution.py:282
  16.0 27.4 %collective-permute-start.3 = (bf16[128,1536]{1,0:T(8,128)(2,1)S(1)}, bf16[128,1536]{1,0:T(8,128)(2,1)S(1)}, u32[]{:S(2)}, u32[]{:S(2)}) collective-permute-start(bf16[128,1536]{1,0:T(8,128)(2,1)S(1)} %constant_dynamic-update-slice_fusion.rest_0_), channel_id=1, source_target_pairs={{1,0},{2,1},{3,2},{0,3},{5,4},{6,5},{7,6},{4,7},{9,8},{10,9},{11,1... | collective-permute-start | bytes 1179656 | tf_op jit(solution)/shard_map/ppermute | solution.py:294
  19.7 23.7 %collective-permute-start.2 = (bf16[128,1536]{1,0:T(8,128)(2,1)S(1)}, bf16[128,1536]{1,0:T(8,128)(2,1)S(1)}, u32[]{:S(2)}, u32[]{:S(2)}) collective-permute-start(bf16[128,1536]{1,0:T(8,128)(2,1)S(1)} %constant_dynamic-update-slice_fusion.rest_0_), channel_id=1, source_target_pairs={{0,1},{1,2},{2,3},{3,0},{4,5},{5,6},{6,7},{7,4},{8,9},{9,10},{10,1... | collective-permute-start | bytes 1179656 | tf_op jit(solution)/shard_map/ppermute | solution.py:293
  19.7 25.0 %collective-permute-start.6 = (bf16[128,1536]{1,0:T(8,128)(2,1)S(1)}, bf16[128,1536]{1,0:T(8,128)(2,1)S(1)}, u32[]{:S(2)}, u32[]{:S(2)}) collective-permute-start(bf16[128,1536]{1,0:T(8,128)(2,1)S(1)} %constant_dynamic-update-slice_fusion.rest_0_), channel_id=1, source_target_pairs={{0,4},{4,0},{8,12},{12,8},{1,5},{5,1},{9,13},{13,9},{2,6},{6,2},{1... | collective-permute-start | bytes 1179656 | tf_op jit(solution)/shard_map/ppermute | solution.py:276
  19.9 16.9 %collective-permute-start.13 = (bf16[10,1,1536]{2,1,0:T(2,128)(2,1)S(1)}, bf16[10,1,1536]{2,1,0:T(2,128)(2,1)S(1)}, u32[]{:S(2)}, u32[]{:S(2)}) collective-permute-start(bf16[10,1,1536]{2,1,0:T(2,128)(2,1)S(1)} %get-tuple-element.18), channel_id=1, source_target_pairs={{0,1},{1,2},{2,3},{4,5},{5,6},{6,7},{8,9},{9,10},{10,11},{12,13},{... | collective-permute-start | bytes 92168 | tf_op jit(solution)/shard_map/ppermute | solution.py:29
  21.9 23.6 %collective-permute-start.22 = (bf16[512,512]{1,0:T(8,128)(2,1)S(1)}, bf16[512,512]{1,0:T(8,128)(2,1)S(1)}, u32[]{:S(2)}, u32[]{:S(2)}) collective-permute-start(bf16[512,512]{1,0:T(8,128)(2,1)S(1)} %pad_maximum_fusion.6), channel_id=1, source_target_pairs={{0,8},{4,12},{8,0},{12,4},{1,9},{5,13},{9,1},{13,5},{2,10},{6,14},... | collective-permute-start | bytes 1572872 | tf_op jit(solution)/shard_map/ppermute | solution.py:290
  36.8 6.6 %collective-permute-start.14 = (bf16[10,1,1536]{2,1,0:T(2,128)(2,1)S(1)}, bf16[10,1,1536]{2,1,0:T(2,128)(2,1)S(1)}, u32[]{:S(2)}, u32[]{:S(2)}) collective-permute-start(bf16[10,1,1536]{2,1,0:T(2,128)(2,1)S(1)} %get-tuple-element.19), channel_id=1, source_target_pairs={{1,0},{2,1},{3,2},{5,4},{6,5},{7,6},{9,8},{10,9},{11,10},{13,12},{... | collective-permute-start | bytes 92168 | tf_op jit(solution)/shard_map/ppermute | solution.py:31
  43.4 4.2 %collective-permute-start.21 = (bf16[512,512]{1,0:T(8,128)(2,1)S(1)}, bf16[512,512]{1,0:T(8,128)(2,1)S(1)}, u32[]{:S(2)}, u32[]{:S(2)}) collective-permute-start(bf16[512,512]{1,0:T(8,128)(2,1)S(1)} %pad_maximum_fusion.6), channel_id=1, source_target_pairs={{0,4},{4,0},{8,12},{12,8},{1,5},{5,1},{9,13},{13,9},{2,6},{6,2},{1... | collective-permute-start | bytes 1572872 | tf_op jit(solution)/shard_map/ppermute | solution.py:276
  43.4 14.7 %collective-permute-start.19 = (bf16[512,512]{1,0:T(8,128)(2,1)S(1)}, bf16[512,512]{1,0:T(8,128)(2,1)S(1)}, u32[]{:S(2)}, u32[]{:S(2)}) collective-permute-start(bf16[512,512]{1,0:T(8,128)(2,1)S(1)} %pad_maximum_fusion.5), channel_id=1, source_target_pairs={{0,8},{4,12},{8,0},{12,4},{1,9},{5,13},{9,1},{13,5},{2,10},{6,14},... | collective-permute-start | bytes 1572872 | tf_op jit(solution)/shard_map/ppermute | solution.py:290
  43.4 14.7 %collective-permute-start.5 = (bf16[128,1536]{1,0:T(8,128)(2,1)S(1)}, bf16[128,1536]{1,0:T(8,128)(2,1)S(1)}, u32[]{:S(2)}, u32[]{:S(2)}) collective-permute-start(bf16[128,1536]{1,0:T(8,128)(2,1)S(1)} %collective-permute-done.3.rest_2_), channel_id=1, source_target_pairs={{1,0},{2,1},{5,4},{6,5},{9,8},{10,9},{13,12},{14,13},{17,16},{18,1... | collective-permute-start | bytes 1179656 | tf_op jit(solution)/shard_map/ppermute | solution.py:296
  44.7 13.9 %collective-permute-start.4 = (bf16[128,1536]{1,0:T(8,128)(2,1)S(1)}, bf16[128,1536]{1,0:T(8,128)(2,1)S(1)}, u32[]{:S(2)}, u32[]{:S(2)}) collective-permute-start(bf16[128,1536]{1,0:T(8,128)(2,1)S(1)} %collective-permute-done.2.rest_1_), channel_id=1, source_target_pairs={{1,2},{2,3},{5,6},{6,7},{9,10},{10,11},{13,14},{14,15},{17,18},{18... | collective-permute-start | bytes 1179656 | tf_op jit(solution)/shard_map/ppermute | solution.py:295
  45.4 23.5 %collective-permute-start.16 = (bf16[512,512]{1,0:T(8,128)(2,1)S(1)}, bf16[512,512]{1,0:T(8,128)(2,1)S(1)}, u32[]{:S(2)}, u32[]{:S(2)}) collective-permute-start(bf16[512,512]{1,0:T(8,128)(2,1)S(1)} %pad_maximum_fusion.4), channel_id=1, source_target_pairs={{0,8},{4,12},{8,0},{12,4},{1,9},{5,13},{9,1},{13,5},{2,10},{6,14},... | collective-permute-start | bytes 1572872 | tf_op jit(solution)/shard_map/ppermute | solution.py:290
  47.5 21.4 %collective-permute-start.7 = (bf16[128,1536]{1,0:T(8,128)(2,1)S(1)}, bf16[128,1536]{1,0:T(8,128)(2,1)S(1)}, u32[]{:S(2)}, u32[]{:S(2)}) collective-permute-start(bf16[128,1536]{1,0:T(8,128)(2,1)S(1)} %collective-permute-done.2.rest_1_), channel_id=1, source_target_pairs={{0,4},{4,0},{8,12},{12,8},{1,5},{5,1},{9,13},{13,9},{2,6},{6,2},{1... | collective-permute-start | bytes 1179656 | tf_op jit(solution)/shard_map/ppermute | solution.py:276
  58.1 11.4 %collective-permute-start.8 = (bf16[128,1536]{1,0:T(8,128)(2,1)S(1)}, bf16[128,1536]{1,0:T(8,128)(2,1)S(1)}, u32[]{:S(2)}, u32[]{:S(2)}) collective-permute-start(bf16[128,1536]{1,0:T(8,128)(2,1)S(1)} %collective-permute-done.3.rest_2_), channel_id=1, source_target_pairs={{0,4},{4,0},{8,12},{12,8},{1,5},{5,1},{9,13},{13,9},{2,6},{6,2},{1... | collective-permute-start | bytes 1179656 | tf_op jit(solution)/shard_map/ppermute | solution.py:276
  58.1 11.4 %collective-permute-start.10 = (bf16[128,1536]{1,0:T(8,128)(2,1)S(1)}, bf16[128,1536]{1,0:T(8,128)(2,1)S(1)}, u32[]{:S(2)}, u32[]{:S(2)}) collective-permute-start(bf16[128,1536]{1,0:T(8,128)(2,1)S(1)} %collective-permute-done.5.rest_4_), channel_id=1, source_target_pairs={{0,4},{4,0},{8,12},{12,8},{1,5},{5,1},{9,13},{13,9},{2,6},{6,2},{1... | collective-permute-start | bytes 1179656 | tf_op jit(solution)/shard_map/ppermute | solution.py:276
  58.6 11.4 %collective-permute-start.9 = (bf16[128,1536]{1,0:T(8,128)(2,1)S(1)}, bf16[128,1536]{1,0:T(8,128)(2,1)S(1)}, u32[]{:S(2)}, u32[]{:S(2)}) collective-permute-start(bf16[128,1536]{1,0:T(8,128)(2,1)S(1)} %collective-permute-done.4.rest_3_), channel_id=1, source_target_pairs={{0,4},{4,0},{8,12},{12,8},{1,5},{5,1},{9,13},{13,9},{2,6},{6,2},{1... | collective-permute-start | bytes 1179656 | tf_op jit(solution)/shard_map/ppermute | solution.py:276
  68.9 23.4 %collective-permute-start.18 = (bf16[512,512]{1,0:T(8,128)(2,1)S(1)}, bf16[512,512]{1,0:T(8,128)(2,1)S(1)}, u32[]{:S(2)}, u32[]{:S(2)}) collective-permute-start(bf16[512,512]{1,0:T(8,128)(2,1)S(1)} %pad_maximum_fusion.5), channel_id=1, source_target_pairs={{0,4},{4,0},{8,12},{12,8},{1,5},{5,1},{9,13},{13,9},{2,6},{6,2},{1... | collective-permute-start | bytes 1572872 | tf_op jit(solution)/shard_map/ppermute | solution.py:276
  68.9 28.4 %collective-permute-start.15 = (bf16[512,512]{1,0:T(8,128)(2,1)S(1)}, bf16[512,512]{1,0:T(8,128)(2,1)S(1)}, u32[]{:S(2)}, u32[]{:S(2)}) collective-permute-start(bf16[512,512]{1,0:T(8,128)(2,1)S(1)} %pad_maximum_fusion.4), channel_id=1, source_target_pairs={{0,4},{4,0},{8,12},{12,8},{1,5},{5,1},{9,13},{13,9},{2,6},{6,2},{1... | collective-permute-start | bytes 1572872 | tf_op jit(solution)/shard_map/ppermute | solution.py:276
  69.4 16.4 %collective-permute-start.23 = (bf16[512,512]{1,0:T(8,128)(2,1)S(1)}, bf16[512,512]{1,0:T(8,128)(2,1)S(1)}, u32[]{:S(2)}, u32[]{:S(2)}) collective-permute-start(bf16[512,512]{1,0:T(8,128)(2,1)S(1)} %collective-permute-done.22.refs_7_), channel_id=1, source_target_pairs={{0,4},{4,0},{8,12},{12,8},{1,5},{5,1},{9,13},{13,9},{2,6},{6,2},{1... | collective-permute-start | bytes 1572872 | tf_op jit(solution)/shard_map/ppermute | solution.py:276
  69.5 22.8 %collective-permute-start.20 = (bf16[512,512]{1,0:T(8,128)(2,1)S(1)}, bf16[512,512]{1,0:T(8,128)(2,1)S(1)}, u32[]{:S(2)}, u32[]{:S(2)}) collective-permute-start(bf16[512,512]{1,0:T(8,128)(2,1)S(1)} %collective-permute-done.19.across_), channel_id=1, source_target_pairs={{0,4},{4,0},{8,12},{12,8},{1,5},{5,1},{9,13},{13,9},{2,6},{6,2},{1... | collective-permute-start | bytes 1572872 | tf_op jit(solution)/shard_map/ppermute | solution.py:276
  70.0 27.4 %collective-permute-start.17 = (bf16[512,512]{1,0:T(8,128)(2,1)S(1)}, bf16[512,512]{1,0:T(8,128)(2,1)S(1)}, u32[]{:S(2)}, u32[]{:S(2)}) collective-permute-start(bf16[512,512]{1,0:T(8,128)(2,1)S(1)} %collective-permute-done.16.across_), channel_id=1, source_target_pairs={{0,4},{4,0},{8,12},{12,8},{1,5},{5,1},{9,13},{13,9},{2,6},{6,2},{1... | collective-permute-start | bytes 1572872 | tf_op jit(solution)/shard_map/ppermute | solution.py:276
  (9 other events, 83.5 us)

commit v2 on v0

v2 whole, which is shorter than its diff:
```python
import functools
import math

import jax
import jax.numpy as jnp
from jax import lax
from jax.experimental import pallas as pl
from jax.experimental.pallas import tpu as pltpu
from jax.sharding import PartitionSpec as P

HEAD_DIM = 128
BLOCK_ROWS = 4
BLOCK_COLS = 32
PER_BLOCK = BLOCK_ROWS * BLOCK_COLS
SCORE_SCALE = 1.0 / math.sqrt(HEAD_DIM)
EXP2_SCALE = SCORE_SCALE * math.log2(math.e)
CHUNK_HEADS = (4, 5, 3)
GROUP = 8
VMEM_LIMIT = 24 * 1024 * 1024


def extended(cells, sides, width):
    for axis, dim in sides:
        count = lax.axis_size(axis)
        ends = count - 1
        head = lax.slice_in_dim(cells, 0, width, axis=dim)
        tail = lax.slice_in_dim(cells, cells.shape[dim] - width, cells.shape[dim], axis=dim)
        cells = jnp.concatenate(
            [
                lax.ppermute(tail, axis, [(i, (i + 1) % count) for i in range(ends)]),
                cells,
                lax.ppermute(head, axis, [((i + 1) % count, i) for i in range(ends)]),
            ],
            axis=dim,
        )
    return cells


def position(v_fresh, conv_w):
    rows_here, cols_here, feature_width = v_fresh.shape
    rims = extended(v_fresh, (("rows", 0), ("cols", 1)), 1)
    position_term = jnp.zeros((rows_here, cols_here, feature_width), jnp.float32)
    for row_tap in range(3):
        for col_tap in range(3):
            position_term = position_term + conv_w[row_tap, col_tap] * rims[
                row_tap : row_tap + rows_here, col_tap : col_tap + cols_here
            ].astype(jnp.float32)
    return position_term


def split_heads(flat_rows):
    return flat_rows.reshape(flat_rows.shape[:-1] + (flat_rows.shape[-1] // HEAD_DIM, HEAD_DIM))


def attend(softmax_state, queries, key_blocks, value_blocks, allowed):
    old_peak, old_total, old_summed = softmax_state
    scores = (
        jnp.einsum(
            "bqhd,nkhd->bhqnk", queries, key_blocks, preferred_element_type=jnp.float32
        )
        * SCORE_SCALE
    )
    scores = jnp.where(allowed[:, None, None, :, None], scores, -1e30)
    new_peak = jnp.maximum(old_peak, jnp.max(scores, axis=(3, 4)))
    weights = jnp.exp(scores - new_peak[:, :, :, None, None]).astype(jnp.bfloat16)
    factor = jnp.exp(old_peak - new_peak)
    new_total = old_total * factor + jnp.sum(weights.astype(jnp.float32), axis=(3, 4))
    product = jnp.einsum(
        "bhqnk,nkhd->bqhd", weights, value_blocks, preferred_element_type=jnp.float32
    )
    new_summed = old_summed * jnp.transpose(factor, (0, 2, 1))[:, :, :, None] + product
    return (new_peak, new_total, new_summed)


def general_body(
    q_fresh, k_fresh, v_fresh, k_stale, v_stale, text_k, text_v, conv_w, reads, pattern, text_blocks
):
    rows_here, cols_here, feature_width = q_fresh.shape
    blocks_here = rows_here // BLOCK_ROWS
    head_count = feature_width // HEAD_DIM

    def as_blocks(grid_values):
        return split_heads(grid_values.reshape(blocks_here, PER_BLOCK, feature_width))

    queries = as_blocks(q_fresh)
    text_keys, text_values = (
        lax.all_gather(text_k, ("rows", "cols"), axis=0, tiled=True),
        lax.all_gather(text_v, ("rows", "cols"), axis=0, tiled=True),
    )
    text_count = text_keys.shape[0] // PER_BLOCK
    text_keys = split_heads(text_keys.reshape(text_count, PER_BLOCK, feature_width))
    text_values = split_heads(text_values.reshape(text_count, PER_BLOCK, feature_width))
    wanted = pattern[:, 0, :]
    fetch_rows = reads[0, 0, :]
    fetch_count = fetch_rows.shape[0]
    slot_count = blocks_here + fetch_count
    slot_mask = jnp.any(
        wanted[:, :, None] == jnp.arange(slot_count, dtype=jnp.int32)[None, None, :], axis=1
    )
    text_mask = jnp.any(
        text_blocks[:, 0, :, None] == jnp.arange(text_count, dtype=jnp.int32)[None, None, :], axis=1
    )
    softmax_state = (
        jnp.full((blocks_here, head_count, PER_BLOCK), -1e30, jnp.float32),
        jnp.zeros((blocks_here, head_count, PER_BLOCK), jnp.float32),
        jnp.zeros((blocks_here, PER_BLOCK, head_count, HEAD_DIM), jnp.float32),
    )
    softmax_state = attend(
        softmax_state,
        queries,
        jnp.concatenate([as_blocks(k_fresh), text_keys], axis=0),
        jnp.concatenate([as_blocks(v_fresh), text_values], axis=0),
        jnp.concatenate([slot_mask[:, :blocks_here], text_mask], axis=1),
    )
    chosen = jnp.where(
        wanted >= blocks_here, fetch_rows[jnp.clip(wanted - blocks_here, 0, fetch_count - 1)], -1
    )
    piece_keys = lax.all_gather(as_blocks(k_stale), "rows", axis=0, tiled=True)
    piece_values = lax.all_gather(as_blocks(v_stale), "rows", axis=0, tiled=True)
    block_rows = jnp.arange(piece_keys.shape[0], dtype=jnp.int32)
    piece_mask = jnp.any(chosen[:, :, None] == block_rows[None, None, :], axis=1)
    softmax_state = attend(softmax_state, queries, piece_keys, piece_values, piece_mask)
    _, final_total, final_summed = softmax_state
    mixed_rows = final_summed / jnp.transpose(final_total, (0, 2, 1))[:, :, :, None]
    attention = mixed_rows.reshape(rows_here, cols_here, feature_width)
    return attention + position(v_fresh, conv_w)


def head_scores(queries, keys):
    return lax.dot_general(
        queries, keys, (((1,), (1,)), ((), ())), preferred_element_type=jnp.float32
    )


def pack_far_kernel(k_hbm, v_hbm, *refs):
    outs, sems = refs[:-1], refs[-1]
    tokens = k_hbm.shape[0]
    copies = []
    first = 0
    for index, out in enumerate(outs):
        part = pl.ds(first, out.shape[1])
        first += out.shape[1]
        for which, source in enumerate((k_hbm, v_hbm)):
            copies.append(
                pltpu.make_async_copy(
                    source.at[:, part], out.at[pl.ds(which * tokens, tokens)], sems.at[index, which]
                )
            )
    for copy in copies:
        copy.start()
    for copy in copies:
        copy.wait()


def above_below(beside, diagonal):
    first_core = lax.axis_index("rows") % 2 == 0
    return (
        jnp.where(first_core, diagonal, beside),
        jnp.where(first_core, beside, diagonal),
    )


def pack_text_kernel(text_k, text_v, across_k, across_v, cells, beside, diagonal, plus, minus):
    shard = text_k.shape[0]
    rows_here, cols_here, width = cells.shape
    for index, source in enumerate((text_k, text_v, across_k, across_v)):
        part = pl.ds(index * shard, shard)
        value = source[...]
        plus[part, :] = value
        minus[part, :] = value
    above, below = above_below(beside[...], diagonal[...])
    rows = [above] + [cells[i] for i in range(rows_here)] + [below]
    rows = [row.astype(jnp.float32) for row in rows]
    spare = jnp.zeros((16 - len(rows), width), jnp.float32)
    for target, at in ((plus, cols_here - 1), (minus, 0)):
        edge = jnp.concatenate([row[at : at + 1] for row in rows] + [spare], axis=0)
        target[pl.ds(4 * shard, 16), :] = edge.astype(target.dtype)


def term_kernel(cells, beside, diagonal, left, right, weights, out):
    rows_here, cols_here, width = cells.shape
    col = lax.axis_index("cols")
    edge_at = left.shape[0] - 16
    place = lax.broadcasted_iota(jnp.int32, (cols_here, HEAD_DIM), 0)
    for lane in range(width // HEAD_DIM):
        part = pl.ds(lane * HEAD_DIM, HEAD_DIM)
        above, below = above_below(beside[:, part], diagonal[:, part])
        lefts = left[pl.ds(edge_at, 16), part].astype(jnp.float32)
        rights = right[pl.ds(edge_at, 16), part].astype(jnp.float32)
        lefts = jnp.where(col > 0, lefts, 0.0)
        rights = jnp.where(col < 3, rights, 0.0)
        taps = []
        for row in range(rows_here + 2):
            if row == 0:
                centre = above
            elif row == rows_here + 1:
                centre = below
            else:
                centre = cells[row - 1, :, part]
            centre = centre.astype(jnp.float32)
            before = jnp.where(place == 0, lefts[row : row + 1], pltpu.roll(centre, 1, 0))
            after = jnp.where(
                place == cols_here - 1, rights[row : row + 1], pltpu.roll(centre, cols_here - 1, 0)
            )
            taps.append((before, centre, after))
        for row in range(rows_here):
            total = None
            for row_tap in range(3):
                for col_tap in range(3):
                    piece = weights[row_tap, col_tap : col_tap + 1, part] * taps[row + row_tap][col_tap]
                    total = piece if total is None else total + piece
            out[pl.ds(row * cols_here, cols_here), part] = total


def attend_kernel(first_head, reads_ref, pattern_ref, text_ref, q, k, v, *refs):
    pieces, (mate_k, mate_v, across_kv, both_kv, term) = refs[:10], refs[10:15]
    out = refs[-1]
    row, col = lax.axis_index("rows"), lax.axis_index("cols")
    across, core = row // 2, row % 2
    shard = (pieces[0].shape[0] - 16) // 4
    half = across_kv.shape[0] // 2
    head_count = across_kv.shape[1] // HEAD_DIM

    def lanes(head):
        return pl.ds((first_head + head) * HEAD_DIM, HEAD_DIM)

    def text_part(chosen, head, which):
        from_own = chosen % 2 == core
        first = jnp.where(chosen // 2 == across, 0, 2 * shard) + which * shard
        rows = pl.ds(pl.multiple_of(first, shard), shard)
        part = lanes(head)

        def one(own, other):
            return jnp.where(from_own, own[rows, part], other[rows, part])

        last = jnp.where(col >= 2, one(pieces[3], pieces[8]), one(pieces[4], pieces[9]))
        return [one(pieces[i], pieces[i + 5]) for i in range(3)] + [last]

    def far_part(block, head, which):
        slot = pattern_ref[block, 0, 0] + pattern_ref[block, 0, 1] - block - 2
        wanted = reads_ref[0, 0, slot]
        owner = wanted // 2
        first = (wanted % 2) * PER_BLOCK
        rows = pl.ds(pl.multiple_of(first, PER_BLOCK), PER_BLOCK)
        packed = pl.ds(pl.multiple_of(first + which * half, PER_BLOCK), PER_BLOCK)
        mate = (mate_k, mate_v)[which][rows, lanes(head)]
        here = pl.ds(head * HEAD_DIM, HEAD_DIM)
        straight, crossed = across_kv[packed, here], both_kv[packed, here]
        arrived = jnp.where(owner % 2 == core, straight, crossed)
        return jnp.where(owner // 2 == across, mate, arrived)

    def gathered(block, head, which):
        own = (k, v)[which][pl.ds(block * PER_BLOCK, PER_BLOCK), lanes(head)]
        parts = [own]
        for turn in range(2):
            parts += text_part(text_ref[block, 0, turn], head, which)
        return jnp.concatenate(parts + [far_part(block, head, which)], axis=0)

    jobs = [(block, head) for head in range(head_count) for block in range(2)]
    for at in range(0, len(jobs), GROUP):
        group = jobs[at : at + GROUP]
        scores = [
            head_scores(
                q[pl.ds(block * PER_BLOCK, PER_BLOCK), lanes(head)], gathered(block, head, 0)
            )
            for block, head in group
        ]
        peaks = [jnp.max(s, axis=1, keepdims=True) * EXP2_SCALE for s in scores]
        weights = [
            jnp.exp2(s * EXP2_SCALE - peak).astype(jnp.bfloat16) for s, peak in zip(scores, peaks)
        ]
        totals = [jnp.sum(w.astype(jnp.float32), axis=1, keepdims=True) for w in weights]
        products = [
            jnp.dot(w, gathered(block, head, 1), preferred_element_type=jnp.float32)
            for w, (block, head) in zip(weights, group)
        ]
        for product, total, (block, head) in zip(products, totals, group):
            rows = pl.ds(block * PER_BLOCK, PER_BLOCK)
            out[rows, pl.ds(head * HEAD_DIM, HEAD_DIM)] = product / total + term[rows, lanes(head)]


def body(
    q_fresh, k_fresh, v_fresh, k_stale, v_stale, text_k, text_v, conv_w, reads, pattern, text_blocks
):
    rows_here, cols_here, width = q_fresh.shape
    tokens = rows_here * cols_here
    shard = text_k.shape[0]
    swap = [(r, (r + 2) % 4) for r in range(4)]
    mates = [(r, r ^ 1) for r in range(4)]
    row = lax.axis_index("rows")
    in_vmem = pl.BlockSpec(memory_space=pltpu.VMEM)
    anywhere = pl.BlockSpec(memory_space=pl.ANY)
    params = pltpu.CompilerParams(vmem_limit_bytes=VMEM_LIMIT)
    bf16 = jnp.bfloat16

    def flat(grid_values):
        return grid_values.reshape(tokens, width)

    def to_mate(values):
        return lax.ppermute(values, "rows", mates)

    across_k = lax.ppermute(text_k, "rows", swap)
    across_v = lax.ppermute(text_v, "rows", swap)
    beside = to_mate(jnp.where(row % 2 == 0, v_fresh[rows_here - 1], v_fresh[0]))
    diagonal = lax.ppermute(
        jnp.where(row < 2, v_fresh[rows_here - 1], v_fresh[0]), "rows", [(1, 2), (2, 1)]
    )
    packed = pl.pallas_call(
        pack_far_kernel,
        out_shape=tuple(
            jax.ShapeDtypeStruct((2 * tokens, n * HEAD_DIM), bf16) for n in CHUNK_HEADS
        ),
        in_specs=[anywhere] * 2,
        out_specs=(in_vmem,) * len(CHUNK_HEADS),
        scratch_shapes=[pltpu.SemaphoreType.DMA((len(CHUNK_HEADS), 2))],
        compiler_params=params,
        name="pack_far",
    )(flat(k_stale), flat(v_stale))
    far = [lax.ppermute(p, "rows", swap) for p in packed]
    mate_k, mate_v = to_mate(flat(k_stale)), to_mate(flat(v_stale))

    plus, minus = pl.pallas_call(
        pack_text_kernel,
        out_shape=(jax.ShapeDtypeStruct((4 * shard + 16, width), bf16),) * 2,
        in_specs=[in_vmem] * 7,
        out_specs=(in_vmem,) * 2,
        compiler_params=params,
        name="pack_text",
    )(text_k, text_v, across_k, across_v, v_fresh, beside, diagonal)
    left = lax.ppermute(plus, "cols", [(i, (i + 1) % 4) for i in range(4)])
    right = lax.ppermute(minus, "cols", [((i + 1) % 4, i) for i in range(4)])
    upper = lax.ppermute(left, "cols", [(1, 2), (2, 3)])
    lower = lax.ppermute(right, "cols", [(1, 0), (2, 1)])
    pieces = [plus, left, right, upper, lower]
    pieces = pieces + [to_mate(p) for p in pieces]

    term = pl.pallas_call(
        term_kernel,
        out_shape=jax.ShapeDtypeStruct((tokens, width), jnp.float32),
        in_specs=[in_vmem] * 6,
        out_specs=in_vmem,
        compiler_params=params,
        name="term",
    )(v_fresh, beside, diagonal, left, right, conv_w)

    out = None
    first_head = 0
    for chunk, head_count in enumerate(CHUNK_HEADS):
        block = pl.BlockSpec(
            (pl.Element(tokens), pl.Element(head_count * HEAD_DIM)),
            lambda i, *_, at=first_head * HEAD_DIM: (0, at),
        )
        out = pl.pallas_call(
            functools.partial(attend_kernel, first_head),
            out_shape=jax.ShapeDtypeStruct((tokens, width), jnp.float32),
            grid_spec=pltpu.PrefetchScalarGridSpec(
                num_scalar_prefetch=3,
                grid=(1,),
                in_specs=[in_vmem] * 18 + [anywhere] * (out is not None),
                out_specs=block,
            ),
            input_output_aliases={21: 0} if out is not None else {},
            compiler_params=params,
            name=f"attend{chunk}",
        )(
            reads, pattern, text_blocks, flat(q_fresh), flat(k_fresh), flat(v_fresh), *pieces,
            mate_k, mate_v, far[chunk], to_mate(far[chunk]), term, *([out] if out is not None else []),
        )
        first_head += head_count
    return out.reshape(rows_here, cols_here, width)


def fits(mesh, reads, pattern, text_k):
    sizes = dict(mesh.shape)
    return (
        sizes["rows"] == 4
        and sizes["cols"] == 4
        and reads.shape[-1] == 2
        and pattern.shape[-1] == 2
        and pattern.shape[0] == 2 * sizes["groups"] * 4
        and text_k.shape[0] == sizes["groups"] * 4 * PER_BLOCK
    )


def solution(mesh):
    grid = P(("groups", "rows"), "cols", None)
    text = P(("groups", "rows", "cols"), None)
    in_specs = (grid, grid, grid, grid, grid, text, text, P(), grid, grid, grid)

    def program(*args):
        chosen = body if fits(mesh, args[8], args[9], args[5]) else general_body
        return jax.shard_map(
            chosen, mesh=mesh, in_specs=in_specs, out_specs=grid, check_vma=False
        )(*args)

    return program
```

time: 185 us -> 76.3 us (0.41)
  waiting for transfers between devices: 86.7 us -> 38.5 us
  matrix products: 26.7 us -> 0 us
  local copies, waits for them, and re-layouts: 27.6 us -> 5.79 us
  other arithmetic: 20 us -> 0.02 us
  between operations: 13.6 us -> 0.21 us
  Pallas kernels: 0 us -> 10.4 us
  starting transfers between devices: 9.56 us -> 19.9 us
    all_gather x4 -> x0, waiting for transfers between devices: 85.3 us -> none  [the longest x1 36.5 us: body(): lax.all_gather(text_v, ('rows', 'cols'), axis=0, tiled=True)]
    ppermute x4 -> x21, waiting for transfers between devices: 0.01 us -> 38.5 us  [the longest x1 11.6 us: body(): lower = lax.ppermute(right, 'cols', [(1, 0), (2, 1)])]
    dot_general x4 -> x0, matrix products: 26.7 us -> none  [the longest x2 15.8 us: attend(): jnp.einsum('bhqnk,nkhd->bqhd', weights, value_blocks, preferred_element_t...]
    another operation x13 -> x0, local copies, waits for them, and re-layouts: 20.9 us -> none  [split_heads(): flat_rows.reshape(flat_rows.shape[:-1] + (flat_rows.shape[-1] // HEAD_DIM...]
    reduce_sum x2 -> x0, other arithmetic: 13 us -> none  [attend(): jnp.sum(weights.astype(jnp.float32), axis=(3, 4))]
    ppermute x4 -> x21, starting transfers between devices: 9.44 us -> 19.9 us  [the longest x3 4.95 us: body(): far = [lax.ppermute(p, 'rows', swap) for p in packed]]
    pallas_call x0 -> x6, Pallas kernels: none -> 10.4 us  [the longest x3 8.01 us: body(): pl.pallas_call(functools.partial(attend_kernel, first_head), out_shape=ja...]
    add x2 -> x0, other arithmetic: 6.64 us -> none  [the longest x1 6.01 us: body(): return attention + position_term]
  transfers between devices with their start and end apart: 8 -> 21, of which waited for: 4 -> 6; matrix products, arithmetic and copies ran while one was open for 36% -> 0% of each run, Pallas kernels for 0% -> 10%
where the time goes in v2:
time: 76.3 us; the launch traced here: 74.8 us
  waiting for transfers between devices  38.5 us (50%)
  starting transfers between devices  19.9 us (26%)
  Pallas kernels  10.4 us (14%)
  local copies, waits for them, and re-layouts  5.79 us (8%)
    ppermute x1, waiting for transfers between devices, body(): lower = lax.ppermute(right, 'cols', [(1, 0), (2, 1)])  11.6 us
    ppermute x1, waiting for transfers between devices, body(): across_k = lax.ppermute(text_k, 'rows', swap)  10.9 us
    ppermute x1, waiting for transfers between devices, body(): right = lax.ppermute(minus, 'cols', [((i + 1) % 4, i) for i in range(4)])  8.87 us
    pallas_call x3, Pallas kernels, body(): pl.pallas_call(functools.partial(attend_kernel, first_head), out_shape=ja...  8.01 us
    unnamed x28, local copies, waits for them, and re-layouts  5.79 us
    ppermute x3, starting transfers between devices, body(): far = [lax.ppermute(p, 'rows', swap) for p in packed]  4.95 us
    ppermute x1, starting transfers between devices, body(): right = lax.ppermute(minus, 'cols', [((i + 1) % 4, i) for i in range(4)])  4.88 us
    ppermute x1, starting transfers between devices, body(): across_k = lax.ppermute(text_k, 'rows', swap)  3.42 us
  transfers between devices with their start and end apart: 21, of which 6 were waited for; matrix products, arithmetic and copies ran while one was open for 0% of the time, Pallas kernels for 10%

profile of v2, /device:TPU:0, one launch (start us, length us, event | category | flops | bytes accessed | tf_op | source)
XLA Modules:
  0.0 74.8 jit_solution(17808120980105185390)
XLA Ops:
  0.0 1.2 %copy-done.3 = bf16[8,32,1536]{2,1,0:T(8,128)(2,1)S(1)} copy-done((bf16[8,32,1536]{2,1,0:T(8,128)(2,1)S(1)}, bf16[8,32,1536]{2,1,0:T(8,128)(2,1)}, u32[]{:S(2)}) %copy-start.3) | copy-done | bytes 786456
  1.2 1.1 %copy-done.5 = bf16[8,32,1536]{2,1,0:T(8,128)(2,1)S(1)} copy-done((bf16[8,32,1536]{2,1,0:T(8,128)(2,1)S(1)}, bf16[8,32,1536]{2,1,0:T(8,128)(2,1)}, u32[]{:S(2)}) %copy-start.5) | copy-done | bytes 786456
  2.3 1.0 %pack_far.1 = (bf16[512,512]{1,0:T(8,128)(2,1)}, bf16[512,640]{1,0:T(8,128)(2,1)S(1)}, bf16[512,384]{1,0:T(8,128)(2,1)S(1)}) custom-call(bf16[256,1536]{1,0:T(8,128)(2,1)S(1)} %bitcast.19, bf16[256,1536]{1,0:T(8,128)(2,1)S(1)} %bitcast.21), custom_call_target="tpu_custom_call" | custom-call | tf_op jit(solution)/shard_map/pack_far/pallas_call | solution.py:308
  3.4 0.7 copy-done.13
  4.1 2.9 %collective-permute-start.19 = (bf16[512,512]{1,0:T(8,128)(2,1)}, bf16[512,512]{1,0:T(8,128)(2,1)S(1)}, u32[]{:S(2)}, u32[]{:S(2)}) collective-permute-start(bf16[512,512]{1,0:T(8,128)(2,1)} %get-tuple-element.14), channel_id=1, source_target_pairs={{0,8},{4,12},{8,0},{12,4},{1,9},{5,13},{9,1},{13,5},{2,10},{6,14},... | collective-permute-start | bytes 1572872 | tf_op jit(solution)/shard_map/ppermute | solution.py:319
  7.8 3.4 %collective-permute-start = (bf16[32,1536]{1,0:T(8,128)(2,1)}, bf16[32,1536]{1,0:T(8,128)(2,1)S(1)}, u32[]{:S(2)}, u32[]{:S(2)}) collective-permute-start(bf16[32,1536]{1,0:T(8,128)(2,1)} %text_k.1), channel_id=1, source_target_pairs={{0,8},{4,12},{8,0},{12,4},{1,9},{5,13},{9,1},{13,5},{2,10},{6,14},... | collective-permute-start | bytes 294920 | tf_op jit(solution)/shard_map/ppermute | solution.py:302
  11.3 1.9 %collective-permute-start.15 = (bf16[512,384]{1,0:T(8,128)(2,1)}, bf16[512,384]{1,0:T(8,128)(2,1)S(1)}, u32[]{:S(2)}, u32[]{:S(2)}) collective-permute-start(bf16[512,384]{1,0:T(8,128)(2,1)} %copy-done.13), channel_id=1, source_target_pairs={{0,8},{4,12},{8,0},{12,4},{1,9},{5,13},{9,1},{13,5},{2,10},{6,14},... | collective-permute-start | bytes 1179656 | tf_op jit(solution)/shard_map/ppermute | solution.py:319
  13.3 10.9 %collective-permute-done.across_k = bf16[32,1536]{1,0:T(8,128)(2,1)S(1)} collective-permute-done((bf16[32,1536]{1,0:T(8,128)(2,1)}, bf16[32,1536]{1,0:T(8,128)(2,1)S(1)}, u32[]{:S(2)}, u32[]{:S(2)}) %collective-permute-start) | collective-permute-done | bytes 98336 | tf_op jit(solution)/shard_map/ppermute | solution.py:302
  24.2 2.1 %collective-permute-done.1.across_v = bf16[32,1536]{1,0:T(8,128)(2,1)S(1)} collective-permute-done((bf16[32,1536]{1,0:T(8,128)(2,1)}, bf16[32,1536]{1,0:T(8,128)(2,1)S(1)}, u32[]{:S(2)}, u32[]{:S(2)}) %collective-permute-start.1) | collective-permute-done | bytes 98336 | tf_op jit(solution)/shard_map/ppermute | solution.py:303
  26.3 0.9 %copy-done.7 = bf16[32,1536]{1,0:T(8,128)(2,1)S(1)} copy-done((bf16[32,1536]{1,0:T(8,128)(2,1)S(1)}, bf16[32,1536]{1,0:T(8,128)(2,1)}, u32[]{:S(2)}) %copy-start.7) | copy-done | bytes 98328
  27.2 0.9 %copy-done.8 = bf16[32,1536]{1,0:T(8,128)(2,1)S(1)} copy-done((bf16[32,1536]{1,0:T(8,128)(2,1)S(1)}, bf16[32,1536]{1,0:T(8,128)(2,1)}, u32[]{:S(2)}) %copy-start.8) | copy-done | bytes 98328
  28.2 2.2 %collective-permute-start.4 = (bf16[144,1536]{1,0:T(8,128)(2,1)S(1)}, bf16[144,1536]{1,0:T(8,128)(2,1)S(1)}, u32[]{:S(2)}, u32[]{:S(2)}) collective-permute-start(bf16[144,1536]{1,0:T(8,128)(2,1)S(1)} %get-tuple-element.10.refs_0_), channel_id=1, source_target_pairs={{0,1},{1,2},{2,3},{3,0},{4,5},{5,6},{6,7},{7,4},{8,9},{9,10},{10,1... | collective-permute-start | bytes 1327112 | tf_op jit(solution)/shard_map/ppermute | solution.py:330
  30.5 2.3 %collective-permute-done.15.refs_12_ = bf16[512,384]{1,0:T(8,128)(2,1)S(1)} collective-permute-done((bf16[512,384]{1,0:T(8,128)(2,1)}, bf16[512,384]{1,0:T(8,128)(2,1)S(1)}, u32[]{:S(2)}, u32[]{:S(2)}) %collective-permute-start.15) | collective-permute-done | bytes 393248 | tf_op jit(solution)/shard_map/ppermute | solution.py:319
  32.9 4.9 %collective-permute-start.5 = (bf16[144,1536]{1,0:T(8,128)(2,1)S(1)}, bf16[144,1536]{1,0:T(8,128)(2,1)S(1)}, u32[]{:S(2)}, u32[]{:S(2)}) collective-permute-start(bf16[144,1536]{1,0:T(8,128)(2,1)S(1)} %get-tuple-element.11), channel_id=1, source_target_pairs={{1,0},{2,1},{3,2},{0,3},{5,4},{6,5},{7,6},{4,7},{9,8},{10,9},{11,1... | collective-permute-start | bytes 1327112 | tf_op jit(solution)/shard_map/ppermute | solution.py:331
  37.8 2.5 %collective-permute-done.4.left.refs_1_ = bf16[144,1536]{1,0:T(8,128)(2,1)S(1)} collective-permute-done((bf16[144,1536]{1,0:T(8,128)(2,1)S(1)}, bf16[144,1536]{1,0:T(8,128)(2,1)S(1)}, u32[]{:S(2)}, u32[]{:S(2)}) %collective-permute-start.4) | collective-permute-done | bytes 442400 | tf_op jit(solution)/shard_map/ppermute | solution.py:330
  40.3 8.9 %collective-permute-done.5.right.refs_2_ = bf16[144,1536]{1,0:T(8,128)(2,1)S(1)} collective-permute-done((bf16[144,1536]{1,0:T(8,128)(2,1)S(1)}, bf16[144,1536]{1,0:T(8,128)(2,1)S(1)}, u32[]{:S(2)}, u32[]{:S(2)}) %collective-permute-start.5) | collective-permute-done | bytes 442400 | tf_op jit(solution)/shard_map/ppermute | solution.py:331
  49.2 0.7 collective-permute-start.6
  49.9 1.3 %collective-permute-start.7 = (bf16[144,1536]{1,0:T(8,128)(2,1)S(1)}, bf16[144,1536]{1,0:T(8,128)(2,1)S(1)}, u32[]{:S(2)}, u32[]{:S(2)}) collective-permute-start(bf16[144,1536]{1,0:T(8,128)(2,1)S(1)} %collective-permute-done.5.right.refs_2_), channel_id=1, source_target_pairs={{1,0},{2,1},{5,4},{6,5},{9,8},{10,9},{13,12},{14,13},{17,16},{18,1... | collective-permute-start | bytes 1327112 | tf_op jit(solution)/shard_map/ppermute | solution.py:333
  52.3 11.6 %collective-permute-done.7.refs_4_ = bf16[144,1536]{1,0:T(8,128)(2,1)S(1)} collective-permute-done((bf16[144,1536]{1,0:T(8,128)(2,1)S(1)}, bf16[144,1536]{1,0:T(8,128)(2,1)S(1)}, u32[]{:S(2)}, u32[]{:S(2)}) %collective-permute-start.7) | collective-permute-done | bytes 442400 | tf_op jit(solution)/shard_map/ppermute | solution.py:333
  64.5 0.9 %copy-done.9 = f32[3,3,1536]{2,1,0:T(4,128)S(1)} copy-done((f32[3,3,1536]{2,1,0:T(4,128)S(1)}, f32[3,3,1536]{2,1,0:T(4,128)}, u32[]{:S(2)}) %copy-start.9) | copy-done | bytes 55320
  65.4 1.3 %term.1.refs_14_ = f32[256,1536]{1,0:T(8,128)S(1)} custom-call(bf16[8,32,1536]{2,1,0:T(8,128)(2,1)S(1)} %copy-done, bf16[32,1536]{1,0:T(8,128)(2,1)S(1)} %collective-permute-done.2.beside, bf16[32,1536]{1,0:T(8,128)(2,1)S(1)} %collective-permute-done.3.diagonal, bf16[144,1536]{1,0:T(8,128)(2,1)S(1)} %collective-permute-done.4.left.refs_1_, ...), custom_call_target="tpu_custom_call" | custom-call | tf_op jit(solution)/shard_map/term/pallas_call | solution.py:337
  66.8 2.7 %attend0.1.refs_15_ = f32[256,1536]{1,0:T(8,128)} custom-call(s32[1,1,2]{2,1,0:T(1,128)S(1)} %copy-done.12, s32[2,1,2]{2,1,0:T(1,128)S(1)} %copy-done.10, s32[2,1,2]{2,1,0:T(1,128)S(1)} %copy-done.11, bf16[256,1536]{1,0:T(8,128)(2,1)S(1)} %bitcast.13, bf16[256,1536]{1,0:T(8,128)(2,1)S(1)} %bitcast.16, bf16[256,1536]{1,0:T(8,128)(2,1)S(1)} %bitcast.10, ...), custom_call_target="tpu_custom_call" | custom-call | tf_op jit(solution)/shard_map/attend0/pallas_call | solution.py:353
  69.5 3.0 %attend1.1.refs_15_ = f32[256,1536]{1,0:T(8,128)} custom-call(s32[1,1,2]{2,1,0:T(1,128)S(1)} %copy-done.12, s32[2,1,2]{2,1,0:T(1,128)S(1)} %copy-done.10, s32[2,1,2]{2,1,0:T(1,128)S(1)} %copy-done.11, bf16[256,1536]{1,0:T(8,128)(2,1)S(1)} %bitcast.14, bf16[256,1536]{1,0:T(8,128)(2,1)S(1)} %bitcast.17, ...), custom_call_target="tpu_custom_call", output_to_operand_aliasing={{}: (21, {})} | custom-call | tf_op jit(solution)/shard_map/attend1/pallas_call | solution.py:353
  72.6 2.3 %attend2.1 = f32[256,1536]{1,0:T(8,128)} custom-call(s32[1,1,2]{2,1,0:T(1,128)S(1)} %copy-done.12, s32[2,1,2]{2,1,0:T(1,128)S(1)} %copy-done.10, s32[2,1,2]{2,1,0:T(1,128)S(1)} %copy-done.11, bf16[256,1536]{1,0:T(8,128)(2,1)S(1)} %bitcast.15, bf16[256,1536]{1,0:T(8,128)(2,1)S(1)} %bitcast.18, ...), custom_call_target="tpu_custom_call", output_to_operand_aliasing={{}: (21, {})} | custom-call | tf_op jit(solution)/shard_map/attend2/pallas_call | solution.py:353
  (53 shorter events, 2.8 us)
Async XLA Ops:
  4.1 28.8 %collective-permute-start.19 = (bf16[512,512]{1,0:T(8,128)(2,1)}, bf16[512,512]{1,0:T(8,128)(2,1)S(1)}, u32[]{:S(2)}, u32[]{:S(2)}) collective-permute-start(bf16[512,512]{1,0:T(8,128)(2,1)} %get-tuple-element.14), channel_id=1, source_target_pairs={{0,8},{4,12},{8,0},{12,4},{1,9},{5,13},{9,1},{13,5},{2,10},{6,14},... | collective-permute-start | bytes 1572872 | tf_op jit(solution)/shard_map/ppermute | solution.py:319
  7.1 4.3 %collective-permute-start.2 = (bf16[32,1536]{1,0:T(8,128)(2,1)S(1)}, bf16[32,1536]{1,0:T(8,128)(2,1)S(1)}, u32[]{:S(2)}, u32[]{:S(2)}) collective-permute-start(bf16[32,1536]{1,0:T(8,128)(2,1)S(1)} %get-tuple-element.16), channel_id=1, source_target_pairs={{0,4},{4,0},{8,12},{12,8},{1,5},{5,1},{9,13},{13,9},{2,6},{6,2},{1... | collective-permute-start | bytes 294920 | tf_op jit(solution)/shard_map/ppermute | solution.py:300
  7.1 6.1 %collective-permute-start.3 = (bf16[32,1536]{1,0:T(8,128)(2,1)S(1)}, bf16[32,1536]{1,0:T(8,128)(2,1)S(1)}, u32[]{:S(2)}, u32[]{:S(2)}) collective-permute-start(bf16[32,1536]{1,0:T(8,128)(2,1)S(1)} %get-tuple-element.15), channel_id=1, source_target_pairs={{4,8},{8,4},{5,9},{9,5},{6,10},{10,6},{7,11},{11,7},{20,24},{24,20... | collective-permute-start | bytes 294920 | tf_op jit(solution)/shard_map/ppermute | solution.py:305
  7.8 16.4 %collective-permute-start = (bf16[32,1536]{1,0:T(8,128)(2,1)}, bf16[32,1536]{1,0:T(8,128)(2,1)S(1)}, u32[]{:S(2)}, u32[]{:S(2)}) collective-permute-start(bf16[32,1536]{1,0:T(8,128)(2,1)} %text_k.1), channel_id=1, source_target_pairs={{0,8},{4,12},{8,0},{12,4},{1,9},{5,13},{9,1},{13,5},{2,10},{6,14},... | collective-permute-start | bytes 294920 | tf_op jit(solution)/shard_map/ppermute | solution.py:302
  11.2 15.1 %collective-permute-start.1 = (bf16[32,1536]{1,0:T(8,128)(2,1)}, bf16[32,1536]{1,0:T(8,128)(2,1)S(1)}, u32[]{:S(2)}, u32[]{:S(2)}) collective-permute-start(bf16[32,1536]{1,0:T(8,128)(2,1)} %text_v.1), channel_id=1, source_target_pairs={{0,8},{4,12},{8,0},{12,4},{1,9},{5,13},{9,1},{13,5},{2,10},{6,14},... | collective-permute-start | bytes 294920 | tf_op jit(solution)/shard_map/ppermute | solution.py:303
  11.3 21.5 %collective-permute-start.15 = (bf16[512,384]{1,0:T(8,128)(2,1)}, bf16[512,384]{1,0:T(8,128)(2,1)S(1)}, u32[]{:S(2)}, u32[]{:S(2)}) collective-permute-start(bf16[512,384]{1,0:T(8,128)(2,1)} %copy-done.13), channel_id=1, source_target_pairs={{0,8},{4,12},{8,0},{12,4},{1,9},{5,13},{9,1},{13,5},{2,10},{6,14},... | collective-permute-start | bytes 1179656 | tf_op jit(solution)/shard_map/ppermute | solution.py:319
  28.2 12.1 %collective-permute-start.4 = (bf16[144,1536]{1,0:T(8,128)(2,1)S(1)}, bf16[144,1536]{1,0:T(8,128)(2,1)S(1)}, u32[]{:S(2)}, u32[]{:S(2)}) collective-permute-start(bf16[144,1536]{1,0:T(8,128)(2,1)S(1)} %get-tuple-element.10.refs_0_), channel_id=1, source_target_pairs={{0,1},{1,2},{2,3},{3,0},{4,5},{5,6},{6,7},{7,4},{8,9},{9,10},{10,1... | collective-permute-start | bytes 1327112 | tf_op jit(solution)/shard_map/ppermute | solution.py:330
  30.4 20.9 %collective-permute-start.13 = (bf16[256,1536]{1,0:T(8,128)(2,1)S(1)}, bf16[256,1536]{1,0:T(8,128)(2,1)S(1)}, u32[]{:S(2)}, u32[]{:S(2)}) collective-permute-start(bf16[256,1536]{1,0:T(8,128)(2,1)S(1)} %bitcast.20), channel_id=1, source_target_pairs={{0,4},{4,0},{8,12},{12,8},{1,5},{5,1},{9,13},{13,9},{2,6},{6,2},{1... | collective-permute-start | bytes 2359304 | tf_op jit(solution)/shard_map/ppermute | solution.py:300
  30.4 36.3 %copy-start.11 = (s32[2,1,2]{2,1,0:T(1,128)S(1)}, s32[2,1,2]{2,1,0:T(1,128)}, u32[]{:S(2)}) copy-start(s32[2,1,2]{2,1,0:T(1,128)} %text_ref.5) | copy-start | bytes 52
  30.4 20.8 %collective-permute-start.17 = (bf16[512,640]{1,0:T(8,128)(2,1)S(1)}, bf16[512,640]{1,0:T(8,128)(2,1)S(1)}, u32[]{:S(2)}, u32[]{:S(2)}) collective-permute-start(bf16[512,640]{1,0:T(8,128)(2,1)S(1)} %get-tuple-element.13), channel_id=1, source_target_pairs={{0,8},{4,12},{8,0},{12,4},{1,9},{5,13},{9,1},{13,5},{2,10},{6,14},... | collective-permute-start | bytes 1966088 | tf_op jit(solution)/shard_map/ppermute | solution.py:319
  32.9 18.9 %collective-permute-start.14 = (bf16[256,1536]{1,0:T(8,128)(2,1)S(1)}, bf16[256,1536]{1,0:T(8,128)(2,1)S(1)}, u32[]{:S(2)}, u32[]{:S(2)}) collective-permute-start(bf16[256,1536]{1,0:T(8,128)(2,1)S(1)} %bitcast.22), channel_id=1, source_target_pairs={{0,4},{4,0},{8,12},{12,8},{1,5},{5,1},{9,13},{13,9},{2,6},{6,2},{1... | collective-permute-start | bytes 2359304 | tf_op jit(solution)/shard_map/ppermute | solution.py:300
  32.9 33.9 %copy-start.10 = (s32[2,1,2]{2,1,0:T(1,128)S(1)}, s32[2,1,2]{2,1,0:T(1,128)}, u32[]{:S(2)}) copy-start(s32[2,1,2]{2,1,0:T(1,128)} %pattern_ref.5) | copy-start | bytes 52
  32.9 33.9 %copy-start.12 = (s32[1,1,2]{2,1,0:T(1,128)S(1)}, s32[1,1,2]{2,1,0:T(1,128)}, u32[]{:S(2)}) copy-start(s32[1,1,2]{2,1,0:T(1,128)} %reads_ref.5) | copy-start | bytes 28
  32.9 16.3 %collective-permute-start.5 = (bf16[144,1536]{1,0:T(8,128)(2,1)S(1)}, bf16[144,1536]{1,0:T(8,128)(2,1)S(1)}, u32[]{:S(2)}, u32[]{:S(2)}) collective-permute-start(bf16[144,1536]{1,0:T(8,128)(2,1)S(1)} %get-tuple-element.11), channel_id=1, source_target_pairs={{1,0},{2,1},{3,2},{0,3},{5,4},{6,5},{7,6},{4,7},{9,8},{10,9},{11,1... | collective-permute-start | bytes 1327112 | tf_op jit(solution)/shard_map/ppermute | solution.py:331
  40.3 9.6 %collective-permute-start.8 = (bf16[144,1536]{1,0:T(8,128)(2,1)S(1)}, bf16[144,1536]{1,0:T(8,128)(2,1)S(1)}, u32[]{:S(2)}, u32[]{:S(2)}) collective-permute-start(bf16[144,1536]{1,0:T(8,128)(2,1)S(1)} %get-tuple-element.10.refs_0_), channel_id=1, source_target_pairs={{0,4},{4,0},{8,12},{12,8},{1,5},{5,1},{9,13},{13,9},{2,6},{6,2},{1... | collective-permute-start | bytes 1327112 | tf_op jit(solution)/shard_map/ppermute | solution.py:300
  49.2 2.7 %collective-permute-start.6 = (bf16[144,1536]{1,0:T(8,128)(2,1)S(1)}, bf16[144,1536]{1,0:T(8,128)(2,1)S(1)}, u32[]{:S(2)}, u32[]{:S(2)}) collective-permute-start(bf16[144,1536]{1,0:T(8,128)(2,1)S(1)} %collective-permute-done.4.left.refs_1_), channel_id=1, source_target_pairs={{1,2},{2,3},{5,6},{6,7},{9,10},{10,11},{13,14},{14,15},{17,18},{18... | collective-permute-start | bytes 1327112 | tf_op jit(solution)/shard_map/ppermute | solution.py:332
  49.9 14.0 %collective-permute-start.7 = (bf16[144,1536]{1,0:T(8,128)(2,1)S(1)}, bf16[144,1536]{1,0:T(8,128)(2,1)S(1)}, u32[]{:S(2)}, u32[]{:S(2)}) collective-permute-start(bf16[144,1536]{1,0:T(8,128)(2,1)S(1)} %collective-permute-done.5.right.refs_2_), channel_id=1, source_target_pairs={{1,0},{2,1},{5,4},{6,5},{9,8},{10,9},{13,12},{14,13},{17,16},{18,1... | collective-permute-start | bytes 1327112 | tf_op jit(solution)/shard_map/ppermute | solution.py:333
  51.2 12.7 %collective-permute-start.10 = (bf16[144,1536]{1,0:T(8,128)(2,1)S(1)}, bf16[144,1536]{1,0:T(8,128)(2,1)S(1)}, u32[]{:S(2)}, u32[]{:S(2)}) collective-permute-start(bf16[144,1536]{1,0:T(8,128)(2,1)S(1)} %collective-permute-done.5.right.refs_2_), channel_id=1, source_target_pairs={{0,4},{4,0},{8,12},{12,8},{1,5},{5,1},{9,13},{13,9},{2,6},{6,2},{1... | collective-permute-start | bytes 1327112 | tf_op jit(solution)/shard_map/ppermute | solution.py:300
  51.4 13.1 %collective-permute-start.9 = (bf16[144,1536]{1,0:T(8,128)(2,1)S(1)}, bf16[144,1536]{1,0:T(8,128)(2,1)S(1)}, u32[]{:S(2)}, u32[]{:S(2)}) collective-permute-start(bf16[144,1536]{1,0:T(8,128)(2,1)S(1)} %collective-permute-done.4.left.refs_1_), channel_id=1, source_target_pairs={{0,4},{4,0},{8,12},{12,8},{1,5},{5,1},{9,13},{13,9},{2,6},{6,2},{1... | collective-permute-start | bytes 1327112 | tf_op jit(solution)/shard_map/ppermute | solution.py:300
  51.8 17.7 %collective-permute-start.18 = (bf16[512,640]{1,0:T(8,128)(2,1)S(1)}, bf16[512,640]{1,0:T(8,128)(2,1)S(1)}, u32[]{:S(2)}, u32[]{:S(2)}) collective-permute-start(bf16[512,640]{1,0:T(8,128)(2,1)S(1)} %collective-permute-done.17.refs_12_), channel_id=1, source_target_pairs={{0,4},{4,0},{8,12},{12,8},{1,5},{5,1},{9,13},{13,9},{2,6},{6,2},{1... | collective-permute-start | bytes 1966088 | tf_op jit(solution)/shard_map/ppermute | solution.py:300
  51.9 14.8 %collective-permute-start.20 = (bf16[512,512]{1,0:T(8,128)(2,1)S(1)}, bf16[512,512]{1,0:T(8,128)(2,1)S(1)}, u32[]{:S(2)}, u32[]{:S(2)}) collective-permute-start(bf16[512,512]{1,0:T(8,128)(2,1)S(1)} %collective-permute-done.19.refs_12_), channel_id=1, source_target_pairs={{0,4},{4,0},{8,12},{12,8},{1,5},{5,1},{9,13},{13,9},{2,6},{6,2},{1... | collective-permute-start | bytes 1572872 | tf_op jit(solution)/shard_map/ppermute | solution.py:300
  64.0 2.8 %collective-permute-start.11 = (bf16[144,1536]{1,0:T(8,128)(2,1)S(1)}, bf16[144,1536]{1,0:T(8,128)(2,1)S(1)}, u32[]{:S(2)}, u32[]{:S(2)}) collective-permute-start(bf16[144,1536]{1,0:T(8,128)(2,1)S(1)} %collective-permute-done.6.refs_3_), channel_id=1, source_target_pairs={{0,4},{4,0},{8,12},{12,8},{1,5},{5,1},{9,13},{13,9},{2,6},{6,2},{1... | collective-permute-start | bytes 1327112 | tf_op jit(solution)/shard_map/ppermute | solution.py:300
  64.0 2.8 %collective-permute-start.12 = (bf16[144,1536]{1,0:T(8,128)(2,1)S(1)}, bf16[144,1536]{1,0:T(8,128)(2,1)S(1)}, u32[]{:S(2)}, u32[]{:S(2)}) collective-permute-start(bf16[144,1536]{1,0:T(8,128)(2,1)S(1)} %collective-permute-done.7.refs_4_), channel_id=1, source_target_pairs={{0,4},{4,0},{8,12},{12,8},{1,5},{5,1},{9,13},{13,9},{2,6},{6,2},{1... | collective-permute-start | bytes 1327112 | tf_op jit(solution)/shard_map/ppermute | solution.py:300
  64.5 8.1 %collective-permute-start.16 = (bf16[512,384]{1,0:T(8,128)(2,1)S(1)}, bf16[512,384]{1,0:T(8,128)(2,1)S(1)}, u32[]{:S(2)}, u32[]{:S(2)}) collective-permute-start(bf16[512,384]{1,0:T(8,128)(2,1)S(1)} %collective-permute-done.15.refs_12_), channel_id=1, source_target_pairs={{0,4},{4,0},{8,12},{12,8},{1,5},{5,1},{9,13},{13,9},{2,6},{6,2},{1... | collective-permute-start | bytes 1179656 | tf_op jit(solution)/shard_map/ppermute | solution.py:300
  (11 other events, 139.2 us)

commit v3 on v2

--- a/solution.py
+++ b/solution.py
@@ -14,7 +14,7 @@
 PER_BLOCK = BLOCK_ROWS * BLOCK_COLS
 SCORE_SCALE = 1.0 / math.sqrt(HEAD_DIM)
 EXP2_SCALE = SCORE_SCALE * math.log2(math.e)
-CHUNK_HEADS = (4, 5, 3)
+CHUNK_HEADS = (9, 3)
 GROUP = 8
 VMEM_LIMIT = 24 * 1024 * 1024
 
@@ -132,24 +132,53 @@
     )
 
 
-def pack_far_kernel(k_hbm, v_hbm, *refs):
+def pack_kernel(k_hbm, v_hbm, cells, text_k, text_v, passed, diagonal, text, *refs):
     outs, sems = refs[:-1], refs[-1]
-    tokens = k_hbm.shape[0]
+    tokens, shard = k_hbm.shape[0], text_k.shape[0]
+    row = lax.axis_index("rows")
+    end, edges = cells.shape[0] - 1, pl.ds(2 * tokens, cells.shape[1])
     copies = []
+    for which, source in enumerate((text_k, text_v)):
+        copies.append((source, text.at[pl.ds(which * shard, shard)]))
     first = 0
-    for index, out in enumerate(outs):
+    for out in outs:
         part = pl.ds(first, out.shape[1])
         first += out.shape[1]
         for which, source in enumerate((k_hbm, v_hbm)):
-            copies.append(
-                pltpu.make_async_copy(
-                    source.at[:, part], out.at[pl.ds(which * tokens, tokens)], sems.at[index, which]
-                )
-            )
+            copies.append((source.at[:, part], out.at[pl.ds(which * tokens, tokens)]))
+    for which, source in enumerate((k_hbm, v_hbm)):
+        copies.append((source, passed.at[pl.ds(which * tokens, tokens)]))
+    copies.append((cells.at[jnp.where(row % 2 == 0, end, 0)], passed.at[edges]))
+    copies.append((cells.at[jnp.where(row < 2, end, 0)], diagonal))
+    copies = [pltpu.make_async_copy(*pair, sems.at[i]) for i, pair in enumerate(copies)]
     for copy in copies:
         copy.start()
     for copy in copies:
         copy.wait()
+
+
+def bundle_kernel(*refs):
+    out = refs[-1]
+    at = 0
+    for ref in refs[:-1]:
+        out[pl.ds(at, ref.shape[0]), :] = ref[...]
+        at += ref.shape[0]
+
+
+def choose_kernel(upper, lower, out):
+    out[...] = jnp.where(lax.axis_index("cols") >= 2, upper[...], lower[...])
+
+
+def edge_kernel(cells, passed, diagonal, last, first):
+    rows_here, cols_here, width = cells.shape
+    beside = passed[pl.ds(passed.shape[0] - cols_here, cols_here), :]
+    above, below = above_below(beside, diagonal[...])
+    rows = [above] + [cells[i] for i in range(rows_here)] + [below]
+    rows = [row.astype(jnp.float32) for row in rows]
+    spare = jnp.zeros((16 - len(rows), width), jnp.float32)
+    for target, at in ((last, cols_here - 1), (first, 0)):
+        edge = jnp.concatenate([row[at : at + 1] for row in rows] + [spare], axis=0)
+        target[...] = edge.astype(target.dtype)
 
 
 def above_below(beside, diagonal):
@@ -160,33 +189,17 @@
     )
 
 
-def pack_text_kernel(text_k, text_v, across_k, across_v, cells, beside, diagonal, plus, minus):
-    shard = text_k.shape[0]
-    rows_here, cols_here, width = cells.shape
-    for index, source in enumerate((text_k, text_v, across_k, across_v)):
-        part = pl.ds(index * shard, shard)
-        value = source[...]
-        plus[part, :] = value
-        minus[part, :] = value
-    above, below = above_below(beside[...], diagonal[...])
-    rows = [above] + [cells[i] for i in range(rows_here)] + [below]
-    rows = [row.astype(jnp.float32) for row in rows]
-    spare = jnp.zeros((16 - len(rows), width), jnp.float32)
-    for target, at in ((plus, cols_here - 1), (minus, 0)):
-        edge = jnp.concatenate([row[at : at + 1] for row in rows] + [spare], axis=0)
-        target[pl.ds(4 * shard, 16), :] = edge.astype(target.dtype)
-
-
-def term_kernel(cells, beside, diagonal, left, right, weights, out):
+def term_kernel(cells, passed, diagonal, left, right, weights, out):
     rows_here, cols_here, width = cells.shape
     col = lax.axis_index("cols")
-    edge_at = left.shape[0] - 16
     place = lax.broadcasted_iota(jnp.int32, (cols_here, HEAD_DIM), 0)
     for lane in range(width // HEAD_DIM):
         part = pl.ds(lane * HEAD_DIM, HEAD_DIM)
-        above, below = above_below(beside[:, part], diagonal[:, part])
-        lefts = left[pl.ds(edge_at, 16), part].astype(jnp.float32)
-        rights = right[pl.ds(edge_at, 16), part].astype(jnp.float32)
+        above, below = above_below(
+            passed[pl.ds(passed.shape[0] - cols_here, cols_here), part], diagonal[:, part]
+        )
+        lefts = left[:, part].astype(jnp.float32)
+        rights = right[:, part].astype(jnp.float32)
         lefts = jnp.where(col > 0, lefts, 0.0)
         rights = jnp.where(col < 3, rights, 0.0)
         taps = []
@@ -213,11 +226,11 @@
 
 
 def attend_kernel(first_head, reads_ref, pattern_ref, text_ref, q, k, v, *refs):
-    pieces, (mate_k, mate_v, across_kv, both_kv, term) = refs[:10], refs[10:15]
+    near, last, near_mate, last_mate, passed, across_kv, both_kv, term = refs[:8]
     out = refs[-1]
     row, col = lax.axis_index("rows"), lax.axis_index("cols")
     across, core = row // 2, row % 2
-    shard = (pieces[0].shape[0] - 16) // 4
+    shard = last.shape[0] // 4
     half = across_kv.shape[0] // 2
     head_count = across_kv.shape[1] // HEAD_DIM
 
@@ -227,23 +240,21 @@
     def text_part(chosen, head, which):
         from_own = chosen % 2 == core
         first = jnp.where(chosen // 2 == across, 0, 2 * shard) + which * shard
-        rows = pl.ds(pl.multiple_of(first, shard), shard)
         part = lanes(head)
 
-        def one(own, other):
+        def one(own, other, at):
+            rows = pl.ds(pl.multiple_of(first + at, shard), shard)
             return jnp.where(from_own, own[rows, part], other[rows, part])
 
-        last = jnp.where(col >= 2, one(pieces[3], pieces[8]), one(pieces[4], pieces[9]))
-        return [one(pieces[i], pieces[i + 5]) for i in range(3)] + [last]
+        return [one(near, near_mate, 4 * shard * i) for i in range(3)] + [one(last, last_mate, 0)]
 
     def far_part(block, head, which):
         slot = pattern_ref[block, 0, 0] + pattern_ref[block, 0, 1] - block - 2
         wanted = reads_ref[0, 0, slot]
         owner = wanted // 2
         first = (wanted % 2) * PER_BLOCK
-        rows = pl.ds(pl.multiple_of(first, PER_BLOCK), PER_BLOCK)
         packed = pl.ds(pl.multiple_of(first + which * half, PER_BLOCK), PER_BLOCK)
-        mate = (mate_k, mate_v)[which][rows, lanes(head)]
+        mate = passed[packed, lanes(head)]
         here = pl.ds(head * HEAD_DIM, HEAD_DIM)
         straight, crossed = across_kv[packed, here], both_kv[packed, here]
         arrived = jnp.where(owner % 2 == core, straight, crossed)
@@ -257,8 +268,9 @@
         return jnp.concatenate(parts + [far_part(block, head, which)], axis=0)
 
     jobs = [(block, head) for head in range(head_count) for block in range(2)]
-    for at in range(0, len(jobs), GROUP):
-        group = jobs[at : at + GROUP]
+    size = -(-len(jobs) // -(-len(jobs) // GROUP))
+    for at in range(0, len(jobs), size):
+        group = jobs[at : at + size]
         scores = [
             head_scores(
                 q[pl.ds(block * PER_BLOCK, PER_BLOCK), lanes(head)], gathered(block, head, 0)
@@ -287,11 +299,13 @@
     shard = text_k.shape[0]
     swap = [(r, (r + 2) % 4) for r in range(4)]
     mates = [(r, r ^ 1) for r in range(4)]
-    row = lax.axis_index("rows")
     in_vmem = pl.BlockSpec(memory_space=pltpu.VMEM)
-    anywhere = pl.BlockSpec(memory_space=pl.ANY)
+    in_hbm = pl.BlockSpec(memory_space=pltpu.HBM)
     params = pltpu.CompilerParams(vmem_limit_bytes=VMEM_LIMIT)
-    bf16 = jnp.bfloat16
+    cost = pl.CostEstimate(flops=1 << 20, transcendentals=0, bytes_accessed=1 << 16)
+
+    def after(value, *others):
+        return lax.optimization_barrier((value, *others))[0]
 
     def flat(grid_values):
         return grid_values.reshape(tokens, width)
@@ -299,53 +313,71 @@
     def to_mate(values):
         return lax.ppermute(values, "rows", mates)
 
-    across_k = lax.ppermute(text_k, "rows", swap)
-    across_v = lax.ppermute(text_v, "rows", swap)
-    beside = to_mate(jnp.where(row % 2 == 0, v_fresh[rows_here - 1], v_fresh[0]))
-    diagonal = lax.ppermute(
-        jnp.where(row < 2, v_fresh[rows_here - 1], v_fresh[0]), "rows", [(1, 2), (2, 1)]
-    )
-    packed = pl.pallas_call(
-        pack_far_kernel,
-        out_shape=tuple(
-            jax.ShapeDtypeStruct((2 * tokens, n * HEAD_DIM), bf16) for n in CHUNK_HEADS
-        ),
-        in_specs=[anywhere] * 2,
-        out_specs=(in_vmem,) * len(CHUNK_HEADS),
-        scratch_shapes=[pltpu.SemaphoreType.DMA((len(CHUNK_HEADS), 2))],
-        compiler_params=params,
-        name="pack_far",
-    )(flat(k_stale), flat(v_stale))
-    far = [lax.ppermute(p, "rows", swap) for p in packed]
-    mate_k, mate_v = to_mate(flat(k_stale)), to_mate(flat(v_stale))
-
-    plus, minus = pl.pallas_call(
-        pack_text_kernel,
-        out_shape=(jax.ShapeDtypeStruct((4 * shard + 16, width), bf16),) * 2,
-        in_specs=[in_vmem] * 7,
-        out_specs=(in_vmem,) * 2,
-        compiler_params=params,
-        name="pack_text",
-    )(text_k, text_v, across_k, across_v, v_fresh, beside, diagonal)
-    left = lax.ppermute(plus, "cols", [(i, (i + 1) % 4) for i in range(4)])
-    right = lax.ppermute(minus, "cols", [((i + 1) % 4, i) for i in range(4)])
+    def rows_of(*counts):
+        shapes = tuple(jax.ShapeDtypeStruct((n, width), jnp.bfloat16) for n in counts)
+        return shapes if len(shapes) > 1 else shapes[0]
+
+    def local(kernel, name, shapes, *args, specs=None, scratch=()):
+        many = isinstance(shapes, tuple)
+        return pl.pallas_call(
+            kernel,
+            out_shape=shapes,
+            in_specs=specs or [in_vmem] * len(args),
+            out_specs=(in_vmem,) * len(shapes) if many else in_vmem,
+            scratch_shapes=scratch,
+            compiler_params=params,
+            cost_estimate=cost,
+            name=name,
+        )(*args)
+
+    chunks = tuple(
+        jax.ShapeDtypeStruct((2 * tokens, n * HEAD_DIM), jnp.bfloat16) for n in CHUNK_HEADS
+    )
+    in_place = [
+        pltpu.with_memory_space_constraint(value, pltpu.HBM)
+        for value in (flat(k_stale), flat(v_stale), v_fresh, text_k, text_v)
+    ]
+    passed, diagonal, text, *packed = local(
+        pack_kernel,
+        "pack",
+        rows_of(2 * tokens + cols_here, cols_here, 2 * shard) + chunks,
+        *in_place,
+        specs=[in_hbm] * 5,
+        scratch=[pltpu.SemaphoreType.DMA((6 + 2 * len(CHUNK_HEADS),))],
+    )
+    across = lax.ppermute(text, "rows", swap)
+    diagonal = lax.ppermute(diagonal, "rows", [(1, 2), (2, 1)])
+    far = [lax.ppermute(after(packed[0], across, diagonal), "rows", swap)]
+    passed = to_mate(passed)
+
+    text = local(bundle_kernel, "join", rows_of(4 * shard), text, across)
+    left = lax.ppermute(text, "cols", [(i, (i + 1) % 4) for i in range(4)])
+    right = lax.ppermute(text, "cols", [((i + 1) % 4, i) for i in range(4)])
+    far.append(lax.ppermute(after(packed[1], passed), "rows", swap))
     upper = lax.ppermute(left, "cols", [(1, 2), (2, 3)])
     lower = lax.ppermute(right, "cols", [(1, 0), (2, 1)])
-    pieces = [plus, left, right, upper, lower]
-    pieces = pieces + [to_mate(p) for p in pieces]
-
-    term = pl.pallas_call(
+
+    last, first = local(edge_kernel, "edge", rows_of(16, 16), v_fresh, passed, diagonal)
+    last = lax.ppermute(last, "cols", [(i, i + 1) for i in range(3)])
+    first = lax.ppermute(first, "cols", [(i + 1, i) for i in range(3)])
+    near = local(bundle_kernel, "bundle", rows_of(12 * shard), text, left, right)
+    near_mate = to_mate(near)
+    term = local(
         term_kernel,
-        out_shape=jax.ShapeDtypeStruct((tokens, width), jnp.float32),
-        in_specs=[in_vmem] * 6,
-        out_specs=in_vmem,
-        compiler_params=params,
-        name="term",
-    )(v_fresh, beside, diagonal, left, right, conv_w)
+        "term",
+        jax.ShapeDtypeStruct((tokens, width), jnp.float32),
+        v_fresh, passed, diagonal, after(last, near), first, conv_w,
+    )
+    rest = local(choose_kernel, "choose", rows_of(4 * shard), upper, lower)
+    rest_mate = to_mate(rest)
+    far[0] = after(far[0], term, rest)
 
     out = None
     first_head = 0
     for chunk, head_count in enumerate(CHUNK_HEADS):
+        if out is not None:
+            far[chunk] = after(far[chunk], out)
+        far_mate = to_mate(far[chunk])
         block = pl.BlockSpec(
             (pl.Element(tokens), pl.Element(head_count * HEAD_DIM)),
             lambda i, *_, at=first_head * HEAD_DIM: (0, at),
@@ -356,15 +388,17 @@
             grid_spec=pltpu.PrefetchScalarGridSpec(
                 num_scalar_prefetch=3,
                 grid=(1,),
-                in_specs=[in_vmem] * 18 + [anywhere] * (out is not None),
+                in_specs=[in_vmem] * 11 + [in_hbm] * (out is not None),
                 out_specs=block,
             ),
-            input_output_aliases={21: 0} if out is not None else {},
+            input_output_aliases={14: 0} if out is not None else {},
             compiler_params=params,
+            cost_estimate=cost,
             name=f"attend{chunk}",
         )(
-            reads, pattern, text_blocks, flat(q_fresh), flat(k_fresh), flat(v_fresh), *pieces,
-            mate_k, mate_v, far[chunk], to_mate(far[chunk]), term, *([out] if out is not None else []),
+            reads, pattern, text_blocks, flat(q_fresh), flat(k_fresh), flat(v_fresh),
+            near, rest, near_mate, rest_mate, passed, far[chunk], far_mate, term,
+            *([out] if out is not None else []),
         )
         first_head += head_count
     return out.reshape(rows_here, cols_here, width)

time: 76.3 us -> 62 us (0.81); the launches traced: 74.8 us -> 61.8 us
  waiting for transfers between devices: 38.5 us -> 31.1 us
  local copies, waits for them, and re-layouts: 5.79 us -> 0.04 us
    ppermute x1, waiting for transfers between devices: 11.6 us -> 0.82 us  [body(): lower = lax.ppermute(right, 'cols', [(1, 0), (2, 1)])]
    unnamed x28 -> x14, local copies, waits for them, and re-layouts: 5.79 us -> 0.04 us
    ppermute x11 -> x5, waiting for transfers between devices: 0.03 us -> 2.88 us  [to_mate(): return lax.ppermute(values, 'rows', mates)]
    pallas_call x3 -> x2, Pallas kernels: 8.01 us -> 6.5 us  [body(): pl.pallas_call(functools.partial(attend_kernel, first_head), out_shape=ja...]
    pallas_call x3 -> x6, Pallas kernels: 2.41 us -> 3.67 us  [local(): pl.pallas_call(kernel, out_shape=shapes, in_specs=specs or [in_vmem] * le...]
    ppermute x8, starting transfers between devices: 16.2 us -> 17.1 us  [the longest x1 4.29 us: body(): last = lax.ppermute(last, 'cols', [(i, i + 1) for i in range(3)])]
    ppermute x11 -> x5, starting transfers between devices: 1.75 us -> 1.09 us  [to_mate(): return lax.ppermute(values, 'rows', mates)]
  transfers between devices with their start and end apart: 21 -> 15, of which waited for: 6 -> 8; matrix products, arithmetic and copies ran while one was open for 0% -> 0% of each run, Pallas kernels for 10% -> 9%
where the time goes in v3:
time: 62 us; the launch traced here: 61.8 us
  waiting for transfers between devices  31.1 us (50%)
  starting transfers between devices  20.2 us (33%)
  Pallas kernels  10.2 us (16%)
    ppermute x1, waiting for transfers between devices, body(): right = lax.ppermute(text, 'cols', [((i + 1) % 4, i) for i in range(4)])  9.57 us
    pallas_call x2, Pallas kernels, body(): pl.pallas_call(functools.partial(attend_kernel, first_head), out_shape=ja...  6.5 us
    ppermute x1, waiting for transfers between devices, body(): left = lax.ppermute(text, 'cols', [(i, (i + 1) % 4) for i in range(4)])  5.5 us
    ppermute x1, waiting for transfers between devices, body(): across = lax.ppermute(text, 'rows', swap)  4.82 us
    ppermute x1, starting transfers between devices, body(): last = lax.ppermute(last, 'cols', [(i, i + 1) for i in range(3)])  4.29 us
    ppermute x1, waiting for transfers between devices, body(): far.append(lax.ppermute(after(packed[1], passed), 'rows', swap))  3.89 us
    pallas_call x6, Pallas kernels, local(): pl.pallas_call(kernel, out_shape=shapes, in_specs=specs or [in_vmem] * le...  3.67 us
    ppermute x1, starting transfers between devices, body(): right = lax.ppermute(text, 'cols', [((i + 1) % 4, i) for i in range(4)])  3.65 us
  transfers between devices with their start and end apart: 15, of which 8 were waited for; matrix products, arithmetic and copies ran while one was open for 0% of the time, Pallas kernels for 9%

profile of v3, /device:TPU:0, one launch (start us, length us, event | category | flops | bytes accessed | tf_op | source)
XLA Modules:
  0.0 61.8 jit_solution(17630757107349557243)
XLA Ops:
  0.0 2.1 %pack.1 = (bf16[544,1536]{1,0:T(8,128)(2,1)S(1)}, bf16[32,1536]{1,0:T(8,128)(2,1)S(1)}, bf16[64,1536]{1,0:T(8,128)(2,1)S(1)}, bf16[512,1152]{1,0:T(8,128)(2,1)S(1)}, bf16[512,384]{1,0:T(8,128)(2,1)S(1)}) custom-call(bf16[256,1536]{1,0:T(8,128)(2,1)} %bitcast.12, bf16[256,1536]{1,0:T(8,128)(2,1)} %bitcast.13, bf16[8,32,1536]{2,1,0:T(8,128)(2,1)} %cells.5, ...), custom_call_target="tpu_custom_call" | custom-call | flops 1048576 | bytes 65536 | tf_op jit(solution)/shard_map/pack/pallas_call | solution.py:322
  2.1 0.5 collective-permute-start.7
  2.7 2.6 %collective-permute-start = (bf16[64,1536]{1,0:T(8,128)(2,1)S(1)}, bf16[64,1536]{1,0:T(8,128)(2,1)S(1)}, u32[]{:S(2)}, u32[]{:S(2)}) collective-permute-start(bf16[64,1536]{1,0:T(8,128)(2,1)S(1)} %get-tuple-element.17.refs_0_), channel_id=1, source_target_pairs={{0,8},{4,12},{8,0},{12,4},{1,9},{5,13},{9,1},{13,5},{2,10},{6,14},... | collective-permute-start | bytes 589832 | tf_op jit(solution)/shard_map/ppermute | solution.py:348
  5.2 0.7 %collective-permute-start.9 = (bf16[32,1536]{1,0:T(8,128)(2,1)S(1)}, bf16[32,1536]{1,0:T(8,128)(2,1)S(1)}, u32[]{:S(2)}, u32[]{:S(2)}) collective-permute-start(bf16[32,1536]{1,0:T(8,128)(2,1)S(1)} %get-tuple-element.22), channel_id=1, source_target_pairs={{4,8},{8,4},{5,9},{9,5},{6,10},{10,6},{7,11},{11,7},{20,24},{24,20... | collective-permute-start | bytes 294920 | tf_op jit(solution)/shard_map/ppermute | solution.py:349
  5.9 4.8 %collective-permute-done.refs_1_ = bf16[64,1536]{1,0:T(8,128)(2,1)S(1)} collective-permute-done((bf16[64,1536]{1,0:T(8,128)(2,1)S(1)}, bf16[64,1536]{1,0:T(8,128)(2,1)S(1)}, u32[]{:S(2)}, u32[]{:S(2)}) %collective-permute-start) | collective-permute-done | bytes 196640 | tf_op jit(solution)/shard_map/ppermute | solution.py:348
  10.7 2.8 %collective-permute-start.10 = (bf16[512,1152]{1,0:T(8,128)(2,1)S(1)}, bf16[512,1152]{1,0:T(8,128)(2,1)S(1)}, u32[]{:S(2)}, u32[]{:S(2)}) collective-permute-start(bf16[512,1152]{1,0:T(8,128)(2,1)S(1)} %get-tuple-element.23), channel_id=1, source_target_pairs={{0,8},{4,12},{8,0},{12,4},{1,9},{5,13},{9,1},{13,5},{2,10},{6,14},... | collective-permute-start | bytes 3538952 | tf_op jit(solution)/shard_map/ppermute | solution.py:350
  13.6 3.7 %collective-permute-start.2 = (bf16[128,1536]{1,0:T(8,128)(2,1)S(1)}, bf16[128,1536]{1,0:T(8,128)(2,1)S(1)}, u32[]{:S(2)}, u32[]{:S(2)}) collective-permute-start(bf16[128,1536]{1,0:T(8,128)(2,1)S(1)} %join.1.refs_0_), channel_id=1, source_target_pairs={{1,0},{2,1},{3,2},{0,3},{5,4},{6,5},{7,6},{4,7},{9,8},{10,9},{11,1... | collective-permute-start | bytes 1179656 | tf_op jit(solution)/shard_map/ppermute | solution.py:355
  17.2 9.6 %collective-permute-done.2.refs_2_ = bf16[128,1536]{1,0:T(8,128)(2,1)S(1)} collective-permute-done((bf16[128,1536]{1,0:T(8,128)(2,1)S(1)}, bf16[128,1536]{1,0:T(8,128)(2,1)S(1)}, u32[]{:S(2)}, u32[]{:S(2)}) %collective-permute-start.2) | collective-permute-done | bytes 393248 | tf_op jit(solution)/shard_map/ppermute | solution.py:355
  26.8 1.3 %collective-permute-start.4 = (bf16[128,1536]{1,0:T(8,128)(2,1)S(1)}, bf16[128,1536]{1,0:T(8,128)(2,1)S(1)}, u32[]{:S(2)}, u32[]{:S(2)}) collective-permute-start(bf16[128,1536]{1,0:T(8,128)(2,1)S(1)} %collective-permute-done.2.refs_2_), channel_id=1, source_target_pairs={{1,0},{2,1},{5,4},{6,5},{9,8},{10,9},{13,12},{14,13},{17,16},{18,1... | collective-permute-start | bytes 1179656 | tf_op jit(solution)/shard_map/ppermute | solution.py:358
  28.1 5.5 %collective-permute-done.1.refs_1_ = bf16[128,1536]{1,0:T(8,128)(2,1)S(1)} collective-permute-done((bf16[128,1536]{1,0:T(8,128)(2,1)S(1)}, bf16[128,1536]{1,0:T(8,128)(2,1)S(1)}, u32[]{:S(2)}, u32[]{:S(2)}) %collective-permute-start.1) | collective-permute-done | bytes 393248 | tf_op jit(solution)/shard_map/ppermute | solution.py:354
  33.6 0.7 %collective-permute-start.3 = (bf16[128,1536]{1,0:T(8,128)(2,1)S(1)}, bf16[128,1536]{1,0:T(8,128)(2,1)S(1)}, u32[]{:S(2)}, u32[]{:S(2)}) collective-permute-start(bf16[128,1536]{1,0:T(8,128)(2,1)S(1)} %collective-permute-done.1.refs_1_), channel_id=1, source_target_pairs={{1,2},{2,3},{5,6},{6,7},{9,10},{10,11},{13,14},{14,15},{17,18},{18... | collective-permute-start | bytes 1179656 | tf_op jit(solution)/shard_map/ppermute | solution.py:357
  34.3 0.1 edge.1
  34.4 4.3 %collective-permute-start.11 = (bf16[16,1536]{1,0:T(8,128)(2,1)S(1)}, bf16[16,1536]{1,0:T(8,128)(2,1)S(1)}, u32[]{:S(2)}, u32[]{:S(2)}) collective-permute-start(bf16[16,1536]{1,0:T(8,128)(2,1)S(1)} %get-tuple-element.24), channel_id=1, source_target_pairs={{0,1},{1,2},{2,3},{4,5},{5,6},{6,7},{8,9},{9,10},{10,11},{12,13},{... | collective-permute-start | bytes 147464 | tf_op jit(solution)/shard_map/ppermute | solution.py:361
  38.7 1.4 %collective-permute-start.12 = (bf16[16,1536]{1,0:T(8,128)(2,1)S(1)}, bf16[16,1536]{1,0:T(8,128)(2,1)S(1)}, u32[]{:S(2)}, u32[]{:S(2)}) collective-permute-start(bf16[16,1536]{1,0:T(8,128)(2,1)S(1)} %get-tuple-element.26), channel_id=1, source_target_pairs={{1,0},{2,1},{3,2},{5,4},{6,5},{7,6},{9,8},{10,9},{11,10},{13,12},{... | collective-permute-start | bytes 147464 | tf_op jit(solution)/shard_map/ppermute | solution.py:362
  40.2 0.8 %collective-permute-done.4.lower = bf16[128,1536]{1,0:T(8,128)(2,1)S(1)} collective-permute-done((bf16[128,1536]{1,0:T(8,128)(2,1)S(1)}, bf16[128,1536]{1,0:T(8,128)(2,1)S(1)}, u32[]{:S(2)}, u32[]{:S(2)}) %collective-permute-start.4) | collective-permute-done | bytes 393248 | tf_op jit(solution)/shard_map/ppermute | solution.py:358
  41.2 3.7 %collective-permute-done.12.right = bf16[16,1536]{1,0:T(8,128)(2,1)S(1)} collective-permute-done((bf16[16,1536]{1,0:T(8,128)(2,1)S(1)}, bf16[16,1536]{1,0:T(8,128)(2,1)S(1)}, u32[]{:S(2)}, u32[]{:S(2)}) %collective-permute-start.12) | collective-permute-done | bytes 49184 | tf_op jit(solution)/shard_map/ppermute | solution.py:362
  44.8 1.3 %term.1.refs_7_ = f32[256,1536]{1,0:T(8,128)S(1)} custom-call(bf16[8,32,1536]{2,1,0:T(8,128)(2,1)S(1)} %copy-done, bf16[544,1536]{1,0:T(8,128)(2,1)S(1)} %collective-permute-done.7.passed.refs_4_, bf16[32,1536]{1,0:T(8,128)(2,1)S(1)} %collective-permute-done.9.diagonal, bf16[16,1536]{1,0:T(8,128)(2,1)S(1)} %collective-permute-done.11.left, ...), custom_call_target="tpu_custom_call" | custom-call | flops 1048576 | bytes 65536 | tf_op jit(solution)/shard_map/term/pallas_call | solution.py:322
  46.2 0.5 collective-permute-start.6
  46.7 1.7 %collective-permute-start.8 = (bf16[512,384]{1,0:T(8,128)(2,1)S(1)}, bf16[512,384]{1,0:T(8,128)(2,1)S(1)}, u32[]{:S(2)}, u32[]{:S(2)}) collective-permute-start(bf16[512,384]{1,0:T(8,128)(2,1)S(1)} %get-tuple-element.20), channel_id=1, source_target_pairs={{0,8},{4,12},{8,0},{12,4},{1,9},{5,13},{9,1},{13,5},{2,10},{6,14},... | collective-permute-start | bytes 1179656 | tf_op jit(solution)/shard_map/ppermute | solution.py:356
  48.4 1.2 %collective-permute-done.6.refs_3_ = bf16[128,1536]{1,0:T(8,128)(2,1)S(1)} collective-permute-done((bf16[128,1536]{1,0:T(8,128)(2,1)S(1)}, bf16[128,1536]{1,0:T(8,128)(2,1)S(1)}, u32[]{:S(2)}, u32[]{:S(2)}) %collective-permute-start.6) | collective-permute-done | bytes 393248 | tf_op jit(solution)/shard_map/ppermute | solution.py:314
  49.6 4.3 %attend0.1.refs_8_ = f32[256,1536]{1,0:T(8,128)} custom-call(s32[1,1,2]{2,1,0:T(1,128)S(1)} %copy-done.6, s32[2,1,2]{2,1,0:T(1,128)S(1)} %copy-done.4, s32[2,1,2]{2,1,0:T(1,128)S(1)} %copy-done.5, bf16[256,1536]{1,0:T(8,128)(2,1)S(1)} %bitcast.8, bf16[256,1536]{1,0:T(8,128)(2,1)S(1)} %bitcast.10, bf16[256,1536]{1,0:T(8,128)(2,1)S(1)} %bitcast.6, ...), custom_call_target="tpu_custom_call" | custom-call | flops 1048576 | bytes 65536 | tf_op jit(solution)/shard_map/attend0/pallas_call | solution.py:385
  53.9 3.9 %collective-permute-done.8.refs_5_ = bf16[512,384]{1,0:T(8,128)(2,1)S(1)} collective-permute-done((bf16[512,384]{1,0:T(8,128)(2,1)S(1)}, bf16[512,384]{1,0:T(8,128)(2,1)S(1)}, u32[]{:S(2)}, u32[]{:S(2)}) %collective-permute-start.8) | collective-permute-done | bytes 393248 | tf_op jit(solution)/shard_map/ppermute | solution.py:356
  57.8 1.7 %collective-permute-done.14.refs_6_ = bf16[512,384]{1,0:T(8,128)(2,1)S(1)} collective-permute-done((bf16[512,384]{1,0:T(8,128)(2,1)S(1)}, bf16[512,384]{1,0:T(8,128)(2,1)S(1)}, u32[]{:S(2)}, u32[]{:S(2)}) %collective-permute-start.14) | collective-permute-done | bytes 393248 | tf_op jit(solution)/shard_map/ppermute | solution.py:314
  59.5 2.2 %attend1.1 = f32[256,1536]{1,0:T(8,128)} custom-call(s32[1,1,2]{2,1,0:T(1,128)S(1)} %copy-done.6, s32[2,1,2]{2,1,0:T(1,128)S(1)} %copy-done.4, s32[2,1,2]{2,1,0:T(1,128)S(1)} %copy-done.5, bf16[256,1536]{1,0:T(8,128)(2,1)S(1)} %bitcast.9, bf16[256,1536]{1,0:T(8,128)(2,1)S(1)} %bitcast.11, ...), custom_call_target="tpu_custom_call", output_to_operand_aliasing={{}: (14, {})} | custom-call | flops 1048576 | bytes 65536 | tf_op jit(solution)/shard_map/attend1/pallas_call | solution.py:385
  (28 shorter events, 0.3 us)
Async XLA Ops:
  0.0 34.3 %copy-start = (bf16[8,32,1536]{2,1,0:T(8,128)(2,1)S(1)}, bf16[8,32,1536]{2,1,0:T(8,128)(2,1)}, u32[]{:S(2)}) copy-start(bf16[8,32,1536]{2,1,0:T(8,128)(2,1)} %cells.5) | copy-start | bytes 2359300
  2.1 32.1 %collective-permute-start.7 = (bf16[544,1536]{1,0:T(8,128)(2,1)S(1)}, bf16[544,1536]{1,0:T(8,128)(2,1)S(1)}, u32[]{:S(2)}, u32[]{:S(2)}) collective-permute-start(bf16[544,1536]{1,0:T(8,128)(2,1)S(1)} %get-tuple-element.18), channel_id=1, source_target_pairs={{0,4},{4,0},{8,12},{12,8},{1,5},{5,1},{9,13},{13,9},{2,6},{6,2},{1... | collective-permute-start | bytes 5013512 | tf_op jit(solution)/shard_map/ppermute | solution.py:314
  2.7 8.1 %collective-permute-start = (bf16[64,1536]{1,0:T(8,128)(2,1)S(1)}, bf16[64,1536]{1,0:T(8,128)(2,1)S(1)}, u32[]{:S(2)}, u32[]{:S(2)}) collective-permute-start(bf16[64,1536]{1,0:T(8,128)(2,1)S(1)} %get-tuple-element.17.refs_0_), channel_id=1, source_target_pairs={{0,8},{4,12},{8,0},{12,4},{1,9},{5,13},{9,1},{13,5},{2,10},{6,14},... | collective-permute-start | bytes 589832 | tf_op jit(solution)/shard_map/ppermute | solution.py:348
  5.2 0.7 %collective-permute-start.9 = (bf16[32,1536]{1,0:T(8,128)(2,1)S(1)}, bf16[32,1536]{1,0:T(8,128)(2,1)S(1)}, u32[]{:S(2)}, u32[]{:S(2)}) collective-permute-start(bf16[32,1536]{1,0:T(8,128)(2,1)S(1)} %get-tuple-element.22), channel_id=1, source_target_pairs={{4,8},{8,4},{5,9},{9,5},{6,10},{10,6},{7,11},{11,7},{20,24},{24,20... | collective-permute-start | bytes 294920 | tf_op jit(solution)/shard_map/ppermute | solution.py:349
  10.7 35.4 %collective-permute-start.10 = (bf16[512,1152]{1,0:T(8,128)(2,1)S(1)}, bf16[512,1152]{1,0:T(8,128)(2,1)S(1)}, u32[]{:S(2)}, u32[]{:S(2)}) collective-permute-start(bf16[512,1152]{1,0:T(8,128)(2,1)S(1)} %get-tuple-element.23), channel_id=1, source_target_pairs={{0,8},{4,12},{8,0},{12,4},{1,9},{5,13},{9,1},{13,5},{2,10},{6,14},... | collective-permute-start | bytes 3538952 | tf_op jit(solution)/shard_map/ppermute | solution.py:350
  13.6 13.2 %collective-permute-start.2 = (bf16[128,1536]{1,0:T(8,128)(2,1)S(1)}, bf16[128,1536]{1,0:T(8,128)(2,1)S(1)}, u32[]{:S(2)}, u32[]{:S(2)}) collective-permute-start(bf16[128,1536]{1,0:T(8,128)(2,1)S(1)} %join.1.refs_0_), channel_id=1, source_target_pairs={{1,0},{2,1},{3,2},{0,3},{5,4},{6,5},{7,6},{4,7},{9,8},{10,9},{11,1... | collective-permute-start | bytes 1179656 | tf_op jit(solution)/shard_map/ppermute | solution.py:355
  17.2 16.4 %collective-permute-start.1 = (bf16[128,1536]{1,0:T(8,128)(2,1)S(1)}, bf16[128,1536]{1,0:T(8,128)(2,1)S(1)}, u32[]{:S(2)}, u32[]{:S(2)}) collective-permute-start(bf16[128,1536]{1,0:T(8,128)(2,1)S(1)} %join.1.refs_0_), channel_id=1, source_target_pairs={{0,1},{1,2},{2,3},{3,0},{4,5},{5,6},{6,7},{7,4},{8,9},{9,10},{10,1... | collective-permute-start | bytes 1179656 | tf_op jit(solution)/shard_map/ppermute | solution.py:354
  26.8 14.2 %collective-permute-start.4 = (bf16[128,1536]{1,0:T(8,128)(2,1)S(1)}, bf16[128,1536]{1,0:T(8,128)(2,1)S(1)}, u32[]{:S(2)}, u32[]{:S(2)}) collective-permute-start(bf16[128,1536]{1,0:T(8,128)(2,1)S(1)} %collective-permute-done.2.refs_2_), channel_id=1, source_target_pairs={{1,0},{2,1},{5,4},{6,5},{9,8},{10,9},{13,12},{14,13},{17,16},{18,1... | collective-permute-start | bytes 1179656 | tf_op jit(solution)/shard_map/ppermute | solution.py:358
  33.6 7.5 %collective-permute-start.3 = (bf16[128,1536]{1,0:T(8,128)(2,1)S(1)}, bf16[128,1536]{1,0:T(8,128)(2,1)S(1)}, u32[]{:S(2)}, u32[]{:S(2)}) collective-permute-start(bf16[128,1536]{1,0:T(8,128)(2,1)S(1)} %collective-permute-done.1.refs_1_), channel_id=1, source_target_pairs={{1,2},{2,3},{5,6},{6,7},{9,10},{10,11},{13,14},{14,15},{17,18},{18... | collective-permute-start | bytes 1179656 | tf_op jit(solution)/shard_map/ppermute | solution.py:357
  34.4 6.8 %collective-permute-start.11 = (bf16[16,1536]{1,0:T(8,128)(2,1)S(1)}, bf16[16,1536]{1,0:T(8,128)(2,1)S(1)}, u32[]{:S(2)}, u32[]{:S(2)}) collective-permute-start(bf16[16,1536]{1,0:T(8,128)(2,1)S(1)} %get-tuple-element.24), channel_id=1, source_target_pairs={{0,1},{1,2},{2,3},{4,5},{5,6},{6,7},{8,9},{9,10},{10,11},{12,13},{... | collective-permute-start | bytes 147464 | tf_op jit(solution)/shard_map/ppermute | solution.py:361
  38.7 6.1 %copy-start.3 = (f32[3,3,1536]{2,1,0:T(4,128)S(1)}, f32[3,3,1536]{2,1,0:T(4,128)}, u32[]{:S(2)}) copy-start(f32[3,3,1536]{2,1,0:T(4,128)} %weights.1) | copy-start | bytes 165892
  38.7 6.1 %collective-permute-start.12 = (bf16[16,1536]{1,0:T(8,128)(2,1)S(1)}, bf16[16,1536]{1,0:T(8,128)(2,1)S(1)}, u32[]{:S(2)}, u32[]{:S(2)}) collective-permute-start(bf16[16,1536]{1,0:T(8,128)(2,1)S(1)} %get-tuple-element.26), channel_id=1, source_target_pairs={{1,0},{2,1},{3,2},{5,4},{6,5},{7,6},{9,8},{10,9},{11,10},{13,12},{... | collective-permute-start | bytes 147464 | tf_op jit(solution)/shard_map/ppermute | solution.py:362
  41.0 8.6 %collective-permute-start.5 = (bf16[384,1536]{1,0:T(8,128)(2,1)S(1)}, bf16[384,1536]{1,0:T(8,128)(2,1)S(1)}, u32[]{:S(2)}, u32[]{:S(2)}) collective-permute-start(bf16[384,1536]{1,0:T(8,128)(2,1)S(1)} %bundle.1.refs_0_), channel_id=1, source_target_pairs={{0,4},{4,0},{8,12},{12,8},{1,5},{5,1},{9,13},{13,9},{2,6},{6,2},{1... | collective-permute-start | bytes 3538952 | tf_op jit(solution)/shard_map/ppermute | solution.py:314
  41.1 8.5 %copy-start.1 = (bf16[8,32,1536]{2,1,0:T(8,128)(2,1)S(1)}, bf16[8,32,1536]{2,1,0:T(8,128)(2,1)}, u32[]{:S(2)}) copy-start(bf16[8,32,1536]{2,1,0:T(8,128)(2,1)} %param.11) | copy-start | bytes 2359300
  41.1 8.5 %copy-start.2 = (bf16[8,32,1536]{2,1,0:T(8,128)(2,1)S(1)}, bf16[8,32,1536]{2,1,0:T(8,128)(2,1)}, u32[]{:S(2)}) copy-start(bf16[8,32,1536]{2,1,0:T(8,128)(2,1)} %param.12) | copy-start | bytes 2359300
  41.1 8.5 %copy-start.4 = (s32[2,1,2]{2,1,0:T(1,128)S(1)}, s32[2,1,2]{2,1,0:T(1,128)}, u32[]{:S(2)}) copy-start(s32[2,1,2]{2,1,0:T(1,128)} %pattern_ref.3) | copy-start | bytes 52
  41.1 8.5 %copy-start.5 = (s32[2,1,2]{2,1,0:T(1,128)S(1)}, s32[2,1,2]{2,1,0:T(1,128)}, u32[]{:S(2)}) copy-start(s32[2,1,2]{2,1,0:T(1,128)} %text_ref.3) | copy-start | bytes 52
  41.1 8.5 %copy-start.6 = (s32[1,1,2]{2,1,0:T(1,128)S(1)}, s32[1,1,2]{2,1,0:T(1,128)}, u32[]{:S(2)}) copy-start(s32[1,1,2]{2,1,0:T(1,128)} %reads_ref.3) | copy-start | bytes 28
  46.1 3.5 %collective-permute-start.13 = (bf16[512,1152]{1,0:T(8,128)(2,1)S(1)}, bf16[512,1152]{1,0:T(8,128)(2,1)S(1)}, u32[]{:S(2)}, u32[]{:S(2)}) collective-permute-start(bf16[512,1152]{1,0:T(8,128)(2,1)S(1)} %collective-permute-done.10.refs_5_), channel_id=1, source_target_pairs={{0,4},{4,0},{8,12},{12,8},{1,5},{5,1},{9,13},{13,9},{2,6},{6,2},{1... | collective-permute-start | bytes 3538952 | tf_op jit(solution)/shard_map/ppermute | solution.py:314
  46.2 3.4 %collective-permute-start.6 = (bf16[128,1536]{1,0:T(8,128)(2,1)S(1)}, bf16[128,1536]{1,0:T(8,128)(2,1)S(1)}, u32[]{:S(2)}, u32[]{:S(2)}) collective-permute-start(bf16[128,1536]{1,0:T(8,128)(2,1)S(1)} %choose.1.refs_1_), channel_id=1, source_target_pairs={{0,4},{4,0},{8,12},{12,8},{1,5},{5,1},{9,13},{13,9},{2,6},{6,2},{1... | collective-permute-start | bytes 1179656 | tf_op jit(solution)/shard_map/ppermute | solution.py:314
  46.7 11.1 %collective-permute-start.8 = (bf16[512,384]{1,0:T(8,128)(2,1)S(1)}, bf16[512,384]{1,0:T(8,128)(2,1)S(1)}, u32[]{:S(2)}, u32[]{:S(2)}) collective-permute-start(bf16[512,384]{1,0:T(8,128)(2,1)S(1)} %get-tuple-element.20), channel_id=1, source_target_pairs={{0,8},{4,12},{8,0},{12,4},{1,9},{5,13},{9,1},{13,5},{2,10},{6,14},... | collective-permute-start | bytes 1179656 | tf_op jit(solution)/shard_map/ppermute | solution.py:356
  57.8 1.7 %collective-permute-start.14 = (bf16[512,384]{1,0:T(8,128)(2,1)S(1)}, bf16[512,384]{1,0:T(8,128)(2,1)S(1)}, u32[]{:S(2)}, u32[]{:S(2)}) collective-permute-start(bf16[512,384]{1,0:T(8,128)(2,1)S(1)} %collective-permute-done.8.refs_5_), channel_id=1, source_target_pairs={{0,4},{4,0},{8,12},{12,8},{1,5},{5,1},{9,13},{13,9},{2,6},{6,2},{1... | collective-permute-start | bytes 1179656 | tf_op jit(solution)/shard_map/ppermute | solution.py:314

commit v4 on v3

--- a/solution.py
+++ b/solution.py
@@ -15,6 +15,7 @@
 SCORE_SCALE = 1.0 / math.sqrt(HEAD_DIM)
 EXP2_SCALE = SCORE_SCALE * math.log2(math.e)
 CHUNK_HEADS = (9, 3)
+CHUNK_SPARE = (0, 16)
 GROUP = 8
 VMEM_LIMIT = 24 * 1024 * 1024
 
@@ -132,29 +133,59 @@
     )
 
 
-def pack_kernel(k_hbm, v_hbm, cells, text_k, text_v, passed, diagonal, text, *refs):
-    outs, sems = refs[:-1], refs[-1]
-    tokens, shard = k_hbm.shape[0], text_k.shape[0]
-    row = lax.axis_index("rows")
-    end, edges = cells.shape[0] - 1, pl.ds(2 * tokens, cells.shape[1])
-    copies = []
-    for which, source in enumerate((text_k, text_v)):
-        copies.append((source, text.at[pl.ds(which * shard, shard)]))
-    first = 0
-    for out in outs:
-        part = pl.ds(first, out.shape[1])
-        first += out.shape[1]
-        for which, source in enumerate((k_hbm, v_hbm)):
-            copies.append((source.at[:, part], out.at[pl.ds(which * tokens, tokens)]))
-    for which, source in enumerate((k_hbm, v_hbm)):
-        copies.append((source, passed.at[pl.ds(which * tokens, tokens)]))
-    copies.append((cells.at[jnp.where(row % 2 == 0, end, 0)], passed.at[edges]))
-    copies.append((cells.at[jnp.where(row < 2, end, 0)], diagonal))
+def run_copies(copies, sems):
     copies = [pltpu.make_async_copy(*pair, sems.at[i]) for i, pair in enumerate(copies)]
     for copy in copies:
         copy.start()
     for copy in copies:
         copy.wait()
+
+
+def pack_kernel(cells, text_k, text_v, beside, diagonal, text, sems):
+    shard = text_k.shape[0]
+    row = lax.axis_index("rows")
+    end = cells.shape[0] - 1
+    copies = []
+    for which, source in enumerate((text_k, text_v)):
+        copies.append((source, text.at[pl.ds(which * shard, shard)]))
+    copies.append((cells.at[jnp.where(row % 2 == 0, end, 0)], beside))
+    copies.append((cells.at[jnp.where(row < 2, end, 0)], diagonal))
+    run_copies(copies, sems)
+
+
+def send_kernel(wanted, k_hbm, v_hbm, passed_k, passed_v, *refs):
+    outs, sems = refs[:-1], refs[-1]
+    row = lax.axis_index("rows")
+
+    def block_of(owner):
+        found = 0
+        for turn in range(2):
+            entry = wanted[0, 0, turn]
+            found = jnp.where(entry // 2 == owner, entry % 2, found)
+        return pl.multiple_of(found * PER_BLOCK, PER_BLOCK)
+
+    own, other = block_of(row), block_of(row + 1 - 2 * (row % 2))
+    copies = []
+    first = 0
+    for out in outs:
+        part = pl.ds(first, out.shape[1])
+        first += out.shape[1]
+        for which, (source, passed) in enumerate(((k_hbm, passed_k), (v_hbm, passed_v))):
+            at = 2 * PER_BLOCK * which
+            copies.append(
+                (source.at[pl.ds(own, PER_BLOCK), part], out.at[pl.ds(at, PER_BLOCK)])
+            )
+            copies.append(
+                (
+                    passed.at[pl.ds(other, PER_BLOCK), part],
+                    out.at[pl.ds(at + PER_BLOCK, PER_BLOCK)],
+                )
+            )
+    for out, spare in zip(outs, CHUNK_SPARE):
+        if spare:
+            rows = pl.ds(out.shape[0] - spare, spare)
+            out[rows, :] = jnp.zeros((spare, out.shape[1]), out.dtype)
+    run_copies(copies, sems)
 
 
 def bundle_kernel(*refs):
@@ -169,10 +200,9 @@
     out[...] = jnp.where(lax.axis_index("cols") >= 2, upper[...], lower[...])
 
 
-def edge_kernel(cells, passed, diagonal, last, first):
+def edge_kernel(cells, beside, diagonal, last, first):
     rows_here, cols_here, width = cells.shape
-    beside = passed[pl.ds(passed.shape[0] - cols_here, cols_here), :]
-    above, below = above_below(beside, diagonal[...])
+    above, below = above_below(beside[...], diagonal[...])
     rows = [above] + [cells[i] for i in range(rows_here)] + [below]
     rows = [row.astype(jnp.float32) for row in rows]
     spare = jnp.zeros((16 - len(rows), width), jnp.float32)
@@ -189,15 +219,13 @@
     )
 
 
-def term_kernel(cells, passed, diagonal, left, right, weights, out):
+def term_kernel(cells, beside, diagonal, left, right, weights, out):
     rows_here, cols_here, width = cells.shape
     col = lax.axis_index("cols")
     place = lax.broadcasted_iota(jnp.int32, (cols_here, HEAD_DIM), 0)
     for lane in range(width // HEAD_DIM):
         part = pl.ds(lane * HEAD_DIM, HEAD_DIM)
-        above, below = above_below(
-            passed[pl.ds(passed.shape[0] - cols_here, cols_here), part], diagonal[:, part]
-        )
+        above, below = above_below(beside[:, part], diagonal[:, part])
         lefts = left[:, part].astype(jnp.float32)
         rights = right[:, part].astype(jnp.float32)
         lefts = jnp.where(col > 0, lefts, 0.0)
@@ -226,13 +254,13 @@
 
 
 def attend_kernel(first_head, reads_ref, pattern_ref, text_ref, q, k, v, *refs):
-    near, last, near_mate, last_mate, passed, across_kv, both_kv, term = refs[:8]
+    near, last, near_mate, last_mate, passed_k, passed_v, arrived, term = refs[:8]
     out = refs[-1]
     row, col = lax.axis_index("rows"), lax.axis_index("cols")
     across, core = row // 2, row % 2
     shard = last.shape[0] // 4
-    half = across_kv.shape[0] // 2
-    head_count = across_kv.shape[1] // HEAD_DIM
+    half = 2 * PER_BLOCK
+    head_count = arrived.shape[1] // HEAD_DIM
 
     def lanes(head):
         return pl.ds((first_head + head) * HEAD_DIM, HEAD_DIM)
@@ -252,13 +280,13 @@
         slot = pattern_ref[block, 0, 0] + pattern_ref[block, 0, 1] - block - 2
         wanted = reads_ref[0, 0, slot]
         owner = wanted // 2
-        first = (wanted % 2) * PER_BLOCK
-        packed = pl.ds(pl.multiple_of(first + which * half, PER_BLOCK), PER_BLOCK)
-        mate = passed[packed, lanes(head)]
+        mate_at = (wanted % 2) * PER_BLOCK
+        far_at = jnp.where(owner % 2 == core, 0, PER_BLOCK) + which * half
+        passed = (passed_k, passed_v)[which]
+        mate = passed[pl.ds(pl.multiple_of(mate_at, PER_BLOCK), PER_BLOCK), lanes(head)]
         here = pl.ds(head * HEAD_DIM, HEAD_DIM)
-        straight, crossed = across_kv[packed, here], both_kv[packed, here]
-        arrived = jnp.where(owner % 2 == core, straight, crossed)
-        return jnp.where(owner // 2 == across, mate, arrived)
+        far = arrived[pl.ds(pl.multiple_of(far_at, PER_BLOCK), PER_BLOCK), here]
+        return jnp.where(owner // 2 == across, mate, far)
 
     def gathered(block, head, which):
         own = (k, v)[which][pl.ds(block * PER_BLOCK, PER_BLOCK), lanes(head)]
@@ -331,53 +359,64 @@
         )(*args)
 
     chunks = tuple(
-        jax.ShapeDtypeStruct((2 * tokens, n * HEAD_DIM), jnp.bfloat16) for n in CHUNK_HEADS
+        jax.ShapeDtypeStruct((2 * tokens + spare, n * HEAD_DIM), jnp.bfloat16)
+        for n, spare in zip(CHUNK_HEADS, CHUNK_SPARE)
     )
     in_place = [
         pltpu.with_memory_space_constraint(value, pltpu.HBM)
         for value in (flat(k_stale), flat(v_stale), v_fresh, text_k, text_v)
     ]
-    passed, diagonal, text, *packed = local(
+    wanted = lax.ppermute(reads, "rows", swap)
+    beside, diagonal, text = local(
         pack_kernel,
         "pack",
-        rows_of(2 * tokens + cols_here, cols_here, 2 * shard) + chunks,
-        *in_place,
-        specs=[in_hbm] * 5,
-        scratch=[pltpu.SemaphoreType.DMA((6 + 2 * len(CHUNK_HEADS),))],
+        rows_of(cols_here, cols_here, 2 * shard),
+        *in_place[2:],
+        specs=[in_hbm] * 3,
+        scratch=[pltpu.SemaphoreType.DMA((4,))],
     )
     across = lax.ppermute(text, "rows", swap)
     diagonal = lax.ppermute(diagonal, "rows", [(1, 2), (2, 1)])
-    far = [lax.ppermute(after(packed[0], across, diagonal), "rows", swap)]
-    passed = to_mate(passed)
-
-    text = local(bundle_kernel, "join", rows_of(4 * shard), text, across)
+    beside = to_mate(beside)
+    passed = [to_mate(value) for value in in_place[:2]]
+    packed = local(
+        send_kernel,
+        "send",
+        chunks,
+        wanted,
+        *in_place[:2],
+        *passed,
+        specs=[pl.BlockSpec(memory_space=pltpu.SMEM)] + [in_hbm] * 2 + [in_vmem] * 2,
+        scratch=[pltpu.SemaphoreType.DMA((4 * len(CHUNK_HEADS),))],
+    )
+    far = [lax.ppermute(chunk, "rows", swap) for chunk in packed]
+
+    text = local(
+        bundle_kernel, "join", rows_of(4 * shard), after(text, diagonal, packed[0], beside), across
+    )
     left = lax.ppermute(text, "cols", [(i, (i + 1) % 4) for i in range(4)])
     right = lax.ppermute(text, "cols", [((i + 1) % 4, i) for i in range(4)])
-    far.append(lax.ppermute(after(packed[1], passed), "rows", swap))
+    last, first = local(edge_kernel, "edge", rows_of(16, 16), v_fresh, beside, diagonal)
+    last = lax.ppermute(last, "cols", [(i, i + 1) for i in range(3)])
+    first = lax.ppermute(first, "cols", [(i + 1, i) for i in range(3)])
     upper = lax.ppermute(left, "cols", [(1, 2), (2, 3)])
     lower = lax.ppermute(right, "cols", [(1, 0), (2, 1)])
 
-    last, first = local(edge_kernel, "edge", rows_of(16, 16), v_fresh, passed, diagonal)
-    last = lax.ppermute(last, "cols", [(i, i + 1) for i in range(3)])
-    first = lax.ppermute(first, "cols", [(i + 1, i) for i in range(3)])
     near = local(bundle_kernel, "bundle", rows_of(12 * shard), text, left, right)
     near_mate = to_mate(near)
     term = local(
         term_kernel,
         "term",
         jax.ShapeDtypeStruct((tokens, width), jnp.float32),
-        v_fresh, passed, diagonal, after(last, near), first, conv_w,
-    )
-    rest = local(choose_kernel, "choose", rows_of(4 * shard), upper, lower)
+        v_fresh, beside, diagonal, last, first, conv_w,
+    )
+    rest = local(choose_kernel, "choose", rows_of(4 * shard), after(upper, far[0], term), lower)
     rest_mate = to_mate(rest)
-    far[0] = after(far[0], term, rest)
-
     out = None
     first_head = 0
     for chunk, head_count in enumerate(CHUNK_HEADS):
         if out is not None:
             far[chunk] = after(far[chunk], out)
-        far_mate = to_mate(far[chunk])
         block = pl.BlockSpec(
             (pl.Element(tokens), pl.Element(head_count * HEAD_DIM)),
             lambda i, *_, at=first_head * HEAD_DIM: (0, at),
@@ -397,7 +436,7 @@
             name=f"attend{chunk}",
         )(
             reads, pattern, text_blocks, flat(q_fresh), flat(k_fresh), flat(v_fresh),
-            near, rest, near_mate, rest_mate, passed, far[chunk], far_mate, term,
+            near, rest, near_mate, rest_mate, *passed, far[chunk], term,
             *([out] if out is not None else []),
         )
         first_head += head_count

time: 62 us -> 69.1 us (1.11)
  Pallas kernels: 10.2 us -> 14 us
  waiting for transfers between devices: 31.1 us -> 34 us
  local copies, waits for them, and re-layouts: 0.04 us -> 1.84 us
  starting transfers between devices: 20.2 us -> 18.7 us
    ppermute x1, waiting for transfers between devices: 4.82 us -> 0.01 us  [body(): across = lax.ppermute(text, 'rows', swap)]
    ppermute x1, waiting for transfers between devices: 3.65 us -> 7.01 us  [body(): first = lax.ppermute(first, 'cols', [(i + 1, i) for i in range(3)])]
    ppermute x1, waiting for transfers between devices: 5.5 us -> 8.58 us  [body(): left = lax.ppermute(text, 'cols', [(i, (i + 1) % 4) for i in range(4)])]
    pallas_call x2, Pallas kernels: 6.5 us -> 8.85 us  [body(): pl.pallas_call(functools.partial(attend_kernel, first_head), out_shape=ja...]
    ppermute x2 -> x3, starting transfers between devices: 4.56 us -> 2.42 us  [the longest x2 2.34 us: body(): far = [lax.ppermute(chunk, 'rows', swap) for chunk in packed]]
    unnamed x14 -> x18, local copies, waits for them, and re-layouts: 0.04 us -> 1.84 us
    ppermute x1, waiting for transfers between devices: 0.01 us -> 1.73 us  [body(): last = lax.ppermute(last, 'cols', [(i, i + 1) for i in range(3)])]
    pallas_call x6 -> x7, Pallas kernels: 3.67 us -> 5.19 us  [local(): pl.pallas_call(kernel, out_shape=shapes, in_specs=specs or [in_vmem] * le...]
  transfers between devices with their start and end apart: 15 -> 16, of which waited for: 8 -> 7; matrix products, arithmetic and copies ran while one was open for 0% -> 0% of each run, Pallas kernels for 9% -> 12%
where the time goes in v4:
time: 69.1 us; the launch traced here: 68.8 us
  waiting for transfers between devices  34 us (49%)
  starting transfers between devices  18.7 us (27%)
  Pallas kernels  14 us (20%)
  local copies, waits for them, and re-layouts  1.84 us (3%)
    ppermute x1, waiting for transfers between devices, body(): right = lax.ppermute(text, 'cols', [((i + 1) % 4, i) for i in range(4)])  9.51 us
    pallas_call x2, Pallas kernels, body(): pl.pallas_call(functools.partial(attend_kernel, first_head), out_shape=ja...  8.85 us
    ppermute x1, waiting for transfers between devices, body(): left = lax.ppermute(text, 'cols', [(i, (i + 1) % 4) for i in range(4)])  8.58 us
    ppermute x1, waiting for transfers between devices, body(): first = lax.ppermute(first, 'cols', [(i + 1, i) for i in range(3)])  7.01 us
    pallas_call x7, Pallas kernels, local(): pl.pallas_call(kernel, out_shape=shapes, in_specs=specs or [in_vmem] * le...  5.19 us
    ppermute x1, starting transfers between devices, body(): last = lax.ppermute(last, 'cols', [(i, i + 1) for i in range(3)])  5.07 us
    ppermute x1, waiting for transfers between devices, body(): wanted = lax.ppermute(reads, 'rows', swap)  4.39 us
    ppermute x1, starting transfers between devices, body(): right = lax.ppermute(text, 'cols', [((i + 1) % 4, i) for i in range(4)])  3.65 us
  transfers between devices with their start and end apart: 16, of which 7 were waited for; matrix products, arithmetic and copies ran while one was open for 0% of the time, Pallas kernels for 12%

profile of v4, /device:TPU:0, one launch (start us, length us, event | category | flops | bytes accessed | tf_op | source)
XLA Modules:
  0.0 68.8 jit_solution(18096076782128320424)
XLA Ops:
  0.0 0.5 collective-permute-start.2
  0.5 1.1 %pack.1 = (bf16[32,1536]{1,0:T(8,128)(2,1)S(1)}, bf16[32,1536]{1,0:T(8,128)(2,1)S(1)}, bf16[64,1536]{1,0:T(8,128)(2,1)S(1)}) custom-call(bf16[8,32,1536]{2,1,0:T(8,128)(2,1)} %cells.5, bf16[32,1536]{1,0:T(8,128)(2,1)} %text_k.1, bf16[32,1536]{1,0:T(8,128)(2,1)} %text_v.1), custom_call_target="tpu_custom_call" | custom-call | flops 1048576 | bytes 65536 | tf_op jit(solution)/shard_map/pack/pallas_call | solution.py:350
  1.6 3.0 %collective-permute-start.5 = (bf16[64,1536]{1,0:T(8,128)(2,1)S(1)}, bf16[64,1536]{1,0:T(8,128)(2,1)S(1)}, u32[]{:S(2)}, u32[]{:S(2)}) collective-permute-start(bf16[64,1536]{1,0:T(8,128)(2,1)S(1)} %get-tuple-element.19.refs_0_), channel_id=1, source_target_pairs={{0,8},{4,12},{8,0},{12,4},{1,9},{5,13},{9,1},{13,5},{2,10},{6,14},... | collective-permute-start | bytes 589832 | tf_op jit(solution)/shard_map/ppermute | solution.py:378
  4.7 0.7 collective-permute-start
  5.3 4.4 %collective-permute-done.1.wanted = s32[1,1,2]{2,1,0:T(1,128)S(1)} collective-permute-done((s32[1,1,2]{2,1,0:T(1,128)}, s32[1,1,2]{2,1,0:T(1,128)S(1)}, u32[]{:S(2)}, u32[]{:S(2)}) %collective-permute-start.1) | collective-permute-done | bytes 40 | tf_op jit(solution)/shard_map/ppermute | solution.py:369
  9.7 0.9 %copy-done.7 = bf16[256,1536]{1,0:T(8,128)(2,1)} copy-done((bf16[256,1536]{1,0:T(8,128)(2,1)}, bf16[256,1536]{1,0:T(8,128)(2,1)S(1)}, u32[]{:S(2)}) %copy-start.7) | copy-done | bytes 786456
  10.6 0.9 %copy-done.8 = bf16[256,1536]{1,0:T(8,128)(2,1)} copy-done((bf16[256,1536]{1,0:T(8,128)(2,1)}, bf16[256,1536]{1,0:T(8,128)(2,1)S(1)}, u32[]{:S(2)}) %copy-start.8) | copy-done | bytes 786456
  11.5 2.6 %send.1 = (bf16[512,1152]{1,0:T(8,128)(2,1)S(1)}, bf16[528,384]{1,0:T(8,128)(2,1)S(1)}) custom-call(s32[1,1,2]{2,1,0:T(1,128)S(1)} %collective-permute-done.1.wanted, bf16[256,1536]{1,0:T(8,128)(2,1)} %bitcast.13, bf16[256,1536]{1,0:T(8,128)(2,1)} %bitcast.15, bf16[256,1536]{1,0:T(8,128)(2,1)} %copy-done.7, bf16[256,1536]{1,0:T(8,128)(2,1)} %copy-done.8), custom_call_target="tpu_custom_call" | custom-call | flops 1048576 | bytes 65536 | tf_op jit(solution)/shard_map/send/pallas_call | solution.py:350
  14.1 1.8 %collective-permute-start.9 = (bf16[512,1152]{1,0:T(8,128)(2,1)S(1)}, bf16[512,1152]{1,0:T(8,128)(2,1)S(1)}, u32[]{:S(2)}, u32[]{:S(2)}) collective-permute-start(bf16[512,1152]{1,0:T(8,128)(2,1)S(1)} %get-tuple-element.17), channel_id=1, source_target_pairs={{0,8},{4,12},{8,0},{12,4},{1,9},{5,13},{9,1},{13,5},{2,10},{6,14},... | collective-permute-start | bytes 3538952 | tf_op jit(solution)/shard_map/ppermute | solution.py:392
  16.0 3.7 %collective-permute-start.7 = (bf16[128,1536]{1,0:T(8,128)(2,1)S(1)}, bf16[128,1536]{1,0:T(8,128)(2,1)S(1)}, u32[]{:S(2)}, u32[]{:S(2)}) collective-permute-start(bf16[128,1536]{1,0:T(8,128)(2,1)S(1)} %join.1.refs_0_), channel_id=1, source_target_pairs={{1,0},{2,1},{3,2},{0,3},{5,4},{6,5},{7,6},{4,7},{9,8},{10,9},{11,1... | collective-permute-start | bytes 1179656 | tf_op jit(solution)/shard_map/ppermute | solution.py:398
  19.7 9.5 %collective-permute-done.7.refs_2_ = bf16[128,1536]{1,0:T(8,128)(2,1)S(1)} collective-permute-done((bf16[128,1536]{1,0:T(8,128)(2,1)S(1)}, bf16[128,1536]{1,0:T(8,128)(2,1)S(1)}, u32[]{:S(2)}, u32[]{:S(2)}) %collective-permute-start.7) | collective-permute-done | bytes 393248 | tf_op jit(solution)/shard_map/ppermute | solution.py:398
  29.2 8.6 %collective-permute-done.6.refs_1_ = bf16[128,1536]{1,0:T(8,128)(2,1)S(1)} collective-permute-done((bf16[128,1536]{1,0:T(8,128)(2,1)S(1)}, bf16[128,1536]{1,0:T(8,128)(2,1)S(1)}, u32[]{:S(2)}, u32[]{:S(2)}) %collective-permute-start.6) | collective-permute-done | bytes 393248 | tf_op jit(solution)/shard_map/ppermute | solution.py:397
  37.9 0.7 collective-permute-start.8
  38.6 1.3 %collective-permute-start.12 = (bf16[128,1536]{1,0:T(8,128)(2,1)S(1)}, bf16[128,1536]{1,0:T(8,128)(2,1)S(1)}, u32[]{:S(2)}, u32[]{:S(2)}) collective-permute-start(bf16[128,1536]{1,0:T(8,128)(2,1)S(1)} %collective-permute-done.7.refs_2_), channel_id=1, source_target_pairs={{1,0},{2,1},{5,4},{6,5},{9,8},{10,9},{13,12},{14,13},{17,16},{18,1... | collective-permute-start | bytes 1179656 | tf_op jit(solution)/shard_map/ppermute | solution.py:403
  40.0 5.1 %collective-permute-start.10 = (bf16[16,1536]{1,0:T(8,128)(2,1)S(1)}, bf16[16,1536]{1,0:T(8,128)(2,1)S(1)}, u32[]{:S(2)}, u32[]{:S(2)}) collective-permute-start(bf16[16,1536]{1,0:T(8,128)(2,1)S(1)} %get-tuple-element.20), channel_id=1, source_target_pairs={{0,1},{1,2},{2,3},{4,5},{5,6},{6,7},{8,9},{9,10},{10,11},{12,13},{... | collective-permute-start | bytes 147464 | tf_op jit(solution)/shard_map/ppermute | solution.py:400
  45.1 1.7 %collective-permute-done.10.left = bf16[16,1536]{1,0:T(8,128)(2,1)S(1)} collective-permute-done((bf16[16,1536]{1,0:T(8,128)(2,1)S(1)}, bf16[16,1536]{1,0:T(8,128)(2,1)S(1)}, u32[]{:S(2)}, u32[]{:S(2)}) %collective-permute-start.10) | collective-permute-done | bytes 49184 | tf_op jit(solution)/shard_map/ppermute | solution.py:400
  46.9 1.3 %collective-permute-start.11 = (bf16[16,1536]{1,0:T(8,128)(2,1)S(1)}, bf16[16,1536]{1,0:T(8,128)(2,1)S(1)}, u32[]{:S(2)}, u32[]{:S(2)}) collective-permute-start(bf16[16,1536]{1,0:T(8,128)(2,1)S(1)} %get-tuple-element.21), channel_id=1, source_target_pairs={{1,0},{2,1},{3,2},{5,4},{6,5},{7,6},{9,8},{10,9},{11,10},{13,12},{... | collective-permute-start | bytes 147464 | tf_op jit(solution)/shard_map/ppermute | solution.py:401
  48.1 7.0 %collective-permute-done.11.right = bf16[16,1536]{1,0:T(8,128)(2,1)S(1)} collective-permute-done((bf16[16,1536]{1,0:T(8,128)(2,1)S(1)}, bf16[16,1536]{1,0:T(8,128)(2,1)S(1)}, u32[]{:S(2)}, u32[]{:S(2)}) %collective-permute-start.11) | collective-permute-done | bytes 49184 | tf_op jit(solution)/shard_map/ppermute | solution.py:401
  55.2 0.5 collective-permute-start.15
  55.7 1.3 %term.1.refs_7_ = f32[256,1536]{1,0:T(8,128)S(1)} custom-call(bf16[8,32,1536]{2,1,0:T(8,128)(2,1)S(1)} %copy-done, bf16[32,1536]{1,0:T(8,128)(2,1)S(1)} %collective-permute-done.4.beside, bf16[32,1536]{1,0:T(8,128)(2,1)S(1)} %collective-permute-done.diagonal, bf16[16,1536]{1,0:T(8,128)(2,1)S(1)} %collective-permute-done.10.left, ...), custom_call_target="tpu_custom_call" | custom-call | flops 1048576 | bytes 65536 | tf_op jit(solution)/shard_map/term/pallas_call | solution.py:350
  57.2 1.7 %collective-permute-done.14.refs_3_ = bf16[128,1536]{1,0:T(8,128)(2,1)S(1)} collective-permute-done((bf16[128,1536]{1,0:T(8,128)(2,1)S(1)}, bf16[128,1536]{1,0:T(8,128)(2,1)S(1)}, u32[]{:S(2)}, u32[]{:S(2)}) %collective-permute-start.14) | collective-permute-done | bytes 393248 | tf_op jit(solution)/shard_map/ppermute | solution.py:342
  58.9 5.3 %attend0.1.refs_8_ = f32[256,1536]{1,0:T(8,128)} custom-call(s32[1,1,2]{2,1,0:T(1,128)S(1)} %copy-done.6, s32[2,1,2]{2,1,0:T(1,128)S(1)} %copy-done.4, s32[2,1,2]{2,1,0:T(1,128)S(1)} %copy-done.5, bf16[256,1536]{1,0:T(8,128)(2,1)S(1)} %bitcast.8, bf16[256,1536]{1,0:T(8,128)(2,1)S(1)} %bitcast.10, bf16[256,1536]{1,0:T(8,128)(2,1)S(1)} %bitcast.6, ...), custom_call_target="tpu_custom_call" | custom-call | flops 1048576 | bytes 65536 | tf_op jit(solution)/shard_map/attend0/pallas_call | solution.py:424
  64.3 1.0 %collective-permute-done.15.refs_6_ = bf16[528,384]{1,0:T(8,128)(2,1)S(1)} collective-permute-done((bf16[528,384]{1,0:T(8,128)(2,1)S(1)}, bf16[528,384]{1,0:T(8,128)(2,1)S(1)}, u32[]{:S(2)}, u32[]{:S(2)}) %collective-permute-start.15) | collective-permute-done | bytes 405536 | tf_op jit(solution)/shard_map/ppermute | solution.py:392
  65.3 3.5 %attend1.1 = f32[256,1536]{1,0:T(8,128)} custom-call(s32[1,1,2]{2,1,0:T(1,128)S(1)} %copy-done.6, s32[2,1,2]{2,1,0:T(1,128)S(1)} %copy-done.4, s32[2,1,2]{2,1,0:T(1,128)S(1)} %copy-done.5, bf16[256,1536]{1,0:T(8,128)(2,1)S(1)} %bitcast.9, bf16[256,1536]{1,0:T(8,128)(2,1)S(1)} %bitcast.11, ...), custom_call_target="tpu_custom_call", output_to_operand_aliasing={{}: (14, {})} | custom-call | flops 1048576 | bytes 65536 | tf_op jit(solution)/shard_map/attend1/pallas_call | solution.py:424
  (35 shorter events, 0.6 us)
Async XLA Ops:
  0.0 9.7 %collective-permute-start.2 = (bf16[256,1536]{1,0:T(8,128)(2,1)}, bf16[256,1536]{1,0:T(8,128)(2,1)S(1)}, u32[]{:S(2)}, u32[]{:S(2)}) collective-permute-start(bf16[256,1536]{1,0:T(8,128)(2,1)} %bitcast.12), channel_id=1, source_target_pairs={{0,4},{4,0},{8,12},{12,8},{1,5},{5,1},{9,13},{13,9},{2,6},{6,2},{1... | collective-permute-start | bytes 2359304 | tf_op jit(solution)/shard_map/ppermute | solution.py:342
  0.5 9.3 %collective-permute-start.3 = (bf16[256,1536]{1,0:T(8,128)(2,1)}, bf16[256,1536]{1,0:T(8,128)(2,1)S(1)}, u32[]{:S(2)}, u32[]{:S(2)}) collective-permute-start(bf16[256,1536]{1,0:T(8,128)(2,1)} %bitcast.14), channel_id=1, source_target_pairs={{0,4},{4,0},{8,12},{12,8},{1,5},{5,1},{9,13},{13,9},{2,6},{6,2},{1... | collective-permute-start | bytes 2359304 | tf_op jit(solution)/shard_map/ppermute | solution.py:342
  1.6 14.4 %collective-permute-start.5 = (bf16[64,1536]{1,0:T(8,128)(2,1)S(1)}, bf16[64,1536]{1,0:T(8,128)(2,1)S(1)}, u32[]{:S(2)}, u32[]{:S(2)}) collective-permute-start(bf16[64,1536]{1,0:T(8,128)(2,1)S(1)} %get-tuple-element.19.refs_0_), channel_id=1, source_target_pairs={{0,8},{4,12},{8,0},{12,4},{1,9},{5,13},{9,1},{13,5},{2,10},{6,14},... | collective-permute-start | bytes 589832 | tf_op jit(solution)/shard_map/ppermute | solution.py:378
  4.6 5.1 %collective-permute-start.1 = (s32[1,1,2]{2,1,0:T(1,128)}, s32[1,1,2]{2,1,0:T(1,128)S(1)}, u32[]{:S(2)}, u32[]{:S(2)}) collective-permute-start(s32[1,1,2]{2,1,0:T(1,128)} %reads_ref.3), channel_id=1, source_target_pairs={{0,8},{4,12},{8,0},{12,4},{1,9},{5,13},{9,1},{13,5},{2,10},{6,14},... | collective-permute-start | bytes 32 | tf_op jit(solution)/shard_map/ppermute | solution.py:369
  4.7 11.3 %collective-permute-start = (bf16[32,1536]{1,0:T(8,128)(2,1)S(1)}, bf16[32,1536]{1,0:T(8,128)(2,1)S(1)}, u32[]{:S(2)}, u32[]{:S(2)}) collective-permute-start(bf16[32,1536]{1,0:T(8,128)(2,1)S(1)} %get-tuple-element.16), channel_id=1, source_target_pairs={{4,8},{8,4},{5,9},{9,5},{6,10},{10,6},{7,11},{11,7},{20,24},{24,20... | collective-permute-start | bytes 294920 | tf_op jit(solution)/shard_map/ppermute | solution.py:379
  9.7 6.2 %collective-permute-start.4 = (bf16[32,1536]{1,0:T(8,128)(2,1)S(1)}, bf16[32,1536]{1,0:T(8,128)(2,1)S(1)}, u32[]{:S(2)}, u32[]{:S(2)}) collective-permute-start(bf16[32,1536]{1,0:T(8,128)(2,1)S(1)} %get-tuple-element.18), channel_id=1, source_target_pairs={{0,4},{4,0},{8,12},{12,8},{1,5},{5,1},{9,13},{13,9},{2,6},{6,2},{1... | collective-permute-start | bytes 294920 | tf_op jit(solution)/shard_map/ppermute | solution.py:342
  10.6 0.9 %copy-start.8 = (bf16[256,1536]{1,0:T(8,128)(2,1)}, bf16[256,1536]{1,0:T(8,128)(2,1)S(1)}, u32[]{:S(2)}) copy-start(bf16[256,1536]{1,0:T(8,128)(2,1)S(1)} %collective-permute-done.3.passed_v.refs_5_) | copy-start | bytes 2359300
  14.1 42.9 %collective-permute-start.9 = (bf16[512,1152]{1,0:T(8,128)(2,1)S(1)}, bf16[512,1152]{1,0:T(8,128)(2,1)S(1)}, u32[]{:S(2)}, u32[]{:S(2)}) collective-permute-start(bf16[512,1152]{1,0:T(8,128)(2,1)S(1)} %get-tuple-element.17), channel_id=1, source_target_pairs={{0,8},{4,12},{8,0},{12,4},{1,9},{5,13},{9,1},{13,5},{2,10},{6,14},... | collective-permute-start | bytes 3538952 | tf_op jit(solution)/shard_map/ppermute | solution.py:392
  16.0 23.9 %copy-start = (bf16[8,32,1536]{2,1,0:T(8,128)(2,1)S(1)}, bf16[8,32,1536]{2,1,0:T(8,128)(2,1)}, u32[]{:S(2)}) copy-start(bf16[8,32,1536]{2,1,0:T(8,128)(2,1)} %cells.5) | copy-start | bytes 2359300
  16.0 39.7 %copy-start.3 = (f32[3,3,1536]{2,1,0:T(4,128)S(1)}, f32[3,3,1536]{2,1,0:T(4,128)}, u32[]{:S(2)}) copy-start(f32[3,3,1536]{2,1,0:T(4,128)} %weights.1) | copy-start | bytes 165892
  16.0 13.2 %collective-permute-start.7 = (bf16[128,1536]{1,0:T(8,128)(2,1)S(1)}, bf16[128,1536]{1,0:T(8,128)(2,1)S(1)}, u32[]{:S(2)}, u32[]{:S(2)}) collective-permute-start(bf16[128,1536]{1,0:T(8,128)(2,1)S(1)} %join.1.refs_0_), channel_id=1, source_target_pairs={{1,0},{2,1},{3,2},{0,3},{5,4},{6,5},{7,6},{4,7},{9,8},{10,9},{11,1... | collective-permute-start | bytes 1179656 | tf_op jit(solution)/shard_map/ppermute | solution.py:398
  19.7 18.1 %collective-permute-start.6 = (bf16[128,1536]{1,0:T(8,128)(2,1)S(1)}, bf16[128,1536]{1,0:T(8,128)(2,1)S(1)}, u32[]{:S(2)}, u32[]{:S(2)}) collective-permute-start(bf16[128,1536]{1,0:T(8,128)(2,1)S(1)} %join.1.refs_0_), channel_id=1, source_target_pairs={{0,1},{1,2},{2,3},{3,0},{4,5},{5,6},{6,7},{7,4},{8,9},{9,10},{10,1... | collective-permute-start | bytes 1179656 | tf_op jit(solution)/shard_map/ppermute | solution.py:397
  37.9 19.3 %collective-permute-start.13 = (bf16[384,1536]{1,0:T(8,128)(2,1)S(1)}, bf16[384,1536]{1,0:T(8,128)(2,1)S(1)}, u32[]{:S(2)}, u32[]{:S(2)}) collective-permute-start(bf16[384,1536]{1,0:T(8,128)(2,1)S(1)} %bundle.1.refs_0_), channel_id=1, source_target_pairs={{0,4},{4,0},{8,12},{12,8},{1,5},{5,1},{9,13},{13,9},{2,6},{6,2},{1... | collective-permute-start | bytes 3538952 | tf_op jit(solution)/shard_map/ppermute | solution.py:342
  37.9 19.1 %collective-permute-start.8 = (bf16[128,1536]{1,0:T(8,128)(2,1)S(1)}, bf16[128,1536]{1,0:T(8,128)(2,1)S(1)}, u32[]{:S(2)}, u32[]{:S(2)}) collective-permute-start(bf16[128,1536]{1,0:T(8,128)(2,1)S(1)} %collective-permute-done.6.refs_1_), channel_id=1, source_target_pairs={{1,2},{2,3},{5,6},{6,7},{9,10},{10,11},{13,14},{14,15},{17,18},{18... | collective-permute-start | bytes 1179656 | tf_op jit(solution)/shard_map/ppermute | solution.py:402
  38.6 18.4 %collective-permute-start.12 = (bf16[128,1536]{1,0:T(8,128)(2,1)S(1)}, bf16[128,1536]{1,0:T(8,128)(2,1)S(1)}, u32[]{:S(2)}, u32[]{:S(2)}) collective-permute-start(bf16[128,1536]{1,0:T(8,128)(2,1)S(1)} %collective-permute-done.7.refs_2_), channel_id=1, source_target_pairs={{1,0},{2,1},{5,4},{6,5},{9,8},{10,9},{13,12},{14,13},{17,16},{18,1... | collective-permute-start | bytes 1179656 | tf_op jit(solution)/shard_map/ppermute | solution.py:403
  40.0 6.8 %collective-permute-start.10 = (bf16[16,1536]{1,0:T(8,128)(2,1)S(1)}, bf16[16,1536]{1,0:T(8,128)(2,1)S(1)}, u32[]{:S(2)}, u32[]{:S(2)}) collective-permute-start(bf16[16,1536]{1,0:T(8,128)(2,1)S(1)} %get-tuple-element.20), channel_id=1, source_target_pairs={{0,1},{1,2},{2,3},{4,5},{5,6},{6,7},{8,9},{9,10},{10,11},{12,13},{... | collective-permute-start | bytes 147464 | tf_op jit(solution)/shard_map/ppermute | solution.py:400
  46.9 8.3 %collective-permute-start.11 = (bf16[16,1536]{1,0:T(8,128)(2,1)S(1)}, bf16[16,1536]{1,0:T(8,128)(2,1)S(1)}, u32[]{:S(2)}, u32[]{:S(2)}) collective-permute-start(bf16[16,1536]{1,0:T(8,128)(2,1)S(1)} %get-tuple-element.21), channel_id=1, source_target_pairs={{1,0},{2,1},{3,2},{5,4},{6,5},{7,6},{9,8},{10,9},{11,10},{13,12},{... | collective-permute-start | bytes 147464 | tf_op jit(solution)/shard_map/ppermute | solution.py:401
  55.2 10.1 %collective-permute-start.15 = (bf16[528,384]{1,0:T(8,128)(2,1)S(1)}, bf16[528,384]{1,0:T(8,128)(2,1)S(1)}, u32[]{:S(2)}, u32[]{:S(2)}) collective-permute-start(bf16[528,384]{1,0:T(8,128)(2,1)S(1)} %get-tuple-element.23), channel_id=1, source_target_pairs={{0,8},{4,12},{8,0},{12,4},{1,9},{5,13},{9,1},{13,5},{2,10},{6,14},... | collective-permute-start | bytes 1216520 | tf_op jit(solution)/shard_map/ppermute | solution.py:392
  55.7 3.2 %copy-start.2 = (bf16[8,32,1536]{2,1,0:T(8,128)(2,1)S(1)}, bf16[8,32,1536]{2,1,0:T(8,128)(2,1)}, u32[]{:S(2)}) copy-start(bf16[8,32,1536]{2,1,0:T(8,128)(2,1)} %param.12) | copy-start | bytes 2359300
  57.0 1.9 %copy-start.1 = (bf16[8,32,1536]{2,1,0:T(8,128)(2,1)S(1)}, bf16[8,32,1536]{2,1,0:T(8,128)(2,1)}, u32[]{:S(2)}) copy-start(bf16[8,32,1536]{2,1,0:T(8,128)(2,1)} %param.11) | copy-start | bytes 2359300
  57.0 1.9 %copy-start.4 = (s32[2,1,2]{2,1,0:T(1,128)S(1)}, s32[2,1,2]{2,1,0:T(1,128)}, u32[]{:S(2)}) copy-start(s32[2,1,2]{2,1,0:T(1,128)} %pattern_ref.3) | copy-start | bytes 52
  57.0 1.9 %copy-start.5 = (s32[2,1,2]{2,1,0:T(1,128)S(1)}, s32[2,1,2]{2,1,0:T(1,128)}, u32[]{:S(2)}) copy-start(s32[2,1,2]{2,1,0:T(1,128)} %text_ref.3) | copy-start | bytes 52
  57.0 1.9 %copy-start.6 = (s32[1,1,2]{2,1,0:T(1,128)S(1)}, s32[1,1,2]{2,1,0:T(1,128)}, u32[]{:S(2)}) copy-start(s32[1,1,2]{2,1,0:T(1,128)} %reads_ref.3) | copy-start | bytes 28
  57.1 1.8 %collective-permute-start.14 = (bf16[128,1536]{1,0:T(8,128)(2,1)S(1)}, bf16[128,1536]{1,0:T(8,128)(2,1)S(1)}, u32[]{:S(2)}, u32[]{:S(2)}) collective-permute-start(bf16[128,1536]{1,0:T(8,128)(2,1)S(1)} %choose.1.refs_1_), channel_id=1, source_target_pairs={{0,4},{4,0},{8,12},{12,8},{1,5},{5,1},{9,13},{13,9},{2,6},{6,2},{1... | collective-permute-start | bytes 1179656 | tf_op jit(solution)/shard_map/ppermute | solution.py:342
  (1 other events, 0.9 us)

commit v5 on v4

--- a/solution.py
+++ b/solution.py
@@ -15,7 +15,7 @@
 SCORE_SCALE = 1.0 / math.sqrt(HEAD_DIM)
 EXP2_SCALE = SCORE_SCALE * math.log2(math.e)
 CHUNK_HEADS = (9, 3)
-CHUNK_SPARE = (0, 16)
+CHUNK_SPARE = (0, 0)
 GROUP = 8
 VMEM_LIMIT = 24 * 1024 * 1024
 
@@ -141,93 +141,108 @@
         copy.wait()
 
 
-def pack_kernel(cells, text_k, text_v, beside, diagonal, text, sems):
-    shard = text_k.shape[0]
-    row = lax.axis_index("rows")
-    end = cells.shape[0] - 1
+def pack_kernel(k_hbm, v_hbm, cells, text_k, text_v, stale, ends, text, sems):
+    tokens, shard = k_hbm.shape[0], text_k.shape[0]
     copies = []
     for which, source in enumerate((text_k, text_v)):
         copies.append((source, text.at[pl.ds(which * shard, shard)]))
-    copies.append((cells.at[jnp.where(row % 2 == 0, end, 0)], beside))
-    copies.append((cells.at[jnp.where(row < 2, end, 0)], diagonal))
+    for which, source in enumerate((k_hbm, v_hbm)):
+        copies.append((source, stale.at[pl.ds(which * tokens, tokens)]))
+    for which, at in enumerate((0, cells.shape[0] - 1)):
+        copies.append((cells.at[at], ends.at[pl.ds(which * cells.shape[1], cells.shape[1])]))
     run_copies(copies, sems)
 
 
-def send_kernel(wanted, k_hbm, v_hbm, passed_k, passed_v, *refs):
-    outs, sems = refs[:-1], refs[-1]
+def send_kernel(wanted, stale, passed, *outs):
     row = lax.axis_index("rows")
+    tokens = stale.shape[0] // 2
 
     def block_of(owner):
         found = 0
         for turn in range(2):
             entry = wanted[0, 0, turn]
             found = jnp.where(entry // 2 == owner, entry % 2, found)
-        return pl.multiple_of(found * PER_BLOCK, PER_BLOCK)
-
-    own, other = block_of(row), block_of(row + 1 - 2 * (row % 2))
-    copies = []
+        return found * PER_BLOCK
+
+    starts = block_of(row), block_of(row + 1 - 2 * (row % 2))
     first = 0
-    for out in outs:
+    for out, spare in zip(outs, CHUNK_SPARE):
         part = pl.ds(first, out.shape[1])
         first += out.shape[1]
-        for which, (source, passed) in enumerate(((k_hbm, passed_k), (v_hbm, passed_v))):
-            at = 2 * PER_BLOCK * which
-            copies.append(
-                (source.at[pl.ds(own, PER_BLOCK), part], out.at[pl.ds(at, PER_BLOCK)])
-            )
-            copies.append(
-                (
-                    passed.at[pl.ds(other, PER_BLOCK), part],
-                    out.at[pl.ds(at + PER_BLOCK, PER_BLOCK)],
-                )
-            )
-    for out, spare in zip(outs, CHUNK_SPARE):
+        for which in range(2):
+            for slot, source in enumerate((stale, passed)):
+                rows = pl.ds(pl.multiple_of(which * tokens + starts[slot], PER_BLOCK), PER_BLOCK)
+                at = (2 * which + slot) * PER_BLOCK
+                out[pl.ds(at, PER_BLOCK), :] = source[rows, part]
         if spare:
             rows = pl.ds(out.shape[0] - spare, spare)
             out[rows, :] = jnp.zeros((spare, out.shape[1]), out.dtype)
-    run_copies(copies, sems)
 
 
 def bundle_kernel(*refs):
     out = refs[-1]
-    at = 0
-    for ref in refs[:-1]:
-        out[pl.ds(at, ref.shape[0]), :] = ref[...]
-        at += ref.shape[0]
-
-
-def choose_kernel(upper, lower, out):
-    out[...] = jnp.where(lax.axis_index("cols") >= 2, upper[...], lower[...])
-
-
-def edge_kernel(cells, beside, diagonal, last, first):
+    count = out.shape[0] // (len(refs) - 1)
+    for index, ref in enumerate(refs[:-1]):
+        out[pl.ds(index * count, count), :] = ref[pl.ds(0, count), :]
+
+
+def crop_kernel(source, out):
+    out[...] = source[pl.ds(0, out.shape[0]), :]
+
+
+def choose_kernel(upper, lower, *outs):
+    upwards = lax.axis_index("cols") >= 2
+    for index, out in enumerate(outs):
+        rows = pl.ds(index * out.shape[0], out.shape[0])
+        out[...] = jnp.where(upwards, upper[rows, :], lower[rows, :])
+
+
+def offer_kernel(text, ends_mate, out):
+    count = ends_mate.shape[0] // 2
+    out[pl.ds(0, text.shape[0]), :] = text[...]
+    first_core = lax.axis_index("rows") % 2 == 0
+    out[pl.ds(text.shape[0], count), :] = jnp.where(
+        first_core, ends_mate[pl.ds(count, count), :], ends_mate[pl.ds(0, count), :]
+    )
+
+
+def above_below(ends_mate, across, part):
+    count = ends_mate.shape[0] // 2
+    row = lax.axis_index("rows")
+    beside_first, beside_last = (ends_mate[pl.ds(at, count), part] for at in (0, count))
+    passed = across[pl.ds(across.shape[0] - count, count), part]
+    passed = jnp.where((row > 0) & (row < 3), passed, jnp.zeros_like(passed))
+    first_core = row % 2 == 0
+    return (
+        jnp.where(first_core, passed, beside_last),
+        jnp.where(first_core, beside_first, passed),
+    )
+
+
+def join_kernel(text, across, cells, ends_mate, plus, minus):
+    half = text.shape[0]
     rows_here, cols_here, width = cells.shape
-    above, below = above_below(beside[...], diagonal[...])
+    above, below = above_below(ends_mate, across, slice(None))
     rows = [above] + [cells[i] for i in range(rows_here)] + [below]
     rows = [row.astype(jnp.float32) for row in rows]
     spare = jnp.zeros((16 - len(rows), width), jnp.float32)
-    for target, at in ((last, cols_here - 1), (first, 0)):
+    for target, at in ((plus, cols_here - 1), (minus, 0)):
+        target[pl.ds(0, half), :] = text[...]
+        target[pl.ds(half, half), :] = across[pl.ds(0, half), :]
         edge = jnp.concatenate([row[at : at + 1] for row in rows] + [spare], axis=0)
-        target[...] = edge.astype(target.dtype)
-
-
-def above_below(beside, diagonal):
-    first_core = lax.axis_index("rows") % 2 == 0
-    return (
-        jnp.where(first_core, diagonal, beside),
-        jnp.where(first_core, beside, diagonal),
-    )
-
-
-def term_kernel(cells, beside, diagonal, left, right, weights, out):
+        target[pl.ds(2 * half, 16), :] = edge.astype(target.dtype)
+
+
+def term_kernel(cells, ends_mate, across, left, right, weights, out):
     rows_here, cols_here, width = cells.shape
     col = lax.axis_index("cols")
+    edges = pl.ds(left.shape[0] - 16, 16)
     place = lax.broadcasted_iota(jnp.int32, (cols_here, HEAD_DIM), 0)
     for lane in range(width // HEAD_DIM):
         part = pl.ds(lane * HEAD_DIM, HEAD_DIM)
-        above, below = above_below(beside[:, part], diagonal[:, part])
-        lefts = left[:, part].astype(jnp.float32)
-        rights = right[:, part].astype(jnp.float32)
+        above, below = above_below(ends_mate, across, part)
+        lefts = left[edges, part].astype(jnp.float32)
+        rights = right[edges, part].astype(jnp.float32)
         lefts = jnp.where(col > 0, lefts, 0.0)
         rights = jnp.where(col < 3, rights, 0.0)
         taps = []
@@ -254,11 +269,12 @@
 
 
 def attend_kernel(first_head, reads_ref, pattern_ref, text_ref, q, k, v, *refs):
-    near, last, near_mate, last_mate, passed_k, passed_v, arrived, term = refs[:8]
+    home, home_mate, near, near_mate, passed, arrived, term = refs[:7]
+    last, last_mate = refs[7:9], refs[9:11]
     out = refs[-1]
     row, col = lax.axis_index("rows"), lax.axis_index("cols")
     across, core = row // 2, row % 2
-    shard = last.shape[0] // 4
+    shard = last[0].shape[0] // 2
     half = 2 * PER_BLOCK
     head_count = arrived.shape[1] // HEAD_DIM
 
@@ -267,22 +283,32 @@
 
     def text_part(chosen, head, which):
         from_own = chosen % 2 == core
-        first = jnp.where(chosen // 2 == across, 0, 2 * shard) + which * shard
+        from_side = chosen // 2 == across
         part = lanes(head)
+        first = jnp.where(from_side, 0, 2 * shard) + which * shard
+        rows = pl.ds(which * shard, shard)
 
         def one(own, other, at):
-            rows = pl.ds(pl.multiple_of(first + at, shard), shard)
-            return jnp.where(from_own, own[rows, part], other[rows, part])
-
-        return [one(near, near_mate, 4 * shard * i) for i in range(3)] + [one(last, last_mate, 0)]
+            spot = pl.ds(pl.multiple_of(first + at, shard), shard)
+            return jnp.where(from_own, own[spot, part], other[spot, part])
+
+        sides = [
+            jnp.where(from_own, own[rows, part], other[rows, part])
+            for own, other in zip(last, last_mate)
+        ]
+        return [
+            one(home, home_mate, 0),
+            one(near, near_mate, 0),
+            one(near, near_mate, 4 * shard),
+            jnp.where(from_side, *sides),
+        ]
 
     def far_part(block, head, which):
         slot = pattern_ref[block, 0, 0] + pattern_ref[block, 0, 1] - block - 2
         wanted = reads_ref[0, 0, slot]
         owner = wanted // 2
-        mate_at = (wanted % 2) * PER_BLOCK
+        mate_at = (wanted % 2) * PER_BLOCK + which * half
         far_at = jnp.where(owner % 2 == core, 0, PER_BLOCK) + which * half
-        passed = (passed_k, passed_v)[which]
         mate = passed[pl.ds(pl.multiple_of(mate_at, PER_BLOCK), PER_BLOCK), lanes(head)]
         here = pl.ds(head * HEAD_DIM, HEAD_DIM)
         far = arrived[pl.ds(pl.multiple_of(far_at, PER_BLOCK), PER_BLOCK), here]
@@ -367,51 +393,53 @@
         for value in (flat(k_stale), flat(v_stale), v_fresh, text_k, text_v)
     ]
     wanted = lax.ppermute(reads, "rows", swap)
-    beside, diagonal, text = local(
+    stale, ends, text = local(
         pack_kernel,
         "pack",
-        rows_of(cols_here, cols_here, 2 * shard),
-        *in_place[2:],
-        specs=[in_hbm] * 3,
-        scratch=[pltpu.SemaphoreType.DMA((4,))],
-    )
-    across = lax.ppermute(text, "rows", swap)
-    diagonal = lax.ppermute(diagonal, "rows", [(1, 2), (2, 1)])
-    beside = to_mate(beside)
-    passed = [to_mate(value) for value in in_place[:2]]
+        rows_of(2 * tokens, 2 * cols_here, 2 * shard),
+        *in_place,
+        specs=[in_hbm] * 5,
+        scratch=[pltpu.SemaphoreType.DMA((6,))],
+    )
+    ends_mate = to_mate(ends)
+    offer = local(offer_kernel, "offer", rows_of(2 * shard + cols_here), text, ends_mate)
+    across = lax.ppermute(after(offer, wanted), "rows", swap)
+    passed = to_mate(stale)
     packed = local(
         send_kernel,
         "send",
         chunks,
         wanted,
-        *in_place[:2],
-        *passed,
-        specs=[pl.BlockSpec(memory_space=pltpu.SMEM)] + [in_hbm] * 2 + [in_vmem] * 2,
-        scratch=[pltpu.SemaphoreType.DMA((4 * len(CHUNK_HEADS),))],
+        stale,
+        passed,
+        specs=[pl.BlockSpec(memory_space=pltpu.SMEM)] + [in_vmem] * 2,
     )
     far = [lax.ppermute(chunk, "rows", swap) for chunk in packed]
 
-    text = local(
-        bundle_kernel, "join", rows_of(4 * shard), after(text, diagonal, packed[0], beside), across
-    )
-    left = lax.ppermute(text, "cols", [(i, (i + 1) % 4) for i in range(4)])
-    right = lax.ppermute(text, "cols", [((i + 1) % 4, i) for i in range(4)])
-    last, first = local(edge_kernel, "edge", rows_of(16, 16), v_fresh, beside, diagonal)
-    last = lax.ppermute(last, "cols", [(i, i + 1) for i in range(3)])
-    first = lax.ppermute(first, "cols", [(i + 1, i) for i in range(3)])
-    upper = lax.ppermute(left, "cols", [(1, 2), (2, 3)])
-    lower = lax.ppermute(right, "cols", [(1, 0), (2, 1)])
-
-    near = local(bundle_kernel, "bundle", rows_of(12 * shard), text, left, right)
-    near_mate = to_mate(near)
+    plus, minus = local(
+        join_kernel,
+        "join",
+        rows_of(4 * shard + 16, 4 * shard + 16),
+        after(text, packed[0]),
+        across,
+        v_fresh,
+        ends_mate,
+    )
+    left = lax.ppermute(plus, "cols", [(i, (i + 1) % 4) for i in range(4)])
+    right = lax.ppermute(minus, "cols", [((i + 1) % 4, i) for i in range(4)])
+    upper = lax.ppermute(local(crop_kernel, "crop", rows_of(4 * shard), left), "cols", [(1, 2), (2, 3)])
+    lower = lax.ppermute(local(crop_kernel, "crop", rows_of(4 * shard), right), "cols", [(1, 0), (2, 1)])
+    near = local(bundle_kernel, "bundle", rows_of(8 * shard), left, right)
+    near_mate, plus_mate = to_mate(near), to_mate(plus)
     term = local(
         term_kernel,
         "term",
         jax.ShapeDtypeStruct((tokens, width), jnp.float32),
-        v_fresh, beside, diagonal, last, first, conv_w,
-    )
-    rest = local(choose_kernel, "choose", rows_of(4 * shard), after(upper, far[0], term), lower)
-    rest_mate = to_mate(rest)
+        v_fresh, ends_mate, across, left, right, conv_w,
+    )
+    rest = local(choose_kernel, "choose", rows_of(2 * shard, 2 * shard), after(upper, far[0], term), lower)
+    rest_mate = [to_mate(part) for part in rest]
+
     out = None
     first_head = 0
     for chunk, head_count in enumerate(CHUNK_HEADS):
@@ -427,16 +455,16 @@
             grid_spec=pltpu.PrefetchScalarGridSpec(
                 num_scalar_prefetch=3,
                 grid=(1,),
-                in_specs=[in_vmem] * 11 + [in_hbm] * (out is not None),
+                in_specs=[in_vmem] * 14 + [in_hbm] * (out is not None),
                 out_specs=block,
             ),
-            input_output_aliases={14: 0} if out is not None else {},
+            input_output_aliases={17: 0} if out is not None else {},
             compiler_params=params,
             cost_estimate=cost,
             name=f"attend{chunk}",
         )(
             reads, pattern, text_blocks, flat(q_fresh), flat(k_fresh), flat(v_fresh),
-            near, rest, near_mate, rest_mate, *passed, far[chunk], term,
+            plus, plus_mate, near, near_mate, passed, far[chunk], term, *rest, *rest_mate,
             *([out] if out is not None else []),
         )
         first_head += head_count

time: 69.1 us -> 62.2 us (0.900)
  starting transfers between devices: 18.7 us -> 14.6 us
  Pallas kernels: 14 us -> 10.2 us
  waiting for transfers between devices: 34 us -> 36.8 us
  local copies, waits for them, and re-layouts: 1.84 us -> 0.03 us
    ppermute x8 -> x5, starting transfers between devices: 15.6 us -> 8.23 us  [the longest x1 4.23 us: body(): right = lax.ppermute(minus, 'cols', [((i + 1) % 4, i) for i in range(4)])]
    ppermute x8 -> x5, waiting for transfers between devices: 26.8 us -> 34.1 us  [the longest x1 10.6 us: body(): right = lax.ppermute(minus, 'cols', [((i + 1) % 4, i) for i in range(4)])]
    ppermute x1, waiting for transfers between devices: 4.39 us -> 1.16 us  [body(): wanted = lax.ppermute(reads, 'rows', swap)]
    ppermute x1, starting transfers between devices: 0.08 us -> 2.92 us  [body(): wanted = lax.ppermute(reads, 'rows', swap)]
    pallas_call x2, Pallas kernels: 8.85 us -> 6.36 us  [body(): pl.pallas_call(functools.partial(attend_kernel, first_head), out_shape=ja...]
    unnamed x18 -> x14, local copies, waits for them, and re-layouts: 1.84 us -> 0.03 us
    pallas_call x7 -> x9, Pallas kernels: 5.19 us -> 3.85 us  [local(): pl.pallas_call(kernel, out_shape=shapes, in_specs=specs or [in_vmem] * le...]
    ppermute x5 -> x6, starting transfers between devices: 0.65 us -> 1.79 us  [to_mate(): return lax.ppermute(values, 'rows', mates)]
  transfers between devices with their start and end apart: 16 -> 14, of which waited for: 7 -> 8; matrix products, arithmetic and copies ran while one was open for 0% -> 0% of each run, Pallas kernels for 12% -> 9%
where the time goes in v5:
time: 62.2 us; the launch traced here: 61.8 us
  waiting for transfers between devices  36.8 us (59%)
  starting transfers between devices  14.6 us (23%)
  Pallas kernels  10.2 us (16%)
    ppermute x1, waiting for transfers between devices, body(): right = lax.ppermute(minus, 'cols', [((i + 1) % 4, i) for i in range(4)])  10.6 us
    ppermute x1, waiting for transfers between devices, body(): lax.ppermute(local(crop_kernel, 'crop', rows_of(4 * shard), right), 'cols...  9.18 us
    ppermute x1, waiting for transfers between devices, body(): left = lax.ppermute(plus, 'cols', [(i, (i + 1) % 4) for i in range(4)])  7.29 us
    ppermute x1, waiting for transfers between devices, body(): across = lax.ppermute(after(offer, wanted), 'rows', swap)  7.05 us
    pallas_call x2, Pallas kernels, body(): pl.pallas_call(functools.partial(attend_kernel, first_head), out_shape=ja...  6.36 us
    ppermute x1, starting transfers between devices, body(): right = lax.ppermute(minus, 'cols', [((i + 1) % 4, i) for i in range(4)])  4.23 us
    pallas_call x9, Pallas kernels, local(): pl.pallas_call(kernel, out_shape=shapes, in_specs=specs or [in_vmem] * le...  3.85 us
    ppermute x1, starting transfers between devices, body(): wanted = lax.ppermute(reads, 'rows', swap)  2.92 us
  transfers between devices with their start and end apart: 14, of which 8 were waited for; matrix products, arithmetic and copies ran while one was open for 0% of the time, Pallas kernels for 9%

profile of v5, /device:TPU:0, one launch (start us, length us, event | category | flops | bytes accessed | tf_op | source)
XLA Modules:
  0.0 61.8 jit_solution(1537829571515593146)
XLA Ops:
  0.0 1.6 %pack.1 = (bf16[512,1536]{1,0:T(8,128)(2,1)S(1)}, bf16[64,1536]{1,0:T(8,128)(2,1)S(1)}, bf16[64,1536]{1,0:T(8,128)(2,1)S(1)}) custom-call(bf16[256,1536]{1,0:T(8,128)(2,1)} %bitcast.12, bf16[256,1536]{1,0:T(8,128)(2,1)} %bitcast.13, bf16[8,32,1536]{2,1,0:T(8,128)(2,1)} %cells.5, bf16[32,1536]{1,0:T(8,128)(2,1)} %text_k.1, bf16[32,1536]{1,0:T(8,128)(2,1)} %text_v.1), custom_call_target="tpu_custom_call" | custom-call | flops 1048576 | bytes 65536 | tf_op jit(solution)/shard_map/pack/pallas_call | solution.py:376
  1.6 0.5 collective-permute-start.1
  2.1 0.1 collective-permute-start.2
  2.2 2.9 %collective-permute-start = (s32[1,1,2]{2,1,0:T(1,128)S(1)}, s32[1,1,2]{2,1,0:T(1,128)S(1)}, u32[]{:S(2)}, u32[]{:S(2)}) collective-permute-start(s32[1,1,2]{2,1,0:T(1,128)S(1)} %copy-done.6), channel_id=1, source_target_pairs={{0,8},{4,12},{8,0},{12,4},{1,9},{5,13},{9,1},{13,5},{2,10},{6,14},... | collective-permute-start | bytes 32 | tf_op jit(solution)/shard_map/ppermute | solution.py:395
  5.1 0.3 collective-permute-done.2.ends_mate
  5.4 1.2 %collective-permute-done.wanted = s32[1,1,2]{2,1,0:T(1,128)S(1)} collective-permute-done((s32[1,1,2]{2,1,0:T(1,128)S(1)}, s32[1,1,2]{2,1,0:T(1,128)S(1)}, u32[]{:S(2)}, u32[]{:S(2)}) %collective-permute-start) | collective-permute-done | bytes 40 | tf_op jit(solution)/shard_map/ppermute | solution.py:395
  6.6 2.0 %collective-permute-start.3 = (bf16[96,1536]{1,0:T(8,128)(2,1)S(1)}, bf16[96,1536]{1,0:T(8,128)(2,1)S(1)}, u32[]{:S(2)}, u32[]{:S(2)}) collective-permute-start(bf16[96,1536]{1,0:T(8,128)(2,1)S(1)} %offer.1), channel_id=1, source_target_pairs={{0,8},{4,12},{8,0},{12,4},{1,9},{5,13},{9,1},{13,5},{2,10},{6,14},... | collective-permute-start | bytes 884744 | tf_op jit(solution)/shard_map/ppermute | solution.py:406
  8.6 0.7 %send.1 = (bf16[512,1152]{1,0:T(8,128)(2,1)S(1)}, bf16[512,384]{1,0:T(8,128)(2,1)S(1)}) custom-call(s32[1,1,2]{2,1,0:T(1,128)S(1)} %collective-permute-done.wanted, bf16[512,1536]{1,0:T(8,128)(2,1)S(1)} %get-tuple-element.19.stale, bf16[512,1536]{1,0:T(8,128)(2,1)S(1)} %collective-permute-done.1.passed.refs_4_), custom_call_target="tpu_custom_call" | custom-call | flops 1048576 | bytes 65536 | tf_op jit(solution)/shard_map/send/pallas_call | solution.py:376
  9.4 7.1 %collective-permute-done.3.across = bf16[96,1536]{1,0:T(8,128)(2,1)S(1)} collective-permute-done((bf16[96,1536]{1,0:T(8,128)(2,1)S(1)}, bf16[96,1536]{1,0:T(8,128)(2,1)S(1)}, u32[]{:S(2)}, u32[]{:S(2)}) %collective-permute-start.3) | collective-permute-done | bytes 294944 | tf_op jit(solution)/shard_map/ppermute | solution.py:406
  16.5 0.1 join.1
  16.6 4.2 %collective-permute-start.6 = (bf16[144,1536]{1,0:T(8,128)(2,1)S(1)}, bf16[144,1536]{1,0:T(8,128)(2,1)S(1)}, u32[]{:S(2)}, u32[]{:S(2)}) collective-permute-start(bf16[144,1536]{1,0:T(8,128)(2,1)S(1)} %get-tuple-element.25), channel_id=1, source_target_pairs={{1,0},{2,1},{3,2},{0,3},{5,4},{6,5},{7,6},{4,7},{9,8},{10,9},{11,1... | collective-permute-start | bytes 1327112 | tf_op jit(solution)/shard_map/ppermute | solution.py:429
  20.8 10.6 %collective-permute-done.6.refs_1_.right.source = bf16[144,1536]{1,0:T(8,128)(2,1)S(1)} collective-permute-done((bf16[144,1536]{1,0:T(8,128)(2,1)S(1)}, bf16[144,1536]{1,0:T(8,128)(2,1)S(1)}, u32[]{:S(2)}, u32[]{:S(2)}) %collective-permute-start.6) | collective-permute-done | bytes 442400 | tf_op jit(solution)/shard_map/ppermute | solution.py:429
  31.4 7.3 %collective-permute-done.5.refs_0_.left.source = bf16[144,1536]{1,0:T(8,128)(2,1)S(1)} collective-permute-done((bf16[144,1536]{1,0:T(8,128)(2,1)S(1)}, bf16[144,1536]{1,0:T(8,128)(2,1)S(1)}, u32[]{:S(2)}, u32[]{:S(2)}) %collective-permute-start.5) | collective-permute-done | bytes 442400 | tf_op jit(solution)/shard_map/ppermute | solution.py:428
  38.9 0.7 %collective-permute-start.10 = (bf16[128,1536]{1,0:T(8,128)(2,1)S(1)}, bf16[128,1536]{1,0:T(8,128)(2,1)S(1)}, u32[]{:S(2)}, u32[]{:S(2)}) collective-permute-start(bf16[128,1536]{1,0:T(8,128)(2,1)S(1)} %crop.2), channel_id=1, source_target_pairs={{1,2},{2,3},{5,6},{6,7},{9,10},{10,11},{13,14},{14,15},{17,18},{18... | collective-permute-start | bytes 1179656 | tf_op jit(solution)/shard_map/ppermute | solution.py:430
  39.6 1.3 %collective-permute-start.11 = (bf16[128,1536]{1,0:T(8,128)(2,1)S(1)}, bf16[128,1536]{1,0:T(8,128)(2,1)S(1)}, u32[]{:S(2)}, u32[]{:S(2)}) collective-permute-start(bf16[128,1536]{1,0:T(8,128)(2,1)S(1)} %crop.3), channel_id=1, source_target_pairs={{1,0},{2,1},{5,4},{6,5},{9,8},{10,9},{13,12},{14,13},{17,16},{18,1... | collective-permute-start | bytes 1179656 | tf_op jit(solution)/shard_map/ppermute | solution.py:431
  40.9 0.6 collective-permute-start.4
  41.5 1.6 %collective-permute-start.8 = (bf16[512,384]{1,0:T(8,128)(2,1)S(1)}, bf16[512,384]{1,0:T(8,128)(2,1)S(1)}, u32[]{:S(2)}, u32[]{:S(2)}) collective-permute-start(bf16[512,384]{1,0:T(8,128)(2,1)S(1)} %get-tuple-element.26), channel_id=1, source_target_pairs={{0,8},{4,12},{8,0},{12,4},{1,9},{5,13},{9,1},{13,5},{2,10},{6,14},... | collective-permute-start | bytes 1179656 | tf_op jit(solution)/shard_map/ppermute | solution.py:417
  43.1 1.3 %term.1.refs_6_ = f32[256,1536]{1,0:T(8,128)S(1)} custom-call(bf16[8,32,1536]{2,1,0:T(8,128)(2,1)S(1)} %copy-done, bf16[64,1536]{1,0:T(8,128)(2,1)S(1)} %collective-permute-done.2.ends_mate, bf16[96,1536]{1,0:T(8,128)(2,1)S(1)} %collective-permute-done.3.across, bf16[144,1536]{1,0:T(8,128)(2,1)S(1)} %collective-permute-done.5.refs_0_.left.source, ...), custom_call_target="tpu_custom_call" | custom-call | flops 1048576 | bytes 65536 | tf_op jit(solution)/shard_map/term/pallas_call | solution.py:376
  44.4 9.2 %collective-permute-done.11.lower = bf16[128,1536]{1,0:T(8,128)(2,1)S(1)} collective-permute-done((bf16[128,1536]{1,0:T(8,128)(2,1)S(1)}, bf16[128,1536]{1,0:T(8,128)(2,1)S(1)}, u32[]{:S(2)}, u32[]{:S(2)}) %collective-permute-start.11) | collective-permute-done | bytes 393248 | tf_op jit(solution)/shard_map/ppermute | solution.py:431
  53.7 0.5 collective-permute-start.13
  54.2 0.9 %collective-permute-done.12.refs_9_ = bf16[64,1536]{1,0:T(8,128)(2,1)S(1)} collective-permute-done((bf16[64,1536]{1,0:T(8,128)(2,1)S(1)}, bf16[64,1536]{1,0:T(8,128)(2,1)S(1)}, u32[]{:S(2)}, u32[]{:S(2)}) %collective-permute-start.12) | collective-permute-done | bytes 196640 | tf_op jit(solution)/shard_map/ppermute | solution.py:368
  55.1 0.3 collective-permute-done.13.refs_10_
  55.4 4.1 %attend0.1.refs_11_ = f32[256,1536]{1,0:T(8,128)} custom-call(s32[1,1,2]{2,1,0:T(1,128)S(1)} %copy-done.6, s32[2,1,2]{2,1,0:T(1,128)S(1)} %copy-done.4, s32[2,1,2]{2,1,0:T(1,128)S(1)} %copy-done.5, bf16[256,1536]{1,0:T(8,128)(2,1)S(1)} %bitcast.8, bf16[256,1536]{1,0:T(8,128)(2,1)S(1)} %bitcast.10, bf16[256,1536]{1,0:T(8,128)(2,1)S(1)} %bitcast.6, ...), custom_call_target="tpu_custom_call" | custom-call | flops 1048576 | bytes 65536 | tf_op jit(solution)/shard_map/attend0/pallas_call | solution.py:452
  59.6 2.2 %attend1.1 = f32[256,1536]{1,0:T(8,128)} custom-call(s32[1,1,2]{2,1,0:T(1,128)S(1)} %copy-done.6, s32[2,1,2]{2,1,0:T(1,128)S(1)} %copy-done.4, s32[2,1,2]{2,1,0:T(1,128)S(1)} %copy-done.5, bf16[256,1536]{1,0:T(8,128)(2,1)S(1)} %bitcast.9, bf16[256,1536]{1,0:T(8,128)(2,1)S(1)} %bitcast.11, ...), custom_call_target="tpu_custom_call", output_to_operand_aliasing={{}: (17, {})} | custom-call | flops 1048576 | bytes 65536 | tf_op jit(solution)/shard_map/attend1/pallas_call | solution.py:452
  (29 shorter events, 0.4 us)
Async XLA Ops:
  0.0 2.2 %copy-start.6 = (s32[1,1,2]{2,1,0:T(1,128)S(1)}, s32[1,1,2]{2,1,0:T(1,128)}, u32[]{:S(2)}) copy-start(s32[1,1,2]{2,1,0:T(1,128)} %reads_ref.3) | copy-start | bytes 28
  1.6 7.1 %collective-permute-start.1 = (bf16[512,1536]{1,0:T(8,128)(2,1)S(1)}, bf16[512,1536]{1,0:T(8,128)(2,1)S(1)}, u32[]{:S(2)}, u32[]{:S(2)}) collective-permute-start(bf16[512,1536]{1,0:T(8,128)(2,1)S(1)} %get-tuple-element.19.stale), channel_id=1, source_target_pairs={{0,4},{4,0},{8,12},{12,8},{1,5},{5,1},{9,13},{13,9},{2,6},{6,2},{1... | collective-permute-start | bytes 4718600 | tf_op jit(solution)/shard_map/ppermute | solution.py:368
  2.1 3.3 %collective-permute-start.2 = (bf16[64,1536]{1,0:T(8,128)(2,1)S(1)}, bf16[64,1536]{1,0:T(8,128)(2,1)S(1)}, u32[]{:S(2)}, u32[]{:S(2)}) collective-permute-start(bf16[64,1536]{1,0:T(8,128)(2,1)S(1)} %get-tuple-element.22), channel_id=1, source_target_pairs={{0,4},{4,0},{8,12},{12,8},{1,5},{5,1},{9,13},{13,9},{2,6},{6,2},{1... | collective-permute-start | bytes 589832 | tf_op jit(solution)/shard_map/ppermute | solution.py:368
  2.2 4.4 %collective-permute-start = (s32[1,1,2]{2,1,0:T(1,128)S(1)}, s32[1,1,2]{2,1,0:T(1,128)S(1)}, u32[]{:S(2)}, u32[]{:S(2)}) collective-permute-start(s32[1,1,2]{2,1,0:T(1,128)S(1)} %copy-done.6), channel_id=1, source_target_pairs={{0,8},{4,12},{8,0},{12,4},{1,9},{5,13},{9,1},{13,5},{2,10},{6,14},... | collective-permute-start | bytes 32 | tf_op jit(solution)/shard_map/ppermute | solution.py:395
  5.4 11.0 %copy-start = (bf16[8,32,1536]{2,1,0:T(8,128)(2,1)S(1)}, bf16[8,32,1536]{2,1,0:T(8,128)(2,1)}, u32[]{:S(2)}) copy-start(bf16[8,32,1536]{2,1,0:T(8,128)(2,1)} %cells.5) | copy-start | bytes 2359300
  6.6 9.8 %collective-permute-start.3 = (bf16[96,1536]{1,0:T(8,128)(2,1)S(1)}, bf16[96,1536]{1,0:T(8,128)(2,1)S(1)}, u32[]{:S(2)}, u32[]{:S(2)}) collective-permute-start(bf16[96,1536]{1,0:T(8,128)(2,1)S(1)} %offer.1), channel_id=1, source_target_pairs={{0,8},{4,12},{8,0},{12,4},{1,9},{5,13},{9,1},{13,5},{2,10},{6,14},... | collective-permute-start | bytes 884744 | tf_op jit(solution)/shard_map/ppermute | solution.py:406
  9.3 35.1 %collective-permute-start.9 = (bf16[512,1152]{1,0:T(8,128)(2,1)S(1)}, bf16[512,1152]{1,0:T(8,128)(2,1)S(1)}, u32[]{:S(2)}, u32[]{:S(2)}) collective-permute-start(bf16[512,1152]{1,0:T(8,128)(2,1)S(1)} %get-tuple-element.20), channel_id=1, source_target_pairs={{0,8},{4,12},{8,0},{12,4},{1,9},{5,13},{9,1},{13,5},{2,10},{6,14},... | collective-permute-start | bytes 3538952 | tf_op jit(solution)/shard_map/ppermute | solution.py:417
  16.6 14.9 %collective-permute-start.6 = (bf16[144,1536]{1,0:T(8,128)(2,1)S(1)}, bf16[144,1536]{1,0:T(8,128)(2,1)S(1)}, u32[]{:S(2)}, u32[]{:S(2)}) collective-permute-start(bf16[144,1536]{1,0:T(8,128)(2,1)S(1)} %get-tuple-element.25), channel_id=1, source_target_pairs={{1,0},{2,1},{3,2},{0,3},{5,4},{6,5},{7,6},{4,7},{9,8},{10,9},{11,1... | collective-permute-start | bytes 1327112 | tf_op jit(solution)/shard_map/ppermute | solution.py:429
  20.8 22.3 %copy-start.3 = (f32[3,3,1536]{2,1,0:T(4,128)S(1)}, f32[3,3,1536]{2,1,0:T(4,128)}, u32[]{:S(2)}) copy-start(f32[3,3,1536]{2,1,0:T(4,128)} %weights.1) | copy-start | bytes 165892
  20.8 17.9 %collective-permute-start.5 = (bf16[144,1536]{1,0:T(8,128)(2,1)S(1)}, bf16[144,1536]{1,0:T(8,128)(2,1)S(1)}, u32[]{:S(2)}, u32[]{:S(2)}) collective-permute-start(bf16[144,1536]{1,0:T(8,128)(2,1)S(1)} %get-tuple-element.24.refs_0_), channel_id=1, source_target_pairs={{0,1},{1,2},{2,3},{3,0},{4,5},{5,6},{6,7},{7,4},{8,9},{9,10},{10,1... | collective-permute-start | bytes 1327112 | tf_op jit(solution)/shard_map/ppermute | solution.py:428
  38.8 15.4 %collective-permute-start.7 = (bf16[256,1536]{1,0:T(8,128)(2,1)S(1)}, bf16[256,1536]{1,0:T(8,128)(2,1)S(1)}, u32[]{:S(2)}, u32[]{:S(2)}) collective-permute-start(bf16[256,1536]{1,0:T(8,128)(2,1)S(1)} %bundle.1.refs_2_), channel_id=1, source_target_pairs={{0,4},{4,0},{8,12},{12,8},{1,5},{5,1},{9,13},{13,9},{2,6},{6,2},{1... | collective-permute-start | bytes 2359304 | tf_op jit(solution)/shard_map/ppermute | solution.py:368
  38.9 2.6 %collective-permute-start.10 = (bf16[128,1536]{1,0:T(8,128)(2,1)S(1)}, bf16[128,1536]{1,0:T(8,128)(2,1)S(1)}, u32[]{:S(2)}, u32[]{:S(2)}) collective-permute-start(bf16[128,1536]{1,0:T(8,128)(2,1)S(1)} %crop.2), channel_id=1, source_target_pairs={{1,2},{2,3},{5,6},{6,7},{9,10},{10,11},{13,14},{14,15},{17,18},{18... | collective-permute-start | bytes 1179656 | tf_op jit(solution)/shard_map/ppermute | solution.py:430
  39.6 13.9 %collective-permute-start.11 = (bf16[128,1536]{1,0:T(8,128)(2,1)S(1)}, bf16[128,1536]{1,0:T(8,128)(2,1)S(1)}, u32[]{:S(2)}, u32[]{:S(2)}) collective-permute-start(bf16[128,1536]{1,0:T(8,128)(2,1)S(1)} %crop.3), channel_id=1, source_target_pairs={{1,0},{2,1},{5,4},{6,5},{9,8},{10,9},{13,12},{14,13},{17,16},{18,1... | collective-permute-start | bytes 1179656 | tf_op jit(solution)/shard_map/ppermute | solution.py:431
  40.9 13.3 %collective-permute-start.4 = (bf16[144,1536]{1,0:T(8,128)(2,1)S(1)}, bf16[144,1536]{1,0:T(8,128)(2,1)S(1)}, u32[]{:S(2)}, u32[]{:S(2)}) collective-permute-start(bf16[144,1536]{1,0:T(8,128)(2,1)S(1)} %get-tuple-element.24.refs_0_), channel_id=1, source_target_pairs={{0,4},{4,0},{8,12},{12,8},{1,5},{5,1},{9,13},{13,9},{2,6},{6,2},{1... | collective-permute-start | bytes 1327112 | tf_op jit(solution)/shard_map/ppermute | solution.py:368
  41.5 13.9 %copy-start.1 = (bf16[8,32,1536]{2,1,0:T(8,128)(2,1)S(1)}, bf16[8,32,1536]{2,1,0:T(8,128)(2,1)}, u32[]{:S(2)}) copy-start(bf16[8,32,1536]{2,1,0:T(8,128)(2,1)} %param.11) | copy-start | bytes 2359300
  41.5 13.9 %copy-start.2 = (bf16[8,32,1536]{2,1,0:T(8,128)(2,1)S(1)}, bf16[8,32,1536]{2,1,0:T(8,128)(2,1)}, u32[]{:S(2)}) copy-start(bf16[8,32,1536]{2,1,0:T(8,128)(2,1)} %param.12) | copy-start | bytes 2359300
  41.5 13.9 %copy-start.4 = (s32[2,1,2]{2,1,0:T(1,128)S(1)}, s32[2,1,2]{2,1,0:T(1,128)}, u32[]{:S(2)}) copy-start(s32[2,1,2]{2,1,0:T(1,128)} %pattern_ref.3) | copy-start | bytes 52
  41.5 13.9 %copy-start.5 = (s32[2,1,2]{2,1,0:T(1,128)S(1)}, s32[2,1,2]{2,1,0:T(1,128)}, u32[]{:S(2)}) copy-start(s32[2,1,2]{2,1,0:T(1,128)} %text_ref.3) | copy-start | bytes 52
  41.5 18.1 %collective-permute-start.8 = (bf16[512,384]{1,0:T(8,128)(2,1)S(1)}, bf16[512,384]{1,0:T(8,128)(2,1)S(1)}, u32[]{:S(2)}, u32[]{:S(2)}) collective-permute-start(bf16[512,384]{1,0:T(8,128)(2,1)S(1)} %get-tuple-element.26), channel_id=1, source_target_pairs={{0,8},{4,12},{8,0},{12,4},{1,9},{5,13},{9,1},{13,5},{2,10},{6,14},... | collective-permute-start | bytes 1179656 | tf_op jit(solution)/shard_map/ppermute | solution.py:417
  53.6 1.5 %collective-permute-start.12 = (bf16[64,1536]{1,0:T(8,128)(2,1)S(1)}, bf16[64,1536]{1,0:T(8,128)(2,1)S(1)}, u32[]{:S(2)}, u32[]{:S(2)}) collective-permute-start(bf16[64,1536]{1,0:T(8,128)(2,1)S(1)} %get-tuple-element.28.refs_7_), channel_id=1, source_target_pairs={{0,4},{4,0},{8,12},{12,8},{1,5},{5,1},{9,13},{13,9},{2,6},{6,2},{1... | collective-permute-start | bytes 589832 | tf_op jit(solution)/shard_map/ppermute | solution.py:368
  53.7 1.7 %collective-permute-start.13 = (bf16[64,1536]{1,0:T(8,128)(2,1)S(1)}, bf16[64,1536]{1,0:T(8,128)(2,1)S(1)}, u32[]{:S(2)}, u32[]{:S(2)}) collective-permute-start(bf16[64,1536]{1,0:T(8,128)(2,1)S(1)} %get-tuple-element.29.refs_8_), channel_id=1, source_target_pairs={{0,4},{4,0},{8,12},{12,8},{1,5},{5,1},{9,13},{13,9},{2,6},{6,2},{1... | collective-permute-start | bytes 589832 | tf_op jit(solution)/shard_map/ppermute | solution.py:368

commit v6 on v5

--- a/solution.py
+++ b/solution.py
@@ -15,7 +15,6 @@
 SCORE_SCALE = 1.0 / math.sqrt(HEAD_DIM)
 EXP2_SCALE = SCORE_SCALE * math.log2(math.e)
 CHUNK_HEADS = (9, 3)
-CHUNK_SPARE = (0, 0)
 GROUP = 8
 VMEM_LIMIT = 24 * 1024 * 1024
 
@@ -153,20 +152,38 @@
     run_copies(copies, sems)
 
 
-def send_kernel(wanted, stale, passed, *outs):
+def offer_kernel(reads_ref, text, ends_mate, out):
+    both, width = text.shape
+    count = ends_mate.shape[0] // 2
     row = lax.axis_index("rows")
-    tokens = stale.shape[0] // 2
-
-    def block_of(owner):
+    partner = (row + 2) % 4
+
+    def flag(owner):
         found = 0
         for turn in range(2):
-            entry = wanted[0, 0, turn]
+            entry = reads_ref[0, 0, turn]
             found = jnp.where(entry // 2 == owner, entry % 2, found)
-        return found * PER_BLOCK
-
-    starts = block_of(row), block_of(row + 1 - 2 * (row % 2))
+        return jnp.full((8, width // 2), found.astype(jnp.float32), jnp.float32)
+
+    flags = [flag(owner) for owner in (partner, partner + 1 - 2 * (partner % 2))]
+    out[pl.ds(0, both), :] = text[...]
+    out[pl.ds(both, count), :] = jnp.where(
+        row % 2 == 0, ends_mate[pl.ds(count, count), :], ends_mate[pl.ds(0, count), :]
+    )
+    out[pl.ds(both + count, 8), :] = jnp.concatenate(flags, axis=1).astype(out.dtype)
+
+
+def send_kernel(across, stale, passed, *outs):
+    tokens, width = stale.shape[0] // 2, stale.shape[1]
+
+    def block_of(slot):
+        lanes = pl.ds(slot * (width // 2), HEAD_DIM)
+        flag = jnp.max(across[pl.ds(across.shape[0] - 8, 8), lanes].astype(jnp.float32))
+        return jnp.where(flag > 0.5, PER_BLOCK, 0)
+
+    starts = block_of(0), block_of(1)
     first = 0
-    for out, spare in zip(outs, CHUNK_SPARE):
+    for out in outs:
         part = pl.ds(first, out.shape[1])
         first += out.shape[1]
         for which in range(2):
@@ -174,9 +191,6 @@
                 rows = pl.ds(pl.multiple_of(which * tokens + starts[slot], PER_BLOCK), PER_BLOCK)
                 at = (2 * which + slot) * PER_BLOCK
                 out[pl.ds(at, PER_BLOCK), :] = source[rows, part]
-        if spare:
-            rows = pl.ds(out.shape[0] - spare, spare)
-            out[rows, :] = jnp.zeros((spare, out.shape[1]), out.dtype)
 
 
 def bundle_kernel(*refs):
@@ -186,31 +200,11 @@
         out[pl.ds(index * count, count), :] = ref[pl.ds(0, count), :]
 
 
-def crop_kernel(source, out):
-    out[...] = source[pl.ds(0, out.shape[0]), :]
-
-
-def choose_kernel(upper, lower, *outs):
-    upwards = lax.axis_index("cols") >= 2
-    for index, out in enumerate(outs):
-        rows = pl.ds(index * out.shape[0], out.shape[0])
-        out[...] = jnp.where(upwards, upper[rows, :], lower[rows, :])
-
-
-def offer_kernel(text, ends_mate, out):
-    count = ends_mate.shape[0] // 2
-    out[pl.ds(0, text.shape[0]), :] = text[...]
-    first_core = lax.axis_index("rows") % 2 == 0
-    out[pl.ds(text.shape[0], count), :] = jnp.where(
-        first_core, ends_mate[pl.ds(count, count), :], ends_mate[pl.ds(0, count), :]
-    )
-
-
 def above_below(ends_mate, across, part):
     count = ends_mate.shape[0] // 2
     row = lax.axis_index("rows")
     beside_first, beside_last = (ends_mate[pl.ds(at, count), part] for at in (0, count))
-    passed = across[pl.ds(across.shape[0] - count, count), part]
+    passed = across[pl.ds(across.shape[0] - 8 - count, count), part]
     passed = jnp.where((row > 0) & (row < 3), passed, jnp.zeros_like(passed))
     first_core = row % 2 == 0
     return (
@@ -219,18 +213,18 @@
     )
 
 
-def join_kernel(text, across, cells, ends_mate, plus, minus):
-    half = text.shape[0]
+def join_kernel(across, cells, ends_mate, peer, plus, minus):
+    shard = peer.shape[0] // 2
     rows_here, cols_here, width = cells.shape
     above, below = above_below(ends_mate, across, slice(None))
     rows = [above] + [cells[i] for i in range(rows_here)] + [below]
     rows = [row.astype(jnp.float32) for row in rows]
     spare = jnp.zeros((16 - len(rows), width), jnp.float32)
+    for target in (peer, plus, minus):
+        target[pl.ds(0, 2 * shard), :] = across[pl.ds(0, 2 * shard), :]
     for target, at in ((plus, cols_here - 1), (minus, 0)):
-        target[pl.ds(0, half), :] = text[...]
-        target[pl.ds(half, half), :] = across[pl.ds(0, half), :]
         edge = jnp.concatenate([row[at : at + 1] for row in rows] + [spare], axis=0)
-        target[pl.ds(2 * half, 16), :] = edge.astype(target.dtype)
+        target[pl.ds(2 * shard, 16), :] = edge.astype(target.dtype)
 
 
 def term_kernel(cells, ends_mate, across, left, right, weights, out):
@@ -269,12 +263,12 @@
 
 
 def attend_kernel(first_head, reads_ref, pattern_ref, text_ref, q, k, v, *refs):
-    home, home_mate, near, near_mate, passed, arrived, term = refs[:7]
-    last, last_mate = refs[7:9], refs[9:11]
+    near, near_mate, passed, arrived, term = refs[:5]
+    side, side_mate = refs[5:9], refs[9:13]
     out = refs[-1]
     row, col = lax.axis_index("rows"), lax.axis_index("cols")
     across, core = row // 2, row % 2
-    shard = last[0].shape[0] // 2
+    shard = near.shape[0] // 8
     half = 2 * PER_BLOCK
     head_count = arrived.shape[1] // HEAD_DIM
 
@@ -283,25 +277,19 @@
 
     def text_part(chosen, head, which):
         from_own = chosen % 2 == core
-        from_side = chosen // 2 == across
+        from_near = chosen // 2 == across
         part = lanes(head)
-        first = jnp.where(from_side, 0, 2 * shard) + which * shard
-        rows = pl.ds(which * shard, shard)
-
-        def one(own, other, at):
-            spot = pl.ds(pl.multiple_of(first + at, shard), shard)
-            return jnp.where(from_own, own[spot, part], other[spot, part])
-
-        sides = [
-            jnp.where(from_own, own[rows, part], other[rows, part])
-            for own, other in zip(last, last_mate)
-        ]
-        return [
-            one(home, home_mate, 0),
-            one(near, near_mate, 0),
-            one(near, near_mate, 4 * shard),
-            jnp.where(from_side, *sides),
-        ]
+
+        def one(piece):
+            rows = pl.ds((2 * piece + which) * shard, shard)
+            here = pl.ds(which * shard, shard)
+            return jnp.where(
+                from_near,
+                jnp.where(from_own, near[rows, part], near_mate[rows, part]),
+                jnp.where(from_own, side[piece][here, part], side_mate[piece][here, part]),
+            )
+
+        return [one(piece) for piece in range(4)]
 
     def far_part(block, head, which):
         slot = pattern_ref[block, 0, 0] + pattern_ref[block, 0, 1] - block - 2
@@ -385,14 +373,12 @@
         )(*args)
 
     chunks = tuple(
-        jax.ShapeDtypeStruct((2 * tokens + spare, n * HEAD_DIM), jnp.bfloat16)
-        for n, spare in zip(CHUNK_HEADS, CHUNK_SPARE)
+        jax.ShapeDtypeStruct((2 * tokens, n * HEAD_DIM), jnp.bfloat16) for n in CHUNK_HEADS
     )
     in_place = [
         pltpu.with_memory_space_constraint(value, pltpu.HBM)
         for value in (flat(k_stale), flat(v_stale), v_fresh, text_k, text_v)
     ]
-    wanted = lax.ppermute(reads, "rows", swap)
     stale, ends, text = local(
         pack_kernel,
         "pack",
@@ -401,44 +387,48 @@
         specs=[in_hbm] * 5,
         scratch=[pltpu.SemaphoreType.DMA((6,))],
     )
+    forward = [(i, (i + 1) % 4) for i in range(4)]
+    backward = [(i, (i + 3) % 4) for i in range(4)]
+    opposite = [(i, (i + 2) % 4) for i in range(4)]
+
+    near_parts = [text] + [lax.ppermute(text, "cols", p) for p in (forward, backward, opposite)]
     ends_mate = to_mate(ends)
-    offer = local(offer_kernel, "offer", rows_of(2 * shard + cols_here), text, ends_mate)
-    across = lax.ppermute(after(offer, wanted), "rows", swap)
+    offer = local(
+        offer_kernel,
+        "offer",
+        rows_of(2 * shard + cols_here + 8),
+        reads,
+        text,
+        ends_mate,
+        specs=[pl.BlockSpec(memory_space=pltpu.SMEM)] + [in_vmem] * 2,
+    )
+    across = lax.ppermute(offer, "rows", swap)
     passed = to_mate(stale)
-    packed = local(
-        send_kernel,
-        "send",
-        chunks,
-        wanted,
-        stale,
-        passed,
-        specs=[pl.BlockSpec(memory_space=pltpu.SMEM)] + [in_vmem] * 2,
-    )
+    packed = local(send_kernel, "send", chunks, across, stale, passed)
     far = [lax.ppermute(chunk, "rows", swap) for chunk in packed]
 
-    plus, minus = local(
+    peer, plus, minus = local(
         join_kernel,
         "join",
-        rows_of(4 * shard + 16, 4 * shard + 16),
-        after(text, packed[0]),
-        across,
+        rows_of(2 * shard, 2 * shard + 16, 2 * shard + 16),
+        after(across, packed[0]),
         v_fresh,
         ends_mate,
     )
-    left = lax.ppermute(plus, "cols", [(i, (i + 1) % 4) for i in range(4)])
-    right = lax.ppermute(minus, "cols", [((i + 1) % 4, i) for i in range(4)])
-    upper = lax.ppermute(local(crop_kernel, "crop", rows_of(4 * shard), left), "cols", [(1, 2), (2, 3)])
-    lower = lax.ppermute(local(crop_kernel, "crop", rows_of(4 * shard), right), "cols", [(1, 0), (2, 1)])
-    near = local(bundle_kernel, "bundle", rows_of(8 * shard), left, right)
-    near_mate, plus_mate = to_mate(near), to_mate(plus)
+    left = lax.ppermute(plus, "cols", forward)
+    right = lax.ppermute(minus, "cols", backward)
+    side_parts = [peer, left, right, lax.ppermute(peer, "cols", opposite)]
+    near_parts[0] = after(near_parts[0], packed[0])
+    near = local(bundle_kernel, "bundle", rows_of(8 * shard), *near_parts)
+    near_mate = to_mate(near)
+    side_parts[3] = after(side_parts[3], near_mate)
+    side_mate = [to_mate(part) for part in side_parts]
     term = local(
         term_kernel,
         "term",
         jax.ShapeDtypeStruct((tokens, width), jnp.float32),
         v_fresh, ends_mate, across, left, right, conv_w,
     )
-    rest = local(choose_kernel, "choose", rows_of(2 * shard, 2 * shard), after(upper, far[0], term), lower)
-    rest_mate = [to_mate(part) for part in rest]
 
     out = None
     first_head = 0
@@ -455,16 +445,16 @@
             grid_spec=pltpu.PrefetchScalarGridSpec(
                 num_scalar_prefetch=3,
                 grid=(1,),
-                in_specs=[in_vmem] * 14 + [in_hbm] * (out is not None),
+                in_specs=[in_vmem] * 16 + [in_hbm] * (out is not None),
                 out_specs=block,
             ),
-            input_output_aliases={17: 0} if out is not None else {},
+            input_output_aliases={19: 0} if out is not None else {},
             compiler_params=params,
             cost_estimate=cost,
             name=f"attend{chunk}",
         )(
             reads, pattern, text_blocks, flat(q_fresh), flat(k_fresh), flat(v_fresh),
-            plus, plus_mate, near, near_mate, passed, far[chunk], term, *rest, *rest_mate,
+            near, near_mate, passed, far[chunk], term, *side_parts, *side_mate,
             *([out] if out is not None else []),
         )
         first_head += head_count

time: 62.2 us -> 64 us (1.029)
  the two profiles are of different devices: /device:TPU:0 before, /device:TPU:24 now
where the time goes in v6:
time: 64 us; the launch traced here: 63.9 us
  waiting for transfers between devices  38.1 us (60%)
  starting transfers between devices  15.1 us (24%)
  Pallas kernels  10.4 us (16%)
    ppermute x1, waiting for transfers between devices, body(): side_parts = [peer, left, right, lax.ppermute(peer, 'cols', opposite)]  20 us
    pallas_call x2, Pallas kernels, body(): pl.pallas_call(functools.partial(attend_kernel, first_head), out_shape=ja...  6.59 us
    ppermute x3, waiting for transfers between devices, body(): lax.ppermute(text, 'cols', p)  6.33 us
    ppermute x1, starting transfers between devices, body(): side_parts = [peer, left, right, lax.ppermute(peer, 'cols', opposite)]  4.78 us
    ppermute x2, waiting for transfers between devices, body(): far = [lax.ppermute(chunk, 'rows', swap) for chunk in packed]  4.33 us
    ppermute x3, starting transfers between devices, body(): lax.ppermute(text, 'cols', p)  4.16 us
    ppermute x1, waiting for transfers between devices, body(): across = lax.ppermute(offer, 'rows', swap)  3.92 us
    pallas_call x6, Pallas kernels, local(): pl.pallas_call(kernel, out_shape=shapes, in_specs=specs or [in_vmem] * le...  3.85 us
  transfers between devices with their start and end apart: 16, of which 7 were waited for; matrix products, arithmetic and copies ran while one was open for 0% of the time, Pallas kernels for 10%

profile of v6, /device:TPU:24, one launch (start us, length us, event | category | flops | bytes accessed | tf_op | source)
XLA Modules:
  0.0 63.9 jit_solution(12401632052375538246)
XLA Ops:
  0.0 1.6 %pack.1 = (bf16[512,1536]{1,0:T(8,128)(2,1)S(1)}, bf16[64,1536]{1,0:T(8,128)(2,1)S(1)}, bf16[64,1536]{1,0:T(8,128)(2,1)S(1)}) custom-call(bf16[256,1536]{1,0:T(8,128)(2,1)} %bitcast.12, bf16[256,1536]{1,0:T(8,128)(2,1)} %bitcast.13, bf16[8,32,1536]{2,1,0:T(8,128)(2,1)} %cells.5, bf16[32,1536]{1,0:T(8,128)(2,1)} %text_k.1, bf16[32,1536]{1,0:T(8,128)(2,1)} %text_v.1), custom_call_target="tpu_custom_call" | custom-call | flops 1048576 | bytes 65536 | tf_op jit(solution)/shard_map/pack/pallas_call | solution.py:364
  1.6 0.5 collective-permute-start
  2.1 3.2 %collective-permute-done.ends_mate = bf16[64,1536]{1,0:T(8,128)(2,1)S(1)} collective-permute-done((bf16[64,1536]{1,0:T(8,128)(2,1)S(1)}, bf16[64,1536]{1,0:T(8,128)(2,1)S(1)}, u32[]{:S(2)}, u32[]{:S(2)}) %collective-permute-start) | collective-permute-done | bytes 196640 | tf_op jit(solution)/shard_map/ppermute | solution.py:356
  5.3 0.6 offer.1
  5.9 1.6 %collective-permute-start.1 = (bf16[104,1536]{1,0:T(8,128)(2,1)S(1)}, bf16[104,1536]{1,0:T(8,128)(2,1)S(1)}, u32[]{:S(2)}, u32[]{:S(2)}) collective-permute-start(bf16[104,1536]{1,0:T(8,128)(2,1)S(1)} %offer.1), channel_id=1, source_target_pairs={{0,8},{4,12},{8,0},{12,4},{1,9},{5,13},{9,1},{13,5},{2,10},{6,14},... | collective-permute-start | bytes 958472 | tf_op jit(solution)/shard_map/ppermute | solution.py:405
  7.5 0.3 collective-permute-start.5
  7.8 0.4 collective-permute-start.4
  8.3 3.4 %collective-permute-start.3 = (bf16[64,1536]{1,0:T(8,128)(2,1)S(1)}, bf16[64,1536]{1,0:T(8,128)(2,1)S(1)}, u32[]{:S(2)}, u32[]{:S(2)}) collective-permute-start(bf16[64,1536]{1,0:T(8,128)(2,1)S(1)} %get-tuple-element.21.text.refs_0_), channel_id=1, source_target_pairs={{0,1},{1,2},{2,3},{3,0},{4,5},{5,6},{6,7},{7,4},{8,9},{9,10},{10,1... | collective-permute-start | bytes 589832 | tf_op jit(solution)/shard_map/ppermute | solution.py:394
  11.6 3.9 %collective-permute-done.1.across = bf16[104,1536]{1,0:T(8,128)(2,1)S(1)} collective-permute-done((bf16[104,1536]{1,0:T(8,128)(2,1)S(1)}, bf16[104,1536]{1,0:T(8,128)(2,1)S(1)}, u32[]{:S(2)}, u32[]{:S(2)}) %collective-permute-start.1) | collective-permute-done | bytes 319520 | tf_op jit(solution)/shard_map/ppermute | solution.py:405
  15.6 0.2 send.1
  15.8 1.6 %collective-permute-start.8 = (bf16[512,1152]{1,0:T(8,128)(2,1)S(1)}, bf16[512,1152]{1,0:T(8,128)(2,1)S(1)}, u32[]{:S(2)}, u32[]{:S(2)}) collective-permute-start(bf16[512,1152]{1,0:T(8,128)(2,1)S(1)} %get-tuple-element.20), channel_id=1, source_target_pairs={{0,8},{4,12},{8,0},{12,4},{1,9},{5,13},{9,1},{13,5},{2,10},{6,14},... | collective-permute-start | bytes 3538952 | tf_op jit(solution)/shard_map/ppermute | solution.py:408
  17.4 6.1 %collective-permute-done.5.refs_3_ = bf16[64,1536]{1,0:T(8,128)(2,1)S(1)} collective-permute-done((bf16[64,1536]{1,0:T(8,128)(2,1)S(1)}, bf16[64,1536]{1,0:T(8,128)(2,1)S(1)}, u32[]{:S(2)}, u32[]{:S(2)}) %collective-permute-start.5) | collective-permute-done | bytes 196640 | tf_op jit(solution)/shard_map/ppermute | solution.py:394
  23.5 0.2 collective-permute-done.3.refs_1_
  24.0 1.2 %collective-permute-start.9 = (bf16[80,1536]{1,0:T(8,128)(2,1)S(1)}, bf16[80,1536]{1,0:T(8,128)(2,1)S(1)}, u32[]{:S(2)}, u32[]{:S(2)}) collective-permute-start(bf16[80,1536]{1,0:T(8,128)(2,1)S(1)} %get-tuple-element.24), channel_id=1, source_target_pairs={{0,1},{1,2},{2,3},{3,0},{4,5},{5,6},{6,7},{7,4},{8,9},{9,10},{10,1... | collective-permute-start | bytes 737288 | tf_op jit(solution)/shard_map/ppermute | solution.py:418
  25.2 4.8 %collective-permute-start.11 = (bf16[64,1536]{1,0:T(8,128)(2,1)S(1)}, bf16[64,1536]{1,0:T(8,128)(2,1)S(1)}, u32[]{:S(2)}, u32[]{:S(2)}) collective-permute-start(bf16[64,1536]{1,0:T(8,128)(2,1)S(1)} %get-tuple-element.26.refs_5_), channel_id=1, source_target_pairs={{0,2},{1,3},{2,0},{3,1},{4,6},{5,7},{6,4},{7,5},{8,10},{9,11},{10,... | collective-permute-start | bytes 589832 | tf_op jit(solution)/shard_map/ppermute | solution.py:420
  30.0 20.0 %collective-permute-done.11.refs_8_ = bf16[64,1536]{1,0:T(8,128)(2,1)S(1)} collective-permute-done((bf16[64,1536]{1,0:T(8,128)(2,1)S(1)}, bf16[64,1536]{1,0:T(8,128)(2,1)S(1)}, u32[]{:S(2)}, u32[]{:S(2)}) %collective-permute-start.11) | collective-permute-done | bytes 196640 | tf_op jit(solution)/shard_map/ppermute | solution.py:420
  50.0 0.6 collective-permute-start.7
  50.6 0.2 collective-permute-start.13
  50.8 0.3 collective-permute-start.14
  51.1 0.3 collective-permute-done.12.refs_9_
  51.6 1.3 %term.1.refs_4_ = f32[256,1536]{1,0:T(8,128)S(1)} custom-call(bf16[8,32,1536]{2,1,0:T(8,128)(2,1)S(1)} %copy-done, bf16[64,1536]{1,0:T(8,128)(2,1)S(1)} %collective-permute-done.ends_mate, bf16[104,1536]{1,0:T(8,128)(2,1)S(1)} %collective-permute-done.1.across, bf16[80,1536]{1,0:T(8,128)(2,1)S(1)} %collective-permute-done.9.left.refs_6_, ...), custom_call_target="tpu_custom_call" | custom-call | flops 1048576 | bytes 65536 | tf_op jit(solution)/shard_map/term/pallas_call | solution.py:364
  52.9 4.3 %attend0.1.refs_13_ = f32[256,1536]{1,0:T(8,128)} custom-call(s32[1,1,2]{2,1,0:T(1,128)S(1)} %copy-done.4, s32[2,1,2]{2,1,0:T(1,128)S(1)} %copy-done.5, s32[2,1,2]{2,1,0:T(1,128)S(1)} %copy-done.6, bf16[256,1536]{1,0:T(8,128)(2,1)S(1)} %bitcast.8, bf16[256,1536]{1,0:T(8,128)(2,1)S(1)} %bitcast.10, bf16[256,1536]{1,0:T(8,128)(2,1)S(1)} %bitcast.6, ...), custom_call_target="tpu_custom_call" | custom-call | flops 1048576 | bytes 65536 | tf_op jit(solution)/shard_map/attend0/pallas_call | solution.py:442
  57.3 4.3 %collective-permute-done.7.refs_3_ = bf16[512,384]{1,0:T(8,128)(2,1)S(1)} collective-permute-done((bf16[512,384]{1,0:T(8,128)(2,1)S(1)}, bf16[512,384]{1,0:T(8,128)(2,1)S(1)}, u32[]{:S(2)}, u32[]{:S(2)}) %collective-permute-start.7) | collective-permute-done | bytes 393248 | tf_op jit(solution)/shard_map/ppermute | solution.py:408
  61.6 2.3 %attend1.1 = f32[256,1536]{1,0:T(8,128)} custom-call(s32[1,1,2]{2,1,0:T(1,128)S(1)} %copy-done.4, s32[2,1,2]{2,1,0:T(1,128)S(1)} %copy-done.5, s32[2,1,2]{2,1,0:T(1,128)S(1)} %copy-done.6, bf16[256,1536]{1,0:T(8,128)(2,1)S(1)} %bitcast.9, bf16[256,1536]{1,0:T(8,128)(2,1)S(1)} %bitcast.11, ...), custom_call_target="tpu_custom_call", output_to_operand_aliasing={{}: (19, {})} | custom-call | flops 1048576 | bytes 65536 | tf_op jit(solution)/shard_map/attend1/pallas_call | solution.py:442
  (30 shorter events, 0.5 us)
Async XLA Ops:
  0.0 5.3 %copy-start.4 = (s32[1,1,2]{2,1,0:T(1,128)S(1)}, s32[1,1,2]{2,1,0:T(1,128)}, u32[]{:S(2)}) copy-start(s32[1,1,2]{2,1,0:T(1,128)} %reads_ref.5) | copy-start | bytes 28
  1.6 14.0 %collective-permute-start.2 = (bf16[512,1536]{1,0:T(8,128)(2,1)S(1)}, bf16[512,1536]{1,0:T(8,128)(2,1)S(1)}, u32[]{:S(2)}, u32[]{:S(2)}) collective-permute-start(bf16[512,1536]{1,0:T(8,128)(2,1)S(1)} %get-tuple-element.19.stale), channel_id=1, source_target_pairs={{0,4},{4,0},{8,12},{12,8},{1,5},{5,1},{9,13},{13,9},{2,6},{6,2},{1... | collective-permute-start | bytes 4718600 | tf_op jit(solution)/shard_map/ppermute | solution.py:356
  1.6 3.7 %collective-permute-start = (bf16[64,1536]{1,0:T(8,128)(2,1)S(1)}, bf16[64,1536]{1,0:T(8,128)(2,1)S(1)}, u32[]{:S(2)}, u32[]{:S(2)}) collective-permute-start(bf16[64,1536]{1,0:T(8,128)(2,1)S(1)} %get-tuple-element.18), channel_id=1, source_target_pairs={{0,4},{4,0},{8,12},{12,8},{1,5},{5,1},{9,13},{13,9},{2,6},{6,2},{1... | collective-permute-start | bytes 589832 | tf_op jit(solution)/shard_map/ppermute | solution.py:356
  5.9 9.6 %collective-permute-start.1 = (bf16[104,1536]{1,0:T(8,128)(2,1)S(1)}, bf16[104,1536]{1,0:T(8,128)(2,1)S(1)}, u32[]{:S(2)}, u32[]{:S(2)}) collective-permute-start(bf16[104,1536]{1,0:T(8,128)(2,1)S(1)} %offer.1), channel_id=1, source_target_pairs={{0,8},{4,12},{8,0},{12,4},{1,9},{5,13},{9,1},{13,5},{2,10},{6,14},... | collective-permute-start | bytes 958472 | tf_op jit(solution)/shard_map/ppermute | solution.py:405
  7.5 16.0 %collective-permute-start.5 = (bf16[64,1536]{1,0:T(8,128)(2,1)S(1)}, bf16[64,1536]{1,0:T(8,128)(2,1)S(1)}, u32[]{:S(2)}, u32[]{:S(2)}) collective-permute-start(bf16[64,1536]{1,0:T(8,128)(2,1)S(1)} %get-tuple-element.21.text.refs_0_), channel_id=1, source_target_pairs={{0,2},{1,3},{2,0},{3,1},{4,6},{5,7},{6,4},{7,5},{8,10},{9,11},{10,... | collective-permute-start | bytes 589832 | tf_op jit(solution)/shard_map/ppermute | solution.py:394
  7.8 15.7 %collective-permute-start.4 = (bf16[64,1536]{1,0:T(8,128)(2,1)S(1)}, bf16[64,1536]{1,0:T(8,128)(2,1)S(1)}, u32[]{:S(2)}, u32[]{:S(2)}) collective-permute-start(bf16[64,1536]{1,0:T(8,128)(2,1)S(1)} %get-tuple-element.21.text.refs_0_), channel_id=1, source_target_pairs={{0,3},{1,0},{2,1},{3,2},{4,7},{5,4},{6,5},{7,6},{8,11},{9,8},{10,9... | collective-permute-start | bytes 589832 | tf_op jit(solution)/shard_map/ppermute | solution.py:394
  8.3 15.5 %collective-permute-start.3 = (bf16[64,1536]{1,0:T(8,128)(2,1)S(1)}, bf16[64,1536]{1,0:T(8,128)(2,1)S(1)}, u32[]{:S(2)}, u32[]{:S(2)}) collective-permute-start(bf16[64,1536]{1,0:T(8,128)(2,1)S(1)} %get-tuple-element.21.text.refs_0_), channel_id=1, source_target_pairs={{0,1},{1,2},{2,3},{3,0},{4,5},{5,6},{6,7},{7,4},{8,9},{9,10},{10,1... | collective-permute-start | bytes 589832 | tf_op jit(solution)/shard_map/ppermute | solution.py:394
  15.8 8.0 %copy-start = (bf16[8,32,1536]{2,1,0:T(8,128)(2,1)S(1)}, bf16[8,32,1536]{2,1,0:T(8,128)(2,1)}, u32[]{:S(2)}) copy-start(bf16[8,32,1536]{2,1,0:T(8,128)(2,1)} %cells.5) | copy-start | bytes 2359300
  15.8 35.7 %copy-start.3 = (f32[3,3,1536]{2,1,0:T(4,128)S(1)}, f32[3,3,1536]{2,1,0:T(4,128)}, u32[]{:S(2)}) copy-start(f32[3,3,1536]{2,1,0:T(4,128)} %weights.1) | copy-start | bytes 165892
  15.8 37.1 %collective-permute-start.8 = (bf16[512,1152]{1,0:T(8,128)(2,1)S(1)}, bf16[512,1152]{1,0:T(8,128)(2,1)S(1)}, u32[]{:S(2)}, u32[]{:S(2)}) collective-permute-start(bf16[512,1152]{1,0:T(8,128)(2,1)S(1)} %get-tuple-element.20), channel_id=1, source_target_pairs={{0,8},{4,12},{8,0},{12,4},{1,9},{5,13},{9,1},{13,5},{2,10},{6,14},... | collective-permute-start | bytes 3538952 | tf_op jit(solution)/shard_map/ppermute | solution.py:408
  23.8 27.1 %collective-permute-start.6 = (bf16[256,1536]{1,0:T(8,128)(2,1)S(1)}, bf16[256,1536]{1,0:T(8,128)(2,1)S(1)}, u32[]{:S(2)}, u32[]{:S(2)}) collective-permute-start(bf16[256,1536]{1,0:T(8,128)(2,1)S(1)} %bundle.1.refs_0_), channel_id=1, source_target_pairs={{0,4},{4,0},{8,12},{12,8},{1,5},{5,1},{9,13},{13,9},{2,6},{6,2},{1... | collective-permute-start | bytes 2359304 | tf_op jit(solution)/shard_map/ppermute | solution.py:356
  24.0 26.0 %collective-permute-start.9 = (bf16[80,1536]{1,0:T(8,128)(2,1)S(1)}, bf16[80,1536]{1,0:T(8,128)(2,1)S(1)}, u32[]{:S(2)}, u32[]{:S(2)}) collective-permute-start(bf16[80,1536]{1,0:T(8,128)(2,1)S(1)} %get-tuple-element.24), channel_id=1, source_target_pairs={{0,1},{1,2},{2,3},{3,0},{4,5},{5,6},{6,7},{7,4},{8,9},{9,10},{10,1... | collective-permute-start | bytes 737288 | tf_op jit(solution)/shard_map/ppermute | solution.py:418
  25.2 24.8 %collective-permute-start.11 = (bf16[64,1536]{1,0:T(8,128)(2,1)S(1)}, bf16[64,1536]{1,0:T(8,128)(2,1)S(1)}, u32[]{:S(2)}, u32[]{:S(2)}) collective-permute-start(bf16[64,1536]{1,0:T(8,128)(2,1)S(1)} %get-tuple-element.26.refs_5_), channel_id=1, source_target_pairs={{0,2},{1,3},{2,0},{3,1},{4,6},{5,7},{6,4},{7,5},{8,10},{9,11},{10,... | collective-permute-start | bytes 589832 | tf_op jit(solution)/shard_map/ppermute | solution.py:420
  30.0 20.7 %collective-permute-start.10 = (bf16[80,1536]{1,0:T(8,128)(2,1)S(1)}, bf16[80,1536]{1,0:T(8,128)(2,1)S(1)}, u32[]{:S(2)}, u32[]{:S(2)}) collective-permute-start(bf16[80,1536]{1,0:T(8,128)(2,1)S(1)} %get-tuple-element.25), channel_id=1, source_target_pairs={{0,3},{1,0},{2,1},{3,2},{4,7},{5,4},{6,5},{7,6},{8,11},{9,8},{10,9... | collective-permute-start | bytes 737288 | tf_op jit(solution)/shard_map/ppermute | solution.py:419
  50.0 1.4 %collective-permute-start.12 = (bf16[64,1536]{1,0:T(8,128)(2,1)S(1)}, bf16[64,1536]{1,0:T(8,128)(2,1)S(1)}, u32[]{:S(2)}, u32[]{:S(2)}) collective-permute-start(bf16[64,1536]{1,0:T(8,128)(2,1)S(1)} %get-tuple-element.26.refs_5_), channel_id=1, source_target_pairs={{0,4},{4,0},{8,12},{12,8},{1,5},{5,1},{9,13},{13,9},{2,6},{6,2},{1... | collective-permute-start | bytes 589832 | tf_op jit(solution)/shard_map/ppermute | solution.py:356
  50.0 2.9 %copy-start.1 = (bf16[8,32,1536]{2,1,0:T(8,128)(2,1)S(1)}, bf16[8,32,1536]{2,1,0:T(8,128)(2,1)}, u32[]{:S(2)}) copy-start(bf16[8,32,1536]{2,1,0:T(8,128)(2,1)} %param.11) | copy-start | bytes 2359300
  50.0 2.9 %copy-start.2 = (bf16[8,32,1536]{2,1,0:T(8,128)(2,1)S(1)}, bf16[8,32,1536]{2,1,0:T(8,128)(2,1)}, u32[]{:S(2)}) copy-start(bf16[8,32,1536]{2,1,0:T(8,128)(2,1)} %param.12) | copy-start | bytes 2359300
  50.0 2.9 %copy-start.5 = (s32[2,1,2]{2,1,0:T(1,128)S(1)}, s32[2,1,2]{2,1,0:T(1,128)}, u32[]{:S(2)}) copy-start(s32[2,1,2]{2,1,0:T(1,128)} %pattern_ref.3) | copy-start | bytes 52
  50.0 2.9 %copy-start.6 = (s32[2,1,2]{2,1,0:T(1,128)S(1)}, s32[2,1,2]{2,1,0:T(1,128)}, u32[]{:S(2)}) copy-start(s32[2,1,2]{2,1,0:T(1,128)} %text_ref.3) | copy-start | bytes 52
  50.0 11.6 %collective-permute-start.7 = (bf16[512,384]{1,0:T(8,128)(2,1)S(1)}, bf16[512,384]{1,0:T(8,128)(2,1)S(1)}, u32[]{:S(2)}, u32[]{:S(2)}) collective-permute-start(bf16[512,384]{1,0:T(8,128)(2,1)S(1)} %get-tuple-element.22), channel_id=1, source_target_pairs={{0,8},{4,12},{8,0},{12,4},{1,9},{5,13},{9,1},{13,5},{2,10},{6,14},... | collective-permute-start | bytes 1179656 | tf_op jit(solution)/shard_map/ppermute | solution.py:408
  50.6 2.2 %collective-permute-start.13 = (bf16[80,1536]{1,0:T(8,128)(2,1)S(1)}, bf16[80,1536]{1,0:T(8,128)(2,1)S(1)}, u32[]{:S(2)}, u32[]{:S(2)}) collective-permute-start(bf16[80,1536]{1,0:T(8,128)(2,1)S(1)} %collective-permute-done.9.left.refs_6_), channel_id=1, source_target_pairs={{0,4},{4,0},{8,12},{12,8},{1,5},{5,1},{9,13},{13,9},{2,6},{6,2},{1... | collective-permute-start | bytes 737288 | tf_op jit(solution)/shard_map/ppermute | solution.py:356
  50.8 2.0 %collective-permute-start.14 = (bf16[80,1536]{1,0:T(8,128)(2,1)S(1)}, bf16[80,1536]{1,0:T(8,128)(2,1)S(1)}, u32[]{:S(2)}, u32[]{:S(2)}) collective-permute-start(bf16[80,1536]{1,0:T(8,128)(2,1)S(1)} %collective-permute-done.10.right.refs_7_), channel_id=1, source_target_pairs={{0,4},{4,0},{8,12},{12,8},{1,5},{5,1},{9,13},{13,9},{2,6},{6,2},{1... | collective-permute-start | bytes 737288 | tf_op jit(solution)/shard_map/ppermute | solution.py:356
  51.4 1.5 %collective-permute-start.15 = (bf16[64,1536]{1,0:T(8,128)(2,1)S(1)}, bf16[64,1536]{1,0:T(8,128)(2,1)S(1)}, u32[]{:S(2)}, u32[]{:S(2)}) collective-permute-start(bf16[64,1536]{1,0:T(8,128)(2,1)S(1)} %collective-permute-done.11.refs_8_), channel_id=1, source_target_pairs={{0,4},{4,0},{8,12},{12,8},{1,5},{5,1},{9,13},{13,9},{2,6},{6,2},{1... | collective-permute-start | bytes 589832 | tf_op jit(solution)/shard_map/ppermute | solution.py:356

commit v7 on v6

--- a/solution.py
+++ b/solution.py
@@ -263,12 +263,12 @@
 
 
 def attend_kernel(first_head, reads_ref, pattern_ref, text_ref, q, k, v, *refs):
-    near, near_mate, passed, arrived, term = refs[:5]
-    side, side_mate = refs[5:9], refs[9:13]
+    home, home_mate, near, near_mate, passed, arrived, term = refs[:7]
+    side, side_mate = refs[7:11], refs[11:15]
     out = refs[-1]
     row, col = lax.axis_index("rows"), lax.axis_index("cols")
     across, core = row // 2, row % 2
-    shard = near.shape[0] // 8
+    shard = home.shape[0] // 2
     half = 2 * PER_BLOCK
     head_count = arrived.shape[1] // HEAD_DIM
 
@@ -281,11 +281,12 @@
         part = lanes(head)
 
         def one(piece):
-            rows = pl.ds((2 * piece + which) * shard, shard)
             here = pl.ds(which * shard, shard)
+            rows = here if piece == 0 else pl.ds((2 * piece - 2 + which) * shard, shard)
+            own, other = (home, home_mate) if piece == 0 else (near, near_mate)
             return jnp.where(
                 from_near,
-                jnp.where(from_own, near[rows, part], near_mate[rows, part]),
+                jnp.where(from_own, own[rows, part], other[rows, part]),
                 jnp.where(from_own, side[piece][here, part], side_mate[piece][here, part]),
             )
 
@@ -391,7 +392,7 @@
     backward = [(i, (i + 3) % 4) for i in range(4)]
     opposite = [(i, (i + 2) % 4) for i in range(4)]
 
-    near_parts = [text] + [lax.ppermute(text, "cols", p) for p in (forward, backward, opposite)]
+    near_parts = [lax.ppermute(text, "cols", p) for p in (forward, backward, opposite)]
     ends_mate = to_mate(ends)
     offer = local(
         offer_kernel,
@@ -403,25 +404,25 @@
         specs=[pl.BlockSpec(memory_space=pltpu.SMEM)] + [in_vmem] * 2,
     )
     across = lax.ppermute(offer, "rows", swap)
-    passed = to_mate(stale)
+    passed = to_mate(after(stale, ends_mate))
     packed = local(send_kernel, "send", chunks, across, stale, passed)
     far = [lax.ppermute(chunk, "rows", swap) for chunk in packed]
 
+    text_mate = to_mate(text)
     peer, plus, minus = local(
         join_kernel,
         "join",
         rows_of(2 * shard, 2 * shard + 16, 2 * shard + 16),
-        after(across, packed[0]),
+        after(across, packed[0], text_mate),
         v_fresh,
         ends_mate,
     )
+    near_parts[0] = after(near_parts[0], packed[0])
+    near = local(bundle_kernel, "bundle", rows_of(6 * shard), *near_parts)
+    near_mate = to_mate(near)
     left = lax.ppermute(plus, "cols", forward)
-    right = lax.ppermute(minus, "cols", backward)
+    right = lax.ppermute(after(minus, near_mate), "cols", backward)
     side_parts = [peer, left, right, lax.ppermute(peer, "cols", opposite)]
-    near_parts[0] = after(near_parts[0], packed[0])
-    near = local(bundle_kernel, "bundle", rows_of(8 * shard), *near_parts)
-    near_mate = to_mate(near)
-    side_parts[3] = after(side_parts[3], near_mate)
     side_mate = [to_mate(part) for part in side_parts]
     term = local(
         term_kernel,
@@ -445,16 +446,16 @@
             grid_spec=pltpu.PrefetchScalarGridSpec(
                 num_scalar_prefetch=3,
                 grid=(1,),
-                in_specs=[in_vmem] * 16 + [in_hbm] * (out is not None),
+                in_specs=[in_vmem] * 18 + [in_hbm] * (out is not None),
                 out_specs=block,
             ),
-            input_output_aliases={19: 0} if out is not None else {},
+            input_output_aliases={21: 0} if out is not None else {},
             compiler_params=params,
             cost_estimate=cost,
             name=f"attend{chunk}",
         )(
             reads, pattern, text_blocks, flat(q_fresh), flat(k_fresh), flat(v_fresh),
-            near, near_mate, passed, far[chunk], term, *side_parts, *side_mate,
+            text, text_mate, near, near_mate, passed, far[chunk], term, *side_parts, *side_mate,
             *([out] if out is not None else []),
         )
         first_head += head_count

time: 64 us -> 61 us (0.953)
  the two profiles are of different devices: /device:TPU:24 before, /device:TPU:0 now
where the time goes in v7:
time: 61 us; the launch traced here: 60.8 us
  waiting for transfers between devices  31.6 us (52%)
  starting transfers between devices  18.7 us (31%)
  Pallas kernels  10.4 us (17%)
    ppermute x1, waiting for transfers between devices, body(): side_parts = [peer, left, right, lax.ppermute(peer, 'cols', opposite)]  8.39 us
    ppermute x3, waiting for transfers between devices, body(): lax.ppermute(text, 'cols', p)  7.17 us
    pallas_call x2, Pallas kernels, body(): pl.pallas_call(functools.partial(attend_kernel, first_head), out_shape=ja...  6.59 us
    ppermute x1, waiting for transfers between devices, body(): left = lax.ppermute(plus, 'cols', forward)  5.63 us
    ppermute x3, starting transfers between devices, body(): lax.ppermute(text, 'cols', p)  5.51 us
    ppermute x1, waiting for transfers between devices, body(): right = lax.ppermute(after(minus, near_mate), 'cols', backward)  4.92 us
    ppermute x1, starting transfers between devices, body(): left = lax.ppermute(plus, 'cols', forward)  4.69 us
    pallas_call x6, Pallas kernels, local(): pl.pallas_call(kernel, out_shape=shapes, in_specs=specs or [in_vmem] * le...  3.84 us
  transfers between devices with their start and end apart: 17, of which 8 were waited for; matrix products, arithmetic and copies ran while one was open for 0% of the time, Pallas kernels for 10%

profile of v7, /device:TPU:0, one launch (start us, length us, event | category | flops | bytes accessed | tf_op | source)
XLA Modules:
  0.0 60.8 jit_solution(6466526279444720858)
XLA Ops:
  0.0 1.6 %pack.1 = (bf16[512,1536]{1,0:T(8,128)(2,1)S(1)}, bf16[64,1536]{1,0:T(8,128)(2,1)S(1)}, bf16[64,1536]{1,0:T(8,128)(2,1)S(1)}) custom-call(bf16[256,1536]{1,0:T(8,128)(2,1)} %bitcast.12, bf16[256,1536]{1,0:T(8,128)(2,1)} %bitcast.13, bf16[8,32,1536]{2,1,0:T(8,128)(2,1)} %cells.5, bf16[32,1536]{1,0:T(8,128)(2,1)} %text_k.1, bf16[32,1536]{1,0:T(8,128)(2,1)} %text_v.1), custom_call_target="tpu_custom_call" | custom-call | flops 1048576 | bytes 65536 | tf_op jit(solution)/shard_map/pack/pallas_call | solution.py:365
  1.6 0.5 collective-permute-start.2
  2.1 1.1 %collective-permute-done.2.ends_mate = bf16[64,1536]{1,0:T(8,128)(2,1)S(1)} collective-permute-done((bf16[64,1536]{1,0:T(8,128)(2,1)S(1)}, bf16[64,1536]{1,0:T(8,128)(2,1)S(1)}, u32[]{:S(2)}, u32[]{:S(2)}) %collective-permute-start.2) | collective-permute-done | bytes 196640 | tf_op jit(solution)/shard_map/ppermute | solution.py:357
  3.2 0.4 collective-permute-start.4
  3.5 0.6 offer.1
  4.1 2.7 %collective-permute-start.3 = (bf16[104,1536]{1,0:T(8,128)(2,1)S(1)}, bf16[104,1536]{1,0:T(8,128)(2,1)S(1)}, u32[]{:S(2)}, u32[]{:S(2)}) collective-permute-start(bf16[104,1536]{1,0:T(8,128)(2,1)S(1)} %offer.1), channel_id=1, source_target_pairs={{0,8},{4,12},{8,0},{12,4},{1,9},{5,13},{9,1},{13,5},{2,10},{6,14},... | collective-permute-start | bytes 958472 | tf_op jit(solution)/shard_map/ppermute | solution.py:406
  6.8 1.6 %collective-permute-start.1 = (bf16[64,1536]{1,0:T(8,128)(2,1)S(1)}, bf16[64,1536]{1,0:T(8,128)(2,1)S(1)}, u32[]{:S(2)}, u32[]{:S(2)}) collective-permute-start(bf16[64,1536]{1,0:T(8,128)(2,1)S(1)} %get-tuple-element.18.text.refs_0_), channel_id=1, source_target_pairs={{0,1},{1,2},{2,3},{3,0},{4,5},{5,6},{6,7},{7,4},{8,9},{9,10},{10,1... | collective-permute-start | bytes 589832 | tf_op jit(solution)/shard_map/ppermute | solution.py:395
  8.4 2.6 %collective-permute-start.6 = (bf16[64,1536]{1,0:T(8,128)(2,1)S(1)}, bf16[64,1536]{1,0:T(8,128)(2,1)S(1)}, u32[]{:S(2)}, u32[]{:S(2)}) collective-permute-start(bf16[64,1536]{1,0:T(8,128)(2,1)S(1)} %get-tuple-element.18.text.refs_0_), channel_id=1, source_target_pairs={{0,2},{1,3},{2,0},{3,1},{4,6},{5,7},{6,4},{7,5},{8,10},{9,11},{10,... | collective-permute-start | bytes 589832 | tf_op jit(solution)/shard_map/ppermute | solution.py:395
  11.0 1.3 %collective-permute-start.5 = (bf16[64,1536]{1,0:T(8,128)(2,1)S(1)}, bf16[64,1536]{1,0:T(8,128)(2,1)S(1)}, u32[]{:S(2)}, u32[]{:S(2)}) collective-permute-start(bf16[64,1536]{1,0:T(8,128)(2,1)S(1)} %get-tuple-element.18.text.refs_0_), channel_id=1, source_target_pairs={{0,3},{1,0},{2,1},{3,2},{4,7},{5,4},{6,5},{7,6},{8,11},{9,8},{10,9... | collective-permute-start | bytes 589832 | tf_op jit(solution)/shard_map/ppermute | solution.py:395
  12.3 2.5 %collective-permute-done.3.across = bf16[104,1536]{1,0:T(8,128)(2,1)S(1)} collective-permute-done((bf16[104,1536]{1,0:T(8,128)(2,1)S(1)}, bf16[104,1536]{1,0:T(8,128)(2,1)S(1)}, u32[]{:S(2)}, u32[]{:S(2)}) %collective-permute-start.3) | collective-permute-done | bytes 319520 | tf_op jit(solution)/shard_map/ppermute | solution.py:406
  15.1 1.8 %collective-permute-start.9 = (bf16[512,1152]{1,0:T(8,128)(2,1)S(1)}, bf16[512,1152]{1,0:T(8,128)(2,1)S(1)}, u32[]{:S(2)}, u32[]{:S(2)}) collective-permute-start(bf16[512,1152]{1,0:T(8,128)(2,1)S(1)} %get-tuple-element.22), channel_id=1, source_target_pairs={{0,8},{4,12},{8,0},{12,4},{1,9},{5,13},{9,1},{13,5},{2,10},{6,14},... | collective-permute-start | bytes 3538952 | tf_op jit(solution)/shard_map/ppermute | solution.py:409
  17.0 7.2 %collective-permute-done.6.refs_2_ = bf16[64,1536]{1,0:T(8,128)(2,1)S(1)} collective-permute-done((bf16[64,1536]{1,0:T(8,128)(2,1)S(1)}, bf16[64,1536]{1,0:T(8,128)(2,1)S(1)}, u32[]{:S(2)}, u32[]{:S(2)}) %collective-permute-start.6) | collective-permute-done | bytes 196640 | tf_op jit(solution)/shard_map/ppermute | solution.py:395
  24.2 0.5 collective-permute-start
  24.7 1.8 %collective-permute-done.refs_1_ = bf16[64,1536]{1,0:T(8,128)(2,1)S(1)} collective-permute-done((bf16[64,1536]{1,0:T(8,128)(2,1)S(1)}, bf16[64,1536]{1,0:T(8,128)(2,1)S(1)}, u32[]{:S(2)}, u32[]{:S(2)}) %collective-permute-start) | collective-permute-done | bytes 196640 | tf_op jit(solution)/shard_map/ppermute | solution.py:357
  26.9 4.7 %collective-permute-start.10 = (bf16[80,1536]{1,0:T(8,128)(2,1)S(1)}, bf16[80,1536]{1,0:T(8,128)(2,1)S(1)}, u32[]{:S(2)}, u32[]{:S(2)}) collective-permute-start(bf16[80,1536]{1,0:T(8,128)(2,1)S(1)} %get-tuple-element.26), channel_id=1, source_target_pairs={{0,1},{1,2},{2,3},{3,0},{4,5},{5,6},{6,7},{7,4},{8,9},{9,10},{10,1... | collective-permute-start | bytes 737288 | tf_op jit(solution)/shard_map/ppermute | solution.py:423
  31.6 1.1 %collective-permute-start.11 = (bf16[80,1536]{1,0:T(8,128)(2,1)S(1)}, bf16[80,1536]{1,0:T(8,128)(2,1)S(1)}, u32[]{:S(2)}, u32[]{:S(2)}) collective-permute-start(bf16[80,1536]{1,0:T(8,128)(2,1)S(1)} %get-tuple-element.28), channel_id=1, source_target_pairs={{0,3},{1,0},{2,1},{3,2},{4,7},{5,4},{6,5},{7,6},{8,11},{9,8},{10,9... | collective-permute-start | bytes 737288 | tf_op jit(solution)/shard_map/ppermute | solution.py:424
  32.6 0.6 collective-permute-start.12
  33.2 0.6 collective-permute-start.8
  33.8 5.6 %collective-permute-done.10.left.refs_8_ = bf16[80,1536]{1,0:T(8,128)(2,1)S(1)} collective-permute-done((bf16[80,1536]{1,0:T(8,128)(2,1)S(1)}, bf16[80,1536]{1,0:T(8,128)(2,1)S(1)}, u32[]{:S(2)}, u32[]{:S(2)}) %collective-permute-start.10) | collective-permute-done | bytes 245792 | tf_op jit(solution)/shard_map/ppermute | solution.py:423
  39.4 4.9 %collective-permute-done.11.right.refs_9_ = bf16[80,1536]{1,0:T(8,128)(2,1)S(1)} collective-permute-done((bf16[80,1536]{1,0:T(8,128)(2,1)S(1)}, bf16[80,1536]{1,0:T(8,128)(2,1)S(1)}, u32[]{:S(2)}, u32[]{:S(2)}) %collective-permute-start.11) | collective-permute-done | bytes 245792 | tf_op jit(solution)/shard_map/ppermute | solution.py:424
  44.4 8.4 %collective-permute-done.12.refs_10_ = bf16[64,1536]{1,0:T(8,128)(2,1)S(1)} collective-permute-done((bf16[64,1536]{1,0:T(8,128)(2,1)S(1)}, bf16[64,1536]{1,0:T(8,128)(2,1)S(1)}, u32[]{:S(2)}, u32[]{:S(2)}) %collective-permute-start.12) | collective-permute-done | bytes 196640 | tf_op jit(solution)/shard_map/ppermute | solution.py:425
  52.8 1.3 %term.1.refs_6_ = f32[256,1536]{1,0:T(8,128)S(1)} custom-call(bf16[8,32,1536]{2,1,0:T(8,128)(2,1)S(1)} %copy-done, bf16[64,1536]{1,0:T(8,128)(2,1)S(1)} %collective-permute-done.2.ends_mate, bf16[104,1536]{1,0:T(8,128)(2,1)S(1)} %collective-permute-done.3.across, bf16[80,1536]{1,0:T(8,128)(2,1)S(1)} %collective-permute-done.10.left.refs_8_, ...), custom_call_target="tpu_custom_call" | custom-call | flops 1048576 | bytes 65536 | tf_op jit(solution)/shard_map/term/pallas_call | solution.py:365
  54.3 4.3 %attend0.1.refs_15_ = f32[256,1536]{1,0:T(8,128)} custom-call(s32[1,1,2]{2,1,0:T(1,128)S(1)} %copy-done.4, s32[2,1,2]{2,1,0:T(1,128)S(1)} %copy-done.5, s32[2,1,2]{2,1,0:T(1,128)S(1)} %copy-done.6, bf16[256,1536]{1,0:T(8,128)(2,1)S(1)} %bitcast.8, bf16[256,1536]{1,0:T(8,128)(2,1)S(1)} %bitcast.10, bf16[256,1536]{1,0:T(8,128)(2,1)S(1)} %bitcast.6, ...), custom_call_target="tpu_custom_call" | custom-call | flops 1048576 | bytes 65536 | tf_op jit(solution)/shard_map/attend0/pallas_call | solution.py:443
  58.6 2.3 %attend1.1 = f32[256,1536]{1,0:T(8,128)} custom-call(s32[1,1,2]{2,1,0:T(1,128)S(1)} %copy-done.4, s32[2,1,2]{2,1,0:T(1,128)S(1)} %copy-done.5, s32[2,1,2]{2,1,0:T(1,128)S(1)} %copy-done.6, bf16[256,1536]{1,0:T(8,128)(2,1)S(1)} %bitcast.9, bf16[256,1536]{1,0:T(8,128)(2,1)S(1)} %bitcast.11, ...), custom_call_target="tpu_custom_call", output_to_operand_aliasing={{}: (21, {})} | custom-call | flops 1048576 | bytes 65536 | tf_op jit(solution)/shard_map/attend1/pallas_call | solution.py:443
  (32 shorter events, 0.9 us)
Async XLA Ops:
  0.0 3.5 %copy-start.4 = (s32[1,1,2]{2,1,0:T(1,128)S(1)}, s32[1,1,2]{2,1,0:T(1,128)}, u32[]{:S(2)}) copy-start(s32[1,1,2]{2,1,0:T(1,128)} %reads_ref.5) | copy-start | bytes 28
  1.6 1.6 %collective-permute-start.2 = (bf16[64,1536]{1,0:T(8,128)(2,1)S(1)}, bf16[64,1536]{1,0:T(8,128)(2,1)S(1)}, u32[]{:S(2)}, u32[]{:S(2)}) collective-permute-start(bf16[64,1536]{1,0:T(8,128)(2,1)S(1)} %get-tuple-element.19), channel_id=1, source_target_pairs={{0,4},{4,0},{8,12},{12,8},{1,5},{5,1},{9,13},{13,9},{2,6},{6,2},{1... | collective-permute-start | bytes 589832 | tf_op jit(solution)/shard_map/ppermute | solution.py:357
  3.2 11.7 %collective-permute-start.4 = (bf16[512,1536]{1,0:T(8,128)(2,1)S(1)}, bf16[512,1536]{1,0:T(8,128)(2,1)S(1)}, u32[]{:S(2)}, u32[]{:S(2)}) collective-permute-start(bf16[512,1536]{1,0:T(8,128)(2,1)S(1)} %get-tuple-element.21.stale), channel_id=1, source_target_pairs={{0,4},{4,0},{8,12},{12,8},{1,5},{5,1},{9,13},{13,9},{2,6},{6,2},{1... | collective-permute-start | bytes 4718600 | tf_op jit(solution)/shard_map/ppermute | solution.py:357
  4.1 22.4 %copy-start = (bf16[8,32,1536]{2,1,0:T(8,128)(2,1)S(1)}, bf16[8,32,1536]{2,1,0:T(8,128)(2,1)}, u32[]{:S(2)}) copy-start(bf16[8,32,1536]{2,1,0:T(8,128)(2,1)} %cells.5) | copy-start | bytes 2359300
  4.1 10.8 %collective-permute-start.3 = (bf16[104,1536]{1,0:T(8,128)(2,1)S(1)}, bf16[104,1536]{1,0:T(8,128)(2,1)S(1)}, u32[]{:S(2)}, u32[]{:S(2)}) collective-permute-start(bf16[104,1536]{1,0:T(8,128)(2,1)S(1)} %offer.1), channel_id=1, source_target_pairs={{0,8},{4,12},{8,0},{12,4},{1,9},{5,13},{9,1},{13,5},{2,10},{6,14},... | collective-permute-start | bytes 958472 | tf_op jit(solution)/shard_map/ppermute | solution.py:406
  6.8 10.1 %collective-permute-start.1 = (bf16[64,1536]{1,0:T(8,128)(2,1)S(1)}, bf16[64,1536]{1,0:T(8,128)(2,1)S(1)}, u32[]{:S(2)}, u32[]{:S(2)}) collective-permute-start(bf16[64,1536]{1,0:T(8,128)(2,1)S(1)} %get-tuple-element.18.text.refs_0_), channel_id=1, source_target_pairs={{0,1},{1,2},{2,3},{3,0},{4,5},{5,6},{6,7},{7,4},{8,9},{9,10},{10,1... | collective-permute-start | bytes 589832 | tf_op jit(solution)/shard_map/ppermute | solution.py:395
  8.4 15.7 %collective-permute-start.6 = (bf16[64,1536]{1,0:T(8,128)(2,1)S(1)}, bf16[64,1536]{1,0:T(8,128)(2,1)S(1)}, u32[]{:S(2)}, u32[]{:S(2)}) collective-permute-start(bf16[64,1536]{1,0:T(8,128)(2,1)S(1)} %get-tuple-element.18.text.refs_0_), channel_id=1, source_target_pairs={{0,2},{1,3},{2,0},{3,1},{4,6},{5,7},{6,4},{7,5},{8,10},{9,11},{10,... | collective-permute-start | bytes 589832 | tf_op jit(solution)/shard_map/ppermute | solution.py:395
  11.0 13.1 %collective-permute-start.5 = (bf16[64,1536]{1,0:T(8,128)(2,1)S(1)}, bf16[64,1536]{1,0:T(8,128)(2,1)S(1)}, u32[]{:S(2)}, u32[]{:S(2)}) collective-permute-start(bf16[64,1536]{1,0:T(8,128)(2,1)S(1)} %get-tuple-element.18.text.refs_0_), channel_id=1, source_target_pairs={{0,3},{1,0},{2,1},{3,2},{4,7},{5,4},{6,5},{7,6},{8,11},{9,8},{10,9... | collective-permute-start | bytes 589832 | tf_op jit(solution)/shard_map/ppermute | solution.py:395
  15.1 37.7 %copy-start.3 = (f32[3,3,1536]{2,1,0:T(4,128)S(1)}, f32[3,3,1536]{2,1,0:T(4,128)}, u32[]{:S(2)}) copy-start(f32[3,3,1536]{2,1,0:T(4,128)} %weights.1) | copy-start | bytes 165892
  15.1 39.1 %collective-permute-start.9 = (bf16[512,1152]{1,0:T(8,128)(2,1)S(1)}, bf16[512,1152]{1,0:T(8,128)(2,1)S(1)}, u32[]{:S(2)}, u32[]{:S(2)}) collective-permute-start(bf16[512,1152]{1,0:T(8,128)(2,1)S(1)} %get-tuple-element.22), channel_id=1, source_target_pairs={{0,8},{4,12},{8,0},{12,4},{1,9},{5,13},{9,1},{13,5},{2,10},{6,14},... | collective-permute-start | bytes 3538952 | tf_op jit(solution)/shard_map/ppermute | solution.py:409
  24.2 7.4 %collective-permute-start.7 = (bf16[192,1536]{1,0:T(8,128)(2,1)S(1)}, bf16[192,1536]{1,0:T(8,128)(2,1)S(1)}, u32[]{:S(2)}, u32[]{:S(2)}) collective-permute-start(bf16[192,1536]{1,0:T(8,128)(2,1)S(1)} %bundle.1.refs_2_), channel_id=1, source_target_pairs={{0,4},{4,0},{8,12},{12,8},{1,5},{5,1},{9,13},{13,9},{2,6},{6,2},{1... | collective-permute-start | bytes 1769480 | tf_op jit(solution)/shard_map/ppermute | solution.py:357
  24.2 2.3 %collective-permute-start = (bf16[64,1536]{1,0:T(8,128)(2,1)S(1)}, bf16[64,1536]{1,0:T(8,128)(2,1)S(1)}, u32[]{:S(2)}, u32[]{:S(2)}) collective-permute-start(bf16[64,1536]{1,0:T(8,128)(2,1)S(1)} %get-tuple-element.18.text.refs_0_), channel_id=1, source_target_pairs={{0,4},{4,0},{8,12},{12,8},{1,5},{5,1},{9,13},{13,9},{2,6},{6,2},{1... | collective-permute-start | bytes 589832 | tf_op jit(solution)/shard_map/ppermute | solution.py:357
  26.7 6.5 %collective-permute-start.13 = (bf16[64,1536]{1,0:T(8,128)(2,1)S(1)}, bf16[64,1536]{1,0:T(8,128)(2,1)S(1)}, u32[]{:S(2)}, u32[]{:S(2)}) collective-permute-start(bf16[64,1536]{1,0:T(8,128)(2,1)S(1)} %get-tuple-element.29.refs_7_), channel_id=1, source_target_pairs={{0,4},{4,0},{8,12},{12,8},{1,5},{5,1},{9,13},{13,9},{2,6},{6,2},{1... | collective-permute-start | bytes 589832 | tf_op jit(solution)/shard_map/ppermute | solution.py:357
  26.9 12.6 %collective-permute-start.10 = (bf16[80,1536]{1,0:T(8,128)(2,1)S(1)}, bf16[80,1536]{1,0:T(8,128)(2,1)S(1)}, u32[]{:S(2)}, u32[]{:S(2)}) collective-permute-start(bf16[80,1536]{1,0:T(8,128)(2,1)S(1)} %get-tuple-element.26), channel_id=1, source_target_pairs={{0,1},{1,2},{2,3},{3,0},{4,5},{5,6},{6,7},{7,4},{8,9},{9,10},{10,1... | collective-permute-start | bytes 737288 | tf_op jit(solution)/shard_map/ppermute | solution.py:423
  31.6 12.8 %collective-permute-start.11 = (bf16[80,1536]{1,0:T(8,128)(2,1)S(1)}, bf16[80,1536]{1,0:T(8,128)(2,1)S(1)}, u32[]{:S(2)}, u32[]{:S(2)}) collective-permute-start(bf16[80,1536]{1,0:T(8,128)(2,1)S(1)} %get-tuple-element.28), channel_id=1, source_target_pairs={{0,3},{1,0},{2,1},{3,2},{4,7},{5,4},{6,5},{7,6},{8,11},{9,8},{10,9... | collective-permute-start | bytes 737288 | tf_op jit(solution)/shard_map/ppermute | solution.py:424
  32.6 20.2 %collective-permute-start.12 = (bf16[64,1536]{1,0:T(8,128)(2,1)S(1)}, bf16[64,1536]{1,0:T(8,128)(2,1)S(1)}, u32[]{:S(2)}, u32[]{:S(2)}) collective-permute-start(bf16[64,1536]{1,0:T(8,128)(2,1)S(1)} %get-tuple-element.29.refs_7_), channel_id=1, source_target_pairs={{0,2},{1,3},{2,0},{3,1},{4,6},{5,7},{6,4},{7,5},{8,10},{9,11},{10,... | collective-permute-start | bytes 589832 | tf_op jit(solution)/shard_map/ppermute | solution.py:425
  33.2 21.1 %copy-start.1 = (bf16[8,32,1536]{2,1,0:T(8,128)(2,1)S(1)}, bf16[8,32,1536]{2,1,0:T(8,128)(2,1)}, u32[]{:S(2)}) copy-start(bf16[8,32,1536]{2,1,0:T(8,128)(2,1)} %param.11) | copy-start | bytes 2359300
  33.2 21.1 %copy-start.2 = (bf16[8,32,1536]{2,1,0:T(8,128)(2,1)S(1)}, bf16[8,32,1536]{2,1,0:T(8,128)(2,1)}, u32[]{:S(2)}) copy-start(bf16[8,32,1536]{2,1,0:T(8,128)(2,1)} %param.12) | copy-start | bytes 2359300
  33.2 21.1 %copy-start.5 = (s32[2,1,2]{2,1,0:T(1,128)S(1)}, s32[2,1,2]{2,1,0:T(1,128)}, u32[]{:S(2)}) copy-start(s32[2,1,2]{2,1,0:T(1,128)} %pattern_ref.3) | copy-start | bytes 52
  33.2 21.1 %copy-start.6 = (s32[2,1,2]{2,1,0:T(1,128)S(1)}, s32[2,1,2]{2,1,0:T(1,128)}, u32[]{:S(2)}) copy-start(s32[2,1,2]{2,1,0:T(1,128)} %text_ref.3) | copy-start | bytes 52
  33.2 25.4 %collective-permute-start.8 = (bf16[512,384]{1,0:T(8,128)(2,1)S(1)}, bf16[512,384]{1,0:T(8,128)(2,1)S(1)}, u32[]{:S(2)}, u32[]{:S(2)}) collective-permute-start(bf16[512,384]{1,0:T(8,128)(2,1)S(1)} %get-tuple-element.24), channel_id=1, source_target_pairs={{0,8},{4,12},{8,0},{12,4},{1,9},{5,13},{9,1},{13,5},{2,10},{6,14},... | collective-permute-start | bytes 1179656 | tf_op jit(solution)/shard_map/ppermute | solution.py:409
  39.4 14.8 %collective-permute-start.14 = (bf16[80,1536]{1,0:T(8,128)(2,1)S(1)}, bf16[80,1536]{1,0:T(8,128)(2,1)S(1)}, u32[]{:S(2)}, u32[]{:S(2)}) collective-permute-start(bf16[80,1536]{1,0:T(8,128)(2,1)S(1)} %collective-permute-done.10.left.refs_8_), channel_id=1, source_target_pairs={{0,4},{4,0},{8,12},{12,8},{1,5},{5,1},{9,13},{13,9},{2,6},{6,2},{1... | collective-permute-start | bytes 737288 | tf_op jit(solution)/shard_map/ppermute | solution.py:357
  44.3 9.9 %collective-permute-start.15 = (bf16[80,1536]{1,0:T(8,128)(2,1)S(1)}, bf16[80,1536]{1,0:T(8,128)(2,1)S(1)}, u32[]{:S(2)}, u32[]{:S(2)}) collective-permute-start(bf16[80,1536]{1,0:T(8,128)(2,1)S(1)} %collective-permute-done.11.right.refs_9_), channel_id=1, source_target_pairs={{0,4},{4,0},{8,12},{12,8},{1,5},{5,1},{9,13},{13,9},{2,6},{6,2},{1... | collective-permute-start | bytes 737288 | tf_op jit(solution)/shard_map/ppermute | solution.py:357
  52.8 1.4 %collective-permute-start.16 = (bf16[64,1536]{1,0:T(8,128)(2,1)S(1)}, bf16[64,1536]{1,0:T(8,128)(2,1)S(1)}, u32[]{:S(2)}, u32[]{:S(2)}) collective-permute-start(bf16[64,1536]{1,0:T(8,128)(2,1)S(1)} %collective-permute-done.12.refs_10_), channel_id=1, source_target_pairs={{0,4},{4,0},{8,12},{12,8},{1,5},{5,1},{9,13},{13,9},{2,6},{6,2},{1... | collective-permute-start | bytes 589832 | tf_op jit(solution)/shard_map/ppermute | solution.py:357

commit v8 on v6

--- a/solution.py
+++ b/solution.py
@@ -193,11 +193,10 @@
                 out[pl.ds(at, PER_BLOCK), :] = source[rows, part]
 
 
-def bundle_kernel(*refs):
-    out = refs[-1]
-    count = out.shape[0] // (len(refs) - 1)
-    for index, ref in enumerate(refs[:-1]):
-        out[pl.ds(index * count, count), :] = ref[pl.ds(0, count), :]
+def split_kernel(source, first, second):
+    half = first.shape[0]
+    first[...] = source[pl.ds(0, half), :]
+    second[...] = source[pl.ds(half, half), :]
 
 
 def above_below(ends_mate, across, part):
@@ -213,14 +212,16 @@
     )
 
 
-def join_kernel(across, cells, ends_mate, peer, plus, minus):
-    shard = peer.shape[0] // 2
+def join_kernel(text, across, cells, ends_mate, both, plus, minus):
+    shard = text.shape[0] // 2
     rows_here, cols_here, width = cells.shape
     above, below = above_below(ends_mate, across, slice(None))
     rows = [above] + [cells[i] for i in range(rows_here)] + [below]
     rows = [row.astype(jnp.float32) for row in rows]
     spare = jnp.zeros((16 - len(rows), width), jnp.float32)
-    for target in (peer, plus, minus):
+    both[pl.ds(0, 2 * shard), :] = text[...]
+    both[pl.ds(2 * shard, 2 * shard), :] = across[pl.ds(0, 2 * shard), :]
+    for target in (plus, minus):
         target[pl.ds(0, 2 * shard), :] = across[pl.ds(0, 2 * shard), :]
     for target, at in ((plus, cols_here - 1), (minus, 0)):
         edge = jnp.concatenate([row[at : at + 1] for row in rows] + [spare], axis=0)
@@ -263,12 +264,12 @@
 
 
 def attend_kernel(first_head, reads_ref, pattern_ref, text_ref, q, k, v, *refs):
-    near, near_mate, passed, arrived, term = refs[:5]
-    side, side_mate = refs[5:9], refs[9:13]
+    passed, arrived, term = refs[:3]
+    near, near_mate, side, side_mate = (refs[3 + 4 * i : 7 + 4 * i] for i in range(4))
     out = refs[-1]
     row, col = lax.axis_index("rows"), lax.axis_index("cols")
     across, core = row // 2, row % 2
-    shard = near.shape[0] // 8
+    shard = near[0].shape[0] // 2
     half = 2 * PER_BLOCK
     head_count = arrived.shape[1] // HEAD_DIM
 
@@ -281,12 +282,11 @@
         part = lanes(head)
 
         def one(piece):
-            rows = pl.ds((2 * piece + which) * shard, shard)
-            here = pl.ds(which * shard, shard)
+            rows = pl.ds(which * shard, shard)
             return jnp.where(
                 from_near,
-                jnp.where(from_own, near[rows, part], near_mate[rows, part]),
-                jnp.where(from_own, side[piece][here, part], side_mate[piece][here, part]),
+                jnp.where(from_own, near[piece][rows, part], near_mate[piece][rows, part]),
+                jnp.where(from_own, side[piece][rows, part], side_mate[piece][rows, part]),
             )
 
         return [one(piece) for piece in range(4)]
@@ -391,7 +391,7 @@
     backward = [(i, (i + 3) % 4) for i in range(4)]
     opposite = [(i, (i + 2) % 4) for i in range(4)]
 
-    near_parts = [text] + [lax.ppermute(text, "cols", p) for p in (forward, backward, opposite)]
+    near_parts = [lax.ppermute(text, "cols", p) for p in (forward, backward)]
     ends_mate = to_mate(ends)
     offer = local(
         offer_kernel,
@@ -403,25 +403,31 @@
         specs=[pl.BlockSpec(memory_space=pltpu.SMEM)] + [in_vmem] * 2,
     )
     across = lax.ppermute(offer, "rows", swap)
-    passed = to_mate(stale)
-    packed = local(send_kernel, "send", chunks, across, stale, passed)
+    passed = to_mate(after(stale, ends_mate))
+    packed = local(
+        send_kernel, "send", chunks, after(across, *near_parts), stale, passed
+    )
     far = [lax.ppermute(chunk, "rows", swap) for chunk in packed]
 
-    peer, plus, minus = local(
+    both, plus, minus = local(
         join_kernel,
         "join",
-        rows_of(2 * shard, 2 * shard + 16, 2 * shard + 16),
-        after(across, packed[0]),
+        rows_of(4 * shard, 2 * shard + 16, 2 * shard + 16),
+        text,
+        after(across, packed[0], *near_parts),
         v_fresh,
         ends_mate,
     )
     left = lax.ppermute(plus, "cols", forward)
     right = lax.ppermute(minus, "cols", backward)
-    side_parts = [peer, left, right, lax.ppermute(peer, "cols", opposite)]
-    near_parts[0] = after(near_parts[0], packed[0])
-    near = local(bundle_kernel, "bundle", rows_of(8 * shard), *near_parts)
-    near_mate = to_mate(near)
-    side_parts[3] = after(side_parts[3], near_mate)
+    across_cols = lax.ppermute(both, "cols", opposite)
+    own_side, far_side = (
+        local(split_kernel, "split", rows_of(2 * shard, 2 * shard), value)
+        for value in (both, across_cols)
+    )
+    near_parts = [text, *near_parts, far_side[0]]
+    side_parts = [own_side[1], left, right, far_side[1]]
+    near_mate = [to_mate(part) for part in near_parts]
     side_mate = [to_mate(part) for part in side_parts]
     term = local(
         term_kernel,
@@ -445,16 +451,16 @@
             grid_spec=pltpu.PrefetchScalarGridSpec(
                 num_scalar_prefetch=3,
                 grid=(1,),
-                in_specs=[in_vmem] * 16 + [in_hbm] * (out is not None),
+                in_specs=[in_vmem] * 22 + [in_hbm] * (out is not None),
                 out_specs=block,
             ),
-            input_output_aliases={19: 0} if out is not None else {},
+            input_output_aliases={25: 0} if out is not None else {},
             compiler_params=params,
             cost_estimate=cost,
             name=f"attend{chunk}",
         )(
             reads, pattern, text_blocks, flat(q_fresh), flat(k_fresh), flat(v_fresh),
-            near, near_mate, passed, far[chunk], term, *side_parts, *side_mate,
+            passed, far[chunk], term, *near_parts, *near_mate, *side_parts, *side_mate,
             *([out] if out is not None else []),
         )
         first_head += head_count

time: 64 us -> 64.4 us (level)
  the two profiles are of different devices: /device:TPU:24 before, /device:TPU:8 now
where the time goes in v8:
time: 64.4 us; the launch traced here: 64.2 us
  waiting for transfers between devices  42.3 us (66%)
  Pallas kernels  11.2 us (17%)
  starting transfers between devices  10.5 us (16%)
    ppermute x1, waiting for transfers between devices, body(): right = lax.ppermute(minus, 'cols', backward)  20.7 us
    ppermute x2, waiting for transfers between devices, body(): near_parts = [lax.ppermute(text, 'cols', p) for p in (forward, backward)]  11.1 us
    pallas_call x2, Pallas kernels, body(): pl.pallas_call(functools.partial(attend_kernel, first_head), out_shape=ja...  6.71 us
    ppermute x1, waiting for transfers between devices, body(): left = lax.ppermute(plus, 'cols', forward)  5.97 us
    pallas_call x7, Pallas kernels, local(): pl.pallas_call(kernel, out_shape=shapes, in_specs=specs or [in_vmem] * le...  4.54 us
    ppermute x2, waiting for transfers between devices, body(): far = [lax.ppermute(chunk, 'rows', swap) for chunk in packed]  2.96 us
    ppermute x1, starting transfers between devices, body(): across_cols = lax.ppermute(both, 'cols', opposite)  2.75 us
    ppermute x2, starting transfers between devices, body(): far = [lax.ppermute(chunk, 'rows', swap) for chunk in packed]  2.09 us
  transfers between devices with their start and end apart: 18, of which 7 were waited for; matrix products, arithmetic and copies ran while one was open for 0% of the time, Pallas kernels for 11%

profile of v8, /device:TPU:8, one launch (start us, length us, event | category | flops | bytes accessed | tf_op | source)
XLA Modules:
  0.0 64.2 jit_solution(12757744009361638431)
XLA Ops:
  0.0 1.6 %pack.1 = (bf16[512,1536]{1,0:T(8,128)(2,1)S(1)}, bf16[64,1536]{1,0:T(8,128)(2,1)S(1)}, bf16[64,1536]{1,0:T(8,128)(2,1)S(1)}) custom-call(bf16[256,1536]{1,0:T(8,128)(2,1)} %bitcast.12, bf16[256,1536]{1,0:T(8,128)(2,1)} %bitcast.13, bf16[8,32,1536]{2,1,0:T(8,128)(2,1)} %cells.5, bf16[32,1536]{1,0:T(8,128)(2,1)} %text_k.1, bf16[32,1536]{1,0:T(8,128)(2,1)} %text_v.1), custom_call_target="tpu_custom_call" | custom-call | flops 1048576 | bytes 65536 | tf_op jit(solution)/shard_map/pack/pallas_call | solution.py:364
  1.6 1.4 %collective-permute-done.ends_mate = bf16[64,1536]{1,0:T(8,128)(2,1)S(1)} collective-permute-done((bf16[64,1536]{1,0:T(8,128)(2,1)S(1)}, bf16[64,1536]{1,0:T(8,128)(2,1)S(1)}, u32[]{:S(2)}, u32[]{:S(2)}) %collective-permute-start) | collective-permute-done | bytes 196640 | tf_op jit(solution)/shard_map/ppermute | solution.py:356
  3.1 0.1 collective-permute-start.1
  3.2 0.6 offer.1
  3.8 1.6 %collective-permute-start.2 = (bf16[104,1536]{1,0:T(8,128)(2,1)S(1)}, bf16[104,1536]{1,0:T(8,128)(2,1)S(1)}, u32[]{:S(2)}, u32[]{:S(2)}) collective-permute-start(bf16[104,1536]{1,0:T(8,128)(2,1)S(1)} %offer.1), channel_id=1, source_target_pairs={{0,8},{4,12},{8,0},{12,4},{1,9},{5,13},{9,1},{13,5},{2,10},{6,14},... | collective-permute-start | bytes 958472 | tf_op jit(solution)/shard_map/ppermute | solution.py:405
  5.4 0.4 collective-permute-start.4
  5.8 1.6 %collective-permute-start.3 = (bf16[64,1536]{1,0:T(8,128)(2,1)S(1)}, bf16[64,1536]{1,0:T(8,128)(2,1)S(1)}, u32[]{:S(2)}, u32[]{:S(2)}) collective-permute-start(bf16[64,1536]{1,0:T(8,128)(2,1)S(1)} %get-tuple-element.23.text.refs_3_), channel_id=1, source_target_pairs={{0,1},{1,2},{2,3},{3,0},{4,5},{5,6},{6,7},{7,4},{8,9},{9,10},{10,1... | collective-permute-start | bytes 589832 | tf_op jit(solution)/shard_map/ppermute | solution.py:394
  7.4 4.9 %collective-permute-done.4.refs_5_ = bf16[64,1536]{1,0:T(8,128)(2,1)S(1)} collective-permute-done((bf16[64,1536]{1,0:T(8,128)(2,1)S(1)}, bf16[64,1536]{1,0:T(8,128)(2,1)S(1)}, u32[]{:S(2)}, u32[]{:S(2)}) %collective-permute-start.4) | collective-permute-done | bytes 196640 | tf_op jit(solution)/shard_map/ppermute | solution.py:394
  12.3 6.3 %collective-permute-done.3.refs_4_ = bf16[64,1536]{1,0:T(8,128)(2,1)S(1)} collective-permute-done((bf16[64,1536]{1,0:T(8,128)(2,1)S(1)}, bf16[64,1536]{1,0:T(8,128)(2,1)S(1)}, u32[]{:S(2)}, u32[]{:S(2)}) %collective-permute-start.3) | collective-permute-done | bytes 196640 | tf_op jit(solution)/shard_map/ppermute | solution.py:394
  18.6 0.2 send.1
  18.8 0.6 collective-permute-start.6
  19.4 0.5 collective-permute-start.12
  19.9 0.1 join.1
  20.1 2.8 %collective-permute-start.9 = (bf16[128,1536]{1,0:T(8,128)(2,1)S(1)}, bf16[128,1536]{1,0:T(8,128)(2,1)S(1)}, u32[]{:S(2)}, u32[]{:S(2)}) collective-permute-start(bf16[128,1536]{1,0:T(8,128)(2,1)S(1)} %get-tuple-element.30.source), channel_id=1, source_target_pairs={{0,2},{1,3},{2,0},{3,1},{4,6},{5,7},{6,4},{7,5},{8,10},{9,11},{10,... | collective-permute-start | bytes 1179656 | tf_op jit(solution)/shard_map/ppermute | solution.py:423
  23.0 6.0 %collective-permute-done.7.left.refs_12_ = bf16[80,1536]{1,0:T(8,128)(2,1)S(1)} collective-permute-done((bf16[80,1536]{1,0:T(8,128)(2,1)S(1)}, bf16[80,1536]{1,0:T(8,128)(2,1)S(1)}, u32[]{:S(2)}, u32[]{:S(2)}) %collective-permute-start.7) | collective-permute-done | bytes 245792 | tf_op jit(solution)/shard_map/ppermute | solution.py:421
  29.0 0.7 %split.3 = (bf16[64,1536]{1,0:T(8,128)(2,1)}, bf16[64,1536]{1,0:T(8,128)(2,1)S(1)}) custom-call(bf16[128,1536]{1,0:T(8,128)(2,1)S(1)} %get-tuple-element.30.source), custom_call_target="tpu_custom_call" | custom-call | flops 1048576 | bytes 65536 | tf_op jit(solution)/shard_map/split/pallas_call | solution.py:364
  29.7 0.5 collective-permute-start.14
  30.2 20.7 %collective-permute-done.8.right.refs_13_ = bf16[80,1536]{1,0:T(8,128)(2,1)S(1)} collective-permute-done((bf16[80,1536]{1,0:T(8,128)(2,1)S(1)}, bf16[80,1536]{1,0:T(8,128)(2,1)S(1)}, u32[]{:S(2)}, u32[]{:S(2)}) %collective-permute-start.8) | collective-permute-done | bytes 245792 | tf_op jit(solution)/shard_map/ppermute | solution.py:422
  50.9 1.5 %collective-permute-start.5 = (bf16[512,384]{1,0:T(8,128)(2,1)S(1)}, bf16[512,384]{1,0:T(8,128)(2,1)S(1)}, u32[]{:S(2)}, u32[]{:S(2)}) collective-permute-start(bf16[512,384]{1,0:T(8,128)(2,1)S(1)} %get-tuple-element.25), channel_id=1, source_target_pairs={{0,8},{4,12},{8,0},{12,4},{1,9},{5,13},{9,1},{13,5},{2,10},{6,14},... | collective-permute-start | bytes 1179656 | tf_op jit(solution)/shard_map/ppermute | solution.py:410
  52.4 0.6 collective-permute-start.13
  53.1 1.3 %term.1.refs_2_ = f32[256,1536]{1,0:T(8,128)S(1)} custom-call(bf16[8,32,1536]{2,1,0:T(8,128)(2,1)S(1)} %copy-done, bf16[64,1536]{1,0:T(8,128)(2,1)S(1)} %collective-permute-done.ends_mate, bf16[104,1536]{1,0:T(8,128)(2,1)S(1)} %collective-permute-done.2.across, bf16[80,1536]{1,0:T(8,128)(2,1)S(1)} %collective-permute-done.7.left.refs_12_, ...), custom_call_target="tpu_custom_call" | custom-call | flops 1048576 | bytes 65536 | tf_op jit(solution)/shard_map/term/pallas_call | solution.py:364
  54.6 4.4 %attend0.1.refs_19_ = f32[256,1536]{1,0:T(8,128)} custom-call(s32[1,1,2]{2,1,0:T(1,128)S(1)} %copy-done.4, s32[2,1,2]{2,1,0:T(1,128)S(1)} %copy-done.5, s32[2,1,2]{2,1,0:T(1,128)S(1)} %copy-done.6, bf16[256,1536]{1,0:T(8,128)(2,1)S(1)} %bitcast.8, bf16[256,1536]{1,0:T(8,128)(2,1)S(1)} %bitcast.10, bf16[256,1536]{1,0:T(8,128)(2,1)S(1)} %bitcast.6, ...), custom_call_target="tpu_custom_call" | custom-call | flops 1048576 | bytes 65536 | tf_op jit(solution)/shard_map/attend0/pallas_call | solution.py:448
  59.0 3.0 %collective-permute-done.5.refs_1_ = bf16[512,384]{1,0:T(8,128)(2,1)S(1)} collective-permute-done((bf16[512,384]{1,0:T(8,128)(2,1)S(1)}, bf16[512,384]{1,0:T(8,128)(2,1)S(1)}, u32[]{:S(2)}, u32[]{:S(2)}) %collective-permute-start.5) | collective-permute-done | bytes 393248 | tf_op jit(solution)/shard_map/ppermute | solution.py:410
  61.9 2.3 %attend1.1 = f32[256,1536]{1,0:T(8,128)} custom-call(s32[1,1,2]{2,1,0:T(1,128)S(1)} %copy-done.4, s32[2,1,2]{2,1,0:T(1,128)S(1)} %copy-done.5, s32[2,1,2]{2,1,0:T(1,128)S(1)} %copy-done.6, bf16[256,1536]{1,0:T(8,128)(2,1)S(1)} %bitcast.9, bf16[256,1536]{1,0:T(8,128)(2,1)S(1)} %bitcast.11, ...), custom_call_target="tpu_custom_call", output_to_operand_aliasing={{}: (25, {})} | custom-call | flops 1048576 | bytes 65536 | tf_op jit(solution)/shard_map/attend1/pallas_call | solution.py:448
  (35 shorter events, 0.5 us)
Async XLA Ops:
  0.0 3.2 %copy-start.4 = (s32[1,1,2]{2,1,0:T(1,128)S(1)}, s32[1,1,2]{2,1,0:T(1,128)}, u32[]{:S(2)}) copy-start(s32[1,1,2]{2,1,0:T(1,128)} %reads_ref.5) | copy-start | bytes 28
  1.6 1.5 %collective-permute-start = (bf16[64,1536]{1,0:T(8,128)(2,1)S(1)}, bf16[64,1536]{1,0:T(8,128)(2,1)S(1)}, u32[]{:S(2)}, u32[]{:S(2)}) collective-permute-start(bf16[64,1536]{1,0:T(8,128)(2,1)S(1)} %get-tuple-element.21), channel_id=1, source_target_pairs={{0,4},{4,0},{8,12},{12,8},{1,5},{5,1},{9,13},{13,9},{2,6},{6,2},{1... | collective-permute-start | bytes 589832 | tf_op jit(solution)/shard_map/ppermute | solution.py:356
  3.1 15.5 %collective-permute-start.1 = (bf16[512,1536]{1,0:T(8,128)(2,1)S(1)}, bf16[512,1536]{1,0:T(8,128)(2,1)S(1)}, u32[]{:S(2)}, u32[]{:S(2)}) collective-permute-start(bf16[512,1536]{1,0:T(8,128)(2,1)S(1)} %get-tuple-element.22.stale), channel_id=1, source_target_pairs={{0,4},{4,0},{8,12},{12,8},{1,5},{5,1},{9,13},{13,9},{2,6},{6,2},{1... | collective-permute-start | bytes 4718600 | tf_op jit(solution)/shard_map/ppermute | solution.py:356
  3.8 16.1 %copy-start = (bf16[8,32,1536]{2,1,0:T(8,128)(2,1)S(1)}, bf16[8,32,1536]{2,1,0:T(8,128)(2,1)}, u32[]{:S(2)}) copy-start(bf16[8,32,1536]{2,1,0:T(8,128)(2,1)} %cells.5) | copy-start | bytes 2359300
  3.8 14.7 %collective-permute-start.2 = (bf16[104,1536]{1,0:T(8,128)(2,1)S(1)}, bf16[104,1536]{1,0:T(8,128)(2,1)S(1)}, u32[]{:S(2)}, u32[]{:S(2)}) collective-permute-start(bf16[104,1536]{1,0:T(8,128)(2,1)S(1)} %offer.1), channel_id=1, source_target_pairs={{0,8},{4,12},{8,0},{12,4},{1,9},{5,13},{9,1},{13,5},{2,10},{6,14},... | collective-permute-start | bytes 958472 | tf_op jit(solution)/shard_map/ppermute | solution.py:405
  5.4 6.9 %collective-permute-start.4 = (bf16[64,1536]{1,0:T(8,128)(2,1)S(1)}, bf16[64,1536]{1,0:T(8,128)(2,1)S(1)}, u32[]{:S(2)}, u32[]{:S(2)}) collective-permute-start(bf16[64,1536]{1,0:T(8,128)(2,1)S(1)} %get-tuple-element.23.text.refs_3_), channel_id=1, source_target_pairs={{0,3},{1,0},{2,1},{3,2},{4,7},{5,4},{6,5},{7,6},{8,11},{9,8},{10,9... | collective-permute-start | bytes 589832 | tf_op jit(solution)/shard_map/ppermute | solution.py:394
  5.8 12.7 %collective-permute-start.3 = (bf16[64,1536]{1,0:T(8,128)(2,1)S(1)}, bf16[64,1536]{1,0:T(8,128)(2,1)S(1)}, u32[]{:S(2)}, u32[]{:S(2)}) collective-permute-start(bf16[64,1536]{1,0:T(8,128)(2,1)S(1)} %get-tuple-element.23.text.refs_3_), channel_id=1, source_target_pairs={{0,1},{1,2},{2,3},{3,0},{4,5},{5,6},{6,7},{7,4},{8,9},{9,10},{10,1... | collective-permute-start | bytes 589832 | tf_op jit(solution)/shard_map/ppermute | solution.py:394
  18.8 34.3 %copy-start.3 = (f32[3,3,1536]{2,1,0:T(4,128)S(1)}, f32[3,3,1536]{2,1,0:T(4,128)}, u32[]{:S(2)}) copy-start(f32[3,3,1536]{2,1,0:T(4,128)} %weights.1) | copy-start | bytes 165892
  18.8 35.7 %collective-permute-start.6 = (bf16[512,1152]{1,0:T(8,128)(2,1)S(1)}, bf16[512,1152]{1,0:T(8,128)(2,1)S(1)}, u32[]{:S(2)}, u32[]{:S(2)}) collective-permute-start(bf16[512,1152]{1,0:T(8,128)(2,1)S(1)} %get-tuple-element.26), channel_id=1, source_target_pairs={{0,8},{4,12},{8,0},{12,4},{1,9},{5,13},{9,1},{13,5},{2,10},{6,14},... | collective-permute-start | bytes 3538952 | tf_op jit(solution)/shard_map/ppermute | solution.py:410
  19.4 3.5 %collective-permute-start.10 = (bf16[64,1536]{1,0:T(8,128)(2,1)S(1)}, bf16[64,1536]{1,0:T(8,128)(2,1)S(1)}, u32[]{:S(2)}, u32[]{:S(2)}) collective-permute-start(bf16[64,1536]{1,0:T(8,128)(2,1)S(1)} %get-tuple-element.23.text.refs_3_), channel_id=1, source_target_pairs={{0,4},{4,0},{8,12},{12,8},{1,5},{5,1},{9,13},{13,9},{2,6},{6,2},{1... | collective-permute-start | bytes 589832 | tf_op jit(solution)/shard_map/ppermute | solution.py:356
  19.4 3.5 %collective-permute-start.12 = (bf16[64,1536]{1,0:T(8,128)(2,1)S(1)}, bf16[64,1536]{1,0:T(8,128)(2,1)S(1)}, u32[]{:S(2)}, u32[]{:S(2)}) collective-permute-start(bf16[64,1536]{1,0:T(8,128)(2,1)S(1)} %collective-permute-done.4.refs_5_), channel_id=1, source_target_pairs={{0,4},{4,0},{8,12},{12,8},{1,5},{5,1},{9,13},{13,9},{2,6},{6,2},{1... | collective-permute-start | bytes 589832 | tf_op jit(solution)/shard_map/ppermute | solution.py:356
  20.1 8.9 %collective-permute-start.7 = (bf16[80,1536]{1,0:T(8,128)(2,1)S(1)}, bf16[80,1536]{1,0:T(8,128)(2,1)S(1)}, u32[]{:S(2)}, u32[]{:S(2)}) collective-permute-start(bf16[80,1536]{1,0:T(8,128)(2,1)S(1)} %get-tuple-element.28), channel_id=1, source_target_pairs={{0,1},{1,2},{2,3},{3,0},{4,5},{5,6},{6,7},{7,4},{8,9},{9,10},{10,1... | collective-permute-start | bytes 737288 | tf_op jit(solution)/shard_map/ppermute | solution.py:421
  20.1 32.2 %collective-permute-start.9 = (bf16[128,1536]{1,0:T(8,128)(2,1)S(1)}, bf16[128,1536]{1,0:T(8,128)(2,1)S(1)}, u32[]{:S(2)}, u32[]{:S(2)}) collective-permute-start(bf16[128,1536]{1,0:T(8,128)(2,1)S(1)} %get-tuple-element.30.source), channel_id=1, source_target_pairs={{0,2},{1,3},{2,0},{3,1},{4,6},{5,7},{6,4},{7,5},{8,10},{9,11},{10,... | collective-permute-start | bytes 1179656 | tf_op jit(solution)/shard_map/ppermute | solution.py:423
  22.9 28.0 %collective-permute-start.8 = (bf16[80,1536]{1,0:T(8,128)(2,1)S(1)}, bf16[80,1536]{1,0:T(8,128)(2,1)S(1)}, u32[]{:S(2)}, u32[]{:S(2)}) collective-permute-start(bf16[80,1536]{1,0:T(8,128)(2,1)S(1)} %get-tuple-element.29), channel_id=1, source_target_pairs={{0,3},{1,0},{2,1},{3,2},{4,7},{5,4},{6,5},{7,6},{8,11},{9,8},{10,9... | collective-permute-start | bytes 737288 | tf_op jit(solution)/shard_map/ppermute | solution.py:422
  22.9 6.8 %collective-permute-start.11 = (bf16[64,1536]{1,0:T(8,128)(2,1)S(1)}, bf16[64,1536]{1,0:T(8,128)(2,1)S(1)}, u32[]{:S(2)}, u32[]{:S(2)}) collective-permute-start(bf16[64,1536]{1,0:T(8,128)(2,1)S(1)} %collective-permute-done.3.refs_4_), channel_id=1, source_target_pairs={{0,4},{4,0},{8,12},{12,8},{1,5},{5,1},{9,13},{13,9},{2,6},{6,2},{1... | collective-permute-start | bytes 589832 | tf_op jit(solution)/shard_map/ppermute | solution.py:356
  29.0 24.1 %collective-permute-start.15 = (bf16[80,1536]{1,0:T(8,128)(2,1)S(1)}, bf16[80,1536]{1,0:T(8,128)(2,1)S(1)}, u32[]{:S(2)}, u32[]{:S(2)}) collective-permute-start(bf16[80,1536]{1,0:T(8,128)(2,1)S(1)} %collective-permute-done.7.left.refs_12_), channel_id=1, source_target_pairs={{0,4},{4,0},{8,12},{12,8},{1,5},{5,1},{9,13},{13,9},{2,6},{6,2},{1... | collective-permute-start | bytes 737288 | tf_op jit(solution)/shard_map/ppermute | solution.py:356
  29.7 22.8 %collective-permute-start.14 = (bf16[64,1536]{1,0:T(8,128)(2,1)S(1)}, bf16[64,1536]{1,0:T(8,128)(2,1)S(1)}, u32[]{:S(2)}, u32[]{:S(2)}) collective-permute-start(bf16[64,1536]{1,0:T(8,128)(2,1)S(1)} %get-tuple-element.32.refs_11_), channel_id=1, source_target_pairs={{0,4},{4,0},{8,12},{12,8},{1,5},{5,1},{9,13},{13,9},{2,6},{6,2},{1... | collective-permute-start | bytes 589832 | tf_op jit(solution)/shard_map/ppermute | solution.py:356
  50.9 11.0 %collective-permute-start.5 = (bf16[512,384]{1,0:T(8,128)(2,1)S(1)}, bf16[512,384]{1,0:T(8,128)(2,1)S(1)}, u32[]{:S(2)}, u32[]{:S(2)}) collective-permute-start(bf16[512,384]{1,0:T(8,128)(2,1)S(1)} %get-tuple-element.25), channel_id=1, source_target_pairs={{0,8},{4,12},{8,0},{12,4},{1,9},{5,13},{9,1},{13,5},{2,10},{6,14},... | collective-permute-start | bytes 1179656 | tf_op jit(solution)/shard_map/ppermute | solution.py:410
  52.4 2.1 %collective-permute-start.16 = (bf16[80,1536]{1,0:T(8,128)(2,1)S(1)}, bf16[80,1536]{1,0:T(8,128)(2,1)S(1)}, u32[]{:S(2)}, u32[]{:S(2)}) collective-permute-start(bf16[80,1536]{1,0:T(8,128)(2,1)S(1)} %collective-permute-done.8.right.refs_13_), channel_id=1, source_target_pairs={{0,4},{4,0},{8,12},{12,8},{1,5},{5,1},{9,13},{13,9},{2,6},{6,2},{1... | collective-permute-start | bytes 737288 | tf_op jit(solution)/shard_map/ppermute | solution.py:356
  52.4 2.0 %collective-permute-start.13 = (bf16[64,1536]{1,0:T(8,128)(2,1)S(1)}, bf16[64,1536]{1,0:T(8,128)(2,1)S(1)}, u32[]{:S(2)}, u32[]{:S(2)}) collective-permute-start(bf16[64,1536]{1,0:T(8,128)(2,1)S(1)} %get-tuple-element.31.refs_6_), channel_id=1, source_target_pairs={{0,4},{4,0},{8,12},{12,8},{1,5},{5,1},{9,13},{13,9},{2,6},{6,2},{1... | collective-permute-start | bytes 589832 | tf_op jit(solution)/shard_map/ppermute | solution.py:356
  53.0 1.5 %copy-start.2 = (bf16[8,32,1536]{2,1,0:T(8,128)(2,1)S(1)}, bf16[8,32,1536]{2,1,0:T(8,128)(2,1)}, u32[]{:S(2)}) copy-start(bf16[8,32,1536]{2,1,0:T(8,128)(2,1)} %param.12) | copy-start | bytes 2359300
  53.0 1.5 %copy-start.5 = (s32[2,1,2]{2,1,0:T(1,128)S(1)}, s32[2,1,2]{2,1,0:T(1,128)}, u32[]{:S(2)}) copy-start(s32[2,1,2]{2,1,0:T(1,128)} %pattern_ref.3) | copy-start | bytes 52
  53.0 1.5 %copy-start.6 = (s32[2,1,2]{2,1,0:T(1,128)S(1)}, s32[2,1,2]{2,1,0:T(1,128)}, u32[]{:S(2)}) copy-start(s32[2,1,2]{2,1,0:T(1,128)} %text_ref.3) | copy-start | bytes 52
  53.0 1.5 %collective-permute-start.17 = (bf16[64,1536]{1,0:T(8,128)(2,1)S(1)}, bf16[64,1536]{1,0:T(8,128)(2,1)S(1)}, u32[]{:S(2)}, u32[]{:S(2)}) collective-permute-start(bf16[64,1536]{1,0:T(8,128)(2,1)S(1)} %get-tuple-element.33.refs_14_), channel_id=1, source_target_pairs={{0,4},{4,0},{8,12},{12,8},{1,5},{5,1},{9,13},{13,9},{2,6},{6,2},{1... | collective-permute-start | bytes 589832 | tf_op jit(solution)/shard_map/ppermute | solution.py:356
  (1 other events, 1.5 us)

commit v9 on v8

--- a/solution.py
+++ b/solution.py
@@ -14,7 +14,7 @@
 PER_BLOCK = BLOCK_ROWS * BLOCK_COLS
 SCORE_SCALE = 1.0 / math.sqrt(HEAD_DIM)
 EXP2_SCALE = SCORE_SCALE * math.log2(math.e)
-CHUNK_HEADS = (9, 3)
+CHUNK_HEADS = (8, 4)
 GROUP = 8
 VMEM_LIMIT = 24 * 1024 * 1024
 
@@ -191,6 +191,14 @@
                 rows = pl.ds(pl.multiple_of(which * tokens + starts[slot], PER_BLOCK), PER_BLOCK)
                 at = (2 * which + slot) * PER_BLOCK
                 out[pl.ds(at, PER_BLOCK), :] = source[rows, part]
+
+
+def bundle_kernel(*refs):
+    out = refs[-1]
+    at = 0
+    for ref in refs[:-1]:
+        out[pl.ds(at, ref.shape[0]), :] = ref[...]
+        at += ref.shape[0]
 
 
 def split_kernel(source, first, second):
@@ -265,11 +273,11 @@
 
 def attend_kernel(first_head, reads_ref, pattern_ref, text_ref, q, k, v, *refs):
     passed, arrived, term = refs[:3]
-    near, near_mate, side, side_mate = (refs[3 + 4 * i : 7 + 4 * i] for i in range(4))
+    early, early_mate, late, late_mate = refs[3], refs[4], refs[5:9], refs[9:13]
     out = refs[-1]
     row, col = lax.axis_index("rows"), lax.axis_index("cols")
     across, core = row // 2, row % 2
-    shard = near[0].shape[0] // 2
+    shard = early.shape[0] // 8
     half = 2 * PER_BLOCK
     head_count = arrived.shape[1] // HEAD_DIM
 
@@ -282,11 +290,19 @@
         part = lanes(head)
 
         def one(piece):
-            rows = pl.ds(which * shard, shard)
+            def pick(own, other, at):
+                rows = pl.ds((2 * at + which) * shard, shard)
+                return jnp.where(from_own, own[rows, part], other[rows, part])
+
+            near_at, side_at = ((2, 3), (0, None), (1, None), (None, None))[piece]
             return jnp.where(
                 from_near,
-                jnp.where(from_own, near[piece][rows, part], near_mate[piece][rows, part]),
-                jnp.where(from_own, side[piece][rows, part], side_mate[piece][rows, part]),
+                pick(late[0], late_mate[0], 0)
+                if near_at is None
+                else pick(early, early_mate, near_at),
+                pick(late[piece], late_mate[piece], 0)
+                if side_at is None
+                else pick(early, early_mate, side_at),
             )
 
         return [one(piece) for piece in range(4)]
@@ -405,7 +421,7 @@
     across = lax.ppermute(offer, "rows", swap)
     passed = to_mate(after(stale, ends_mate))
     packed = local(
-        send_kernel, "send", chunks, after(across, *near_parts), stale, passed
+        send_kernel, "send", chunks, across, stale, passed
     )
     far = [lax.ppermute(chunk, "rows", swap) for chunk in packed]
 
@@ -414,21 +430,19 @@
         "join",
         rows_of(4 * shard, 2 * shard + 16, 2 * shard + 16),
         text,
-        after(across, packed[0], *near_parts),
+        after(across, packed[0]),
         v_fresh,
         ends_mate,
     )
     left = lax.ppermute(plus, "cols", forward)
     right = lax.ppermute(minus, "cols", backward)
     across_cols = lax.ppermute(both, "cols", opposite)
-    own_side, far_side = (
-        local(split_kernel, "split", rows_of(2 * shard, 2 * shard), value)
-        for value in (both, across_cols)
-    )
-    near_parts = [text, *near_parts, far_side[0]]
-    side_parts = [own_side[1], left, right, far_side[1]]
-    near_mate = [to_mate(part) for part in near_parts]
-    side_mate = [to_mate(part) for part in side_parts]
+    early = local(bundle_kernel, "bundle", rows_of(8 * shard), *near_parts, both)
+    early_mate = to_mate(early)
+    across_cols = after(across_cols, early_mate)
+    far_side = local(split_kernel, "split", rows_of(2 * shard, 2 * shard), across_cols)
+    late = [far_side[0], left, right, far_side[1]]
+    late_mate = [to_mate(part) for part in late]
     term = local(
         term_kernel,
         "term",
@@ -451,16 +465,16 @@
             grid_spec=pltpu.PrefetchScalarGridSpec(
                 num_scalar_prefetch=3,
                 grid=(1,),
-                in_specs=[in_vmem] * 22 + [in_hbm] * (out is not None),
+                in_specs=[in_vmem] * 16 + [in_hbm] * (out is not None),
                 out_specs=block,
             ),
-            input_output_aliases={25: 0} if out is not None else {},
+            input_output_aliases={19: 0} if out is not None else {},
             compiler_params=params,
             cost_estimate=cost,
             name=f"attend{chunk}",
         )(
             reads, pattern, text_blocks, flat(q_fresh), flat(k_fresh), flat(v_fresh),
-            passed, far[chunk], term, *near_parts, *near_mate, *side_parts, *side_mate,
+            passed, far[chunk], term, early, early_mate, *late, *late_mate,
             *([out] if out is not None else []),
         )
         first_head += head_count

time: 64.4 us -> 60.9 us (0.946)
  the two profiles are of different devices: /device:TPU:8 before, /device:TPU:0 now
where the time goes in v9:
time: 60.9 us; the launch traced here: 60.7 us
  waiting for transfers between devices  35.6 us (58%)
  starting transfers between devices  14.2 us (23%)
  Pallas kernels  10.8 us (18%)
    ppermute x1, waiting for transfers between devices, body(): across_cols = lax.ppermute(both, 'cols', opposite)  16 us
    pallas_call x2, Pallas kernels, body(): pl.pallas_call(functools.partial(attend_kernel, first_head), out_shape=ja...  6.94 us
    ppermute x1, waiting for transfers between devices, body(): left = lax.ppermute(plus, 'cols', forward)  6.77 us
    ppermute x1, waiting for transfers between devices, body(): across = lax.ppermute(offer, 'rows', swap)  4.45 us
    ppermute x1, waiting for transfers between devices, body(): right = lax.ppermute(minus, 'cols', backward)  4.39 us
    pallas_call x7, Pallas kernels, local(): pl.pallas_call(kernel, out_shape=shapes, in_specs=specs or [in_vmem] * le...  3.88 us
    ppermute x2, starting transfers between devices, body(): near_parts = [lax.ppermute(text, 'cols', p) for p in (forward, backward)]  3.6 us
    ppermute x2, waiting for transfers between devices, body(): near_parts = [lax.ppermute(text, 'cols', p) for p in (forward, backward)]  2.86 us
  transfers between devices with their start and end apart: 15, of which 7 were waited for; matrix products, arithmetic and copies ran while one was open for 0% of the time, Pallas kernels for 10%

profile of v9, /device:TPU:0, one launch (start us, length us, event | category | flops | bytes accessed | tf_op | source)
XLA Modules:
  0.0 60.7 jit_solution(13152021820584310314)
XLA Ops:
  0.0 1.6 %pack.1 = (bf16[512,1536]{1,0:T(8,128)(2,1)S(1)}, bf16[64,1536]{1,0:T(8,128)(2,1)S(1)}, bf16[64,1536]{1,0:T(8,128)(2,1)S(1)}) custom-call(bf16[256,1536]{1,0:T(8,128)(2,1)} %bitcast.12, bf16[256,1536]{1,0:T(8,128)(2,1)} %bitcast.13, bf16[8,32,1536]{2,1,0:T(8,128)(2,1)} %cells.5, bf16[32,1536]{1,0:T(8,128)(2,1)} %text_k.1, bf16[32,1536]{1,0:T(8,128)(2,1)} %text_v.1), custom_call_target="tpu_custom_call" | custom-call | flops 1048576 | bytes 65536 | tf_op jit(solution)/shard_map/pack/pallas_call | solution.py:380
  1.6 0.5 collective-permute-start
  2.1 1.1 %collective-permute-done.ends_mate = bf16[64,1536]{1,0:T(8,128)(2,1)S(1)} collective-permute-done((bf16[64,1536]{1,0:T(8,128)(2,1)S(1)}, bf16[64,1536]{1,0:T(8,128)(2,1)S(1)}, u32[]{:S(2)}, u32[]{:S(2)}) %collective-permute-start) | collective-permute-done | bytes 196640 | tf_op jit(solution)/shard_map/ppermute | solution.py:372
  3.2 0.4 collective-permute-start.1
  3.5 0.6 offer.1
  4.1 2.7 %collective-permute-start.2 = (bf16[104,1536]{1,0:T(8,128)(2,1)S(1)}, bf16[104,1536]{1,0:T(8,128)(2,1)S(1)}, u32[]{:S(2)}, u32[]{:S(2)}) collective-permute-start(bf16[104,1536]{1,0:T(8,128)(2,1)S(1)} %offer.1), channel_id=1, source_target_pairs={{0,8},{4,12},{8,0},{12,4},{1,9},{5,13},{9,1},{13,5},{2,10},{6,14},... | collective-permute-start | bytes 958472 | tf_op jit(solution)/shard_map/ppermute | solution.py:421
  6.8 3.6 %collective-permute-start.8 = (bf16[64,1536]{1,0:T(8,128)(2,1)S(1)}, bf16[64,1536]{1,0:T(8,128)(2,1)S(1)}, u32[]{:S(2)}, u32[]{:S(2)}) collective-permute-start(bf16[64,1536]{1,0:T(8,128)(2,1)S(1)} %get-tuple-element.22.text), channel_id=1, source_target_pairs={{0,3},{1,0},{2,1},{3,2},{4,7},{5,4},{6,5},{7,6},{8,11},{9,8},{10,9... | collective-permute-start | bytes 589832 | tf_op jit(solution)/shard_map/ppermute | solution.py:410
  10.4 4.5 %collective-permute-done.2.across = bf16[104,1536]{1,0:T(8,128)(2,1)S(1)} collective-permute-done((bf16[104,1536]{1,0:T(8,128)(2,1)S(1)}, bf16[104,1536]{1,0:T(8,128)(2,1)S(1)}, u32[]{:S(2)}, u32[]{:S(2)}) %collective-permute-start.2) | collective-permute-done | bytes 319520 | tf_op jit(solution)/shard_map/ppermute | solution.py:421
  14.9 0.2 send.1
  15.1 1.8 %collective-permute-start.4 = (bf16[512,1024]{1,0:T(8,128)(2,1)S(1)}, bf16[512,1024]{1,0:T(8,128)(2,1)S(1)}, u32[]{:S(2)}, u32[]{:S(2)}) collective-permute-start(bf16[512,1024]{1,0:T(8,128)(2,1)S(1)} %get-tuple-element.24), channel_id=1, source_target_pairs={{0,8},{4,12},{8,0},{12,4},{1,9},{5,13},{9,1},{13,5},{2,10},{6,14},... | collective-permute-start | bytes 3145736 | tf_op jit(solution)/shard_map/ppermute | solution.py:426
  16.9 0.1 join.1
  17.1 2.9 %collective-permute-done.7.refs_0_ = bf16[64,1536]{1,0:T(8,128)(2,1)S(1)} collective-permute-done((bf16[64,1536]{1,0:T(8,128)(2,1)S(1)}, bf16[64,1536]{1,0:T(8,128)(2,1)S(1)}, u32[]{:S(2)}, u32[]{:S(2)}) %collective-permute-start.7) | collective-permute-done | bytes 196640 | tf_op jit(solution)/shard_map/ppermute | solution.py:410
  20.0 0.1 collective-permute-start.9
  20.1 1.7 %collective-permute-start.5 = (bf16[80,1536]{1,0:T(8,128)(2,1)S(1)}, bf16[80,1536]{1,0:T(8,128)(2,1)S(1)}, u32[]{:S(2)}, u32[]{:S(2)}) collective-permute-start(bf16[80,1536]{1,0:T(8,128)(2,1)S(1)} %get-tuple-element.26), channel_id=1, source_target_pairs={{0,1},{1,2},{2,3},{3,0},{4,5},{5,6},{6,7},{7,4},{8,9},{9,10},{10,1... | collective-permute-start | bytes 737288 | tf_op jit(solution)/shard_map/ppermute | solution.py:437
  21.8 2.2 %collective-permute-start.6 = (bf16[80,1536]{1,0:T(8,128)(2,1)S(1)}, bf16[80,1536]{1,0:T(8,128)(2,1)S(1)}, u32[]{:S(2)}, u32[]{:S(2)}) collective-permute-start(bf16[80,1536]{1,0:T(8,128)(2,1)S(1)} %get-tuple-element.27), channel_id=1, source_target_pairs={{0,3},{1,0},{2,1},{3,2},{4,7},{5,4},{6,5},{7,6},{8,11},{9,8},{10,9... | collective-permute-start | bytes 737288 | tf_op jit(solution)/shard_map/ppermute | solution.py:438
  24.0 6.8 %collective-permute-done.5.left.refs_6_ = bf16[80,1536]{1,0:T(8,128)(2,1)S(1)} collective-permute-done((bf16[80,1536]{1,0:T(8,128)(2,1)S(1)}, bf16[80,1536]{1,0:T(8,128)(2,1)S(1)}, u32[]{:S(2)}, u32[]{:S(2)}) %collective-permute-start.5) | collective-permute-done | bytes 245792 | tf_op jit(solution)/shard_map/ppermute | solution.py:437
  30.7 0.5 collective-permute-start.3
  31.3 4.4 %collective-permute-done.6.right.refs_7_ = bf16[80,1536]{1,0:T(8,128)(2,1)S(1)} collective-permute-done((bf16[80,1536]{1,0:T(8,128)(2,1)S(1)}, bf16[80,1536]{1,0:T(8,128)(2,1)S(1)}, u32[]{:S(2)}, u32[]{:S(2)}) %collective-permute-start.6) | collective-permute-done | bytes 245792 | tf_op jit(solution)/shard_map/ppermute | solution.py:438
  35.7 16.0 %collective-permute-done.10.source = bf16[128,1536]{1,0:T(8,128)(2,1)S(1)} collective-permute-done((bf16[128,1536]{1,0:T(8,128)(2,1)S(1)}, bf16[128,1536]{1,0:T(8,128)(2,1)S(1)}, u32[]{:S(2)}, u32[]{:S(2)}) %collective-permute-start.10) | collective-permute-done | bytes 393248 | tf_op jit(solution)/shard_map/ppermute | solution.py:439
  51.7 0.6 collective-permute-start.11
  52.3 0.1 collective-permute-start.14
  52.4 1.3 %term.1.refs_2_ = f32[256,1536]{1,0:T(8,128)S(1)} custom-call(bf16[8,32,1536]{2,1,0:T(8,128)(2,1)S(1)} %copy-done, bf16[64,1536]{1,0:T(8,128)(2,1)S(1)} %collective-permute-done.ends_mate, bf16[104,1536]{1,0:T(8,128)(2,1)S(1)} %collective-permute-done.2.across, bf16[80,1536]{1,0:T(8,128)(2,1)S(1)} %collective-permute-done.5.left.refs_6_, ...), custom_call_target="tpu_custom_call" | custom-call | flops 1048576 | bytes 65536 | tf_op jit(solution)/shard_map/term/pallas_call | solution.py:380
  53.8 4.2 %attend0.1.refs_13_ = f32[256,1536]{1,0:T(8,128)} custom-call(s32[1,1,2]{2,1,0:T(1,128)S(1)} %copy-done.4, s32[2,1,2]{2,1,0:T(1,128)S(1)} %copy-done.5, s32[2,1,2]{2,1,0:T(1,128)S(1)} %copy-done.6, bf16[256,1536]{1,0:T(8,128)(2,1)S(1)} %bitcast.8, bf16[256,1536]{1,0:T(8,128)(2,1)S(1)} %bitcast.10, bf16[256,1536]{1,0:T(8,128)(2,1)S(1)} %bitcast.6, ...), custom_call_target="tpu_custom_call" | custom-call | flops 1048576 | bytes 65536 | tf_op jit(solution)/shard_map/attend0/pallas_call | solution.py:462
  58.0 2.7 %attend1.1 = f32[256,1536]{1,0:T(8,128)} custom-call(s32[1,1,2]{2,1,0:T(1,128)S(1)} %copy-done.4, s32[2,1,2]{2,1,0:T(1,128)S(1)} %copy-done.5, s32[2,1,2]{2,1,0:T(1,128)S(1)} %copy-done.6, bf16[256,1536]{1,0:T(8,128)(2,1)S(1)} %bitcast.9, bf16[256,1536]{1,0:T(8,128)(2,1)S(1)} %bitcast.11, ...), custom_call_target="tpu_custom_call", output_to_operand_aliasing={{}: (19, {})} | custom-call | flops 1048576 | bytes 65536 | tf_op jit(solution)/shard_map/attend1/pallas_call | solution.py:462
  (29 shorter events, 0.2 us)
Async XLA Ops:
  0.0 3.5 %copy-start.4 = (s32[1,1,2]{2,1,0:T(1,128)S(1)}, s32[1,1,2]{2,1,0:T(1,128)}, u32[]{:S(2)}) copy-start(s32[1,1,2]{2,1,0:T(1,128)} %reads_ref.5) | copy-start | bytes 28
  1.6 1.6 %collective-permute-start = (bf16[64,1536]{1,0:T(8,128)(2,1)S(1)}, bf16[64,1536]{1,0:T(8,128)(2,1)S(1)}, u32[]{:S(2)}, u32[]{:S(2)}) collective-permute-start(bf16[64,1536]{1,0:T(8,128)(2,1)S(1)} %get-tuple-element.20), channel_id=1, source_target_pairs={{0,4},{4,0},{8,12},{12,8},{1,5},{5,1},{9,13},{13,9},{2,6},{6,2},{1... | collective-permute-start | bytes 589832 | tf_op jit(solution)/shard_map/ppermute | solution.py:372
  3.2 11.7 %collective-permute-start.1 = (bf16[512,1536]{1,0:T(8,128)(2,1)S(1)}, bf16[512,1536]{1,0:T(8,128)(2,1)S(1)}, u32[]{:S(2)}, u32[]{:S(2)}) collective-permute-start(bf16[512,1536]{1,0:T(8,128)(2,1)S(1)} %get-tuple-element.21.stale), channel_id=1, source_target_pairs={{0,4},{4,0},{8,12},{12,8},{1,5},{5,1},{9,13},{13,9},{2,6},{6,2},{1... | collective-permute-start | bytes 4718600 | tf_op jit(solution)/shard_map/ppermute | solution.py:372
  4.1 12.8 %copy-start = (bf16[8,32,1536]{2,1,0:T(8,128)(2,1)S(1)}, bf16[8,32,1536]{2,1,0:T(8,128)(2,1)}, u32[]{:S(2)}) copy-start(bf16[8,32,1536]{2,1,0:T(8,128)(2,1)} %cells.5) | copy-start | bytes 2359300
  4.1 10.8 %collective-permute-start.2 = (bf16[104,1536]{1,0:T(8,128)(2,1)S(1)}, bf16[104,1536]{1,0:T(8,128)(2,1)S(1)}, u32[]{:S(2)}, u32[]{:S(2)}) collective-permute-start(bf16[104,1536]{1,0:T(8,128)(2,1)S(1)} %offer.1), channel_id=1, source_target_pairs={{0,8},{4,12},{8,0},{12,4},{1,9},{5,13},{9,1},{13,5},{2,10},{6,14},... | collective-permute-start | bytes 958472 | tf_op jit(solution)/shard_map/ppermute | solution.py:421
  6.8 10.3 %collective-permute-start.8 = (bf16[64,1536]{1,0:T(8,128)(2,1)S(1)}, bf16[64,1536]{1,0:T(8,128)(2,1)S(1)}, u32[]{:S(2)}, u32[]{:S(2)}) collective-permute-start(bf16[64,1536]{1,0:T(8,128)(2,1)S(1)} %get-tuple-element.22.text), channel_id=1, source_target_pairs={{0,3},{1,0},{2,1},{3,2},{4,7},{5,4},{6,5},{7,6},{8,11},{9,8},{10,9... | collective-permute-start | bytes 589832 | tf_op jit(solution)/shard_map/ppermute | solution.py:410
  10.4 9.5 %collective-permute-start.7 = (bf16[64,1536]{1,0:T(8,128)(2,1)S(1)}, bf16[64,1536]{1,0:T(8,128)(2,1)S(1)}, u32[]{:S(2)}, u32[]{:S(2)}) collective-permute-start(bf16[64,1536]{1,0:T(8,128)(2,1)S(1)} %get-tuple-element.22.text), channel_id=1, source_target_pairs={{0,1},{1,2},{2,3},{3,0},{4,5},{5,6},{6,7},{7,4},{8,9},{9,10},{10,1... | collective-permute-start | bytes 589832 | tf_op jit(solution)/shard_map/ppermute | solution.py:410
  15.1 37.3 %copy-start.3 = (f32[3,3,1536]{2,1,0:T(4,128)S(1)}, f32[3,3,1536]{2,1,0:T(4,128)}, u32[]{:S(2)}) copy-start(f32[3,3,1536]{2,1,0:T(4,128)} %weights.1) | copy-start | bytes 165892
  15.1 38.6 %collective-permute-start.4 = (bf16[512,1024]{1,0:T(8,128)(2,1)S(1)}, bf16[512,1024]{1,0:T(8,128)(2,1)S(1)}, u32[]{:S(2)}, u32[]{:S(2)}) collective-permute-start(bf16[512,1024]{1,0:T(8,128)(2,1)S(1)} %get-tuple-element.24), channel_id=1, source_target_pairs={{0,8},{4,12},{8,0},{12,4},{1,9},{5,13},{9,1},{13,5},{2,10},{6,14},... | collective-permute-start | bytes 3145736 | tf_op jit(solution)/shard_map/ppermute | solution.py:426
  20.0 31.6 %collective-permute-start.9 = (bf16[256,1536]{1,0:T(8,128)(2,1)S(1)}, bf16[256,1536]{1,0:T(8,128)(2,1)S(1)}, u32[]{:S(2)}, u32[]{:S(2)}) collective-permute-start(bf16[256,1536]{1,0:T(8,128)(2,1)S(1)} %bundle.1.refs_3_), channel_id=1, source_target_pairs={{0,4},{4,0},{8,12},{12,8},{1,5},{5,1},{9,13},{13,9},{2,6},{6,2},{1... | collective-permute-start | bytes 2359304 | tf_op jit(solution)/shard_map/ppermute | solution.py:372
  20.1 10.7 %collective-permute-start.5 = (bf16[80,1536]{1,0:T(8,128)(2,1)S(1)}, bf16[80,1536]{1,0:T(8,128)(2,1)S(1)}, u32[]{:S(2)}, u32[]{:S(2)}) collective-permute-start(bf16[80,1536]{1,0:T(8,128)(2,1)S(1)} %get-tuple-element.26), channel_id=1, source_target_pairs={{0,1},{1,2},{2,3},{3,0},{4,5},{5,6},{6,7},{7,4},{8,9},{9,10},{10,1... | collective-permute-start | bytes 737288 | tf_op jit(solution)/shard_map/ppermute | solution.py:437
  21.8 13.9 %collective-permute-start.6 = (bf16[80,1536]{1,0:T(8,128)(2,1)S(1)}, bf16[80,1536]{1,0:T(8,128)(2,1)S(1)}, u32[]{:S(2)}, u32[]{:S(2)}) collective-permute-start(bf16[80,1536]{1,0:T(8,128)(2,1)S(1)} %get-tuple-element.27), channel_id=1, source_target_pairs={{0,3},{1,0},{2,1},{3,2},{4,7},{5,4},{6,5},{7,6},{8,11},{9,8},{10,9... | collective-permute-start | bytes 737288 | tf_op jit(solution)/shard_map/ppermute | solution.py:438
  24.0 27.7 %collective-permute-start.10 = (bf16[128,1536]{1,0:T(8,128)(2,1)S(1)}, bf16[128,1536]{1,0:T(8,128)(2,1)S(1)}, u32[]{:S(2)}, u32[]{:S(2)}) collective-permute-start(bf16[128,1536]{1,0:T(8,128)(2,1)S(1)} %get-tuple-element.28.refs_2_), channel_id=1, source_target_pairs={{0,2},{1,3},{2,0},{3,1},{4,6},{5,7},{6,4},{7,5},{8,10},{9,11},{10,... | collective-permute-start | bytes 1179656 | tf_op jit(solution)/shard_map/ppermute | solution.py:439
  30.7 27.3 %collective-permute-start.3 = (bf16[512,512]{1,0:T(8,128)(2,1)S(1)}, bf16[512,512]{1,0:T(8,128)(2,1)S(1)}, u32[]{:S(2)}, u32[]{:S(2)}) collective-permute-start(bf16[512,512]{1,0:T(8,128)(2,1)S(1)} %get-tuple-element.23), channel_id=1, source_target_pairs={{0,8},{4,12},{8,0},{12,4},{1,9},{5,13},{9,1},{13,5},{2,10},{6,14},... | collective-permute-start | bytes 1572872 | tf_op jit(solution)/shard_map/ppermute | solution.py:426
  35.7 16.6 %collective-permute-start.12 = (bf16[80,1536]{1,0:T(8,128)(2,1)S(1)}, bf16[80,1536]{1,0:T(8,128)(2,1)S(1)}, u32[]{:S(2)}, u32[]{:S(2)}) collective-permute-start(bf16[80,1536]{1,0:T(8,128)(2,1)S(1)} %collective-permute-done.5.left.refs_6_), channel_id=1, source_target_pairs={{0,4},{4,0},{8,12},{12,8},{1,5},{5,1},{9,13},{13,9},{2,6},{6,2},{1... | collective-permute-start | bytes 737288 | tf_op jit(solution)/shard_map/ppermute | solution.py:372
  51.6 2.1 %collective-permute-start.13 = (bf16[80,1536]{1,0:T(8,128)(2,1)S(1)}, bf16[80,1536]{1,0:T(8,128)(2,1)S(1)}, u32[]{:S(2)}, u32[]{:S(2)}) collective-permute-start(bf16[80,1536]{1,0:T(8,128)(2,1)S(1)} %collective-permute-done.6.right.refs_7_), channel_id=1, source_target_pairs={{0,4},{4,0},{8,12},{12,8},{1,5},{5,1},{9,13},{13,9},{2,6},{6,2},{1... | collective-permute-start | bytes 737288 | tf_op jit(solution)/shard_map/ppermute | solution.py:372
  51.7 2.0 %collective-permute-start.11 = (bf16[64,1536]{1,0:T(8,128)(2,1)S(1)}, bf16[64,1536]{1,0:T(8,128)(2,1)S(1)}, u32[]{:S(2)}, u32[]{:S(2)}) collective-permute-start(bf16[64,1536]{1,0:T(8,128)(2,1)S(1)} %get-tuple-element.30.refs_5_), channel_id=1, source_target_pairs={{0,4},{4,0},{8,12},{12,8},{1,5},{5,1},{9,13},{13,9},{2,6},{6,2},{1... | collective-permute-start | bytes 589832 | tf_op jit(solution)/shard_map/ppermute | solution.py:372
  52.2 1.5 %copy-start.1 = (bf16[8,32,1536]{2,1,0:T(8,128)(2,1)S(1)}, bf16[8,32,1536]{2,1,0:T(8,128)(2,1)}, u32[]{:S(2)}) copy-start(bf16[8,32,1536]{2,1,0:T(8,128)(2,1)} %param.11) | copy-start | bytes 2359300
  52.2 1.5 %copy-start.2 = (bf16[8,32,1536]{2,1,0:T(8,128)(2,1)S(1)}, bf16[8,32,1536]{2,1,0:T(8,128)(2,1)}, u32[]{:S(2)}) copy-start(bf16[8,32,1536]{2,1,0:T(8,128)(2,1)} %param.12) | copy-start | bytes 2359300
  52.2 1.5 %copy-start.5 = (s32[2,1,2]{2,1,0:T(1,128)S(1)}, s32[2,1,2]{2,1,0:T(1,128)}, u32[]{:S(2)}) copy-start(s32[2,1,2]{2,1,0:T(1,128)} %pattern_ref.3) | copy-start | bytes 52
  52.2 1.5 %copy-start.6 = (s32[2,1,2]{2,1,0:T(1,128)S(1)}, s32[2,1,2]{2,1,0:T(1,128)}, u32[]{:S(2)}) copy-start(s32[2,1,2]{2,1,0:T(1,128)} %text_ref.3) | copy-start | bytes 52
  52.3 1.5 %collective-permute-start.14 = (bf16[64,1536]{1,0:T(8,128)(2,1)S(1)}, bf16[64,1536]{1,0:T(8,128)(2,1)S(1)}, u32[]{:S(2)}, u32[]{:S(2)}) collective-permute-start(bf16[64,1536]{1,0:T(8,128)(2,1)S(1)} %get-tuple-element.31.refs_8_), channel_id=1, source_target_pairs={{0,4},{4,0},{8,12},{12,8},{1,5},{5,1},{9,13},{13,9},{2,6},{6,2},{1... | collective-permute-start | bytes 589832 | tf_op jit(solution)/shard_map/ppermute | solution.py:372

commit v10 on v9

--- a/solution.py
+++ b/solution.py
@@ -14,7 +14,7 @@
 PER_BLOCK = BLOCK_ROWS * BLOCK_COLS
 SCORE_SCALE = 1.0 / math.sqrt(HEAD_DIM)
 EXP2_SCALE = SCORE_SCALE * math.log2(math.e)
-CHUNK_HEADS = (8, 4)
+CHUNK_HEADS = (9, 3)
 GROUP = 8
 VMEM_LIMIT = 24 * 1024 * 1024
 
@@ -140,23 +140,23 @@
         copy.wait()
 
 
-def pack_kernel(k_hbm, v_hbm, cells, text_k, text_v, stale, ends, text, sems):
+def pack_kernel(k_hbm, v_hbm, cells, text_k, text_v, stale, beside, diagonal, text, sems):
     tokens, shard = k_hbm.shape[0], text_k.shape[0]
+    row = lax.axis_index("rows")
+    end = cells.shape[0] - 1
     copies = []
     for which, source in enumerate((text_k, text_v)):
         copies.append((source, text.at[pl.ds(which * shard, shard)]))
     for which, source in enumerate((k_hbm, v_hbm)):
         copies.append((source, stale.at[pl.ds(which * tokens, tokens)]))
-    for which, at in enumerate((0, cells.shape[0] - 1)):
-        copies.append((cells.at[at], ends.at[pl.ds(which * cells.shape[1], cells.shape[1])]))
+    copies.append((cells.at[jnp.where(row % 2 == 0, end, 0)], beside))
+    copies.append((cells.at[jnp.where(row < 2, end, 0)], diagonal))
     run_copies(copies, sems)
 
 
-def offer_kernel(reads_ref, text, ends_mate, out):
+def offer_kernel(reads_ref, text, out):
     both, width = text.shape
-    count = ends_mate.shape[0] // 2
-    row = lax.axis_index("rows")
-    partner = (row + 2) % 4
+    partner = (lax.axis_index("rows") + 2) % 4
 
     def flag(owner):
         found = 0
@@ -167,10 +167,7 @@
 
     flags = [flag(owner) for owner in (partner, partner + 1 - 2 * (partner % 2))]
     out[pl.ds(0, both), :] = text[...]
-    out[pl.ds(both, count), :] = jnp.where(
-        row % 2 == 0, ends_mate[pl.ds(count, count), :], ends_mate[pl.ds(0, count), :]
-    )
-    out[pl.ds(both + count, 8), :] = jnp.concatenate(flags, axis=1).astype(out.dtype)
+    out[pl.ds(both, 8), :] = jnp.concatenate(flags, axis=1).astype(out.dtype)
 
 
 def send_kernel(across, stale, passed, *outs):
@@ -197,33 +194,31 @@
     out = refs[-1]
     at = 0
     for ref in refs[:-1]:
-        out[pl.ds(at, ref.shape[0]), :] = ref[...]
-        at += ref.shape[0]
-
-
-def split_kernel(source, first, second):
+        count = ref.shape[0] - ref.shape[0] % 64
+        out[pl.ds(at, count), :] = ref[pl.ds(0, count), :]
+        at += count
+
+
+def choose_kernel(upper, lower, first, second):
+    upwards = lax.axis_index("cols") >= 2
     half = first.shape[0]
-    first[...] = source[pl.ds(0, half), :]
-    second[...] = source[pl.ds(half, half), :]
-
-
-def above_below(ends_mate, across, part):
-    count = ends_mate.shape[0] // 2
-    row = lax.axis_index("rows")
-    beside_first, beside_last = (ends_mate[pl.ds(at, count), part] for at in (0, count))
-    passed = across[pl.ds(across.shape[0] - 8 - count, count), part]
-    passed = jnp.where((row > 0) & (row < 3), passed, jnp.zeros_like(passed))
-    first_core = row % 2 == 0
+    for at, out in ((0, first), (half, second)):
+        rows = pl.ds(at, half)
+        out[...] = jnp.where(upwards, upper[rows, :], lower[rows, :])
+
+
+def above_below(beside, diagonal):
+    first_core = lax.axis_index("rows") % 2 == 0
     return (
-        jnp.where(first_core, passed, beside_last),
-        jnp.where(first_core, beside_first, passed),
-    )
-
-
-def join_kernel(text, across, cells, ends_mate, both, plus, minus):
+        jnp.where(first_core, diagonal, beside),
+        jnp.where(first_core, beside, diagonal),
+    )
+
+
+def join_kernel(text, across, cells, beside, diagonal, both, plus, minus):
     shard = text.shape[0] // 2
     rows_here, cols_here, width = cells.shape
-    above, below = above_below(ends_mate, across, slice(None))
+    above, below = above_below(beside[...], diagonal[...])
     rows = [above] + [cells[i] for i in range(rows_here)] + [below]
     rows = [row.astype(jnp.float32) for row in rows]
     spare = jnp.zeros((16 - len(rows), width), jnp.float32)
@@ -236,14 +231,14 @@
         target[pl.ds(2 * shard, 16), :] = edge.astype(target.dtype)
 
 
-def term_kernel(cells, ends_mate, across, left, right, weights, out):
+def term_kernel(cells, beside, diagonal, left, right, weights, out):
     rows_here, cols_here, width = cells.shape
     col = lax.axis_index("cols")
     edges = pl.ds(left.shape[0] - 16, 16)
     place = lax.broadcasted_iota(jnp.int32, (cols_here, HEAD_DIM), 0)
     for lane in range(width // HEAD_DIM):
         part = pl.ds(lane * HEAD_DIM, HEAD_DIM)
-        above, below = above_below(ends_mate, across, part)
+        above, below = above_below(beside[:, part], diagonal[:, part])
         lefts = left[edges, part].astype(jnp.float32)
         rights = right[edges, part].astype(jnp.float32)
         lefts = jnp.where(col > 0, lefts, 0.0)
@@ -273,11 +268,12 @@
 
 def attend_kernel(first_head, reads_ref, pattern_ref, text_ref, q, k, v, *refs):
     passed, arrived, term = refs[:3]
-    early, early_mate, late, late_mate = refs[3], refs[4], refs[5:9], refs[9:13]
+    both, both_mate, early, early_mate = refs[3:7]
+    late, late_mate = refs[7:11], refs[11:15]
     out = refs[-1]
     row, col = lax.axis_index("rows"), lax.axis_index("cols")
     across, core = row // 2, row % 2
-    shard = early.shape[0] // 8
+    shard = both.shape[0] // 4
     half = 2 * PER_BLOCK
     head_count = arrived.shape[1] // HEAD_DIM
 
@@ -294,16 +290,15 @@
                 rows = pl.ds((2 * at + which) * shard, shard)
                 return jnp.where(from_own, own[rows, part], other[rows, part])
 
-            near_at, side_at = ((2, 3), (0, None), (1, None), (None, None))[piece]
-            return jnp.where(
-                from_near,
-                pick(late[0], late_mate[0], 0)
-                if near_at is None
-                else pick(early, early_mate, near_at),
-                pick(late[piece], late_mate[piece], 0)
-                if side_at is None
-                else pick(early, early_mate, side_at),
-            )
+            if piece == 0:
+                near, side = pick(both, both_mate, 0), pick(both, both_mate, 1)
+            else:
+                side = pick(late[piece], late_mate[piece], 0)
+                if piece < 3:
+                    near = pick(early, early_mate, piece - 1)
+                else:
+                    near = pick(late[0], late_mate[0], 0)
+            return jnp.where(from_near, near, side)
 
         return [one(piece) for piece in range(4)]
 
@@ -395,33 +390,32 @@
         pltpu.with_memory_space_constraint(value, pltpu.HBM)
         for value in (flat(k_stale), flat(v_stale), v_fresh, text_k, text_v)
     ]
-    stale, ends, text = local(
+    stale, beside, diagonal, text = local(
         pack_kernel,
         "pack",
-        rows_of(2 * tokens, 2 * cols_here, 2 * shard),
+        rows_of(2 * tokens, cols_here, cols_here, 2 * shard),
         *in_place,
         specs=[in_hbm] * 5,
         scratch=[pltpu.SemaphoreType.DMA((6,))],
     )
     forward = [(i, (i + 1) % 4) for i in range(4)]
     backward = [(i, (i + 3) % 4) for i in range(4)]
-    opposite = [(i, (i + 2) % 4) for i in range(4)]
 
     near_parts = [lax.ppermute(text, "cols", p) for p in (forward, backward)]
-    ends_mate = to_mate(ends)
+    beside = to_mate(beside)
+    diagonal = lax.ppermute(diagonal, "rows", [(1, 2), (2, 1)])
     offer = local(
         offer_kernel,
         "offer",
-        rows_of(2 * shard + cols_here + 8),
+        rows_of(2 * shard + 8),
         reads,
         text,
-        ends_mate,
-        specs=[pl.BlockSpec(memory_space=pltpu.SMEM)] + [in_vmem] * 2,
+        specs=[pl.BlockSpec(memory_space=pltpu.SMEM), in_vmem],
     )
     across = lax.ppermute(offer, "rows", swap)
-    passed = to_mate(after(stale, ends_mate))
+    passed = to_mate(after(stale, beside))
     packed = local(
-        send_kernel, "send", chunks, across, stale, passed
+        send_kernel, "send", chunks, after(across, diagonal), stale, passed
     )
     far = [lax.ppermute(chunk, "rows", swap) for chunk in packed]
 
@@ -432,22 +426,28 @@
         text,
         after(across, packed[0]),
         v_fresh,
-        ends_mate,
+        beside,
+        diagonal,
     )
     left = lax.ppermute(plus, "cols", forward)
     right = lax.ppermute(minus, "cols", backward)
-    across_cols = lax.ppermute(both, "cols", opposite)
-    early = local(bundle_kernel, "bundle", rows_of(8 * shard), *near_parts, both)
-    early_mate = to_mate(early)
-    across_cols = after(across_cols, early_mate)
-    far_side = local(split_kernel, "split", rows_of(2 * shard, 2 * shard), across_cols)
+    early = local(bundle_kernel, "bundle", rows_of(4 * shard), *near_parts)
+    early_mate, both_mate = to_mate(early), to_mate(both)
+    near_parts[0] = after(near_parts[0], early_mate, both_mate)
+    upper, lower = (
+        local(bundle_kernel, "pair", rows_of(4 * shard), *pair)
+        for pair in ((near_parts[0], left), (near_parts[1], right))
+    )
+    upper = lax.ppermute(upper, "cols", [(1, 2), (2, 3)])
+    lower = lax.ppermute(lower, "cols", [(1, 0), (2, 1)])
+    far_side = local(choose_kernel, "choose", rows_of(2 * shard, 2 * shard), upper, lower)
     late = [far_side[0], left, right, far_side[1]]
     late_mate = [to_mate(part) for part in late]
     term = local(
         term_kernel,
         "term",
         jax.ShapeDtypeStruct((tokens, width), jnp.float32),
-        v_fresh, ends_mate, across, left, right, conv_w,
+        v_fresh, beside, diagonal, left, right, conv_w,
     )
 
     out = None
@@ -465,16 +465,16 @@
             grid_spec=pltpu.PrefetchScalarGridSpec(
                 num_scalar_prefetch=3,
                 grid=(1,),
-                in_specs=[in_vmem] * 16 + [in_hbm] * (out is not None),
+                in_specs=[in_vmem] * 18 + [in_hbm] * (out is not None),
                 out_specs=block,
             ),
-            input_output_aliases={19: 0} if out is not None else {},
+            input_output_aliases={21: 0} if out is not None else {},
             compiler_params=params,
             cost_estimate=cost,
             name=f"attend{chunk}",
         )(
             reads, pattern, text_blocks, flat(q_fresh), flat(k_fresh), flat(v_fresh),
-            passed, far[chunk], term, early, early_mate, *late, *late_mate,
+            passed, far[chunk], term, both, both_mate, early, early_mate, *late, *late_mate,
             *([out] if out is not None else []),
         )
         first_head += head_count

time: 60.9 us -> 58.1 us (0.954)
  the two profiles are of different devices: /device:TPU:0 before, /device:TPU:17 now
where the time goes in v10:
time: 58.1 us; the launch traced here: 57.9 us
  starting transfers between devices  25 us (43%)
  waiting for transfers between devices  22.1 us (38%)
  Pallas kernels  10.5 us (18%)
    ppermute x1, starting transfers between devices, body(): lower = lax.ppermute(lower, 'cols', [(1, 0), (2, 1)])  8.99 us
    ppermute x8, starting transfers between devices, to_mate(): return lax.ppermute(values, 'rows', mates)  6.87 us
    pallas_call x2, Pallas kernels, body(): pl.pallas_call(functools.partial(attend_kernel, first_head), out_shape=ja...  6.6 us
    ppermute x1, waiting for transfers between devices, body(): right = lax.ppermute(minus, 'cols', backward)  5.73 us
    ppermute x2, waiting for transfers between devices, body(): near_parts = [lax.ppermute(text, 'cols', p) for p in (forward, backward)]  5.72 us
    ppermute x1, waiting for transfers between devices, body(): lower = lax.ppermute(lower, 'cols', [(1, 0), (2, 1)])  4.34 us
    pallas_call x9, Pallas kernels, local(): pl.pallas_call(kernel, out_shape=shapes, in_specs=specs or [in_vmem] * le...  3.92 us
    ppermute x1, waiting for transfers between devices, body(): diagonal = lax.ppermute(diagonal, 'rows', [(1, 2), (2, 1)])  3.15 us
  transfers between devices with their start and end apart: 18, of which 7 were waited for; matrix products, arithmetic and copies ran while one was open for 0% of the time, Pallas kernels for 11%

profile of v10, /device:TPU:17, one launch (start us, length us, event | category | flops | bytes accessed | tf_op | source)
XLA Modules:
  0.0 57.9 jit_solution(6088181406521551354)
XLA Ops:
  0.0 1.6 %pack.1 = (bf16[512,1536]{1,0:T(8,128)(2,1)S(1)}, bf16[32,1536]{1,0:T(8,128)(2,1)S(1)}, bf16[32,1536]{1,0:T(8,128)(2,1)S(1)}, bf16[64,1536]{1,0:T(8,128)(2,1)S(1)}) custom-call(bf16[256,1536]{1,0:T(8,128)(2,1)} %bitcast.12, bf16[256,1536]{1,0:T(8,128)(2,1)} %bitcast.13, bf16[8,32,1536]{2,1,0:T(8,128)(2,1)} %cells.5, bf16[32,1536]{1,0:T(8,128)(2,1)} %text_k.1, ...), custom_call_target="tpu_custom_call" | custom-call | flops 1048576 | bytes 65536 | tf_op jit(solution)/shard_map/pack/pallas_call | solution.py:375
  1.6 0.7 %collective-permute-start = (bf16[32,1536]{1,0:T(8,128)(2,1)S(1)}, bf16[32,1536]{1,0:T(8,128)(2,1)S(1)}, u32[]{:S(2)}, u32[]{:S(2)}) collective-permute-start(bf16[32,1536]{1,0:T(8,128)(2,1)S(1)} %get-tuple-element.22), channel_id=1, source_target_pairs={{0,4},{4,0},{8,12},{12,8},{1,5},{5,1},{9,13},{13,9},{2,6},{6,2},{1... | collective-permute-start | bytes 294920 | tf_op jit(solution)/shard_map/ppermute | solution.py:367
  2.3 0.9 %collective-permute-done.beside = bf16[32,1536]{1,0:T(8,128)(2,1)S(1)} collective-permute-done((bf16[32,1536]{1,0:T(8,128)(2,1)S(1)}, bf16[32,1536]{1,0:T(8,128)(2,1)S(1)}, u32[]{:S(2)}, u32[]{:S(2)}) %collective-permute-start) | collective-permute-done | bytes 98336 | tf_op jit(solution)/shard_map/ppermute | solution.py:367
  3.3 0.4 collective-permute-start.1
  3.6 0.6 offer.1
  4.2 1.3 %collective-permute-start.2 = (bf16[72,1536]{1,0:T(8,128)(2,1)S(1)}, bf16[72,1536]{1,0:T(8,128)(2,1)S(1)}, u32[]{:S(2)}, u32[]{:S(2)}) collective-permute-start(bf16[72,1536]{1,0:T(8,128)(2,1)S(1)} %offer.1), channel_id=1, source_target_pairs={{0,8},{4,12},{8,0},{12,4},{1,9},{5,13},{9,1},{13,5},{2,10},{6,14},... | collective-permute-start | bytes 663560 | tf_op jit(solution)/shard_map/ppermute | solution.py:415
  5.5 2.6 %collective-permute-start.3 = (bf16[32,1536]{1,0:T(8,128)(2,1)S(1)}, bf16[32,1536]{1,0:T(8,128)(2,1)S(1)}, u32[]{:S(2)}, u32[]{:S(2)}) collective-permute-start(bf16[32,1536]{1,0:T(8,128)(2,1)S(1)} %get-tuple-element.25), channel_id=1, source_target_pairs={{4,8},{8,4},{5,9},{9,5},{6,10},{10,6},{7,11},{11,7},{20,24},{24,20... | collective-permute-start | bytes 294920 | tf_op jit(solution)/shard_map/ppermute | solution.py:406
  8.3 1.3 %collective-permute-start.9 = (bf16[64,1536]{1,0:T(8,128)(2,1)S(1)}, bf16[64,1536]{1,0:T(8,128)(2,1)S(1)}, u32[]{:S(2)}, u32[]{:S(2)}) collective-permute-start(bf16[64,1536]{1,0:T(8,128)(2,1)S(1)} %get-tuple-element.24.text), channel_id=1, source_target_pairs={{0,1},{1,2},{2,3},{3,0},{4,5},{5,6},{6,7},{7,4},{8,9},{9,10},{10,1... | collective-permute-start | bytes 589832 | tf_op jit(solution)/shard_map/ppermute | solution.py:404
  9.6 3.1 %collective-permute-done.3.diagonal = bf16[32,1536]{1,0:T(8,128)(2,1)S(1)} collective-permute-done((bf16[32,1536]{1,0:T(8,128)(2,1)S(1)}, bf16[32,1536]{1,0:T(8,128)(2,1)S(1)}, u32[]{:S(2)}, u32[]{:S(2)}) %collective-permute-start.3) | collective-permute-done | bytes 98336 | tf_op jit(solution)/shard_map/ppermute | solution.py:406
  13.1 1.8 %collective-permute-done.10.refs_1_.refs_0_ = bf16[64,1536]{1,0:T(8,128)(2,1)S(1)} collective-permute-done((bf16[64,1536]{1,0:T(8,128)(2,1)S(1)}, bf16[64,1536]{1,0:T(8,128)(2,1)S(1)}, u32[]{:S(2)}, u32[]{:S(2)}) %collective-permute-start.10) | collective-permute-done | bytes 196640 | tf_op jit(solution)/shard_map/ppermute | solution.py:404
  14.9 3.9 %collective-permute-done.9.refs_0_ = bf16[64,1536]{1,0:T(8,128)(2,1)S(1)} collective-permute-done((bf16[64,1536]{1,0:T(8,128)(2,1)S(1)}, bf16[64,1536]{1,0:T(8,128)(2,1)S(1)}, u32[]{:S(2)}, u32[]{:S(2)}) %collective-permute-start.9) | collective-permute-done | bytes 196640 | tf_op jit(solution)/shard_map/ppermute | solution.py:404
  19.1 0.5 collective-permute-start.8
  19.6 1.8 %collective-permute-start.7 = (bf16[80,1536]{1,0:T(8,128)(2,1)S(1)}, bf16[80,1536]{1,0:T(8,128)(2,1)S(1)}, u32[]{:S(2)}, u32[]{:S(2)}) collective-permute-start(bf16[80,1536]{1,0:T(8,128)(2,1)S(1)} %get-tuple-element.31), channel_id=1, source_target_pairs={{0,3},{1,0},{2,1},{3,2},{4,7},{5,4},{6,5},{7,6},{8,11},{9,8},{10,9... | collective-permute-start | bytes 737288 | tf_op jit(solution)/shard_map/ppermute | solution.py:433
  21.4 5.7 %collective-permute-done.7.right.refs_1_.refs_9_ = bf16[80,1536]{1,0:T(8,128)(2,1)S(1)} collective-permute-done((bf16[80,1536]{1,0:T(8,128)(2,1)S(1)}, bf16[80,1536]{1,0:T(8,128)(2,1)S(1)}, u32[]{:S(2)}, u32[]{:S(2)}) %collective-permute-start.7) | collective-permute-done | bytes 245792 | tf_op jit(solution)/shard_map/ppermute | solution.py:433
  27.2 9.0 %collective-permute-start.13 = (bf16[128,1536]{1,0:T(8,128)(2,1)S(1)}, bf16[128,1536]{1,0:T(8,128)(2,1)S(1)}, u32[]{:S(2)}, u32[]{:S(2)}) collective-permute-start(bf16[128,1536]{1,0:T(8,128)(2,1)S(1)} %pair.3), channel_id=1, source_target_pairs={{1,0},{2,1},{5,4},{6,5},{9,8},{10,9},{13,12},{14,13},{17,16},{18,1... | collective-permute-start | bytes 1179656 | tf_op jit(solution)/shard_map/ppermute | solution.py:442
  36.2 1.9 %collective-permute-start.12 = (bf16[128,1536]{1,0:T(8,128)(2,1)S(1)}, bf16[128,1536]{1,0:T(8,128)(2,1)S(1)}, u32[]{:S(2)}, u32[]{:S(2)}) collective-permute-start(bf16[128,1536]{1,0:T(8,128)(2,1)S(1)} %pair.2), channel_id=1, source_target_pairs={{1,2},{2,3},{5,6},{6,7},{9,10},{10,11},{13,14},{14,15},{17,18},{18... | collective-permute-start | bytes 1179656 | tf_op jit(solution)/shard_map/ppermute | solution.py:441
  38.2 1.2 %collective-permute-start.15 = (bf16[80,1536]{1,0:T(8,128)(2,1)S(1)}, bf16[80,1536]{1,0:T(8,128)(2,1)S(1)}, u32[]{:S(2)}, u32[]{:S(2)}) collective-permute-start(bf16[80,1536]{1,0:T(8,128)(2,1)S(1)} %collective-permute-done.6.left.refs_1_.refs_8_), channel_id=1, source_target_pairs={{0,4},{4,0},{8,12},{12,8},{1,5},{5,1},{9,13},{13,9},{2,6},{6,2},{1... | collective-permute-start | bytes 737288 | tf_op jit(solution)/shard_map/ppermute | solution.py:367
  39.4 4.3 %collective-permute-done.13.lower = bf16[128,1536]{1,0:T(8,128)(2,1)S(1)} collective-permute-done((bf16[128,1536]{1,0:T(8,128)(2,1)S(1)}, bf16[128,1536]{1,0:T(8,128)(2,1)S(1)}, u32[]{:S(2)}, u32[]{:S(2)}) %collective-permute-start.13) | collective-permute-done | bytes 393248 | tf_op jit(solution)/shard_map/ppermute | solution.py:442
  43.7 1.7 %collective-permute-start.16 = (bf16[80,1536]{1,0:T(8,128)(2,1)S(1)}, bf16[80,1536]{1,0:T(8,128)(2,1)S(1)}, u32[]{:S(2)}, u32[]{:S(2)}) collective-permute-start(bf16[80,1536]{1,0:T(8,128)(2,1)S(1)} %collective-permute-done.7.right.refs_1_.refs_9_), channel_id=1, source_target_pairs={{0,4},{4,0},{8,12},{12,8},{1,5},{5,1},{9,13},{13,9},{2,6},{6,2},{1... | collective-permute-start | bytes 737288 | tf_op jit(solution)/shard_map/ppermute | solution.py:367
  45.5 2.2 %collective-permute-done.12.upper = bf16[128,1536]{1,0:T(8,128)(2,1)S(1)} collective-permute-done((bf16[128,1536]{1,0:T(8,128)(2,1)S(1)}, bf16[128,1536]{1,0:T(8,128)(2,1)S(1)}, u32[]{:S(2)}, u32[]{:S(2)}) %collective-permute-start.12) | collective-permute-done | bytes 393248 | tf_op jit(solution)/shard_map/ppermute | solution.py:441
  47.7 2.1 %collective-permute-start.14 = (bf16[64,1536]{1,0:T(8,128)(2,1)S(1)}, bf16[64,1536]{1,0:T(8,128)(2,1)S(1)}, u32[]{:S(2)}, u32[]{:S(2)}) collective-permute-start(bf16[64,1536]{1,0:T(8,128)(2,1)S(1)} %get-tuple-element.34.refs_7_), channel_id=1, source_target_pairs={{0,4},{4,0},{8,12},{12,8},{1,5},{5,1},{9,13},{13,9},{2,6},{6,2},{1... | collective-permute-start | bytes 589832 | tf_op jit(solution)/shard_map/ppermute | solution.py:367
  49.9 1.3 %term.1.refs_2_ = f32[256,1536]{1,0:T(8,128)S(1)} custom-call(bf16[8,32,1536]{2,1,0:T(8,128)(2,1)S(1)} %copy-done, bf16[32,1536]{1,0:T(8,128)(2,1)S(1)} %collective-permute-done.beside, bf16[32,1536]{1,0:T(8,128)(2,1)S(1)} %collective-permute-done.3.diagonal, bf16[80,1536]{1,0:T(8,128)(2,1)S(1)} %collective-permute-done.6.left.refs_1_.refs_8_, ...), custom_call_target="tpu_custom_call" | custom-call | flops 1048576 | bytes 65536 | tf_op jit(solution)/shard_map/term/pallas_call | solution.py:375
  51.3 4.3 %attend0.1.refs_15_ = f32[256,1536]{1,0:T(8,128)} custom-call(s32[1,1,2]{2,1,0:T(1,128)S(1)} %copy-done.4, s32[2,1,2]{2,1,0:T(1,128)S(1)} %copy-done.5, s32[2,1,2]{2,1,0:T(1,128)S(1)} %copy-done.6, bf16[256,1536]{1,0:T(8,128)(2,1)S(1)} %bitcast.8, bf16[256,1536]{1,0:T(8,128)(2,1)S(1)} %bitcast.10, bf16[256,1536]{1,0:T(8,128)(2,1)S(1)} %bitcast.6, ...), custom_call_target="tpu_custom_call" | custom-call | flops 1048576 | bytes 65536 | tf_op jit(solution)/shard_map/attend0/pallas_call | solution.py:462
  55.6 2.3 %attend1.1 = f32[256,1536]{1,0:T(8,128)} custom-call(s32[1,1,2]{2,1,0:T(1,128)S(1)} %copy-done.4, s32[2,1,2]{2,1,0:T(1,128)S(1)} %copy-done.5, s32[2,1,2]{2,1,0:T(1,128)S(1)} %copy-done.6, bf16[256,1536]{1,0:T(8,128)(2,1)S(1)} %bitcast.9, bf16[256,1536]{1,0:T(8,128)(2,1)S(1)} %bitcast.11, ...), custom_call_target="tpu_custom_call", output_to_operand_aliasing={{}: (21, {})} | custom-call | flops 1048576 | bytes 65536 | tf_op jit(solution)/shard_map/attend1/pallas_call | solution.py:462
  (37 shorter events, 1.1 us)
Async XLA Ops:
  0.0 3.6 %copy-start.4 = (s32[1,1,2]{2,1,0:T(1,128)S(1)}, s32[1,1,2]{2,1,0:T(1,128)}, u32[]{:S(2)}) copy-start(s32[1,1,2]{2,1,0:T(1,128)} %reads_ref.5) | copy-start | bytes 28
  1.6 1.7 %collective-permute-start = (bf16[32,1536]{1,0:T(8,128)(2,1)S(1)}, bf16[32,1536]{1,0:T(8,128)(2,1)S(1)}, u32[]{:S(2)}, u32[]{:S(2)}) collective-permute-start(bf16[32,1536]{1,0:T(8,128)(2,1)S(1)} %get-tuple-element.22), channel_id=1, source_target_pairs={{0,4},{4,0},{8,12},{12,8},{1,5},{5,1},{9,13},{13,9},{2,6},{6,2},{1... | collective-permute-start | bytes 294920 | tf_op jit(solution)/shard_map/ppermute | solution.py:367
  3.3 9.5 %collective-permute-start.1 = (bf16[512,1536]{1,0:T(8,128)(2,1)S(1)}, bf16[512,1536]{1,0:T(8,128)(2,1)S(1)}, u32[]{:S(2)}, u32[]{:S(2)}) collective-permute-start(bf16[512,1536]{1,0:T(8,128)(2,1)S(1)} %get-tuple-element.23.stale), channel_id=1, source_target_pairs={{0,4},{4,0},{8,12},{12,8},{1,5},{5,1},{9,13},{13,9},{2,6},{6,2},{1... | collective-permute-start | bytes 4718600 | tf_op jit(solution)/shard_map/ppermute | solution.py:367
  4.2 8.6 %collective-permute-start.2 = (bf16[72,1536]{1,0:T(8,128)(2,1)S(1)}, bf16[72,1536]{1,0:T(8,128)(2,1)S(1)}, u32[]{:S(2)}, u32[]{:S(2)}) collective-permute-start(bf16[72,1536]{1,0:T(8,128)(2,1)S(1)} %offer.1), channel_id=1, source_target_pairs={{0,8},{4,12},{8,0},{12,4},{1,9},{5,13},{9,1},{13,5},{2,10},{6,14},... | collective-permute-start | bytes 663560 | tf_op jit(solution)/shard_map/ppermute | solution.py:415
  5.5 13.5 %copy-start = (bf16[8,32,1536]{2,1,0:T(8,128)(2,1)S(1)}, bf16[8,32,1536]{2,1,0:T(8,128)(2,1)}, u32[]{:S(2)}) copy-start(bf16[8,32,1536]{2,1,0:T(8,128)(2,1)} %cells.5) | copy-start | bytes 2359300
  5.5 7.3 %collective-permute-start.3 = (bf16[32,1536]{1,0:T(8,128)(2,1)S(1)}, bf16[32,1536]{1,0:T(8,128)(2,1)S(1)}, u32[]{:S(2)}, u32[]{:S(2)}) collective-permute-start(bf16[32,1536]{1,0:T(8,128)(2,1)S(1)} %get-tuple-element.25), channel_id=1, source_target_pairs={{4,8},{8,4},{5,9},{9,5},{6,10},{10,6},{7,11},{11,7},{20,24},{24,20... | collective-permute-start | bytes 294920 | tf_op jit(solution)/shard_map/ppermute | solution.py:406
  8.1 6.8 %collective-permute-start.10 = (bf16[64,1536]{1,0:T(8,128)(2,1)S(1)}, bf16[64,1536]{1,0:T(8,128)(2,1)S(1)}, u32[]{:S(2)}, u32[]{:S(2)}) collective-permute-start(bf16[64,1536]{1,0:T(8,128)(2,1)S(1)} %get-tuple-element.24.text), channel_id=1, source_target_pairs={{0,3},{1,0},{2,1},{3,2},{4,7},{5,4},{6,5},{7,6},{8,11},{9,8},{10,9... | collective-permute-start | bytes 589832 | tf_op jit(solution)/shard_map/ppermute | solution.py:404
  8.3 10.5 %collective-permute-start.9 = (bf16[64,1536]{1,0:T(8,128)(2,1)S(1)}, bf16[64,1536]{1,0:T(8,128)(2,1)S(1)}, u32[]{:S(2)}, u32[]{:S(2)}) collective-permute-start(bf16[64,1536]{1,0:T(8,128)(2,1)S(1)} %get-tuple-element.24.text), channel_id=1, source_target_pairs={{0,1},{1,2},{2,3},{3,0},{4,5},{5,6},{6,7},{7,4},{8,9},{9,10},{10,1... | collective-permute-start | bytes 589832 | tf_op jit(solution)/shard_map/ppermute | solution.py:404
  13.0 38.3 %collective-permute-start.5 = (bf16[512,1152]{1,0:T(8,128)(2,1)S(1)}, bf16[512,1152]{1,0:T(8,128)(2,1)S(1)}, u32[]{:S(2)}, u32[]{:S(2)}) collective-permute-start(bf16[512,1152]{1,0:T(8,128)(2,1)S(1)} %get-tuple-element.28), channel_id=1, source_target_pairs={{0,8},{4,12},{8,0},{12,4},{1,9},{5,13},{9,1},{13,5},{2,10},{6,14},... | collective-permute-start | bytes 3538952 | tf_op jit(solution)/shard_map/ppermute | solution.py:420
  18.8 17.3 %collective-permute-start.11 = (bf16[128,1536]{1,0:T(8,128)(2,1)S(1)}, bf16[128,1536]{1,0:T(8,128)(2,1)S(1)}, u32[]{:S(2)}, u32[]{:S(2)}) collective-permute-start(bf16[128,1536]{1,0:T(8,128)(2,1)S(1)} %bundle.1.refs_5_), channel_id=1, source_target_pairs={{0,4},{4,0},{8,12},{12,8},{1,5},{5,1},{9,13},{13,9},{2,6},{6,2},{1... | collective-permute-start | bytes 1179656 | tf_op jit(solution)/shard_map/ppermute | solution.py:367
  19.1 30.9 %copy-start.3 = (f32[3,3,1536]{2,1,0:T(4,128)S(1)}, f32[3,3,1536]{2,1,0:T(4,128)}, u32[]{:S(2)}) copy-start(f32[3,3,1536]{2,1,0:T(4,128)} %weights.1) | copy-start | bytes 165892
  19.1 17.1 %collective-permute-start.8 = (bf16[128,1536]{1,0:T(8,128)(2,1)S(1)}, bf16[128,1536]{1,0:T(8,128)(2,1)S(1)}, u32[]{:S(2)}, u32[]{:S(2)}) collective-permute-start(bf16[128,1536]{1,0:T(8,128)(2,1)S(1)} %get-tuple-element.32.refs_3_), channel_id=1, source_target_pairs={{0,4},{4,0},{8,12},{12,8},{1,5},{5,1},{9,13},{13,9},{2,6},{6,2},{1... | collective-permute-start | bytes 1179656 | tf_op jit(solution)/shard_map/ppermute | solution.py:367
  19.6 7.5 %collective-permute-start.7 = (bf16[80,1536]{1,0:T(8,128)(2,1)S(1)}, bf16[80,1536]{1,0:T(8,128)(2,1)S(1)}, u32[]{:S(2)}, u32[]{:S(2)}) collective-permute-start(bf16[80,1536]{1,0:T(8,128)(2,1)S(1)} %get-tuple-element.31), channel_id=1, source_target_pairs={{0,3},{1,0},{2,1},{3,2},{4,7},{5,4},{6,5},{7,6},{8,11},{9,8},{10,9... | collective-permute-start | bytes 737288 | tf_op jit(solution)/shard_map/ppermute | solution.py:433
  21.4 14.8 %collective-permute-start.6 = (bf16[80,1536]{1,0:T(8,128)(2,1)S(1)}, bf16[80,1536]{1,0:T(8,128)(2,1)S(1)}, u32[]{:S(2)}, u32[]{:S(2)}) collective-permute-start(bf16[80,1536]{1,0:T(8,128)(2,1)S(1)} %get-tuple-element.30), channel_id=1, source_target_pairs={{0,1},{1,2},{2,3},{3,0},{4,5},{5,6},{6,7},{7,4},{8,9},{9,10},{10,1... | collective-permute-start | bytes 737288 | tf_op jit(solution)/shard_map/ppermute | solution.py:432
  27.2 16.5 %collective-permute-start.13 = (bf16[128,1536]{1,0:T(8,128)(2,1)S(1)}, bf16[128,1536]{1,0:T(8,128)(2,1)S(1)}, u32[]{:S(2)}, u32[]{:S(2)}) collective-permute-start(bf16[128,1536]{1,0:T(8,128)(2,1)S(1)} %pair.3), channel_id=1, source_target_pairs={{1,0},{2,1},{5,4},{6,5},{9,8},{10,9},{13,12},{14,13},{17,16},{18,1... | collective-permute-start | bytes 1179656 | tf_op jit(solution)/shard_map/ppermute | solution.py:442
  36.2 11.4 %collective-permute-start.12 = (bf16[128,1536]{1,0:T(8,128)(2,1)S(1)}, bf16[128,1536]{1,0:T(8,128)(2,1)S(1)}, u32[]{:S(2)}, u32[]{:S(2)}) collective-permute-start(bf16[128,1536]{1,0:T(8,128)(2,1)S(1)} %pair.2), channel_id=1, source_target_pairs={{1,2},{2,3},{5,6},{6,7},{9,10},{10,11},{13,14},{14,15},{17,18},{18... | collective-permute-start | bytes 1179656 | tf_op jit(solution)/shard_map/ppermute | solution.py:441
  38.2 11.7 %collective-permute-start.15 = (bf16[80,1536]{1,0:T(8,128)(2,1)S(1)}, bf16[80,1536]{1,0:T(8,128)(2,1)S(1)}, u32[]{:S(2)}, u32[]{:S(2)}) collective-permute-start(bf16[80,1536]{1,0:T(8,128)(2,1)S(1)} %collective-permute-done.6.left.refs_1_.refs_8_), channel_id=1, source_target_pairs={{0,4},{4,0},{8,12},{12,8},{1,5},{5,1},{9,13},{13,9},{2,6},{6,2},{1... | collective-permute-start | bytes 737288 | tf_op jit(solution)/shard_map/ppermute | solution.py:367
  39.4 16.3 %collective-permute-start.4 = (bf16[512,384]{1,0:T(8,128)(2,1)S(1)}, bf16[512,384]{1,0:T(8,128)(2,1)S(1)}, u32[]{:S(2)}, u32[]{:S(2)}) collective-permute-start(bf16[512,384]{1,0:T(8,128)(2,1)S(1)} %get-tuple-element.27), channel_id=1, source_target_pairs={{0,8},{4,12},{8,0},{12,4},{1,9},{5,13},{9,1},{13,5},{2,10},{6,14},... | collective-permute-start | bytes 1179656 | tf_op jit(solution)/shard_map/ppermute | solution.py:420
  43.7 7.5 %collective-permute-start.16 = (bf16[80,1536]{1,0:T(8,128)(2,1)S(1)}, bf16[80,1536]{1,0:T(8,128)(2,1)S(1)}, u32[]{:S(2)}, u32[]{:S(2)}) collective-permute-start(bf16[80,1536]{1,0:T(8,128)(2,1)S(1)} %collective-permute-done.7.right.refs_1_.refs_9_), channel_id=1, source_target_pairs={{0,4},{4,0},{8,12},{12,8},{1,5},{5,1},{9,13},{13,9},{2,6},{6,2},{1... | collective-permute-start | bytes 737288 | tf_op jit(solution)/shard_map/ppermute | solution.py:367
  47.7 3.6 %copy-start.1 = (bf16[8,32,1536]{2,1,0:T(8,128)(2,1)S(1)}, bf16[8,32,1536]{2,1,0:T(8,128)(2,1)}, u32[]{:S(2)}) copy-start(bf16[8,32,1536]{2,1,0:T(8,128)(2,1)} %param.11) | copy-start | bytes 2359300
  47.7 3.6 %copy-start.2 = (bf16[8,32,1536]{2,1,0:T(8,128)(2,1)S(1)}, bf16[8,32,1536]{2,1,0:T(8,128)(2,1)}, u32[]{:S(2)}) copy-start(bf16[8,32,1536]{2,1,0:T(8,128)(2,1)} %param.12) | copy-start | bytes 2359300
  47.7 3.6 %copy-start.5 = (s32[2,1,2]{2,1,0:T(1,128)S(1)}, s32[2,1,2]{2,1,0:T(1,128)}, u32[]{:S(2)}) copy-start(s32[2,1,2]{2,1,0:T(1,128)} %pattern_ref.3) | copy-start | bytes 52
  47.7 3.5 %collective-permute-start.14 = (bf16[64,1536]{1,0:T(8,128)(2,1)S(1)}, bf16[64,1536]{1,0:T(8,128)(2,1)S(1)}, u32[]{:S(2)}, u32[]{:S(2)}) collective-permute-start(bf16[64,1536]{1,0:T(8,128)(2,1)S(1)} %get-tuple-element.34.refs_7_), channel_id=1, source_target_pairs={{0,4},{4,0},{8,12},{12,8},{1,5},{5,1},{9,13},{13,9},{2,6},{6,2},{1... | collective-permute-start | bytes 589832 | tf_op jit(solution)/shard_map/ppermute | solution.py:367
  49.8 1.4 %collective-permute-start.17 = (bf16[64,1536]{1,0:T(8,128)(2,1)S(1)}, bf16[64,1536]{1,0:T(8,128)(2,1)S(1)}, u32[]{:S(2)}, u32[]{:S(2)}) collective-permute-start(bf16[64,1536]{1,0:T(8,128)(2,1)S(1)} %get-tuple-element.35.refs_10_), channel_id=1, source_target_pairs={{0,4},{4,0},{8,12},{12,8},{1,5},{5,1},{9,13},{13,9},{2,6},{6,2},{1... | collective-permute-start | bytes 589832 | tf_op jit(solution)/shard_map/ppermute | solution.py:367
  (1 other events, 3.6 us)

commit v11 on v10

--- a/solution.py
+++ b/solution.py
@@ -140,23 +140,11 @@
         copy.wait()
 
 
-def pack_kernel(k_hbm, v_hbm, cells, text_k, text_v, stale, beside, diagonal, text, sems):
-    tokens, shard = k_hbm.shape[0], text_k.shape[0]
+def pack_kernel(reads_ref, cells, text_k, text_v, offer, beside, diagonal, text, sems):
+    shard, width = text_k.shape
     row = lax.axis_index("rows")
     end = cells.shape[0] - 1
-    copies = []
-    for which, source in enumerate((text_k, text_v)):
-        copies.append((source, text.at[pl.ds(which * shard, shard)]))
-    for which, source in enumerate((k_hbm, v_hbm)):
-        copies.append((source, stale.at[pl.ds(which * tokens, tokens)]))
-    copies.append((cells.at[jnp.where(row % 2 == 0, end, 0)], beside))
-    copies.append((cells.at[jnp.where(row < 2, end, 0)], diagonal))
-    run_copies(copies, sems)
-
-
-def offer_kernel(reads_ref, text, out):
-    both, width = text.shape
-    partner = (lax.axis_index("rows") + 2) % 4
+    partner = (row + 2) % 4
 
     def flag(owner):
         found = 0
@@ -165,9 +153,27 @@
             found = jnp.where(entry // 2 == owner, entry % 2, found)
         return jnp.full((8, width // 2), found.astype(jnp.float32), jnp.float32)
 
+    copies = []
+    for which, source in enumerate((text_k, text_v)):
+        for target in (text, offer):
+            copies.append((source, target.at[pl.ds(which * shard, shard)]))
+    copies.append((cells.at[jnp.where(row % 2 == 0, end, 0)], beside))
+    copies.append((cells.at[jnp.where(row < 2, end, 0)], diagonal))
     flags = [flag(owner) for owner in (partner, partner + 1 - 2 * (partner % 2))]
-    out[pl.ds(0, both), :] = text[...]
-    out[pl.ds(both, 8), :] = jnp.concatenate(flags, axis=1).astype(out.dtype)
+    offer[pl.ds(2 * shard, 8), :] = jnp.concatenate(flags, axis=1).astype(offer.dtype)
+    run_copies(copies, sems)
+
+
+def fetch_kernel(k_hbm, v_hbm, text, stale, sems):
+    del text
+    tokens = k_hbm.shape[0]
+    run_copies(
+        [
+            (source, stale.at[pl.ds(which * tokens, tokens)])
+            for which, source in enumerate((k_hbm, v_hbm))
+        ],
+        sems,
+    )
 
 
 def send_kernel(across, stale, passed, *outs):
@@ -266,41 +272,85 @@
             out[pl.ds(row * cols_here, cols_here), part] = total
 
 
-def attend_kernel(first_head, reads_ref, pattern_ref, text_ref, q, k, v, *refs):
-    passed, arrived, term = refs[:3]
-    both, both_mate, early, early_mate = refs[3:7]
-    late, late_mate = refs[7:11], refs[11:15]
+def grouped(jobs):
+    size = -(-len(jobs) // -(-len(jobs) // GROUP))
+    return [jobs[at : at + size] for at in range(0, len(jobs), size)]
+
+
+def lanes_of(head):
+    return pl.ds(head * HEAD_DIM, HEAD_DIM)
+
+
+def rows_at(block):
+    return pl.ds(block * PER_BLOCK, PER_BLOCK)
+
+
+def text_choice(chosen):
+    row = lax.axis_index("rows")
+    return chosen % 2 == row % 2, chosen // 2 == row // 2
+
+
+def pick(from_own, own, other, shard, at, part):
+    rows = pl.ds(at * shard, shard)
+    return jnp.where(from_own, own[rows, part], other[rows, part])
+
+
+def early_kernel(
+    text_ref, q, k, v, both, both_mate, early, early_mate, left, left_mate, right, right_mate,
+    sums, stats,
+):
+    shard = both.shape[0] // 4
+    heads = q.shape[1] // HEAD_DIM
+    lane = lax.broadcasted_iota(jnp.int32, (PER_BLOCK, HEAD_DIM), 1)
+
+    def gathered(block, head, which):
+        part = lanes_of(head)
+        parts = [(k, v)[which][rows_at(block), part]]
+        for turn in range(2):
+            from_own, from_near = text_choice(text_ref[block, 0, turn])
+            for near, side in (
+                ((both, both_mate, which), (both, both_mate, 2 + which)),
+                ((early, early_mate, which), (left, left_mate, which)),
+                ((early, early_mate, 2 + which), (right, right_mate, which)),
+            ):
+                parts.append(
+                    jnp.where(
+                        from_near,
+                        pick(from_own, near[0], near[1], shard, near[2], part),
+                        pick(from_own, side[0], side[1], shard, side[2], part),
+                    )
+                )
+        return jnp.concatenate(parts, axis=0)
+
+    kept = [jnp.zeros((PER_BLOCK, HEAD_DIM), jnp.float32) for _ in range(2)]
+    for group in grouped([(block, head) for head in range(heads) for block in range(2)]):
+        scores = [
+            head_scores(q[rows_at(block), lanes_of(head)], gathered(block, head, 0))
+            for block, head in group
+        ]
+        peaks = [jnp.max(s, axis=1, keepdims=True) * EXP2_SCALE for s in scores]
+        weights = [
+            jnp.exp2(s * EXP2_SCALE - peak).astype(jnp.bfloat16) for s, peak in zip(scores, peaks)
+        ]
+        totals = [jnp.sum(w.astype(jnp.float32), axis=1, keepdims=True) for w in weights]
+        for w, peak, total, (block, head) in zip(weights, peaks, totals, group):
+            sums[rows_at(block), lanes_of(head)] = jnp.dot(
+                w, gathered(block, head, 1), preferred_element_type=jnp.float32
+            )
+            kept[block] = jnp.where(lane == head, peak, kept[block])
+            kept[block] = jnp.where(lane == heads + head, total, kept[block])
+    for block in range(2):
+        stats[rows_at(block), :] = kept[block]
+
+
+def late_kernel(first_head, reads_ref, pattern_ref, text_ref, q, *refs):
+    sums, stats, passed, arrived, term, near, near_mate, side, side_mate = refs[:9]
     out = refs[-1]
-    row, col = lax.axis_index("rows"), lax.axis_index("cols")
+    row = lax.axis_index("rows")
     across, core = row // 2, row % 2
-    shard = both.shape[0] // 4
+    shard = near.shape[0] // 2
     half = 2 * PER_BLOCK
-    head_count = arrived.shape[1] // HEAD_DIM
-
-    def lanes(head):
-        return pl.ds((first_head + head) * HEAD_DIM, HEAD_DIM)
-
-    def text_part(chosen, head, which):
-        from_own = chosen % 2 == core
-        from_near = chosen // 2 == across
-        part = lanes(head)
-
-        def one(piece):
-            def pick(own, other, at):
-                rows = pl.ds((2 * at + which) * shard, shard)
-                return jnp.where(from_own, own[rows, part], other[rows, part])
-
-            if piece == 0:
-                near, side = pick(both, both_mate, 0), pick(both, both_mate, 1)
-            else:
-                side = pick(late[piece], late_mate[piece], 0)
-                if piece < 3:
-                    near = pick(early, early_mate, piece - 1)
-                else:
-                    near = pick(late[0], late_mate[0], 0)
-            return jnp.where(from_near, near, side)
-
-        return [one(piece) for piece in range(4)]
+    heads = q.shape[1] // HEAD_DIM
 
     def far_part(block, head, which):
         slot = pattern_ref[block, 0, 0] + pattern_ref[block, 0, 1] - block - 2
@@ -308,40 +358,56 @@
         owner = wanted // 2
         mate_at = (wanted % 2) * PER_BLOCK + which * half
         far_at = jnp.where(owner % 2 == core, 0, PER_BLOCK) + which * half
-        mate = passed[pl.ds(pl.multiple_of(mate_at, PER_BLOCK), PER_BLOCK), lanes(head)]
-        here = pl.ds(head * HEAD_DIM, HEAD_DIM)
-        far = arrived[pl.ds(pl.multiple_of(far_at, PER_BLOCK), PER_BLOCK), here]
-        return jnp.where(owner // 2 == across, mate, far)
+        mate_rows = pl.ds(pl.multiple_of(mate_at, PER_BLOCK), PER_BLOCK)
+        far_rows = pl.ds(pl.multiple_of(far_at, PER_BLOCK), PER_BLOCK)
+        return jnp.where(
+            owner // 2 == across,
+            passed[mate_rows, lanes_of(first_head + head)],
+            arrived[far_rows, lanes_of(head)],
+        )
 
     def gathered(block, head, which):
-        own = (k, v)[which][pl.ds(block * PER_BLOCK, PER_BLOCK), lanes(head)]
-        parts = [own]
+        part = lanes_of(first_head + head)
+        parts = []
         for turn in range(2):
-            parts += text_part(text_ref[block, 0, turn], head, which)
+            from_own, from_near = text_choice(text_ref[block, 0, turn])
+            parts.append(
+                jnp.where(
+                    from_near,
+                    pick(from_own, near, near_mate, shard, which, part),
+                    pick(from_own, side, side_mate, shard, which, part),
+                )
+            )
         return jnp.concatenate(parts + [far_part(block, head, which)], axis=0)
 
-    jobs = [(block, head) for head in range(head_count) for block in range(2)]
-    size = -(-len(jobs) // -(-len(jobs) // GROUP))
-    for at in range(0, len(jobs), size):
-        group = jobs[at : at + size]
+    count = arrived.shape[1] // HEAD_DIM
+    for group in grouped([(block, head) for head in range(count) for block in range(2)]):
         scores = [
-            head_scores(
-                q[pl.ds(block * PER_BLOCK, PER_BLOCK), lanes(head)], gathered(block, head, 0)
-            )
+            head_scores(q[rows_at(block), lanes_of(first_head + head)], gathered(block, head, 0))
             for block, head in group
         ]
-        peaks = [jnp.max(s, axis=1, keepdims=True) * EXP2_SCALE for s in scores]
+        old_peaks = [
+            stats[rows_at(block), first_head + head : first_head + head + 1]
+            for block, head in group
+        ]
+        peaks = [
+            jnp.maximum(old, jnp.max(s, axis=1, keepdims=True) * EXP2_SCALE)
+            for s, old in zip(scores, old_peaks)
+        ]
         weights = [
             jnp.exp2(s * EXP2_SCALE - peak).astype(jnp.bfloat16) for s, peak in zip(scores, peaks)
         ]
+        factors = [jnp.exp2(old - peak) for old, peak in zip(old_peaks, peaks)]
         totals = [jnp.sum(w.astype(jnp.float32), axis=1, keepdims=True) for w in weights]
         products = [
             jnp.dot(w, gathered(block, head, 1), preferred_element_type=jnp.float32)
             for w, (block, head) in zip(weights, group)
         ]
-        for product, total, (block, head) in zip(products, totals, group):
-            rows = pl.ds(block * PER_BLOCK, PER_BLOCK)
-            out[rows, pl.ds(head * HEAD_DIM, HEAD_DIM)] = product / total + term[rows, lanes(head)]
+        for product, total, factor, (block, head) in zip(products, totals, factors, group):
+            rows, part, at = rows_at(block), lanes_of(first_head + head), heads + first_head + head
+            total = stats[rows, at : at + 1] * factor + total
+            summed = sums[rows, part] * factor + product
+            out[rows, lanes_of(head)] = summed / total + term[rows, part]
 
 
 def body(
@@ -390,13 +456,23 @@
         pltpu.with_memory_space_constraint(value, pltpu.HBM)
         for value in (flat(k_stale), flat(v_stale), v_fresh, text_k, text_v)
     ]
-    stale, beside, diagonal, text = local(
+    offer, beside, diagonal, text = local(
         pack_kernel,
         "pack",
-        rows_of(2 * tokens, cols_here, cols_here, 2 * shard),
-        *in_place,
-        specs=[in_hbm] * 5,
+        rows_of(2 * shard + 8, cols_here, cols_here, 2 * shard),
+        reads,
+        *in_place[2:],
+        specs=[pl.BlockSpec(memory_space=pltpu.SMEM)] + [in_hbm] * 3,
         scratch=[pltpu.SemaphoreType.DMA((6,))],
+    )
+    stale = local(
+        fetch_kernel,
+        "fetch",
+        rows_of(2 * tokens),
+        *in_place[:2],
+        text,
+        specs=[in_hbm] * 2 + [in_vmem],
+        scratch=[pltpu.SemaphoreType.DMA((2,))],
     )
     forward = [(i, (i + 1) % 4) for i in range(4)]
     backward = [(i, (i + 3) % 4) for i in range(4)]
@@ -404,16 +480,8 @@
     near_parts = [lax.ppermute(text, "cols", p) for p in (forward, backward)]
     beside = to_mate(beside)
     diagonal = lax.ppermute(diagonal, "rows", [(1, 2), (2, 1)])
-    offer = local(
-        offer_kernel,
-        "offer",
-        rows_of(2 * shard + 8),
-        reads,
-        text,
-        specs=[pl.BlockSpec(memory_space=pltpu.SMEM), in_vmem],
-    )
     across = lax.ppermute(offer, "rows", swap)
-    passed = to_mate(after(stale, beside))
+    passed = to_mate(stale)
     packed = local(
         send_kernel, "send", chunks, after(across, diagonal), stale, passed
     )
@@ -440,9 +508,21 @@
     )
     upper = lax.ppermute(upper, "cols", [(1, 2), (2, 3)])
     lower = lax.ppermute(lower, "cols", [(1, 0), (2, 1)])
+    left_mate, right_mate = to_mate(left), to_mate(right)
+    sums, stats = local(
+        early_kernel,
+        "early",
+        (
+            jax.ShapeDtypeStruct((tokens, width), jnp.float32),
+            jax.ShapeDtypeStruct((tokens, HEAD_DIM), jnp.float32),
+        ),
+        text_blocks, flat(q_fresh), flat(k_fresh), flat(v_fresh),
+        both, both_mate, early, early_mate, left, left_mate, right, right_mate,
+        specs=[pl.BlockSpec(memory_space=pltpu.SMEM)] + [in_vmem] * 11,
+    )
+    upper, lower = after(upper, stats), after(lower, stats)
     far_side = local(choose_kernel, "choose", rows_of(2 * shard, 2 * shard), upper, lower)
-    late = [far_side[0], left, right, far_side[1]]
-    late_mate = [to_mate(part) for part in late]
+    late = [part for side in far_side for part in (side, to_mate(side))]
     term = local(
         term_kernel,
         "term",
@@ -460,21 +540,21 @@
             lambda i, *_, at=first_head * HEAD_DIM: (0, at),
         )
         out = pl.pallas_call(
-            functools.partial(attend_kernel, first_head),
+            functools.partial(late_kernel, first_head),
             out_shape=jax.ShapeDtypeStruct((tokens, width), jnp.float32),
             grid_spec=pltpu.PrefetchScalarGridSpec(
                 num_scalar_prefetch=3,
                 grid=(1,),
-                in_specs=[in_vmem] * 18 + [in_hbm] * (out is not None),
+                in_specs=[in_vmem] * 10 + [in_hbm] * (out is not None),
                 out_specs=block,
             ),
-            input_output_aliases={21: 0} if out is not None else {},
+            input_output_aliases={13: 0} if out is not None else {},
             compiler_params=params,
             cost_estimate=cost,
-            name=f"attend{chunk}",
+            name=f"late{chunk}",
         )(
-            reads, pattern, text_blocks, flat(q_fresh), flat(k_fresh), flat(v_fresh),
-            passed, far[chunk], term, both, both_mate, early, early_mate, *late, *late_mate,
+            reads, pattern, text_blocks, flat(q_fresh), sums, stats,
+            passed, far[chunk], term, *late,
             *([out] if out is not None else []),
         )
         first_head += head_count

time: 58.1 us -> 60.5 us (1.041)
  the two profiles are of different devices: /device:TPU:17 before, /device:TPU:0 now
where the time goes in v11:
time: 60.5 us; the launch traced here: 60.2 us
  waiting for transfers between devices  24.9 us (41%)
  starting transfers between devices  17.7 us (29%)
  Pallas kernels  16.7 us (28%)
  local copies, waits for them, and re-layouts  0.7 us (1%)
    pallas_call x10, Pallas kernels, local(): pl.pallas_call(kernel, out_shape=shapes, in_specs=specs or [in_vmem] * le...  8.36 us
    pallas_call x2, Pallas kernels, body(): pl.pallas_call(functools.partial(late_kernel, first_head), out_shape=jax....  8.31 us
    ppermute x1, waiting for transfers between devices, body(): left = lax.ppermute(plus, 'cols', forward)  6.78 us
    ppermute x1, waiting for transfers between devices, body(): lower = lax.ppermute(lower, 'cols', [(1, 0), (2, 1)])  5.61 us
    ppermute x2, waiting for transfers between devices, body(): near_parts = [lax.ppermute(text, 'cols', p) for p in (forward, backward)]  4.93 us
    ppermute x1, waiting for transfers between devices, body(): right = lax.ppermute(minus, 'cols', backward)  4.6 us
    ppermute x2, starting transfers between devices, body(): near_parts = [lax.ppermute(text, 'cols', p) for p in (forward, backward)]  3.66 us
    ppermute x2, starting transfers between devices, body(): far = [lax.ppermute(chunk, 'rows', swap) for chunk in packed]  2.95 us
  transfers between devices with their start and end apart: 18, of which 6 were waited for; matrix products, arithmetic and copies ran while one was open for 0% of the time, Pallas kernels for 17%

profile of v11, /device:TPU:0, one launch (start us, length us, event | category | flops | bytes accessed | tf_op | source)
XLA Modules:
  0.0 60.2 jit_solution(12706539582136842895)
XLA Ops:
  0.0 0.7 %copy-done.5 = s32[1,1,2]{2,1,0:T(1,128)S(1)} copy-done((s32[1,1,2]{2,1,0:T(1,128)S(1)}, s32[1,1,2]{2,1,0:T(1,128)}, u32[]{:S(2)}) %copy-start.5) | copy-done | bytes 32
  0.7 1.7 %pack.1 = (bf16[72,1536]{1,0:T(8,128)(2,1)S(1)}, bf16[32,1536]{1,0:T(8,128)(2,1)S(1)}, bf16[32,1536]{1,0:T(8,128)(2,1)S(1)}, bf16[64,1536]{1,0:T(8,128)(2,1)S(1)}) custom-call(s32[1,1,2]{2,1,0:T(1,128)S(1)} %copy-done.5, bf16[8,32,1536]{2,1,0:T(8,128)(2,1)} %cells.5, bf16[32,1536]{1,0:T(8,128)(2,1)} %text_k.1, bf16[32,1536]{1,0:T(8,128)(2,1)} %text_v.1), custom_call_target="tpu_custom_call" | custom-call | flops 1048576 | bytes 65536 | tf_op jit(solution)/shard_map/pack/pallas_call | solution.py:441
  2.4 1.4 %fetch.1.stale = bf16[512,1536]{1,0:T(8,128)(2,1)S(1)} custom-call(bf16[256,1536]{1,0:T(8,128)(2,1)} %bitcast.11, bf16[256,1536]{1,0:T(8,128)(2,1)} %bitcast.12, bf16[64,1536]{1,0:T(8,128)(2,1)S(1)} %get-tuple-element.24.text), custom_call_target="tpu_custom_call" | custom-call | flops 1048576 | bytes 65536 | tf_op jit(solution)/shard_map/fetch/pallas_call | solution.py:441
  3.8 0.5 collective-permute-start.2
  4.3 2.6 %collective-permute-start = (bf16[72,1536]{1,0:T(8,128)(2,1)S(1)}, bf16[72,1536]{1,0:T(8,128)(2,1)S(1)}, u32[]{:S(2)}, u32[]{:S(2)}) collective-permute-start(bf16[72,1536]{1,0:T(8,128)(2,1)S(1)} %get-tuple-element.25), channel_id=1, source_target_pairs={{0,8},{4,12},{8,0},{12,4},{1,9},{5,13},{9,1},{13,5},{2,10},{6,14},... | collective-permute-start | bytes 663560 | tf_op jit(solution)/shard_map/ppermute | solution.py:483
  6.9 0.8 %collective-permute-start.1 = (bf16[32,1536]{1,0:T(8,128)(2,1)S(1)}, bf16[32,1536]{1,0:T(8,128)(2,1)S(1)}, u32[]{:S(2)}, u32[]{:S(2)}) collective-permute-start(bf16[32,1536]{1,0:T(8,128)(2,1)S(1)} %get-tuple-element.26), channel_id=1, source_target_pairs={{4,8},{8,4},{5,9},{9,5},{6,10},{10,6},{7,11},{11,7},{20,24},{24,20... | collective-permute-start | bytes 294920 | tf_op jit(solution)/shard_map/ppermute | solution.py:482
  7.7 3.7 %collective-permute-start.6 = (bf16[64,1536]{1,0:T(8,128)(2,1)S(1)}, bf16[64,1536]{1,0:T(8,128)(2,1)S(1)}, u32[]{:S(2)}, u32[]{:S(2)}) collective-permute-start(bf16[64,1536]{1,0:T(8,128)(2,1)S(1)} %get-tuple-element.24.text), channel_id=1, source_target_pairs={{0,3},{1,0},{2,1},{3,2},{4,7},{5,4},{6,5},{7,6},{8,11},{9,8},{10,9... | collective-permute-start | bytes 589832 | tf_op jit(solution)/shard_map/ppermute | solution.py:480
  11.3 1.6 %collective-permute-done.across = bf16[72,1536]{1,0:T(8,128)(2,1)S(1)} collective-permute-done((bf16[72,1536]{1,0:T(8,128)(2,1)S(1)}, bf16[72,1536]{1,0:T(8,128)(2,1)S(1)}, u32[]{:S(2)}, u32[]{:S(2)}) %collective-permute-start) | collective-permute-done | bytes 221216 | tf_op jit(solution)/shard_map/ppermute | solution.py:483
  13.1 2.9 %collective-permute-start.13 = (bf16[512,1152]{1,0:T(8,128)(2,1)S(1)}, bf16[512,1152]{1,0:T(8,128)(2,1)S(1)}, u32[]{:S(2)}, u32[]{:S(2)}) collective-permute-start(bf16[512,1152]{1,0:T(8,128)(2,1)S(1)} %get-tuple-element.28), channel_id=1, source_target_pairs={{0,8},{4,12},{8,0},{12,4},{1,9},{5,13},{9,1},{13,5},{2,10},{6,14},... | collective-permute-start | bytes 3538952 | tf_op jit(solution)/shard_map/ppermute | solution.py:488
  16.0 4.9 %collective-permute-done.5.refs_0_ = bf16[64,1536]{1,0:T(8,128)(2,1)S(1)} collective-permute-done((bf16[64,1536]{1,0:T(8,128)(2,1)S(1)}, bf16[64,1536]{1,0:T(8,128)(2,1)S(1)}, u32[]{:S(2)}, u32[]{:S(2)}) %collective-permute-start.5) | collective-permute-done | bytes 196640 | tf_op jit(solution)/shard_map/ppermute | solution.py:480
  21.0 0.7 %collective-permute-start.7 = (bf16[128,1536]{1,0:T(8,128)(2,1)S(1)}, bf16[128,1536]{1,0:T(8,128)(2,1)S(1)}, u32[]{:S(2)}, u32[]{:S(2)}) collective-permute-start(bf16[128,1536]{1,0:T(8,128)(2,1)S(1)} %bundle.1.early), channel_id=1, source_target_pairs={{0,4},{4,0},{8,12},{12,8},{1,5},{5,1},{9,13},{13,9},{2,6},{6,2},{1... | collective-permute-start | bytes 1179656 | tf_op jit(solution)/shard_map/ppermute | solution.py:433
  21.9 2.0 %collective-permute-start.8 = (bf16[80,1536]{1,0:T(8,128)(2,1)S(1)}, bf16[80,1536]{1,0:T(8,128)(2,1)S(1)}, u32[]{:S(2)}, u32[]{:S(2)}) collective-permute-start(bf16[80,1536]{1,0:T(8,128)(2,1)S(1)} %get-tuple-element.32), channel_id=1, source_target_pairs={{0,1},{1,2},{2,3},{3,0},{4,5},{5,6},{6,7},{7,4},{8,9},{9,10},{10,1... | collective-permute-start | bytes 737288 | tf_op jit(solution)/shard_map/ppermute | solution.py:500
  23.9 1.9 %collective-permute-start.10 = (bf16[80,1536]{1,0:T(8,128)(2,1)S(1)}, bf16[80,1536]{1,0:T(8,128)(2,1)S(1)}, u32[]{:S(2)}, u32[]{:S(2)}) collective-permute-start(bf16[80,1536]{1,0:T(8,128)(2,1)S(1)} %get-tuple-element.33), channel_id=1, source_target_pairs={{0,3},{1,0},{2,1},{3,2},{4,7},{5,4},{6,5},{7,6},{8,11},{9,8},{10,9... | collective-permute-start | bytes 737288 | tf_op jit(solution)/shard_map/ppermute | solution.py:501
  25.8 6.8 %collective-permute-done.8.left.refs_1_ = bf16[80,1536]{1,0:T(8,128)(2,1)S(1)} collective-permute-done((bf16[80,1536]{1,0:T(8,128)(2,1)S(1)}, bf16[80,1536]{1,0:T(8,128)(2,1)S(1)}, u32[]{:S(2)}, u32[]{:S(2)}) %collective-permute-start.8) | collective-permute-done | bytes 245792 | tf_op jit(solution)/shard_map/ppermute | solution.py:500
  32.6 4.6 %collective-permute-done.10.right.refs_1_ = bf16[80,1536]{1,0:T(8,128)(2,1)S(1)} collective-permute-done((bf16[80,1536]{1,0:T(8,128)(2,1)S(1)}, bf16[80,1536]{1,0:T(8,128)(2,1)S(1)}, u32[]{:S(2)}, u32[]{:S(2)}) %collective-permute-start.10) | collective-permute-done | bytes 245792 | tf_op jit(solution)/shard_map/ppermute | solution.py:501
  37.2 1.3 %collective-permute-start.15 = (bf16[128,1536]{1,0:T(8,128)(2,1)S(1)}, bf16[128,1536]{1,0:T(8,128)(2,1)S(1)}, u32[]{:S(2)}, u32[]{:S(2)}) collective-permute-start(bf16[128,1536]{1,0:T(8,128)(2,1)S(1)} %pair.3), channel_id=1, source_target_pairs={{1,0},{2,1},{5,4},{6,5},{9,8},{10,9},{13,12},{14,13},{17,16},{18,1... | collective-permute-start | bytes 1179656 | tf_op jit(solution)/shard_map/ppermute | solution.py:510
  38.6 0.7 %collective-permute-start.14 = (bf16[128,1536]{1,0:T(8,128)(2,1)S(1)}, bf16[128,1536]{1,0:T(8,128)(2,1)S(1)}, u32[]{:S(2)}, u32[]{:S(2)}) collective-permute-start(bf16[128,1536]{1,0:T(8,128)(2,1)S(1)} %pair.2), channel_id=1, source_target_pairs={{1,2},{2,3},{5,6},{6,7},{9,10},{10,11},{13,14},{14,15},{17,18},{18... | collective-permute-start | bytes 1179656 | tf_op jit(solution)/shard_map/ppermute | solution.py:509
  39.4 1.4 %collective-permute-done.11.right_mate = bf16[80,1536]{1,0:T(8,128)(2,1)S(1)} collective-permute-done((bf16[80,1536]{1,0:T(8,128)(2,1)S(1)}, bf16[80,1536]{1,0:T(8,128)(2,1)S(1)}, u32[]{:S(2)}, u32[]{:S(2)}) %collective-permute-start.11) | collective-permute-done | bytes 245792 | tf_op jit(solution)/shard_map/ppermute | solution.py:433
  40.9 3.4 %early.1 = (f32[256,1536]{1,0:T(8,128)S(1)}, f32[256,128]{1,0:T(8,128)S(1)}) custom-call(s32[2,1,2]{2,1,0:T(1,128)S(1)} %copy-done.4, bf16[256,1536]{1,0:T(8,128)(2,1)S(1)} %bitcast.7, bf16[256,1536]{1,0:T(8,128)(2,1)S(1)} %bitcast.10, bf16[256,1536]{1,0:T(8,128)(2,1)S(1)} %bitcast.6, bf16[128,1536]{1,0:T(8,128)(2,1)S(1)} %get-tuple-element.31.both, ...), custom_call_target="tpu_custom_call" | custom-call | flops 1048576 | bytes 65536 | tf_op jit(solution)/shard_map/early/pallas_call | solution.py:441
  44.3 5.6 %collective-permute-done.15.lower = bf16[128,1536]{1,0:T(8,128)(2,1)S(1)} collective-permute-done((bf16[128,1536]{1,0:T(8,128)(2,1)S(1)}, bf16[128,1536]{1,0:T(8,128)(2,1)S(1)}, u32[]{:S(2)}, u32[]{:S(2)}) %collective-permute-start.15) | collective-permute-done | bytes 393248 | tf_op jit(solution)/shard_map/ppermute | solution.py:510
  50.1 0.5 collective-permute-start.17
  50.6 1.3 %term.1.refs_4_ = f32[256,1536]{1,0:T(8,128)S(1)} custom-call(bf16[8,32,1536]{2,1,0:T(8,128)(2,1)S(1)} %copy-done, bf16[32,1536]{1,0:T(8,128)(2,1)S(1)} %collective-permute-done.3.beside, bf16[32,1536]{1,0:T(8,128)(2,1)S(1)} %collective-permute-done.1.diagonal, bf16[80,1536]{1,0:T(8,128)(2,1)S(1)} %collective-permute-done.8.left.refs_1_, ...), custom_call_target="tpu_custom_call" | custom-call | flops 1048576 | bytes 65536 | tf_op jit(solution)/shard_map/term/pallas_call | solution.py:441
  51.9 5.4 %late0.1.refs_9_ = f32[256,1536]{1,0:T(8,128)} custom-call(s32[1,1,2]{2,1,0:T(1,128)S(1)} %copy-done.6, s32[2,1,2]{2,1,0:T(1,128)S(1)} %copy-done.7, s32[2,1,2]{2,1,0:T(1,128)S(1)} %copy-done.4, bf16[256,1536]{1,0:T(8,128)(2,1)S(1)} %bitcast.8, f32[256,1536]{1,0:T(8,128)S(1)} %get-tuple-element.34.refs_0_, f32[256,128]{1,0:T(8,128)S(1)} %get-tuple-element.35.refs_1_, ...), custom_call_target="tpu_custom_call" | custom-call | flops 1048576 | bytes 65536 | tf_op jit(solution)/shard_map/late0/pallas_call | solution.py:542
  57.3 2.9 %late1.1 = f32[256,1536]{1,0:T(8,128)} custom-call(s32[1,1,2]{2,1,0:T(1,128)S(1)} %copy-done.6, s32[2,1,2]{2,1,0:T(1,128)S(1)} %copy-done.7, s32[2,1,2]{2,1,0:T(1,128)S(1)} %copy-done.4, bf16[256,1536]{1,0:T(8,128)(2,1)S(1)} %bitcast.9, f32[256,1536]{1,0:T(8,128)S(1)} %get-tuple-element.34.refs_0_, ...), custom_call_target="tpu_custom_call", output_to_operand_aliasing={{}: (13, {})} | custom-call | flops 1048576 | bytes 65536 | tf_op jit(solution)/shard_map/late1/pallas_call | solution.py:542
  (40 shorter events, 0.9 us)
Async XLA Ops:
  3.8 9.1 %collective-permute-start.2 = (bf16[512,1536]{1,0:T(8,128)(2,1)S(1)}, bf16[512,1536]{1,0:T(8,128)(2,1)S(1)}, u32[]{:S(2)}, u32[]{:S(2)}) collective-permute-start(bf16[512,1536]{1,0:T(8,128)(2,1)S(1)} %fetch.1.stale), channel_id=1, source_target_pairs={{0,4},{4,0},{8,12},{12,8},{1,5},{5,1},{9,13},{13,9},{2,6},{6,2},{1... | collective-permute-start | bytes 4718600 | tf_op jit(solution)/shard_map/ppermute | solution.py:433
  4.3 8.6 %collective-permute-start = (bf16[72,1536]{1,0:T(8,128)(2,1)S(1)}, bf16[72,1536]{1,0:T(8,128)(2,1)S(1)}, u32[]{:S(2)}, u32[]{:S(2)}) collective-permute-start(bf16[72,1536]{1,0:T(8,128)(2,1)S(1)} %get-tuple-element.25), channel_id=1, source_target_pairs={{0,8},{4,12},{8,0},{12,4},{1,9},{5,13},{9,1},{13,5},{2,10},{6,14},... | collective-permute-start | bytes 663560 | tf_op jit(solution)/shard_map/ppermute | solution.py:483
  6.9 14.8 %copy-start = (bf16[8,32,1536]{2,1,0:T(8,128)(2,1)S(1)}, bf16[8,32,1536]{2,1,0:T(8,128)(2,1)}, u32[]{:S(2)}) copy-start(bf16[8,32,1536]{2,1,0:T(8,128)(2,1)} %cells.5) | copy-start | bytes 2359300
  6.9 4.5 %collective-permute-start.1 = (bf16[32,1536]{1,0:T(8,128)(2,1)S(1)}, bf16[32,1536]{1,0:T(8,128)(2,1)S(1)}, u32[]{:S(2)}, u32[]{:S(2)}) collective-permute-start(bf16[32,1536]{1,0:T(8,128)(2,1)S(1)} %get-tuple-element.26), channel_id=1, source_target_pairs={{4,8},{8,4},{5,9},{9,5},{6,10},{10,6},{7,11},{11,7},{20,24},{24,20... | collective-permute-start | bytes 294920 | tf_op jit(solution)/shard_map/ppermute | solution.py:482
  7.7 8.4 %collective-permute-start.6 = (bf16[64,1536]{1,0:T(8,128)(2,1)S(1)}, bf16[64,1536]{1,0:T(8,128)(2,1)S(1)}, u32[]{:S(2)}, u32[]{:S(2)}) collective-permute-start(bf16[64,1536]{1,0:T(8,128)(2,1)S(1)} %get-tuple-element.24.text), channel_id=1, source_target_pairs={{0,3},{1,0},{2,1},{3,2},{4,7},{5,4},{6,5},{7,6},{8,11},{9,8},{10,9... | collective-permute-start | bytes 589832 | tf_op jit(solution)/shard_map/ppermute | solution.py:480
  11.3 9.6 %collective-permute-start.5 = (bf16[64,1536]{1,0:T(8,128)(2,1)S(1)}, bf16[64,1536]{1,0:T(8,128)(2,1)S(1)}, u32[]{:S(2)}, u32[]{:S(2)}) collective-permute-start(bf16[64,1536]{1,0:T(8,128)(2,1)S(1)} %get-tuple-element.24.text), channel_id=1, source_target_pairs={{0,1},{1,2},{2,3},{3,0},{4,5},{5,6},{6,7},{7,4},{8,9},{9,10},{10,1... | collective-permute-start | bytes 589832 | tf_op jit(solution)/shard_map/ppermute | solution.py:480
  13.1 38.7 %collective-permute-start.13 = (bf16[512,1152]{1,0:T(8,128)(2,1)S(1)}, bf16[512,1152]{1,0:T(8,128)(2,1)S(1)}, u32[]{:S(2)}, u32[]{:S(2)}) collective-permute-start(bf16[512,1152]{1,0:T(8,128)(2,1)S(1)} %get-tuple-element.28), channel_id=1, source_target_pairs={{0,8},{4,12},{8,0},{12,4},{1,9},{5,13},{9,1},{13,5},{2,10},{6,14},... | collective-permute-start | bytes 3538952 | tf_op jit(solution)/shard_map/ppermute | solution.py:488
  16.0 5.7 %collective-permute-start.3 = (bf16[32,1536]{1,0:T(8,128)(2,1)S(1)}, bf16[32,1536]{1,0:T(8,128)(2,1)S(1)}, u32[]{:S(2)}, u32[]{:S(2)}) collective-permute-start(bf16[32,1536]{1,0:T(8,128)(2,1)S(1)} %get-tuple-element.30), channel_id=1, source_target_pairs={{0,4},{4,0},{8,12},{12,8},{1,5},{5,1},{9,13},{13,9},{2,6},{6,2},{1... | collective-permute-start | bytes 294920 | tf_op jit(solution)/shard_map/ppermute | solution.py:433
  21.0 19.8 %copy-start.1 = (bf16[8,32,1536]{2,1,0:T(8,128)(2,1)S(1)}, bf16[8,32,1536]{2,1,0:T(8,128)(2,1)}, u32[]{:S(2)}) copy-start(bf16[8,32,1536]{2,1,0:T(8,128)(2,1)} %param.11) | copy-start | bytes 2359300
  21.0 19.8 %copy-start.2 = (bf16[8,32,1536]{2,1,0:T(8,128)(2,1)S(1)}, bf16[8,32,1536]{2,1,0:T(8,128)(2,1)}, u32[]{:S(2)}) copy-start(bf16[8,32,1536]{2,1,0:T(8,128)(2,1)} %param.12) | copy-start | bytes 2359300
  21.0 19.8 %copy-start.4 = (s32[2,1,2]{2,1,0:T(1,128)S(1)}, s32[2,1,2]{2,1,0:T(1,128)}, u32[]{:S(2)}) copy-start(s32[2,1,2]{2,1,0:T(1,128)} %text_ref.5) | copy-start | bytes 52
  21.0 17.5 %collective-permute-start.7 = (bf16[128,1536]{1,0:T(8,128)(2,1)S(1)}, bf16[128,1536]{1,0:T(8,128)(2,1)S(1)}, u32[]{:S(2)}, u32[]{:S(2)}) collective-permute-start(bf16[128,1536]{1,0:T(8,128)(2,1)S(1)} %bundle.1.early), channel_id=1, source_target_pairs={{0,4},{4,0},{8,12},{12,8},{1,5},{5,1},{9,13},{13,9},{2,6},{6,2},{1... | collective-permute-start | bytes 1179656 | tf_op jit(solution)/shard_map/ppermute | solution.py:433
  21.8 16.7 %collective-permute-start.4 = (bf16[128,1536]{1,0:T(8,128)(2,1)S(1)}, bf16[128,1536]{1,0:T(8,128)(2,1)S(1)}, u32[]{:S(2)}, u32[]{:S(2)}) collective-permute-start(bf16[128,1536]{1,0:T(8,128)(2,1)S(1)} %get-tuple-element.31.both), channel_id=1, source_target_pairs={{0,4},{4,0},{8,12},{12,8},{1,5},{5,1},{9,13},{13,9},{2,6},{6,2},{1... | collective-permute-start | bytes 1179656 | tf_op jit(solution)/shard_map/ppermute | solution.py:433
  21.9 10.6 %collective-permute-start.8 = (bf16[80,1536]{1,0:T(8,128)(2,1)S(1)}, bf16[80,1536]{1,0:T(8,128)(2,1)S(1)}, u32[]{:S(2)}, u32[]{:S(2)}) collective-permute-start(bf16[80,1536]{1,0:T(8,128)(2,1)S(1)} %get-tuple-element.32), channel_id=1, source_target_pairs={{0,1},{1,2},{2,3},{3,0},{4,5},{5,6},{6,7},{7,4},{8,9},{9,10},{10,1... | collective-permute-start | bytes 737288 | tf_op jit(solution)/shard_map/ppermute | solution.py:500
  23.9 13.3 %collective-permute-start.10 = (bf16[80,1536]{1,0:T(8,128)(2,1)S(1)}, bf16[80,1536]{1,0:T(8,128)(2,1)S(1)}, u32[]{:S(2)}, u32[]{:S(2)}) collective-permute-start(bf16[80,1536]{1,0:T(8,128)(2,1)S(1)} %get-tuple-element.33), channel_id=1, source_target_pairs={{0,3},{1,0},{2,1},{3,2},{4,7},{5,4},{6,5},{7,6},{8,11},{9,8},{10,9... | collective-permute-start | bytes 737288 | tf_op jit(solution)/shard_map/ppermute | solution.py:501
  32.6 6.8 %collective-permute-start.9 = (bf16[80,1536]{1,0:T(8,128)(2,1)S(1)}, bf16[80,1536]{1,0:T(8,128)(2,1)S(1)}, u32[]{:S(2)}, u32[]{:S(2)}) collective-permute-start(bf16[80,1536]{1,0:T(8,128)(2,1)S(1)} %collective-permute-done.8.left.refs_1_), channel_id=1, source_target_pairs={{0,4},{4,0},{8,12},{12,8},{1,5},{5,1},{9,13},{13,9},{2,6},{6,2},{1... | collective-permute-start | bytes 737288 | tf_op jit(solution)/shard_map/ppermute | solution.py:433
  37.2 12.7 %collective-permute-start.15 = (bf16[128,1536]{1,0:T(8,128)(2,1)S(1)}, bf16[128,1536]{1,0:T(8,128)(2,1)S(1)}, u32[]{:S(2)}, u32[]{:S(2)}) collective-permute-start(bf16[128,1536]{1,0:T(8,128)(2,1)S(1)} %pair.3), channel_id=1, source_target_pairs={{1,0},{2,1},{5,4},{6,5},{9,8},{10,9},{13,12},{14,13},{17,16},{18,1... | collective-permute-start | bytes 1179656 | tf_op jit(solution)/shard_map/ppermute | solution.py:510
  38.6 11.4 %collective-permute-start.14 = (bf16[128,1536]{1,0:T(8,128)(2,1)S(1)}, bf16[128,1536]{1,0:T(8,128)(2,1)S(1)}, u32[]{:S(2)}, u32[]{:S(2)}) collective-permute-start(bf16[128,1536]{1,0:T(8,128)(2,1)S(1)} %pair.2), channel_id=1, source_target_pairs={{1,2},{2,3},{5,6},{6,7},{9,10},{10,11},{13,14},{14,15},{17,18},{18... | collective-permute-start | bytes 1179656 | tf_op jit(solution)/shard_map/ppermute | solution.py:509
  39.3 1.6 %collective-permute-start.11 = (bf16[80,1536]{1,0:T(8,128)(2,1)S(1)}, bf16[80,1536]{1,0:T(8,128)(2,1)S(1)}, u32[]{:S(2)}, u32[]{:S(2)}) collective-permute-start(bf16[80,1536]{1,0:T(8,128)(2,1)S(1)} %collective-permute-done.10.right.refs_1_), channel_id=1, source_target_pairs={{0,4},{4,0},{8,12},{12,8},{1,5},{5,1},{9,13},{13,9},{2,6},{6,2},{1... | collective-permute-start | bytes 737288 | tf_op jit(solution)/shard_map/ppermute | solution.py:433
  39.4 17.9 %collective-permute-start.12 = (bf16[512,384]{1,0:T(8,128)(2,1)S(1)}, bf16[512,384]{1,0:T(8,128)(2,1)S(1)}, u32[]{:S(2)}, u32[]{:S(2)}) collective-permute-start(bf16[512,384]{1,0:T(8,128)(2,1)S(1)} %get-tuple-element.36), channel_id=1, source_target_pairs={{0,8},{4,12},{8,0},{12,4},{1,9},{5,13},{9,1},{13,5},{2,10},{6,14},... | collective-permute-start | bytes 1179656 | tf_op jit(solution)/shard_map/ppermute | solution.py:488
  40.8 9.7 %copy-start.3 = (f32[3,3,1536]{2,1,0:T(4,128)S(1)}, f32[3,3,1536]{2,1,0:T(4,128)}, u32[]{:S(2)}) copy-start(f32[3,3,1536]{2,1,0:T(4,128)} %weights.1) | copy-start | bytes 165892
  50.0 1.9 %copy-start.6 = (s32[1,1,2]{2,1,0:T(1,128)S(1)}, s32[1,1,2]{2,1,0:T(1,128)}, u32[]{:S(2)}) copy-start(s32[1,1,2]{2,1,0:T(1,128)} %reads_ref.5) | copy-start | bytes 28
  50.0 1.9 %collective-permute-start.16 = (bf16[64,1536]{1,0:T(8,128)(2,1)S(1)}, bf16[64,1536]{1,0:T(8,128)(2,1)S(1)}, u32[]{:S(2)}, u32[]{:S(2)}) collective-permute-start(bf16[64,1536]{1,0:T(8,128)(2,1)S(1)} %get-tuple-element.40.refs_5_), channel_id=1, source_target_pairs={{0,4},{4,0},{8,12},{12,8},{1,5},{5,1},{9,13},{13,9},{2,6},{6,2},{1... | collective-permute-start | bytes 589832 | tf_op jit(solution)/shard_map/ppermute | solution.py:433
  50.1 1.8 %collective-permute-start.17 = (bf16[64,1536]{1,0:T(8,128)(2,1)S(1)}, bf16[64,1536]{1,0:T(8,128)(2,1)S(1)}, u32[]{:S(2)}, u32[]{:S(2)}) collective-permute-start(bf16[64,1536]{1,0:T(8,128)(2,1)S(1)} %get-tuple-element.41.refs_7_), channel_id=1, source_target_pairs={{0,4},{4,0},{8,12},{12,8},{1,5},{5,1},{9,13},{13,9},{2,6},{6,2},{1... | collective-permute-start | bytes 589832 | tf_op jit(solution)/shard_map/ppermute | solution.py:433
  (2 other events, 2.6 us)

commit v12 on v11

--- a/solution.py
+++ b/solution.py
@@ -140,11 +140,23 @@
         copy.wait()
 
 
-def pack_kernel(reads_ref, cells, text_k, text_v, offer, beside, diagonal, text, sems):
-    shard, width = text_k.shape
+def pack_kernel(k_hbm, v_hbm, cells, text_k, text_v, stale, beside, diagonal, text, sems):
+    tokens, shard = k_hbm.shape[0], text_k.shape[0]
     row = lax.axis_index("rows")
     end = cells.shape[0] - 1
-    partner = (row + 2) % 4
+    copies = []
+    for which, source in enumerate((text_k, text_v)):
+        copies.append((source, text.at[pl.ds(which * shard, shard)]))
+    for which, source in enumerate((k_hbm, v_hbm)):
+        copies.append((source, stale.at[pl.ds(which * tokens, tokens)]))
+    copies.append((cells.at[jnp.where(row % 2 == 0, end, 0)], beside))
+    copies.append((cells.at[jnp.where(row < 2, end, 0)], diagonal))
+    run_copies(copies, sems)
+
+
+def offer_kernel(reads_ref, text, out):
+    both, width = text.shape
+    partner = (lax.axis_index("rows") + 2) % 4
 
     def flag(owner):
         found = 0
@@ -153,27 +165,9 @@
             found = jnp.where(entry // 2 == owner, entry % 2, found)
         return jnp.full((8, width // 2), found.astype(jnp.float32), jnp.float32)
 
-    copies = []
-    for which, source in enumerate((text_k, text_v)):
-        for target in (text, offer):
-            copies.append((source, target.at[pl.ds(which * shard, shard)]))
-    copies.append((cells.at[jnp.where(row % 2 == 0, end, 0)], beside))
-    copies.append((cells.at[jnp.where(row < 2, end, 0)], diagonal))
     flags = [flag(owner) for owner in (partner, partner + 1 - 2 * (partner % 2))]
-    offer[pl.ds(2 * shard, 8), :] = jnp.concatenate(flags, axis=1).astype(offer.dtype)
-    run_copies(copies, sems)
-
-
-def fetch_kernel(k_hbm, v_hbm, text, stale, sems):
-    del text
-    tokens = k_hbm.shape[0]
-    run_copies(
-        [
-            (source, stale.at[pl.ds(which * tokens, tokens)])
-            for which, source in enumerate((k_hbm, v_hbm))
-        ],
-        sems,
-    )
+    out[pl.ds(0, both), :] = text[...]
+    out[pl.ds(both, 8), :] = jnp.concatenate(flags, axis=1).astype(out.dtype)
 
 
 def send_kernel(across, stale, passed, *outs):
@@ -297,11 +291,10 @@
 
 def early_kernel(
     text_ref, q, k, v, both, both_mate, early, early_mate, left, left_mate, right, right_mate,
-    sums, stats,
+    sums, peaks_out, totals_out,
 ):
     shard = both.shape[0] // 4
     heads = q.shape[1] // HEAD_DIM
-    lane = lax.broadcasted_iota(jnp.int32, (PER_BLOCK, HEAD_DIM), 1)
 
     def gathered(block, head, which):
         part = lanes_of(head)
@@ -322,7 +315,6 @@
                 )
         return jnp.concatenate(parts, axis=0)
 
-    kept = [jnp.zeros((PER_BLOCK, HEAD_DIM), jnp.float32) for _ in range(2)]
     for group in grouped([(block, head) for head in range(heads) for block in range(2)]):
         scores = [
             head_scores(q[rows_at(block), lanes_of(head)], gathered(block, head, 0))
@@ -337,20 +329,19 @@
             sums[rows_at(block), lanes_of(head)] = jnp.dot(
                 w, gathered(block, head, 1), preferred_element_type=jnp.float32
             )
-            kept[block] = jnp.where(lane == head, peak, kept[block])
-            kept[block] = jnp.where(lane == heads + head, total, kept[block])
-    for block in range(2):
-        stats[rows_at(block), :] = kept[block]
+            spread = (PER_BLOCK, HEAD_DIM)
+            peaks_out[rows_at(block), lanes_of(head)] = jnp.broadcast_to(peak, spread)
+            totals_out[rows_at(block), lanes_of(head)] = jnp.broadcast_to(total, spread)
 
 
 def late_kernel(first_head, reads_ref, pattern_ref, text_ref, q, *refs):
-    sums, stats, passed, arrived, term, near, near_mate, side, side_mate = refs[:9]
+    sums, old_peaks, old_totals, passed, arrived, term = refs[:6]
+    near, near_mate, side, side_mate = refs[6:10]
     out = refs[-1]
     row = lax.axis_index("rows")
     across, core = row // 2, row % 2
     shard = near.shape[0] // 2
     half = 2 * PER_BLOCK
-    heads = q.shape[1] // HEAD_DIM
 
     def far_part(block, head, which):
         slot = pattern_ref[block, 0, 0] + pattern_ref[block, 0, 1] - block - 2
@@ -368,7 +359,7 @@
 
     def gathered(block, head, which):
         part = lanes_of(first_head + head)
-        parts = []
+        parts = [far_part(block, head, which)]
         for turn in range(2):
             from_own, from_near = text_choice(text_ref[block, 0, turn])
             parts.append(
@@ -378,7 +369,7 @@
                     pick(from_own, side, side_mate, shard, which, part),
                 )
             )
-        return jnp.concatenate(parts + [far_part(block, head, which)], axis=0)
+        return jnp.concatenate(parts, axis=0)
 
     count = arrived.shape[1] // HEAD_DIM
     for group in grouped([(block, head) for head in range(count) for block in range(2)]):
@@ -386,26 +377,24 @@
             head_scores(q[rows_at(block), lanes_of(first_head + head)], gathered(block, head, 0))
             for block, head in group
         ]
-        old_peaks = [
-            stats[rows_at(block), first_head + head : first_head + head + 1]
-            for block, head in group
-        ]
+        olds = [old_peaks[rows_at(block), lanes_of(first_head + head)] for block, head in group]
         peaks = [
             jnp.maximum(old, jnp.max(s, axis=1, keepdims=True) * EXP2_SCALE)
-            for s, old in zip(scores, old_peaks)
+            for s, old in zip(scores, olds)
         ]
-        weights = [
-            jnp.exp2(s * EXP2_SCALE - peak).astype(jnp.bfloat16) for s, peak in zip(scores, peaks)
-        ]
-        factors = [jnp.exp2(old - peak) for old, peak in zip(old_peaks, peaks)]
+        weights = []
+        for s, peak in zip(scores, peaks):
+            wide = jnp.concatenate([peak, peak[:, : s.shape[1] - HEAD_DIM]], axis=1)
+            weights.append(jnp.exp2(s * EXP2_SCALE - wide).astype(jnp.bfloat16))
         totals = [jnp.sum(w.astype(jnp.float32), axis=1, keepdims=True) for w in weights]
         products = [
             jnp.dot(w, gathered(block, head, 1), preferred_element_type=jnp.float32)
             for w, (block, head) in zip(weights, group)
         ]
-        for product, total, factor, (block, head) in zip(products, totals, factors, group):
-            rows, part, at = rows_at(block), lanes_of(first_head + head), heads + first_head + head
-            total = stats[rows, at : at + 1] * factor + total
+        for product, total, old, peak, (block, head) in zip(products, totals, olds, peaks, group):
+            rows, part = rows_at(block), lanes_of(first_head + head)
+            factor = jnp.exp2(old - peak)
+            total = old_totals[rows, part] * factor + total
             summed = sums[rows, part] * factor + product
             out[rows, lanes_of(head)] = summed / total + term[rows, part]
 
@@ -456,23 +445,13 @@
         pltpu.with_memory_space_constraint(value, pltpu.HBM)
         for value in (flat(k_stale), flat(v_stale), v_fresh, text_k, text_v)
     ]
-    offer, beside, diagonal, text = local(
+    stale, beside, diagonal, text = local(
         pack_kernel,
         "pack",
-        rows_of(2 * shard + 8, cols_here, cols_here, 2 * shard),
-        reads,
-        *in_place[2:],
-        specs=[pl.BlockSpec(memory_space=pltpu.SMEM)] + [in_hbm] * 3,
+        rows_of(2 * tokens, cols_here, cols_here, 2 * shard),
+        *in_place,
+        specs=[in_hbm] * 5,
         scratch=[pltpu.SemaphoreType.DMA((6,))],
-    )
-    stale = local(
-        fetch_kernel,
-        "fetch",
-        rows_of(2 * tokens),
-        *in_place[:2],
-        text,
-        specs=[in_hbm] * 2 + [in_vmem],
-        scratch=[pltpu.SemaphoreType.DMA((2,))],
     )
     forward = [(i, (i + 1) % 4) for i in range(4)]
     backward = [(i, (i + 3) % 4) for i in range(4)]
@@ -480,8 +459,16 @@
     near_parts = [lax.ppermute(text, "cols", p) for p in (forward, backward)]
     beside = to_mate(beside)
     diagonal = lax.ppermute(diagonal, "rows", [(1, 2), (2, 1)])
+    offer = local(
+        offer_kernel,
+        "offer",
+        rows_of(2 * shard + 8),
+        reads,
+        text,
+        specs=[pl.BlockSpec(memory_space=pltpu.SMEM), in_vmem],
+    )
     across = lax.ppermute(offer, "rows", swap)
-    passed = to_mate(stale)
+    passed = to_mate(after(stale, beside))
     packed = local(
         send_kernel, "send", chunks, after(across, diagonal), stale, passed
     )
@@ -509,18 +496,15 @@
     upper = lax.ppermute(upper, "cols", [(1, 2), (2, 3)])
     lower = lax.ppermute(lower, "cols", [(1, 0), (2, 1)])
     left_mate, right_mate = to_mate(left), to_mate(right)
-    sums, stats = local(
+    sums, peaks, totals = local(
         early_kernel,
         "early",
-        (
-            jax.ShapeDtypeStruct((tokens, width), jnp.float32),
-            jax.ShapeDtypeStruct((tokens, HEAD_DIM), jnp.float32),
-        ),
+        (jax.ShapeDtypeStruct((tokens, width), jnp.float32),) * 3,
         text_blocks, flat(q_fresh), flat(k_fresh), flat(v_fresh),
         both, both_mate, early, early_mate, left, left_mate, right, right_mate,
         specs=[pl.BlockSpec(memory_space=pltpu.SMEM)] + [in_vmem] * 11,
     )
-    upper, lower = after(upper, stats), after(lower, stats)
+    upper, lower = after(upper, sums), after(lower, sums)
     far_side = local(choose_kernel, "choose", rows_of(2 * shard, 2 * shard), upper, lower)
     late = [part for side in far_side for part in (side, to_mate(side))]
     term = local(
@@ -545,15 +529,15 @@
             grid_spec=pltpu.PrefetchScalarGridSpec(
                 num_scalar_prefetch=3,
                 grid=(1,),
-                in_specs=[in_vmem] * 10 + [in_hbm] * (out is not None),
+                in_specs=[in_vmem] * 11 + [in_hbm] * (out is not None),
                 out_specs=block,
             ),
-            input_output_aliases={13: 0} if out is not None else {},
+            input_output_aliases={14: 0} if out is not None else {},
             compiler_params=params,
             cost_estimate=cost,
             name=f"late{chunk}",
         )(
-            reads, pattern, text_blocks, flat(q_fresh), sums, stats,
+            reads, pattern, text_blocks, flat(q_fresh), sums, peaks, totals,
             passed, far[chunk], term, *late,
             *([out] if out is not None else []),
         )

time: 60.5 us -> 53.2 us (0.88)
  Pallas kernels: 16.7 us -> 12.7 us
  waiting for transfers between devices: 24.9 us -> 23.1 us
  starting transfers between devices: 17.7 us -> 16.5 us
  local copies, waits for them, and re-layouts: 0.7 us -> 0.04 us
    ppermute x1, waiting for transfers between devices: 5.61 us -> 2.9 us  [body(): lower = lax.ppermute(lower, 'cols', [(1, 0), (2, 1)])]
    pallas_call x2, Pallas kernels: 8.31 us -> 5.63 us  [body(): pl.pallas_call(functools.partial(late_kernel, first_head), out_shape=jax....]
    ppermute x1, waiting for transfers between devices: 6.78 us -> 4.38 us  [body(): left = lax.ppermute(plus, 'cols', forward)]
    ppermute x1, starting transfers between devices: 1.95 us -> 0.01 us  [body(): left = lax.ppermute(plus, 'cols', forward)]
    ppermute x1, waiting for transfers between devices: 4.6 us -> 6.32 us  [body(): right = lax.ppermute(minus, 'cols', backward)]
    pallas_call x10, Pallas kernels: 8.36 us -> 7.04 us  [local(): pl.pallas_call(kernel, out_shape=shapes, in_specs=specs or [in_vmem] * le...]
    ppermute x8, waiting for transfers between devices: 1.43 us -> 2.37 us  [to_mate(): return lax.ppermute(values, 'rows', mates)]
    ppermute x2, waiting for transfers between devices: 0.01 us -> 0.78 us  [body(): far = [lax.ppermute(chunk, 'rows', swap) for chunk in packed]]
  transfers between devices with their start and end apart: 18 -> 18, of which waited for: 6 -> 9; matrix products, arithmetic and copies ran while one was open for 0% -> 0% of each run, Pallas kernels for 17% -> 17%
where the time goes in v12:
time: 53.2 us; the launch traced here: 52.5 us
  waiting for transfers between devices  23.1 us (43%)
  starting transfers between devices  16.5 us (31%)
  Pallas kernels  12.7 us (24%)
    pallas_call x10, Pallas kernels, local(): pl.pallas_call(kernel, out_shape=shapes, in_specs=specs or [in_vmem] * le...  7.04 us
    ppermute x1, waiting for transfers between devices, body(): right = lax.ppermute(minus, 'cols', backward)  6.32 us
    pallas_call x2, Pallas kernels, body(): pl.pallas_call(functools.partial(late_kernel, first_head), out_shape=jax....  5.63 us
    ppermute x2, waiting for transfers between devices, body(): near_parts = [lax.ppermute(text, 'cols', p) for p in (forward, backward)]  5.04 us
    ppermute x1, waiting for transfers between devices, body(): left = lax.ppermute(plus, 'cols', forward)  4.38 us
    ppermute x2, starting transfers between devices, body(): near_parts = [lax.ppermute(text, 'cols', p) for p in (forward, backward)]  3.88 us
    ppermute x2, starting transfers between devices, body(): far = [lax.ppermute(chunk, 'rows', swap) for chunk in packed]  2.93 us
    ppermute x1, waiting for transfers between devices, body(): lower = lax.ppermute(lower, 'cols', [(1, 0), (2, 1)])  2.9 us
  transfers between devices with their start and end apart: 18, of which 9 were waited for; matrix products, arithmetic and copies ran while one was open for 0% of the time, Pallas kernels for 17%

profile of v12, /device:TPU:0, one launch (start us, length us, event | category | flops | bytes accessed | tf_op | source)
XLA Modules:
  0.0 52.5 jit_solution(11034441939149529450)
XLA Ops:
  0.0 1.6 %pack.1 = (bf16[512,1536]{1,0:T(8,128)(2,1)S(1)}, bf16[32,1536]{1,0:T(8,128)(2,1)S(1)}, bf16[32,1536]{1,0:T(8,128)(2,1)S(1)}, bf16[64,1536]{1,0:T(8,128)(2,1)S(1)}) custom-call(bf16[256,1536]{1,0:T(8,128)(2,1)} %bitcast.11, bf16[256,1536]{1,0:T(8,128)(2,1)} %bitcast.12, bf16[8,32,1536]{2,1,0:T(8,128)(2,1)} %cells.5, bf16[32,1536]{1,0:T(8,128)(2,1)} %text_k.1, ...), custom_call_target="tpu_custom_call" | custom-call | flops 1048576 | bytes 65536 | tf_op jit(solution)/shard_map/pack/pallas_call | solution.py:430
  1.6 0.5 collective-permute-start.2
  2.1 0.9 %collective-permute-done.2.beside = bf16[32,1536]{1,0:T(8,128)(2,1)S(1)} collective-permute-done((bf16[32,1536]{1,0:T(8,128)(2,1)S(1)}, bf16[32,1536]{1,0:T(8,128)(2,1)S(1)}, u32[]{:S(2)}, u32[]{:S(2)}) %collective-permute-start.2) | collective-permute-done | bytes 98336 | tf_op jit(solution)/shard_map/ppermute | solution.py:422
  3.4 0.6 %offer.1 = bf16[72,1536]{1,0:T(8,128)(2,1)S(1)} custom-call(s32[1,1,2]{2,1,0:T(1,128)S(1)} %copy-done.5, bf16[64,1536]{1,0:T(8,128)(2,1)S(1)} %get-tuple-element.26.text), custom_call_target="tpu_custom_call" | custom-call | flops 1048576 | bytes 65536 | tf_op jit(solution)/shard_map/offer/pallas_call | solution.py:430
  4.0 2.7 %collective-permute-start = (bf16[72,1536]{1,0:T(8,128)(2,1)S(1)}, bf16[72,1536]{1,0:T(8,128)(2,1)S(1)}, u32[]{:S(2)}, u32[]{:S(2)}) collective-permute-start(bf16[72,1536]{1,0:T(8,128)(2,1)S(1)} %offer.1), channel_id=1, source_target_pairs={{0,8},{4,12},{8,0},{12,4},{1,9},{5,13},{9,1},{13,5},{2,10},{6,14},... | collective-permute-start | bytes 663560 | tf_op jit(solution)/shard_map/ppermute | solution.py:470
  6.7 0.8 %collective-permute-start.1 = (bf16[32,1536]{1,0:T(8,128)(2,1)S(1)}, bf16[32,1536]{1,0:T(8,128)(2,1)S(1)}, u32[]{:S(2)}, u32[]{:S(2)}) collective-permute-start(bf16[32,1536]{1,0:T(8,128)(2,1)S(1)} %get-tuple-element.27), channel_id=1, source_target_pairs={{4,8},{8,4},{5,9},{9,5},{6,10},{10,6},{7,11},{11,7},{20,24},{24,20... | collective-permute-start | bytes 294920 | tf_op jit(solution)/shard_map/ppermute | solution.py:461
  7.5 1.6 %collective-permute-start.5 = (bf16[64,1536]{1,0:T(8,128)(2,1)S(1)}, bf16[64,1536]{1,0:T(8,128)(2,1)S(1)}, u32[]{:S(2)}, u32[]{:S(2)}) collective-permute-start(bf16[64,1536]{1,0:T(8,128)(2,1)S(1)} %get-tuple-element.26.text), channel_id=1, source_target_pairs={{0,1},{1,2},{2,3},{3,0},{4,5},{5,6},{6,7},{7,4},{8,9},{9,10},{10,1... | collective-permute-start | bytes 589832 | tf_op jit(solution)/shard_map/ppermute | solution.py:459
  9.1 2.2 %collective-permute-start.6 = (bf16[64,1536]{1,0:T(8,128)(2,1)S(1)}, bf16[64,1536]{1,0:T(8,128)(2,1)S(1)}, u32[]{:S(2)}, u32[]{:S(2)}) collective-permute-start(bf16[64,1536]{1,0:T(8,128)(2,1)S(1)} %get-tuple-element.26.text), channel_id=1, source_target_pairs={{0,3},{1,0},{2,1},{3,2},{4,7},{5,4},{6,5},{7,6},{8,11},{9,8},{10,9... | collective-permute-start | bytes 589832 | tf_op jit(solution)/shard_map/ppermute | solution.py:459
  11.4 1.3 %collective-permute-done.across = bf16[72,1536]{1,0:T(8,128)(2,1)S(1)} collective-permute-done((bf16[72,1536]{1,0:T(8,128)(2,1)S(1)}, bf16[72,1536]{1,0:T(8,128)(2,1)S(1)}, u32[]{:S(2)}, u32[]{:S(2)}) %collective-permute-start) | collective-permute-done | bytes 221216 | tf_op jit(solution)/shard_map/ppermute | solution.py:470
  12.9 2.9 %collective-permute-start.13 = (bf16[512,1152]{1,0:T(8,128)(2,1)S(1)}, bf16[512,1152]{1,0:T(8,128)(2,1)S(1)}, u32[]{:S(2)}, u32[]{:S(2)}) collective-permute-start(bf16[512,1152]{1,0:T(8,128)(2,1)S(1)} %get-tuple-element.32), channel_id=1, source_target_pairs={{0,8},{4,12},{8,0},{12,4},{1,9},{5,13},{9,1},{13,5},{2,10},{6,14},... | collective-permute-start | bytes 3538952 | tf_op jit(solution)/shard_map/ppermute | solution.py:475
  15.7 0.5 %collective-permute-done.5.refs_0_ = bf16[64,1536]{1,0:T(8,128)(2,1)S(1)} collective-permute-done((bf16[64,1536]{1,0:T(8,128)(2,1)S(1)}, bf16[64,1536]{1,0:T(8,128)(2,1)S(1)}, u32[]{:S(2)}, u32[]{:S(2)}) %collective-permute-start.5) | collective-permute-done | bytes 196640 | tf_op jit(solution)/shard_map/ppermute | solution.py:459
  16.3 4.5 %collective-permute-done.6.refs_1_.refs_0_ = bf16[64,1536]{1,0:T(8,128)(2,1)S(1)} collective-permute-done((bf16[64,1536]{1,0:T(8,128)(2,1)S(1)}, bf16[64,1536]{1,0:T(8,128)(2,1)S(1)}, u32[]{:S(2)}, u32[]{:S(2)}) %collective-permute-start.6) | collective-permute-done | bytes 196640 | tf_op jit(solution)/shard_map/ppermute | solution.py:459
  21.6 2.0 %collective-permute-start.10 = (bf16[80,1536]{1,0:T(8,128)(2,1)S(1)}, bf16[80,1536]{1,0:T(8,128)(2,1)S(1)}, u32[]{:S(2)}, u32[]{:S(2)}) collective-permute-start(bf16[80,1536]{1,0:T(8,128)(2,1)S(1)} %get-tuple-element.36), channel_id=1, source_target_pairs={{0,3},{1,0},{2,1},{3,2},{4,7},{5,4},{6,5},{7,6},{8,11},{9,8},{10,9... | collective-permute-start | bytes 737288 | tf_op jit(solution)/shard_map/ppermute | solution.py:488
  23.7 6.3 %collective-permute-done.10.right.refs_1_ = bf16[80,1536]{1,0:T(8,128)(2,1)S(1)} collective-permute-done((bf16[80,1536]{1,0:T(8,128)(2,1)S(1)}, bf16[80,1536]{1,0:T(8,128)(2,1)S(1)}, u32[]{:S(2)}, u32[]{:S(2)}) %collective-permute-start.10) | collective-permute-done | bytes 245792 | tf_op jit(solution)/shard_map/ppermute | solution.py:488
  30.0 1.3 %collective-permute-start.15 = (bf16[128,1536]{1,0:T(8,128)(2,1)S(1)}, bf16[128,1536]{1,0:T(8,128)(2,1)S(1)}, u32[]{:S(2)}, u32[]{:S(2)}) collective-permute-start(bf16[128,1536]{1,0:T(8,128)(2,1)S(1)} %pair.3), channel_id=1, source_target_pairs={{1,0},{2,1},{5,4},{6,5},{9,8},{10,9},{13,12},{14,13},{17,16},{18,1... | collective-permute-start | bytes 1179656 | tf_op jit(solution)/shard_map/ppermute | solution.py:497
  31.3 4.4 %collective-permute-done.8.left.refs_1_ = bf16[80,1536]{1,0:T(8,128)(2,1)S(1)} collective-permute-done((bf16[80,1536]{1,0:T(8,128)(2,1)S(1)}, bf16[80,1536]{1,0:T(8,128)(2,1)S(1)}, u32[]{:S(2)}, u32[]{:S(2)}) %collective-permute-start.8) | collective-permute-done | bytes 245792 | tf_op jit(solution)/shard_map/ppermute | solution.py:487
  35.7 0.7 %collective-permute-start.14 = (bf16[128,1536]{1,0:T(8,128)(2,1)S(1)}, bf16[128,1536]{1,0:T(8,128)(2,1)S(1)}, u32[]{:S(2)}, u32[]{:S(2)}) collective-permute-start(bf16[128,1536]{1,0:T(8,128)(2,1)S(1)} %pair.2), channel_id=1, source_target_pairs={{1,2},{2,3},{5,6},{6,7},{9,10},{10,11},{13,14},{14,15},{17,18},{18... | collective-permute-start | bytes 1179656 | tf_op jit(solution)/shard_map/ppermute | solution.py:496
  36.6 1.4 %collective-permute-done.9.left_mate = bf16[80,1536]{1,0:T(8,128)(2,1)S(1)} collective-permute-done((bf16[80,1536]{1,0:T(8,128)(2,1)S(1)}, bf16[80,1536]{1,0:T(8,128)(2,1)S(1)}, u32[]{:S(2)}, u32[]{:S(2)}) %collective-permute-start.9) | collective-permute-done | bytes 245792 | tf_op jit(solution)/shard_map/ppermute | solution.py:422
  38.0 3.1 %early.1 = (f32[256,1536]{1,0:T(8,128)S(1)}, f32[256,1536]{1,0:T(8,128)S(1)}, f32[256,1536]{1,0:T(8,128)S(1)}) custom-call(s32[2,1,2]{2,1,0:T(1,128)S(1)} %copy-done.4, bf16[256,1536]{1,0:T(8,128)(2,1)S(1)} %bitcast.7, bf16[256,1536]{1,0:T(8,128)(2,1)S(1)} %bitcast.10, bf16[256,1536]{1,0:T(8,128)(2,1)S(1)} %bitcast.6, ...), custom_call_target="tpu_custom_call" | custom-call | flops 1048576 | bytes 65536 | tf_op jit(solution)/shard_map/early/pallas_call | solution.py:430
  41.2 2.9 %collective-permute-done.15.lower = bf16[128,1536]{1,0:T(8,128)(2,1)S(1)} collective-permute-done((bf16[128,1536]{1,0:T(8,128)(2,1)S(1)}, bf16[128,1536]{1,0:T(8,128)(2,1)S(1)}, u32[]{:S(2)}, u32[]{:S(2)}) %collective-permute-start.15) | collective-permute-done | bytes 393248 | tf_op jit(solution)/shard_map/ppermute | solution.py:497
  44.7 1.3 %term.1.refs_5_ = f32[256,1536]{1,0:T(8,128)S(1)} custom-call(bf16[8,32,1536]{2,1,0:T(8,128)(2,1)S(1)} %copy-done, bf16[32,1536]{1,0:T(8,128)(2,1)S(1)} %collective-permute-done.2.beside, bf16[32,1536]{1,0:T(8,128)(2,1)S(1)} %collective-permute-done.1.diagonal, bf16[80,1536]{1,0:T(8,128)(2,1)S(1)} %collective-permute-done.8.left.refs_1_, ...), custom_call_target="tpu_custom_call" | custom-call | flops 1048576 | bytes 65536 | tf_op jit(solution)/shard_map/term/pallas_call | solution.py:430
  46.1 3.6 %late0.1.refs_10_ = f32[256,1536]{1,0:T(8,128)} custom-call(s32[1,1,2]{2,1,0:T(1,128)S(1)} %copy-done.5, s32[2,1,2]{2,1,0:T(1,128)S(1)} %copy-done.6, s32[2,1,2]{2,1,0:T(1,128)S(1)} %copy-done.4, bf16[256,1536]{1,0:T(8,128)(2,1)S(1)} %bitcast.8, f32[256,1536]{1,0:T(8,128)S(1)} %get-tuple-element.37.refs_0_, f32[256,1536]{1,0:T(8,128)S(1)} %get-tuple-element.38.refs_1_, ...), custom_call_target="tpu_custom_call" | custom-call | flops 1048576 | bytes 65536 | tf_op jit(solution)/shard_map/late0/pallas_call | solution.py:526
  49.6 0.8 %collective-permute-done.12.refs_4_ = bf16[512,384]{1,0:T(8,128)(2,1)S(1)} collective-permute-done((bf16[512,384]{1,0:T(8,128)(2,1)S(1)}, bf16[512,384]{1,0:T(8,128)(2,1)S(1)}, u32[]{:S(2)}, u32[]{:S(2)}) %collective-permute-start.12) | collective-permute-done | bytes 393248 | tf_op jit(solution)/shard_map/ppermute | solution.py:475
  50.4 2.0 %late1.1 = f32[256,1536]{1,0:T(8,128)} custom-call(s32[1,1,2]{2,1,0:T(1,128)S(1)} %copy-done.5, s32[2,1,2]{2,1,0:T(1,128)S(1)} %copy-done.6, s32[2,1,2]{2,1,0:T(1,128)S(1)} %copy-done.4, bf16[256,1536]{1,0:T(8,128)(2,1)S(1)} %bitcast.9, f32[256,1536]{1,0:T(8,128)S(1)} %get-tuple-element.37.refs_0_, ...), custom_call_target="tpu_custom_call", output_to_operand_aliasing={{}: (14, {})} | custom-call | flops 1048576 | bytes 65536 | tf_op jit(solution)/shard_map/late1/pallas_call | solution.py:526
  (38 shorter events, 2.3 us)
Async XLA Ops:
  0.0 3.4 %copy-start.5 = (s32[1,1,2]{2,1,0:T(1,128)S(1)}, s32[1,1,2]{2,1,0:T(1,128)}, u32[]{:S(2)}) copy-start(s32[1,1,2]{2,1,0:T(1,128)} %reads_ref.5) | copy-start | bytes 28
  1.6 1.5 %collective-permute-start.2 = (bf16[32,1536]{1,0:T(8,128)(2,1)S(1)}, bf16[32,1536]{1,0:T(8,128)(2,1)S(1)}, u32[]{:S(2)}, u32[]{:S(2)}) collective-permute-start(bf16[32,1536]{1,0:T(8,128)(2,1)S(1)} %get-tuple-element.30), channel_id=1, source_target_pairs={{0,4},{4,0},{8,12},{12,8},{1,5},{5,1},{9,13},{13,9},{2,6},{6,2},{1... | collective-permute-start | bytes 294920 | tf_op jit(solution)/shard_map/ppermute | solution.py:422
  3.0 9.6 %collective-permute-start.3 = (bf16[512,1536]{1,0:T(8,128)(2,1)S(1)}, bf16[512,1536]{1,0:T(8,128)(2,1)S(1)}, u32[]{:S(2)}, u32[]{:S(2)}) collective-permute-start(bf16[512,1536]{1,0:T(8,128)(2,1)S(1)} %get-tuple-element.31.stale), channel_id=1, source_target_pairs={{0,4},{4,0},{8,12},{12,8},{1,5},{5,1},{9,13},{13,9},{2,6},{6,2},{1... | collective-permute-start | bytes 4718600 | tf_op jit(solution)/shard_map/ppermute | solution.py:422
  4.0 8.7 %collective-permute-start = (bf16[72,1536]{1,0:T(8,128)(2,1)S(1)}, bf16[72,1536]{1,0:T(8,128)(2,1)S(1)}, u32[]{:S(2)}, u32[]{:S(2)}) collective-permute-start(bf16[72,1536]{1,0:T(8,128)(2,1)S(1)} %offer.1), channel_id=1, source_target_pairs={{0,8},{4,12},{8,0},{12,4},{1,9},{5,13},{9,1},{13,5},{2,10},{6,14},... | collective-permute-start | bytes 663560 | tf_op jit(solution)/shard_map/ppermute | solution.py:470
  6.7 14.7 %copy-start = (bf16[8,32,1536]{2,1,0:T(8,128)(2,1)S(1)}, bf16[8,32,1536]{2,1,0:T(8,128)(2,1)}, u32[]{:S(2)}) copy-start(bf16[8,32,1536]{2,1,0:T(8,128)(2,1)} %cells.5) | copy-start | bytes 2359300
  6.7 4.7 %collective-permute-start.1 = (bf16[32,1536]{1,0:T(8,128)(2,1)S(1)}, bf16[32,1536]{1,0:T(8,128)(2,1)S(1)}, u32[]{:S(2)}, u32[]{:S(2)}) collective-permute-start(bf16[32,1536]{1,0:T(8,128)(2,1)S(1)} %get-tuple-element.27), channel_id=1, source_target_pairs={{4,8},{8,4},{5,9},{9,5},{6,10},{10,6},{7,11},{11,7},{20,24},{24,20... | collective-permute-start | bytes 294920 | tf_op jit(solution)/shard_map/ppermute | solution.py:461
  7.5 8.8 %collective-permute-start.5 = (bf16[64,1536]{1,0:T(8,128)(2,1)S(1)}, bf16[64,1536]{1,0:T(8,128)(2,1)S(1)}, u32[]{:S(2)}, u32[]{:S(2)}) collective-permute-start(bf16[64,1536]{1,0:T(8,128)(2,1)S(1)} %get-tuple-element.26.text), channel_id=1, source_target_pairs={{0,1},{1,2},{2,3},{3,0},{4,5},{5,6},{6,7},{7,4},{8,9},{9,10},{10,1... | collective-permute-start | bytes 589832 | tf_op jit(solution)/shard_map/ppermute | solution.py:459
  9.1 11.7 %collective-permute-start.6 = (bf16[64,1536]{1,0:T(8,128)(2,1)S(1)}, bf16[64,1536]{1,0:T(8,128)(2,1)S(1)}, u32[]{:S(2)}, u32[]{:S(2)}) collective-permute-start(bf16[64,1536]{1,0:T(8,128)(2,1)S(1)} %get-tuple-element.26.text), channel_id=1, source_target_pairs={{0,3},{1,0},{2,1},{3,2},{4,7},{5,4},{6,5},{7,6},{8,11},{9,8},{10,9... | collective-permute-start | bytes 589832 | tf_op jit(solution)/shard_map/ppermute | solution.py:459
  12.9 33.2 %collective-permute-start.13 = (bf16[512,1152]{1,0:T(8,128)(2,1)S(1)}, bf16[512,1152]{1,0:T(8,128)(2,1)S(1)}, u32[]{:S(2)}, u32[]{:S(2)}) collective-permute-start(bf16[512,1152]{1,0:T(8,128)(2,1)S(1)} %get-tuple-element.32), channel_id=1, source_target_pairs={{0,8},{4,12},{8,0},{12,4},{1,9},{5,13},{9,1},{13,5},{2,10},{6,14},... | collective-permute-start | bytes 3538952 | tf_op jit(solution)/shard_map/ppermute | solution.py:475
  20.8 17.2 %copy-start.1 = (bf16[8,32,1536]{2,1,0:T(8,128)(2,1)S(1)}, bf16[8,32,1536]{2,1,0:T(8,128)(2,1)}, u32[]{:S(2)}) copy-start(bf16[8,32,1536]{2,1,0:T(8,128)(2,1)} %param.11) | copy-start | bytes 2359300
  20.8 17.2 %copy-start.2 = (bf16[8,32,1536]{2,1,0:T(8,128)(2,1)S(1)}, bf16[8,32,1536]{2,1,0:T(8,128)(2,1)}, u32[]{:S(2)}) copy-start(bf16[8,32,1536]{2,1,0:T(8,128)(2,1)} %param.12) | copy-start | bytes 2359300
  20.8 17.2 %copy-start.4 = (s32[2,1,2]{2,1,0:T(1,128)S(1)}, s32[2,1,2]{2,1,0:T(1,128)}, u32[]{:S(2)}) copy-start(s32[2,1,2]{2,1,0:T(1,128)} %text_ref.5) | copy-start | bytes 52
  20.8 9.2 %collective-permute-start.7 = (bf16[128,1536]{1,0:T(8,128)(2,1)S(1)}, bf16[128,1536]{1,0:T(8,128)(2,1)S(1)}, u32[]{:S(2)}, u32[]{:S(2)}) collective-permute-start(bf16[128,1536]{1,0:T(8,128)(2,1)S(1)} %bundle.1.early), channel_id=1, source_target_pairs={{0,4},{4,0},{8,12},{12,8},{1,5},{5,1},{9,13},{13,9},{2,6},{6,2},{1... | collective-permute-start | bytes 1179656 | tf_op jit(solution)/shard_map/ppermute | solution.py:422
  21.5 9.8 %collective-permute-start.4 = (bf16[128,1536]{1,0:T(8,128)(2,1)S(1)}, bf16[128,1536]{1,0:T(8,128)(2,1)S(1)}, u32[]{:S(2)}, u32[]{:S(2)}) collective-permute-start(bf16[128,1536]{1,0:T(8,128)(2,1)S(1)} %get-tuple-element.34.both), channel_id=1, source_target_pairs={{0,4},{4,0},{8,12},{12,8},{1,5},{5,1},{9,13},{13,9},{2,6},{6,2},{1... | collective-permute-start | bytes 1179656 | tf_op jit(solution)/shard_map/ppermute | solution.py:422
  21.6 8.3 %collective-permute-start.10 = (bf16[80,1536]{1,0:T(8,128)(2,1)S(1)}, bf16[80,1536]{1,0:T(8,128)(2,1)S(1)}, u32[]{:S(2)}, u32[]{:S(2)}) collective-permute-start(bf16[80,1536]{1,0:T(8,128)(2,1)S(1)} %get-tuple-element.36), channel_id=1, source_target_pairs={{0,3},{1,0},{2,1},{3,2},{4,7},{5,4},{6,5},{7,6},{8,11},{9,8},{10,9... | collective-permute-start | bytes 737288 | tf_op jit(solution)/shard_map/ppermute | solution.py:488
  23.7 12.1 %collective-permute-start.8 = (bf16[80,1536]{1,0:T(8,128)(2,1)S(1)}, bf16[80,1536]{1,0:T(8,128)(2,1)S(1)}, u32[]{:S(2)}, u32[]{:S(2)}) collective-permute-start(bf16[80,1536]{1,0:T(8,128)(2,1)S(1)} %get-tuple-element.35), channel_id=1, source_target_pairs={{0,1},{1,2},{2,3},{3,0},{4,5},{5,6},{6,7},{7,4},{8,9},{9,10},{10,1... | collective-permute-start | bytes 737288 | tf_op jit(solution)/shard_map/ppermute | solution.py:487
  30.0 6.5 %collective-permute-start.11 = (bf16[80,1536]{1,0:T(8,128)(2,1)S(1)}, bf16[80,1536]{1,0:T(8,128)(2,1)S(1)}, u32[]{:S(2)}, u32[]{:S(2)}) collective-permute-start(bf16[80,1536]{1,0:T(8,128)(2,1)S(1)} %collective-permute-done.10.right.refs_1_), channel_id=1, source_target_pairs={{0,4},{4,0},{8,12},{12,8},{1,5},{5,1},{9,13},{13,9},{2,6},{6,2},{1... | collective-permute-start | bytes 737288 | tf_op jit(solution)/shard_map/ppermute | solution.py:422
  30.0 14.1 %collective-permute-start.15 = (bf16[128,1536]{1,0:T(8,128)(2,1)S(1)}, bf16[128,1536]{1,0:T(8,128)(2,1)S(1)}, u32[]{:S(2)}, u32[]{:S(2)}) collective-permute-start(bf16[128,1536]{1,0:T(8,128)(2,1)S(1)} %pair.3), channel_id=1, source_target_pairs={{1,0},{2,1},{5,4},{6,5},{9,8},{10,9},{13,12},{14,13},{17,16},{18,1... | collective-permute-start | bytes 1179656 | tf_op jit(solution)/shard_map/ppermute | solution.py:497
  35.7 8.3 %collective-permute-start.14 = (bf16[128,1536]{1,0:T(8,128)(2,1)S(1)}, bf16[128,1536]{1,0:T(8,128)(2,1)S(1)}, u32[]{:S(2)}, u32[]{:S(2)}) collective-permute-start(bf16[128,1536]{1,0:T(8,128)(2,1)S(1)} %pair.2), channel_id=1, source_target_pairs={{1,2},{2,3},{5,6},{6,7},{9,10},{10,11},{13,14},{14,15},{17,18},{18... | collective-permute-start | bytes 1179656 | tf_op jit(solution)/shard_map/ppermute | solution.py:496
  36.4 1.6 %collective-permute-start.9 = (bf16[80,1536]{1,0:T(8,128)(2,1)S(1)}, bf16[80,1536]{1,0:T(8,128)(2,1)S(1)}, u32[]{:S(2)}, u32[]{:S(2)}) collective-permute-start(bf16[80,1536]{1,0:T(8,128)(2,1)S(1)} %collective-permute-done.8.left.refs_1_), channel_id=1, source_target_pairs={{0,4},{4,0},{8,12},{12,8},{1,5},{5,1},{9,13},{13,9},{2,6},{6,2},{1... | collective-permute-start | bytes 737288 | tf_op jit(solution)/shard_map/ppermute | solution.py:422
  36.5 13.9 %collective-permute-start.12 = (bf16[512,384]{1,0:T(8,128)(2,1)S(1)}, bf16[512,384]{1,0:T(8,128)(2,1)S(1)}, u32[]{:S(2)}, u32[]{:S(2)}) collective-permute-start(bf16[512,384]{1,0:T(8,128)(2,1)S(1)} %get-tuple-element.40), channel_id=1, source_target_pairs={{0,8},{4,12},{8,0},{12,4},{1,9},{5,13},{9,1},{13,5},{2,10},{6,14},... | collective-permute-start | bytes 1179656 | tf_op jit(solution)/shard_map/ppermute | solution.py:475
  38.0 6.7 %copy-start.3 = (f32[3,3,1536]{2,1,0:T(4,128)S(1)}, f32[3,3,1536]{2,1,0:T(4,128)}, u32[]{:S(2)}) copy-start(f32[3,3,1536]{2,1,0:T(4,128)} %weights.1) | copy-start | bytes 165892
  44.1 1.9 %collective-permute-start.16 = (bf16[64,1536]{1,0:T(8,128)(2,1)S(1)}, bf16[64,1536]{1,0:T(8,128)(2,1)S(1)}, u32[]{:S(2)}, u32[]{:S(2)}) collective-permute-start(bf16[64,1536]{1,0:T(8,128)(2,1)S(1)} %get-tuple-element.44.refs_6_), channel_id=1, source_target_pairs={{0,4},{4,0},{8,12},{12,8},{1,5},{5,1},{9,13},{13,9},{2,6},{6,2},{1... | collective-permute-start | bytes 589832 | tf_op jit(solution)/shard_map/ppermute | solution.py:422
  44.3 1.7 %collective-permute-start.17 = (bf16[64,1536]{1,0:T(8,128)(2,1)S(1)}, bf16[64,1536]{1,0:T(8,128)(2,1)S(1)}, u32[]{:S(2)}, u32[]{:S(2)}) collective-permute-start(bf16[64,1536]{1,0:T(8,128)(2,1)S(1)} %get-tuple-element.45.refs_8_), channel_id=1, source_target_pairs={{0,4},{4,0},{8,12},{12,8},{1,5},{5,1},{9,13},{13,9},{2,6},{6,2},{1... | collective-permute-start | bytes 589832 | tf_op jit(solution)/shard_map/ppermute | solution.py:422
  (1 other events, 1.9 us)

commit v13 on v12

--- a/solution.py
+++ b/solution.py
@@ -14,7 +14,7 @@
 PER_BLOCK = BLOCK_ROWS * BLOCK_COLS
 SCORE_SCALE = 1.0 / math.sqrt(HEAD_DIM)
 EXP2_SCALE = SCORE_SCALE * math.log2(math.e)
-CHUNK_HEADS = (9, 3)
+CHUNK_HEADS = (10, 2)
 GROUP = 8
 VMEM_LIMIT = 24 * 1024 * 1024
 
@@ -468,7 +468,7 @@
         specs=[pl.BlockSpec(memory_space=pltpu.SMEM), in_vmem],
     )
     across = lax.ppermute(offer, "rows", swap)
-    passed = to_mate(after(stale, beside))
+    passed = to_mate(stale)
     packed = local(
         send_kernel, "send", chunks, after(across, diagonal), stale, passed
     )

time: 53.2 us -> 57.8 us (1.086)
  the two profiles are of different devices: /device:TPU:0 before, /device:TPU:23 now
where the time goes in v13:
time: 57.8 us; the launch traced here: 57.6 us
  waiting for transfers between devices  26 us (45%)
  starting transfers between devices  18.6 us (32%)
  Pallas kernels  12.7 us (22%)
    ppermute x8, starting transfers between devices, to_mate(): return lax.ppermute(values, 'rows', mates)  7.89 us
    ppermute x2, waiting for transfers between devices, body(): near_parts = [lax.ppermute(text, 'cols', p) for p in (forward, backward)]  7.59 us
    pallas_call x10, Pallas kernels, local(): pl.pallas_call(kernel, out_shape=shapes, in_specs=specs or [in_vmem] * le...  7.03 us
    ppermute x1, waiting for transfers between devices, body(): across = lax.ppermute(offer, 'rows', swap)  5.98 us
    pallas_call x2, Pallas kernels, body(): pl.pallas_call(functools.partial(late_kernel, first_head), out_shape=jax....  5.69 us
    ppermute x1, waiting for transfers between devices, body(): right = lax.ppermute(minus, 'cols', backward)  5.62 us
    ppermute x1, waiting for transfers between devices, body(): left = lax.ppermute(plus, 'cols', forward)  3.14 us
    ppermute x1, starting transfers between devices, body(): lower = lax.ppermute(lower, 'cols', [(1, 0), (2, 1)])  2.94 us
  transfers between devices with their start and end apart: 18, of which 9 were waited for; matrix products, arithmetic and copies ran while one was open for 0% of the time, Pallas kernels for 16%

profile of v13, /device:TPU:23, one launch (start us, length us, event | category | flops | bytes accessed | tf_op | source)
XLA Modules:
  0.0 57.6 jit_solution(7253682102875624794)
XLA Ops:
  0.0 1.6 %pack.1 = (bf16[512,1536]{1,0:T(8,128)(2,1)S(1)}, bf16[32,1536]{1,0:T(8,128)(2,1)S(1)}, bf16[32,1536]{1,0:T(8,128)(2,1)S(1)}, bf16[64,1536]{1,0:T(8,128)(2,1)S(1)}) custom-call(bf16[256,1536]{1,0:T(8,128)(2,1)} %bitcast.11, bf16[256,1536]{1,0:T(8,128)(2,1)} %bitcast.12, bf16[8,32,1536]{2,1,0:T(8,128)(2,1)} %cells.5, bf16[32,1536]{1,0:T(8,128)(2,1)} %text_k.1, ...), custom_call_target="tpu_custom_call" | custom-call | flops 1048576 | bytes 65536 | tf_op jit(solution)/shard_map/pack/pallas_call | solution.py:430
  1.6 0.7 %collective-permute-start.2 = (bf16[512,1536]{1,0:T(8,128)(2,1)S(1)}, bf16[512,1536]{1,0:T(8,128)(2,1)S(1)}, u32[]{:S(2)}, u32[]{:S(2)}) collective-permute-start(bf16[512,1536]{1,0:T(8,128)(2,1)S(1)} %get-tuple-element.28.stale), channel_id=1, source_target_pairs={{0,4},{4,0},{8,12},{12,8},{1,5},{5,1},{9,13},{13,9},{2,6},{6,2},{1... | collective-permute-start | bytes 4718600 | tf_op jit(solution)/shard_map/ppermute | solution.py:422
  2.3 0.6 offer.1
  3.2 0.8 %collective-permute-start.1 = (bf16[32,1536]{1,0:T(8,128)(2,1)S(1)}, bf16[32,1536]{1,0:T(8,128)(2,1)S(1)}, u32[]{:S(2)}, u32[]{:S(2)}) collective-permute-start(bf16[32,1536]{1,0:T(8,128)(2,1)S(1)} %get-tuple-element.26), channel_id=1, source_target_pairs={{4,8},{8,4},{5,9},{9,5},{6,10},{10,6},{7,11},{11,7},{20,24},{24,20... | collective-permute-start | bytes 294920 | tf_op jit(solution)/shard_map/ppermute | solution.py:461
  4.0 6.0 %collective-permute-done.across = bf16[72,1536]{1,0:T(8,128)(2,1)S(1)} collective-permute-done((bf16[72,1536]{1,0:T(8,128)(2,1)S(1)}, bf16[72,1536]{1,0:T(8,128)(2,1)S(1)}, u32[]{:S(2)}, u32[]{:S(2)}) %collective-permute-start) | collective-permute-done | bytes 221216 | tf_op jit(solution)/shard_map/ppermute | solution.py:470
  10.2 1.5 %collective-permute-start.13 = (bf16[512,1280]{1,0:T(8,128)(2,1)S(1)}, bf16[512,1280]{1,0:T(8,128)(2,1)S(1)}, u32[]{:S(2)}, u32[]{:S(2)}) collective-permute-start(bf16[512,1280]{1,0:T(8,128)(2,1)S(1)} %get-tuple-element.29), channel_id=1, source_target_pairs={{0,8},{4,12},{8,0},{12,4},{1,9},{5,13},{9,1},{13,5},{2,10},{6,14},... | collective-permute-start | bytes 3932168 | tf_op jit(solution)/shard_map/ppermute | solution.py:475
  11.7 1.3 %collective-permute-start.5 = (bf16[64,1536]{1,0:T(8,128)(2,1)S(1)}, bf16[64,1536]{1,0:T(8,128)(2,1)S(1)}, u32[]{:S(2)}, u32[]{:S(2)}) collective-permute-start(bf16[64,1536]{1,0:T(8,128)(2,1)S(1)} %get-tuple-element.25.text), channel_id=1, source_target_pairs={{0,1},{1,2},{2,3},{3,0},{4,5},{5,6},{6,7},{7,4},{8,9},{9,10},{10,1... | collective-permute-start | bytes 589832 | tf_op jit(solution)/shard_map/ppermute | solution.py:459
  13.2 1.1 %collective-permute-start.3 = (bf16[32,1536]{1,0:T(8,128)(2,1)S(1)}, bf16[32,1536]{1,0:T(8,128)(2,1)S(1)}, u32[]{:S(2)}, u32[]{:S(2)}) collective-permute-start(bf16[32,1536]{1,0:T(8,128)(2,1)S(1)} %get-tuple-element.31), channel_id=1, source_target_pairs={{0,4},{4,0},{8,12},{12,8},{1,5},{5,1},{9,13},{13,9},{2,6},{6,2},{1... | collective-permute-start | bytes 294920 | tf_op jit(solution)/shard_map/ppermute | solution.py:422
  14.2 3.5 %collective-permute-done.5.refs_0_ = bf16[64,1536]{1,0:T(8,128)(2,1)S(1)} collective-permute-done((bf16[64,1536]{1,0:T(8,128)(2,1)S(1)}, bf16[64,1536]{1,0:T(8,128)(2,1)S(1)}, u32[]{:S(2)}, u32[]{:S(2)}) %collective-permute-start.5) | collective-permute-done | bytes 196640 | tf_op jit(solution)/shard_map/ppermute | solution.py:459
  17.8 4.1 %collective-permute-done.6.refs_1_.refs_0_ = bf16[64,1536]{1,0:T(8,128)(2,1)S(1)} collective-permute-done((bf16[64,1536]{1,0:T(8,128)(2,1)S(1)}, bf16[64,1536]{1,0:T(8,128)(2,1)S(1)}, u32[]{:S(2)}, u32[]{:S(2)}) %collective-permute-start.6) | collective-permute-done | bytes 196640 | tf_op jit(solution)/shard_map/ppermute | solution.py:459
  21.9 1.5 %collective-permute-start.7 = (bf16[128,1536]{1,0:T(8,128)(2,1)S(1)}, bf16[128,1536]{1,0:T(8,128)(2,1)S(1)}, u32[]{:S(2)}, u32[]{:S(2)}) collective-permute-start(bf16[128,1536]{1,0:T(8,128)(2,1)S(1)} %bundle.1.early), channel_id=1, source_target_pairs={{0,4},{4,0},{8,12},{12,8},{1,5},{5,1},{9,13},{13,9},{2,6},{6,2},{1... | collective-permute-start | bytes 1179656 | tf_op jit(solution)/shard_map/ppermute | solution.py:422
  23.6 1.0 %collective-permute-start.10 = (bf16[80,1536]{1,0:T(8,128)(2,1)S(1)}, bf16[80,1536]{1,0:T(8,128)(2,1)S(1)}, u32[]{:S(2)}, u32[]{:S(2)}) collective-permute-start(bf16[80,1536]{1,0:T(8,128)(2,1)S(1)} %get-tuple-element.34), channel_id=1, source_target_pairs={{0,3},{1,0},{2,1},{3,2},{4,7},{5,4},{6,5},{7,6},{8,11},{9,8},{10,9... | collective-permute-start | bytes 737288 | tf_op jit(solution)/shard_map/ppermute | solution.py:488
  25.1 5.6 %collective-permute-done.10.right.refs_1_ = bf16[80,1536]{1,0:T(8,128)(2,1)S(1)} collective-permute-done((bf16[80,1536]{1,0:T(8,128)(2,1)S(1)}, bf16[80,1536]{1,0:T(8,128)(2,1)S(1)}, u32[]{:S(2)}, u32[]{:S(2)}) %collective-permute-start.10) | collective-permute-done | bytes 245792 | tf_op jit(solution)/shard_map/ppermute | solution.py:488
  30.8 2.9 %collective-permute-start.15 = (bf16[128,1536]{1,0:T(8,128)(2,1)S(1)}, bf16[128,1536]{1,0:T(8,128)(2,1)S(1)}, u32[]{:S(2)}, u32[]{:S(2)}) collective-permute-start(bf16[128,1536]{1,0:T(8,128)(2,1)S(1)} %pair.3), channel_id=1, source_target_pairs={{1,0},{2,1},{5,4},{6,5},{9,8},{10,9},{13,12},{14,13},{17,16},{18,1... | collective-permute-start | bytes 1179656 | tf_op jit(solution)/shard_map/ppermute | solution.py:497
  33.8 3.1 %collective-permute-done.8.left.refs_1_ = bf16[80,1536]{1,0:T(8,128)(2,1)S(1)} collective-permute-done((bf16[80,1536]{1,0:T(8,128)(2,1)S(1)}, bf16[80,1536]{1,0:T(8,128)(2,1)S(1)}, u32[]{:S(2)}, u32[]{:S(2)}) %collective-permute-start.8) | collective-permute-done | bytes 245792 | tf_op jit(solution)/shard_map/ppermute | solution.py:487
  36.9 2.2 %collective-permute-start.14 = (bf16[128,1536]{1,0:T(8,128)(2,1)S(1)}, bf16[128,1536]{1,0:T(8,128)(2,1)S(1)}, u32[]{:S(2)}, u32[]{:S(2)}) collective-permute-start(bf16[128,1536]{1,0:T(8,128)(2,1)S(1)} %pair.2), channel_id=1, source_target_pairs={{1,2},{2,3},{5,6},{6,7},{9,10},{10,11},{13,14},{14,15},{17,18},{18... | collective-permute-start | bytes 1179656 | tf_op jit(solution)/shard_map/ppermute | solution.py:496
  39.1 1.9 %collective-permute-start.11 = (bf16[80,1536]{1,0:T(8,128)(2,1)S(1)}, bf16[80,1536]{1,0:T(8,128)(2,1)S(1)}, u32[]{:S(2)}, u32[]{:S(2)}) collective-permute-start(bf16[80,1536]{1,0:T(8,128)(2,1)S(1)} %collective-permute-done.10.right.refs_1_), channel_id=1, source_target_pairs={{0,4},{4,0},{8,12},{12,8},{1,5},{5,1},{9,13},{13,9},{2,6},{6,2},{1... | collective-permute-start | bytes 737288 | tf_op jit(solution)/shard_map/ppermute | solution.py:422
  41.1 1.1 %collective-permute-done.11.right_mate = bf16[80,1536]{1,0:T(8,128)(2,1)S(1)} collective-permute-done((bf16[80,1536]{1,0:T(8,128)(2,1)S(1)}, bf16[80,1536]{1,0:T(8,128)(2,1)S(1)}, u32[]{:S(2)}, u32[]{:S(2)}) %collective-permute-start.11) | collective-permute-done | bytes 245792 | tf_op jit(solution)/shard_map/ppermute | solution.py:422
  42.6 3.1 %early.1 = (f32[256,1536]{1,0:T(8,128)S(1)}, f32[256,1536]{1,0:T(8,128)S(1)}, f32[256,1536]{1,0:T(8,128)S(1)}) custom-call(s32[2,1,2]{2,1,0:T(1,128)S(1)} %copy-done.4, bf16[256,1536]{1,0:T(8,128)(2,1)S(1)} %bitcast.7, bf16[256,1536]{1,0:T(8,128)(2,1)S(1)} %bitcast.10, bf16[256,1536]{1,0:T(8,128)(2,1)S(1)} %bitcast.6, ...), custom_call_target="tpu_custom_call" | custom-call | flops 1048576 | bytes 65536 | tf_op jit(solution)/shard_map/early/pallas_call | solution.py:430
  45.7 2.3 %collective-permute-done.14.upper = bf16[128,1536]{1,0:T(8,128)(2,1)S(1)} collective-permute-done((bf16[128,1536]{1,0:T(8,128)(2,1)S(1)}, bf16[128,1536]{1,0:T(8,128)(2,1)S(1)}, u32[]{:S(2)}, u32[]{:S(2)}) %collective-permute-start.14) | collective-permute-done | bytes 393248 | tf_op jit(solution)/shard_map/ppermute | solution.py:496
  48.1 2.4 %collective-permute-start.16 = (bf16[64,1536]{1,0:T(8,128)(2,1)S(1)}, bf16[64,1536]{1,0:T(8,128)(2,1)S(1)}, u32[]{:S(2)}, u32[]{:S(2)}) collective-permute-start(bf16[64,1536]{1,0:T(8,128)(2,1)S(1)} %get-tuple-element.42.refs_6_), channel_id=1, source_target_pairs={{0,4},{4,0},{8,12},{12,8},{1,5},{5,1},{9,13},{13,9},{2,6},{6,2},{1... | collective-permute-start | bytes 589832 | tf_op jit(solution)/shard_map/ppermute | solution.py:422
  50.6 1.3 %term.1.refs_5_ = f32[256,1536]{1,0:T(8,128)S(1)} custom-call(bf16[8,32,1536]{2,1,0:T(8,128)(2,1)S(1)} %copy-done, bf16[32,1536]{1,0:T(8,128)(2,1)S(1)} %collective-permute-done.3.beside, bf16[32,1536]{1,0:T(8,128)(2,1)S(1)} %collective-permute-done.1.diagonal, bf16[80,1536]{1,0:T(8,128)(2,1)S(1)} %collective-permute-done.8.left.refs_1_, ...), custom_call_target="tpu_custom_call" | custom-call | flops 1048576 | bytes 65536 | tf_op jit(solution)/shard_map/term/pallas_call | solution.py:430
  51.9 3.8 %late0.1.refs_10_ = f32[256,1536]{1,0:T(8,128)} custom-call(s32[1,1,2]{2,1,0:T(1,128)S(1)} %copy-done.5, s32[2,1,2]{2,1,0:T(1,128)S(1)} %copy-done.6, s32[2,1,2]{2,1,0:T(1,128)S(1)} %copy-done.4, bf16[256,1536]{1,0:T(8,128)(2,1)S(1)} %bitcast.8, f32[256,1536]{1,0:T(8,128)S(1)} %get-tuple-element.35.refs_0_, f32[256,1536]{1,0:T(8,128)S(1)} %get-tuple-element.36.refs_1_, ...), custom_call_target="tpu_custom_call" | custom-call | flops 1048576 | bytes 65536 | tf_op jit(solution)/shard_map/late0/pallas_call | solution.py:526
  55.8 1.8 %late1.1 = f32[256,1536]{1,0:T(8,128)} custom-call(s32[1,1,2]{2,1,0:T(1,128)S(1)} %copy-done.5, s32[2,1,2]{2,1,0:T(1,128)S(1)} %copy-done.6, s32[2,1,2]{2,1,0:T(1,128)S(1)} %copy-done.4, bf16[256,1536]{1,0:T(8,128)(2,1)S(1)} %bitcast.9, f32[256,1536]{1,0:T(8,128)S(1)} %get-tuple-element.35.refs_0_, ...), custom_call_target="tpu_custom_call", output_to_operand_aliasing={{}: (14, {})} | custom-call | flops 1048576 | bytes 65536 | tf_op jit(solution)/shard_map/late1/pallas_call | solution.py:526
  (38 shorter events, 2.2 us)
Async XLA Ops:
  1.6 8.4 %collective-permute-start.2 = (bf16[512,1536]{1,0:T(8,128)(2,1)S(1)}, bf16[512,1536]{1,0:T(8,128)(2,1)S(1)}, u32[]{:S(2)}, u32[]{:S(2)}) collective-permute-start(bf16[512,1536]{1,0:T(8,128)(2,1)S(1)} %get-tuple-element.28.stale), channel_id=1, source_target_pairs={{0,4},{4,0},{8,12},{12,8},{1,5},{5,1},{9,13},{13,9},{2,6},{6,2},{1... | collective-permute-start | bytes 4718600 | tf_op jit(solution)/shard_map/ppermute | solution.py:422
  2.9 7.1 %collective-permute-start = (bf16[72,1536]{1,0:T(8,128)(2,1)S(1)}, bf16[72,1536]{1,0:T(8,128)(2,1)S(1)}, u32[]{:S(2)}, u32[]{:S(2)}) collective-permute-start(bf16[72,1536]{1,0:T(8,128)(2,1)S(1)} %offer.1), channel_id=1, source_target_pairs={{0,8},{4,12},{8,0},{12,4},{1,9},{5,13},{9,1},{13,5},{2,10},{6,14},... | collective-permute-start | bytes 663560 | tf_op jit(solution)/shard_map/ppermute | solution.py:470
  3.2 20.2 %copy-start = (bf16[8,32,1536]{2,1,0:T(8,128)(2,1)S(1)}, bf16[8,32,1536]{2,1,0:T(8,128)(2,1)}, u32[]{:S(2)}) copy-start(bf16[8,32,1536]{2,1,0:T(8,128)(2,1)} %cells.5) | copy-start | bytes 2359300
  3.2 0.8 %collective-permute-start.1 = (bf16[32,1536]{1,0:T(8,128)(2,1)S(1)}, bf16[32,1536]{1,0:T(8,128)(2,1)S(1)}, u32[]{:S(2)}, u32[]{:S(2)}) collective-permute-start(bf16[32,1536]{1,0:T(8,128)(2,1)S(1)} %get-tuple-element.26), channel_id=1, source_target_pairs={{4,8},{8,4},{5,9},{9,5},{6,10},{10,6},{7,11},{11,7},{20,24},{24,20... | collective-permute-start | bytes 294920 | tf_op jit(solution)/shard_map/ppermute | solution.py:461
  10.2 41.7 %collective-permute-start.13 = (bf16[512,1280]{1,0:T(8,128)(2,1)S(1)}, bf16[512,1280]{1,0:T(8,128)(2,1)S(1)}, u32[]{:S(2)}, u32[]{:S(2)}) collective-permute-start(bf16[512,1280]{1,0:T(8,128)(2,1)S(1)} %get-tuple-element.29), channel_id=1, source_target_pairs={{0,8},{4,12},{8,0},{12,4},{1,9},{5,13},{9,1},{13,5},{2,10},{6,14},... | collective-permute-start | bytes 3932168 | tf_op jit(solution)/shard_map/ppermute | solution.py:475
  11.7 6.1 %collective-permute-start.5 = (bf16[64,1536]{1,0:T(8,128)(2,1)S(1)}, bf16[64,1536]{1,0:T(8,128)(2,1)S(1)}, u32[]{:S(2)}, u32[]{:S(2)}) collective-permute-start(bf16[64,1536]{1,0:T(8,128)(2,1)S(1)} %get-tuple-element.25.text), channel_id=1, source_target_pairs={{0,1},{1,2},{2,3},{3,0},{4,5},{5,6},{6,7},{7,4},{8,9},{9,10},{10,1... | collective-permute-start | bytes 589832 | tf_op jit(solution)/shard_map/ppermute | solution.py:459
  13.0 8.8 %collective-permute-start.6 = (bf16[64,1536]{1,0:T(8,128)(2,1)S(1)}, bf16[64,1536]{1,0:T(8,128)(2,1)S(1)}, u32[]{:S(2)}, u32[]{:S(2)}) collective-permute-start(bf16[64,1536]{1,0:T(8,128)(2,1)S(1)} %get-tuple-element.25.text), channel_id=1, source_target_pairs={{0,3},{1,0},{2,1},{3,2},{4,7},{5,4},{6,5},{7,6},{8,11},{9,8},{10,9... | collective-permute-start | bytes 589832 | tf_op jit(solution)/shard_map/ppermute | solution.py:459
  13.2 10.2 %collective-permute-start.3 = (bf16[32,1536]{1,0:T(8,128)(2,1)S(1)}, bf16[32,1536]{1,0:T(8,128)(2,1)S(1)}, u32[]{:S(2)}, u32[]{:S(2)}) collective-permute-start(bf16[32,1536]{1,0:T(8,128)(2,1)S(1)} %get-tuple-element.31), channel_id=1, source_target_pairs={{0,4},{4,0},{8,12},{12,8},{1,5},{5,1},{9,13},{13,9},{2,6},{6,2},{1... | collective-permute-start | bytes 294920 | tf_op jit(solution)/shard_map/ppermute | solution.py:422
  21.9 20.7 %copy-start.1 = (bf16[8,32,1536]{2,1,0:T(8,128)(2,1)S(1)}, bf16[8,32,1536]{2,1,0:T(8,128)(2,1)}, u32[]{:S(2)}) copy-start(bf16[8,32,1536]{2,1,0:T(8,128)(2,1)} %param.11) | copy-start | bytes 2359300
  21.9 20.7 %copy-start.2 = (bf16[8,32,1536]{2,1,0:T(8,128)(2,1)S(1)}, bf16[8,32,1536]{2,1,0:T(8,128)(2,1)}, u32[]{:S(2)}) copy-start(bf16[8,32,1536]{2,1,0:T(8,128)(2,1)} %param.12) | copy-start | bytes 2359300
  21.9 20.7 %copy-start.4 = (s32[2,1,2]{2,1,0:T(1,128)S(1)}, s32[2,1,2]{2,1,0:T(1,128)}, u32[]{:S(2)}) copy-start(s32[2,1,2]{2,1,0:T(1,128)} %text_ref.5) | copy-start | bytes 52
  21.9 11.8 %collective-permute-start.7 = (bf16[128,1536]{1,0:T(8,128)(2,1)S(1)}, bf16[128,1536]{1,0:T(8,128)(2,1)S(1)}, u32[]{:S(2)}, u32[]{:S(2)}) collective-permute-start(bf16[128,1536]{1,0:T(8,128)(2,1)S(1)} %bundle.1.early), channel_id=1, source_target_pairs={{0,4},{4,0},{8,12},{12,8},{1,5},{5,1},{9,13},{13,9},{2,6},{6,2},{1... | collective-permute-start | bytes 1179656 | tf_op jit(solution)/shard_map/ppermute | solution.py:422
  23.5 10.2 %collective-permute-start.4 = (bf16[128,1536]{1,0:T(8,128)(2,1)S(1)}, bf16[128,1536]{1,0:T(8,128)(2,1)S(1)}, u32[]{:S(2)}, u32[]{:S(2)}) collective-permute-start(bf16[128,1536]{1,0:T(8,128)(2,1)S(1)} %get-tuple-element.32.both), channel_id=1, source_target_pairs={{0,4},{4,0},{8,12},{12,8},{1,5},{5,1},{9,13},{13,9},{2,6},{6,2},{1... | collective-permute-start | bytes 1179656 | tf_op jit(solution)/shard_map/ppermute | solution.py:422
  23.6 7.1 %collective-permute-start.10 = (bf16[80,1536]{1,0:T(8,128)(2,1)S(1)}, bf16[80,1536]{1,0:T(8,128)(2,1)S(1)}, u32[]{:S(2)}, u32[]{:S(2)}) collective-permute-start(bf16[80,1536]{1,0:T(8,128)(2,1)S(1)} %get-tuple-element.34), channel_id=1, source_target_pairs={{0,3},{1,0},{2,1},{3,2},{4,7},{5,4},{6,5},{7,6},{8,11},{9,8},{10,9... | collective-permute-start | bytes 737288 | tf_op jit(solution)/shard_map/ppermute | solution.py:488
  24.7 12.2 %collective-permute-start.8 = (bf16[80,1536]{1,0:T(8,128)(2,1)S(1)}, bf16[80,1536]{1,0:T(8,128)(2,1)S(1)}, u32[]{:S(2)}, u32[]{:S(2)}) collective-permute-start(bf16[80,1536]{1,0:T(8,128)(2,1)S(1)} %get-tuple-element.33), channel_id=1, source_target_pairs={{0,1},{1,2},{2,3},{3,0},{4,5},{5,6},{6,7},{7,4},{8,9},{9,10},{10,1... | collective-permute-start | bytes 737288 | tf_op jit(solution)/shard_map/ppermute | solution.py:487
  30.8 15.0 %collective-permute-start.15 = (bf16[128,1536]{1,0:T(8,128)(2,1)S(1)}, bf16[128,1536]{1,0:T(8,128)(2,1)S(1)}, u32[]{:S(2)}, u32[]{:S(2)}) collective-permute-start(bf16[128,1536]{1,0:T(8,128)(2,1)S(1)} %pair.3), channel_id=1, source_target_pairs={{1,0},{2,1},{5,4},{6,5},{9,8},{10,9},{13,12},{14,13},{17,16},{18,1... | collective-permute-start | bytes 1179656 | tf_op jit(solution)/shard_map/ppermute | solution.py:497
  36.9 11.1 %collective-permute-start.14 = (bf16[128,1536]{1,0:T(8,128)(2,1)S(1)}, bf16[128,1536]{1,0:T(8,128)(2,1)S(1)}, u32[]{:S(2)}, u32[]{:S(2)}) collective-permute-start(bf16[128,1536]{1,0:T(8,128)(2,1)S(1)} %pair.2), channel_id=1, source_target_pairs={{1,2},{2,3},{5,6},{6,7},{9,10},{10,11},{13,14},{14,15},{17,18},{18... | collective-permute-start | bytes 1179656 | tf_op jit(solution)/shard_map/ppermute | solution.py:496
  39.1 3.1 %collective-permute-start.11 = (bf16[80,1536]{1,0:T(8,128)(2,1)S(1)}, bf16[80,1536]{1,0:T(8,128)(2,1)S(1)}, u32[]{:S(2)}, u32[]{:S(2)}) collective-permute-start(bf16[80,1536]{1,0:T(8,128)(2,1)S(1)} %collective-permute-done.10.right.refs_1_), channel_id=1, source_target_pairs={{0,4},{4,0},{8,12},{12,8},{1,5},{5,1},{9,13},{13,9},{2,6},{6,2},{1... | collective-permute-start | bytes 737288 | tf_op jit(solution)/shard_map/ppermute | solution.py:422
  41.1 1.5 %collective-permute-start.9 = (bf16[80,1536]{1,0:T(8,128)(2,1)S(1)}, bf16[80,1536]{1,0:T(8,128)(2,1)S(1)}, u32[]{:S(2)}, u32[]{:S(2)}) collective-permute-start(bf16[80,1536]{1,0:T(8,128)(2,1)S(1)} %collective-permute-done.8.left.refs_1_), channel_id=1, source_target_pairs={{0,4},{4,0},{8,12},{12,8},{1,5},{5,1},{9,13},{13,9},{2,6},{6,2},{1... | collective-permute-start | bytes 737288 | tf_op jit(solution)/shard_map/ppermute | solution.py:422
  42.2 13.6 %collective-permute-start.12 = (bf16[512,256]{1,0:T(8,128)(2,1)S(1)}, bf16[512,256]{1,0:T(8,128)(2,1)S(1)}, u32[]{:S(2)}, u32[]{:S(2)}) collective-permute-start(bf16[512,256]{1,0:T(8,128)(2,1)S(1)} %get-tuple-element.38), channel_id=1, source_target_pairs={{0,8},{4,12},{8,0},{12,4},{1,9},{5,13},{9,1},{13,5},{2,10},{6,14},... | collective-permute-start | bytes 786440 | tf_op jit(solution)/shard_map/ppermute | solution.py:475
  42.6 8.0 %copy-start.3 = (f32[3,3,1536]{2,1,0:T(4,128)S(1)}, f32[3,3,1536]{2,1,0:T(4,128)}, u32[]{:S(2)}) copy-start(f32[3,3,1536]{2,1,0:T(4,128)} %weights.1) | copy-start | bytes 165892
  48.1 3.9 %copy-start.6 = (s32[2,1,2]{2,1,0:T(1,128)S(1)}, s32[2,1,2]{2,1,0:T(1,128)}, u32[]{:S(2)}) copy-start(s32[2,1,2]{2,1,0:T(1,128)} %pattern_ref.3) | copy-start | bytes 52
  48.1 3.8 %collective-permute-start.16 = (bf16[64,1536]{1,0:T(8,128)(2,1)S(1)}, bf16[64,1536]{1,0:T(8,128)(2,1)S(1)}, u32[]{:S(2)}, u32[]{:S(2)}) collective-permute-start(bf16[64,1536]{1,0:T(8,128)(2,1)S(1)} %get-tuple-element.42.refs_6_), channel_id=1, source_target_pairs={{0,4},{4,0},{8,12},{12,8},{1,5},{5,1},{9,13},{13,9},{2,6},{6,2},{1... | collective-permute-start | bytes 589832 | tf_op jit(solution)/shard_map/ppermute | solution.py:422
  50.5 1.4 %collective-permute-start.17 = (bf16[64,1536]{1,0:T(8,128)(2,1)S(1)}, bf16[64,1536]{1,0:T(8,128)(2,1)S(1)}, u32[]{:S(2)}, u32[]{:S(2)}) collective-permute-start(bf16[64,1536]{1,0:T(8,128)(2,1)S(1)} %get-tuple-element.43.refs_8_), channel_id=1, source_target_pairs={{0,4},{4,0},{8,12},{12,8},{1,5},{5,1},{9,13},{13,9},{2,6},{6,2},{1... | collective-permute-start | bytes 589832 | tf_op jit(solution)/shard_map/ppermute | solution.py:422
  (1 other events, 2.3 us)

commit v14 on v13

--- a/solution.py
+++ b/solution.py
@@ -14,7 +14,7 @@
 PER_BLOCK = BLOCK_ROWS * BLOCK_COLS
 SCORE_SCALE = 1.0 / math.sqrt(HEAD_DIM)
 EXP2_SCALE = SCORE_SCALE * math.log2(math.e)
-CHUNK_HEADS = (10, 2)
+CHUNK_HEADS = (9, 3)
 GROUP = 8
 VMEM_LIMIT = 24 * 1024 * 1024
 

time: 57.8 us -> 51.8 us (0.90)
  the two profiles are of different devices: /device:TPU:23 before, /device:TPU:0 now
where the time goes in v14:
time: 51.8 us; the launch traced here: 51.2 us
  waiting for transfers between devices  22.3 us (43%)
  starting transfers between devices  16 us (31%)
  Pallas kernels  12.7 us (25%)
    pallas_call x10, Pallas kernels, local(): pl.pallas_call(kernel, out_shape=shapes, in_specs=specs or [in_vmem] * le...  7.04 us
    ppermute x1, waiting for transfers between devices, body(): right = lax.ppermute(minus, 'cols', backward)  6.32 us
    pallas_call x2, Pallas kernels, body(): pl.pallas_call(functools.partial(late_kernel, first_head), out_shape=jax....  5.62 us
    ppermute x2, waiting for transfers between devices, body(): near_parts = [lax.ppermute(text, 'cols', p) for p in (forward, backward)]  4.89 us
    ppermute x1, waiting for transfers between devices, body(): left = lax.ppermute(plus, 'cols', forward)  4.38 us
    ppermute x2, starting transfers between devices, body(): near_parts = [lax.ppermute(text, 'cols', p) for p in (forward, backward)]  3.88 us
    ppermute x2, starting transfers between devices, body(): far = [lax.ppermute(chunk, 'rows', swap) for chunk in packed]  2.93 us
    ppermute x1, waiting for transfers between devices, body(): lower = lax.ppermute(lower, 'cols', [(1, 0), (2, 1)])  2.9 us
  transfers between devices with their start and end apart: 18, of which 8 were waited for; matrix products, arithmetic and copies ran while one was open for 0% of the time, Pallas kernels for 17%

profile of v14, /device:TPU:0, one launch (start us, length us, event | category | flops | bytes accessed | tf_op | source)
XLA Modules:
  0.0 51.2 jit_solution(7777555268591156622)
XLA Ops:
  0.0 1.6 %pack.1 = (bf16[512,1536]{1,0:T(8,128)(2,1)S(1)}, bf16[32,1536]{1,0:T(8,128)(2,1)S(1)}, bf16[32,1536]{1,0:T(8,128)(2,1)S(1)}, bf16[64,1536]{1,0:T(8,128)(2,1)S(1)}) custom-call(bf16[256,1536]{1,0:T(8,128)(2,1)} %bitcast.11, bf16[256,1536]{1,0:T(8,128)(2,1)} %bitcast.12, bf16[8,32,1536]{2,1,0:T(8,128)(2,1)} %cells.5, bf16[32,1536]{1,0:T(8,128)(2,1)} %text_k.1, ...), custom_call_target="tpu_custom_call" | custom-call | flops 1048576 | bytes 65536 | tf_op jit(solution)/shard_map/pack/pallas_call | solution.py:430
  1.6 0.5 %collective-permute-start.2 = (bf16[512,1536]{1,0:T(8,128)(2,1)S(1)}, bf16[512,1536]{1,0:T(8,128)(2,1)S(1)}, u32[]{:S(2)}, u32[]{:S(2)}) collective-permute-start(bf16[512,1536]{1,0:T(8,128)(2,1)S(1)} %get-tuple-element.28.stale), channel_id=1, source_target_pairs={{0,4},{4,0},{8,12},{12,8},{1,5},{5,1},{9,13},{13,9},{2,6},{6,2},{1... | collective-permute-start | bytes 4718600 | tf_op jit(solution)/shard_map/ppermute | solution.py:422
  2.1 0.6 %offer.1 = bf16[72,1536]{1,0:T(8,128)(2,1)S(1)} custom-call(s32[1,1,2]{2,1,0:T(1,128)S(1)} %copy-done.5, bf16[64,1536]{1,0:T(8,128)(2,1)S(1)} %get-tuple-element.25.text), custom_call_target="tpu_custom_call" | custom-call | flops 1048576 | bytes 65536 | tf_op jit(solution)/shard_map/offer/pallas_call | solution.py:430
  2.7 2.6 %collective-permute-start = (bf16[72,1536]{1,0:T(8,128)(2,1)S(1)}, bf16[72,1536]{1,0:T(8,128)(2,1)S(1)}, u32[]{:S(2)}, u32[]{:S(2)}) collective-permute-start(bf16[72,1536]{1,0:T(8,128)(2,1)S(1)} %offer.1), channel_id=1, source_target_pairs={{0,8},{4,12},{8,0},{12,4},{1,9},{5,13},{9,1},{13,5},{2,10},{6,14},... | collective-permute-start | bytes 663560 | tf_op jit(solution)/shard_map/ppermute | solution.py:470
  5.2 0.8 %collective-permute-start.1 = (bf16[32,1536]{1,0:T(8,128)(2,1)S(1)}, bf16[32,1536]{1,0:T(8,128)(2,1)S(1)}, u32[]{:S(2)}, u32[]{:S(2)}) collective-permute-start(bf16[32,1536]{1,0:T(8,128)(2,1)S(1)} %get-tuple-element.26), channel_id=1, source_target_pairs={{4,8},{8,4},{5,9},{9,5},{6,10},{10,6},{7,11},{11,7},{20,24},{24,20... | collective-permute-start | bytes 294920 | tf_op jit(solution)/shard_map/ppermute | solution.py:461
  6.0 1.6 %collective-permute-start.5 = (bf16[64,1536]{1,0:T(8,128)(2,1)S(1)}, bf16[64,1536]{1,0:T(8,128)(2,1)S(1)}, u32[]{:S(2)}, u32[]{:S(2)}) collective-permute-start(bf16[64,1536]{1,0:T(8,128)(2,1)S(1)} %get-tuple-element.25.text), channel_id=1, source_target_pairs={{0,1},{1,2},{2,3},{3,0},{4,5},{5,6},{6,7},{7,4},{8,9},{9,10},{10,1... | collective-permute-start | bytes 589832 | tf_op jit(solution)/shard_map/ppermute | solution.py:459
  7.7 2.2 %collective-permute-start.6 = (bf16[64,1536]{1,0:T(8,128)(2,1)S(1)}, bf16[64,1536]{1,0:T(8,128)(2,1)S(1)}, u32[]{:S(2)}, u32[]{:S(2)}) collective-permute-start(bf16[64,1536]{1,0:T(8,128)(2,1)S(1)} %get-tuple-element.25.text), channel_id=1, source_target_pairs={{0,3},{1,0},{2,1},{3,2},{4,7},{5,4},{6,5},{7,6},{8,11},{9,8},{10,9... | collective-permute-start | bytes 589832 | tf_op jit(solution)/shard_map/ppermute | solution.py:459
  9.9 1.4 %collective-permute-done.across = bf16[72,1536]{1,0:T(8,128)(2,1)S(1)} collective-permute-done((bf16[72,1536]{1,0:T(8,128)(2,1)S(1)}, bf16[72,1536]{1,0:T(8,128)(2,1)S(1)}, u32[]{:S(2)}, u32[]{:S(2)}) %collective-permute-start) | collective-permute-done | bytes 221216 | tf_op jit(solution)/shard_map/ppermute | solution.py:470
  11.6 2.9 %collective-permute-start.13 = (bf16[512,1152]{1,0:T(8,128)(2,1)S(1)}, bf16[512,1152]{1,0:T(8,128)(2,1)S(1)}, u32[]{:S(2)}, u32[]{:S(2)}) collective-permute-start(bf16[512,1152]{1,0:T(8,128)(2,1)S(1)} %get-tuple-element.29), channel_id=1, source_target_pairs={{0,8},{4,12},{8,0},{12,4},{1,9},{5,13},{9,1},{13,5},{2,10},{6,14},... | collective-permute-start | bytes 3538952 | tf_op jit(solution)/shard_map/ppermute | solution.py:475
  14.8 4.5 %collective-permute-done.6.refs_1_.refs_0_ = bf16[64,1536]{1,0:T(8,128)(2,1)S(1)} collective-permute-done((bf16[64,1536]{1,0:T(8,128)(2,1)S(1)}, bf16[64,1536]{1,0:T(8,128)(2,1)S(1)}, u32[]{:S(2)}, u32[]{:S(2)}) %collective-permute-start.6) | collective-permute-done | bytes 196640 | tf_op jit(solution)/shard_map/ppermute | solution.py:459
  19.4 0.5 collective-permute-start.7
  20.2 2.0 %collective-permute-start.10 = (bf16[80,1536]{1,0:T(8,128)(2,1)S(1)}, bf16[80,1536]{1,0:T(8,128)(2,1)S(1)}, u32[]{:S(2)}, u32[]{:S(2)}) collective-permute-start(bf16[80,1536]{1,0:T(8,128)(2,1)S(1)} %get-tuple-element.34), channel_id=1, source_target_pairs={{0,3},{1,0},{2,1},{3,2},{4,7},{5,4},{6,5},{7,6},{8,11},{9,8},{10,9... | collective-permute-start | bytes 737288 | tf_op jit(solution)/shard_map/ppermute | solution.py:488
  22.2 6.3 %collective-permute-done.10.right.refs_1_ = bf16[80,1536]{1,0:T(8,128)(2,1)S(1)} collective-permute-done((bf16[80,1536]{1,0:T(8,128)(2,1)S(1)}, bf16[80,1536]{1,0:T(8,128)(2,1)S(1)}, u32[]{:S(2)}, u32[]{:S(2)}) %collective-permute-start.10) | collective-permute-done | bytes 245792 | tf_op jit(solution)/shard_map/ppermute | solution.py:488
  28.6 1.3 %collective-permute-start.15 = (bf16[128,1536]{1,0:T(8,128)(2,1)S(1)}, bf16[128,1536]{1,0:T(8,128)(2,1)S(1)}, u32[]{:S(2)}, u32[]{:S(2)}) collective-permute-start(bf16[128,1536]{1,0:T(8,128)(2,1)S(1)} %pair.3), channel_id=1, source_target_pairs={{1,0},{2,1},{5,4},{6,5},{9,8},{10,9},{13,12},{14,13},{17,16},{18,1... | collective-permute-start | bytes 1179656 | tf_op jit(solution)/shard_map/ppermute | solution.py:497
  29.9 4.4 %collective-permute-done.8.left.refs_1_ = bf16[80,1536]{1,0:T(8,128)(2,1)S(1)} collective-permute-done((bf16[80,1536]{1,0:T(8,128)(2,1)S(1)}, bf16[80,1536]{1,0:T(8,128)(2,1)S(1)}, u32[]{:S(2)}, u32[]{:S(2)}) %collective-permute-start.8) | collective-permute-done | bytes 245792 | tf_op jit(solution)/shard_map/ppermute | solution.py:487
  34.3 0.7 %collective-permute-start.14 = (bf16[128,1536]{1,0:T(8,128)(2,1)S(1)}, bf16[128,1536]{1,0:T(8,128)(2,1)S(1)}, u32[]{:S(2)}, u32[]{:S(2)}) collective-permute-start(bf16[128,1536]{1,0:T(8,128)(2,1)S(1)} %pair.2), channel_id=1, source_target_pairs={{1,2},{2,3},{5,6},{6,7},{9,10},{10,11},{13,14},{14,15},{17,18},{18... | collective-permute-start | bytes 1179656 | tf_op jit(solution)/shard_map/ppermute | solution.py:496
  35.2 1.4 %collective-permute-done.9.left_mate = bf16[80,1536]{1,0:T(8,128)(2,1)S(1)} collective-permute-done((bf16[80,1536]{1,0:T(8,128)(2,1)S(1)}, bf16[80,1536]{1,0:T(8,128)(2,1)S(1)}, u32[]{:S(2)}, u32[]{:S(2)}) %collective-permute-start.9) | collective-permute-done | bytes 245792 | tf_op jit(solution)/shard_map/ppermute | solution.py:422
  36.6 3.1 %early.1 = (f32[256,1536]{1,0:T(8,128)S(1)}, f32[256,1536]{1,0:T(8,128)S(1)}, f32[256,1536]{1,0:T(8,128)S(1)}) custom-call(s32[2,1,2]{2,1,0:T(1,128)S(1)} %copy-done.4, bf16[256,1536]{1,0:T(8,128)(2,1)S(1)} %bitcast.7, bf16[256,1536]{1,0:T(8,128)(2,1)S(1)} %bitcast.10, bf16[256,1536]{1,0:T(8,128)(2,1)S(1)} %bitcast.6, ...), custom_call_target="tpu_custom_call" | custom-call | flops 1048576 | bytes 65536 | tf_op jit(solution)/shard_map/early/pallas_call | solution.py:430
  39.7 2.9 %collective-permute-done.15.lower = bf16[128,1536]{1,0:T(8,128)(2,1)S(1)} collective-permute-done((bf16[128,1536]{1,0:T(8,128)(2,1)S(1)}, bf16[128,1536]{1,0:T(8,128)(2,1)S(1)}, u32[]{:S(2)}, u32[]{:S(2)}) %collective-permute-start.15) | collective-permute-done | bytes 393248 | tf_op jit(solution)/shard_map/ppermute | solution.py:497
  42.8 0.4 collective-permute-start.17
  43.3 1.3 %term.1.refs_5_ = f32[256,1536]{1,0:T(8,128)S(1)} custom-call(bf16[8,32,1536]{2,1,0:T(8,128)(2,1)S(1)} %copy-done, bf16[32,1536]{1,0:T(8,128)(2,1)S(1)} %collective-permute-done.3.beside, bf16[32,1536]{1,0:T(8,128)(2,1)S(1)} %collective-permute-done.1.diagonal, bf16[80,1536]{1,0:T(8,128)(2,1)S(1)} %collective-permute-done.8.left.refs_1_, ...), custom_call_target="tpu_custom_call" | custom-call | flops 1048576 | bytes 65536 | tf_op jit(solution)/shard_map/term/pallas_call | solution.py:430
  44.6 3.6 %late0.1.refs_10_ = f32[256,1536]{1,0:T(8,128)} custom-call(s32[1,1,2]{2,1,0:T(1,128)S(1)} %copy-done.5, s32[2,1,2]{2,1,0:T(1,128)S(1)} %copy-done.6, s32[2,1,2]{2,1,0:T(1,128)S(1)} %copy-done.4, bf16[256,1536]{1,0:T(8,128)(2,1)S(1)} %bitcast.8, f32[256,1536]{1,0:T(8,128)S(1)} %get-tuple-element.35.refs_0_, f32[256,1536]{1,0:T(8,128)S(1)} %get-tuple-element.36.refs_1_, ...), custom_call_target="tpu_custom_call" | custom-call | flops 1048576 | bytes 65536 | tf_op jit(solution)/shard_map/late0/pallas_call | solution.py:526
  48.2 0.9 %collective-permute-done.12.refs_4_ = bf16[512,384]{1,0:T(8,128)(2,1)S(1)} collective-permute-done((bf16[512,384]{1,0:T(8,128)(2,1)S(1)}, bf16[512,384]{1,0:T(8,128)(2,1)S(1)}, u32[]{:S(2)}, u32[]{:S(2)}) %collective-permute-start.12) | collective-permute-done | bytes 393248 | tf_op jit(solution)/shard_map/ppermute | solution.py:475
  49.1 2.0 %late1.1 = f32[256,1536]{1,0:T(8,128)} custom-call(s32[1,1,2]{2,1,0:T(1,128)S(1)} %copy-done.5, s32[2,1,2]{2,1,0:T(1,128)S(1)} %copy-done.6, s32[2,1,2]{2,1,0:T(1,128)S(1)} %copy-done.4, bf16[256,1536]{1,0:T(8,128)(2,1)S(1)} %bitcast.9, f32[256,1536]{1,0:T(8,128)S(1)} %get-tuple-element.35.refs_0_, ...), custom_call_target="tpu_custom_call", output_to_operand_aliasing={{}: (14, {})} | custom-call | flops 1048576 | bytes 65536 | tf_op jit(solution)/shard_map/late1/pallas_call | solution.py:526
  (38 shorter events, 1.4 us)
Async XLA Ops:
  0.0 2.1 %copy-start.5 = (s32[1,1,2]{2,1,0:T(1,128)S(1)}, s32[1,1,2]{2,1,0:T(1,128)}, u32[]{:S(2)}) copy-start(s32[1,1,2]{2,1,0:T(1,128)} %reads_ref.5) | copy-start | bytes 28
  1.6 9.8 %collective-permute-start.2 = (bf16[512,1536]{1,0:T(8,128)(2,1)S(1)}, bf16[512,1536]{1,0:T(8,128)(2,1)S(1)}, u32[]{:S(2)}, u32[]{:S(2)}) collective-permute-start(bf16[512,1536]{1,0:T(8,128)(2,1)S(1)} %get-tuple-element.28.stale), channel_id=1, source_target_pairs={{0,4},{4,0},{8,12},{12,8},{1,5},{5,1},{9,13},{13,9},{2,6},{6,2},{1... | collective-permute-start | bytes 4718600 | tf_op jit(solution)/shard_map/ppermute | solution.py:422
  2.7 8.7 %collective-permute-start = (bf16[72,1536]{1,0:T(8,128)(2,1)S(1)}, bf16[72,1536]{1,0:T(8,128)(2,1)S(1)}, u32[]{:S(2)}, u32[]{:S(2)}) collective-permute-start(bf16[72,1536]{1,0:T(8,128)(2,1)S(1)} %offer.1), channel_id=1, source_target_pairs={{0,8},{4,12},{8,0},{12,4},{1,9},{5,13},{9,1},{13,5},{2,10},{6,14},... | collective-permute-start | bytes 663560 | tf_op jit(solution)/shard_map/ppermute | solution.py:470
  5.2 14.7 %copy-start = (bf16[8,32,1536]{2,1,0:T(8,128)(2,1)S(1)}, bf16[8,32,1536]{2,1,0:T(8,128)(2,1)}, u32[]{:S(2)}) copy-start(bf16[8,32,1536]{2,1,0:T(8,128)(2,1)} %cells.5) | copy-start | bytes 2359300
  5.2 4.7 %collective-permute-start.1 = (bf16[32,1536]{1,0:T(8,128)(2,1)S(1)}, bf16[32,1536]{1,0:T(8,128)(2,1)S(1)}, u32[]{:S(2)}, u32[]{:S(2)}) collective-permute-start(bf16[32,1536]{1,0:T(8,128)(2,1)S(1)} %get-tuple-element.26), channel_id=1, source_target_pairs={{4,8},{8,4},{5,9},{9,5},{6,10},{10,6},{7,11},{11,7},{20,24},{24,20... | collective-permute-start | bytes 294920 | tf_op jit(solution)/shard_map/ppermute | solution.py:461
  6.0 8.8 %collective-permute-start.5 = (bf16[64,1536]{1,0:T(8,128)(2,1)S(1)}, bf16[64,1536]{1,0:T(8,128)(2,1)S(1)}, u32[]{:S(2)}, u32[]{:S(2)}) collective-permute-start(bf16[64,1536]{1,0:T(8,128)(2,1)S(1)} %get-tuple-element.25.text), channel_id=1, source_target_pairs={{0,1},{1,2},{2,3},{3,0},{4,5},{5,6},{6,7},{7,4},{8,9},{9,10},{10,1... | collective-permute-start | bytes 589832 | tf_op jit(solution)/shard_map/ppermute | solution.py:459
  7.7 11.7 %collective-permute-start.6 = (bf16[64,1536]{1,0:T(8,128)(2,1)S(1)}, bf16[64,1536]{1,0:T(8,128)(2,1)S(1)}, u32[]{:S(2)}, u32[]{:S(2)}) collective-permute-start(bf16[64,1536]{1,0:T(8,128)(2,1)S(1)} %get-tuple-element.25.text), channel_id=1, source_target_pairs={{0,3},{1,0},{2,1},{3,2},{4,7},{5,4},{6,5},{7,6},{8,11},{9,8},{10,9... | collective-permute-start | bytes 589832 | tf_op jit(solution)/shard_map/ppermute | solution.py:459
  11.6 33.0 %collective-permute-start.13 = (bf16[512,1152]{1,0:T(8,128)(2,1)S(1)}, bf16[512,1152]{1,0:T(8,128)(2,1)S(1)}, u32[]{:S(2)}, u32[]{:S(2)}) collective-permute-start(bf16[512,1152]{1,0:T(8,128)(2,1)S(1)} %get-tuple-element.29), channel_id=1, source_target_pairs={{0,8},{4,12},{8,0},{12,4},{1,9},{5,13},{9,1},{13,5},{2,10},{6,14},... | collective-permute-start | bytes 3538952 | tf_op jit(solution)/shard_map/ppermute | solution.py:475
  14.4 5.5 %collective-permute-start.3 = (bf16[32,1536]{1,0:T(8,128)(2,1)S(1)}, bf16[32,1536]{1,0:T(8,128)(2,1)S(1)}, u32[]{:S(2)}, u32[]{:S(2)}) collective-permute-start(bf16[32,1536]{1,0:T(8,128)(2,1)S(1)} %get-tuple-element.31), channel_id=1, source_target_pairs={{0,4},{4,0},{8,12},{12,8},{1,5},{5,1},{9,13},{13,9},{2,6},{6,2},{1... | collective-permute-start | bytes 294920 | tf_op jit(solution)/shard_map/ppermute | solution.py:422
  19.4 17.2 %copy-start.1 = (bf16[8,32,1536]{2,1,0:T(8,128)(2,1)S(1)}, bf16[8,32,1536]{2,1,0:T(8,128)(2,1)}, u32[]{:S(2)}) copy-start(bf16[8,32,1536]{2,1,0:T(8,128)(2,1)} %param.11) | copy-start | bytes 2359300
  19.4 17.2 %copy-start.2 = (bf16[8,32,1536]{2,1,0:T(8,128)(2,1)S(1)}, bf16[8,32,1536]{2,1,0:T(8,128)(2,1)}, u32[]{:S(2)}) copy-start(bf16[8,32,1536]{2,1,0:T(8,128)(2,1)} %param.12) | copy-start | bytes 2359300
  19.4 17.2 %copy-start.4 = (s32[2,1,2]{2,1,0:T(1,128)S(1)}, s32[2,1,2]{2,1,0:T(1,128)}, u32[]{:S(2)}) copy-start(s32[2,1,2]{2,1,0:T(1,128)} %text_ref.5) | copy-start | bytes 52
  19.4 9.2 %collective-permute-start.7 = (bf16[128,1536]{1,0:T(8,128)(2,1)S(1)}, bf16[128,1536]{1,0:T(8,128)(2,1)S(1)}, u32[]{:S(2)}, u32[]{:S(2)}) collective-permute-start(bf16[128,1536]{1,0:T(8,128)(2,1)S(1)} %bundle.1.early), channel_id=1, source_target_pairs={{0,4},{4,0},{8,12},{12,8},{1,5},{5,1},{9,13},{13,9},{2,6},{6,2},{1... | collective-permute-start | bytes 1179656 | tf_op jit(solution)/shard_map/ppermute | solution.py:422
  20.1 9.8 %collective-permute-start.4 = (bf16[128,1536]{1,0:T(8,128)(2,1)S(1)}, bf16[128,1536]{1,0:T(8,128)(2,1)S(1)}, u32[]{:S(2)}, u32[]{:S(2)}) collective-permute-start(bf16[128,1536]{1,0:T(8,128)(2,1)S(1)} %get-tuple-element.32.both), channel_id=1, source_target_pairs={{0,4},{4,0},{8,12},{12,8},{1,5},{5,1},{9,13},{13,9},{2,6},{6,2},{1... | collective-permute-start | bytes 1179656 | tf_op jit(solution)/shard_map/ppermute | solution.py:422
  20.2 8.3 %collective-permute-start.10 = (bf16[80,1536]{1,0:T(8,128)(2,1)S(1)}, bf16[80,1536]{1,0:T(8,128)(2,1)S(1)}, u32[]{:S(2)}, u32[]{:S(2)}) collective-permute-start(bf16[80,1536]{1,0:T(8,128)(2,1)S(1)} %get-tuple-element.34), channel_id=1, source_target_pairs={{0,3},{1,0},{2,1},{3,2},{4,7},{5,4},{6,5},{7,6},{8,11},{9,8},{10,9... | collective-permute-start | bytes 737288 | tf_op jit(solution)/shard_map/ppermute | solution.py:488
  22.2 12.1 %collective-permute-start.8 = (bf16[80,1536]{1,0:T(8,128)(2,1)S(1)}, bf16[80,1536]{1,0:T(8,128)(2,1)S(1)}, u32[]{:S(2)}, u32[]{:S(2)}) collective-permute-start(bf16[80,1536]{1,0:T(8,128)(2,1)S(1)} %get-tuple-element.33), channel_id=1, source_target_pairs={{0,1},{1,2},{2,3},{3,0},{4,5},{5,6},{6,7},{7,4},{8,9},{9,10},{10,1... | collective-permute-start | bytes 737288 | tf_op jit(solution)/shard_map/ppermute | solution.py:487
  28.5 6.5 %collective-permute-start.11 = (bf16[80,1536]{1,0:T(8,128)(2,1)S(1)}, bf16[80,1536]{1,0:T(8,128)(2,1)S(1)}, u32[]{:S(2)}, u32[]{:S(2)}) collective-permute-start(bf16[80,1536]{1,0:T(8,128)(2,1)S(1)} %collective-permute-done.10.right.refs_1_), channel_id=1, source_target_pairs={{0,4},{4,0},{8,12},{12,8},{1,5},{5,1},{9,13},{13,9},{2,6},{6,2},{1... | collective-permute-start | bytes 737288 | tf_op jit(solution)/shard_map/ppermute | solution.py:422
  28.6 14.1 %collective-permute-start.15 = (bf16[128,1536]{1,0:T(8,128)(2,1)S(1)}, bf16[128,1536]{1,0:T(8,128)(2,1)S(1)}, u32[]{:S(2)}, u32[]{:S(2)}) collective-permute-start(bf16[128,1536]{1,0:T(8,128)(2,1)S(1)} %pair.3), channel_id=1, source_target_pairs={{1,0},{2,1},{5,4},{6,5},{9,8},{10,9},{13,12},{14,13},{17,16},{18,1... | collective-permute-start | bytes 1179656 | tf_op jit(solution)/shard_map/ppermute | solution.py:497
  34.3 8.3 %collective-permute-start.14 = (bf16[128,1536]{1,0:T(8,128)(2,1)S(1)}, bf16[128,1536]{1,0:T(8,128)(2,1)S(1)}, u32[]{:S(2)}, u32[]{:S(2)}) collective-permute-start(bf16[128,1536]{1,0:T(8,128)(2,1)S(1)} %pair.2), channel_id=1, source_target_pairs={{1,2},{2,3},{5,6},{6,7},{9,10},{10,11},{13,14},{14,15},{17,18},{18... | collective-permute-start | bytes 1179656 | tf_op jit(solution)/shard_map/ppermute | solution.py:496
  35.0 1.6 %collective-permute-start.9 = (bf16[80,1536]{1,0:T(8,128)(2,1)S(1)}, bf16[80,1536]{1,0:T(8,128)(2,1)S(1)}, u32[]{:S(2)}, u32[]{:S(2)}) collective-permute-start(bf16[80,1536]{1,0:T(8,128)(2,1)S(1)} %collective-permute-done.8.left.refs_1_), channel_id=1, source_target_pairs={{0,4},{4,0},{8,12},{12,8},{1,5},{5,1},{9,13},{13,9},{2,6},{6,2},{1... | collective-permute-start | bytes 737288 | tf_op jit(solution)/shard_map/ppermute | solution.py:422
  35.1 14.0 %collective-permute-start.12 = (bf16[512,384]{1,0:T(8,128)(2,1)S(1)}, bf16[512,384]{1,0:T(8,128)(2,1)S(1)}, u32[]{:S(2)}, u32[]{:S(2)}) collective-permute-start(bf16[512,384]{1,0:T(8,128)(2,1)S(1)} %get-tuple-element.38), channel_id=1, source_target_pairs={{0,8},{4,12},{8,0},{12,4},{1,9},{5,13},{9,1},{13,5},{2,10},{6,14},... | collective-permute-start | bytes 1179656 | tf_op jit(solution)/shard_map/ppermute | solution.py:475
  36.6 6.7 %copy-start.3 = (f32[3,3,1536]{2,1,0:T(4,128)S(1)}, f32[3,3,1536]{2,1,0:T(4,128)}, u32[]{:S(2)}) copy-start(f32[3,3,1536]{2,1,0:T(4,128)} %weights.1) | copy-start | bytes 165892
  42.7 1.9 %collective-permute-start.16 = (bf16[64,1536]{1,0:T(8,128)(2,1)S(1)}, bf16[64,1536]{1,0:T(8,128)(2,1)S(1)}, u32[]{:S(2)}, u32[]{:S(2)}) collective-permute-start(bf16[64,1536]{1,0:T(8,128)(2,1)S(1)} %get-tuple-element.42.refs_6_), channel_id=1, source_target_pairs={{0,4},{4,0},{8,12},{12,8},{1,5},{5,1},{9,13},{13,9},{2,6},{6,2},{1... | collective-permute-start | bytes 589832 | tf_op jit(solution)/shard_map/ppermute | solution.py:422
  42.8 1.7 %collective-permute-start.17 = (bf16[64,1536]{1,0:T(8,128)(2,1)S(1)}, bf16[64,1536]{1,0:T(8,128)(2,1)S(1)}, u32[]{:S(2)}, u32[]{:S(2)}) collective-permute-start(bf16[64,1536]{1,0:T(8,128)(2,1)S(1)} %get-tuple-element.43.refs_8_), channel_id=1, source_target_pairs={{0,4},{4,0},{8,12},{12,8},{1,5},{5,1},{9,13},{13,9},{2,6},{6,2},{1... | collective-permute-start | bytes 589832 | tf_op jit(solution)/shard_map/ppermute | solution.py:422
  (1 other events, 1.9 us)

commit v15 on v14

--- a/solution.py
+++ b/solution.py
@@ -337,7 +337,8 @@
 def late_kernel(first_head, reads_ref, pattern_ref, text_ref, q, *refs):
     sums, old_peaks, old_totals, passed, arrived, term = refs[:6]
     near, near_mate, side, side_mate = refs[6:10]
-    out = refs[-1]
+    target, out, sems = refs[-3:]
+    copies = []
     row = lax.axis_index("rows")
     across, core = row // 2, row % 2
     shard = near.shape[0] // 2
@@ -397,6 +398,17 @@
             total = old_totals[rows, part] * factor + total
             summed = sums[rows, part] * factor + product
             out[rows, lanes_of(head)] = summed / total + term[rows, part]
+        first, width = group[0][1], (group[-1][1] + 1 - group[0][1]) * HEAD_DIM
+        copies.append(
+            pltpu.make_async_copy(
+                out.at[:, pl.ds(first * HEAD_DIM, width)],
+                target.at[:, pl.ds((first_head + first) * HEAD_DIM, width)],
+                sems.at[len(copies)],
+            )
+        )
+        copies[-1].start()
+    for copy in copies:
+        copy.wait()
 
 
 def body(
@@ -519,10 +531,6 @@
     for chunk, head_count in enumerate(CHUNK_HEADS):
         if out is not None:
             far[chunk] = after(far[chunk], out)
-        block = pl.BlockSpec(
-            (pl.Element(tokens), pl.Element(head_count * HEAD_DIM)),
-            lambda i, *_, at=first_head * HEAD_DIM: (0, at),
-        )
         out = pl.pallas_call(
             functools.partial(late_kernel, first_head),
             out_shape=jax.ShapeDtypeStruct((tokens, width), jnp.float32),
@@ -530,7 +538,11 @@
                 num_scalar_prefetch=3,
                 grid=(1,),
                 in_specs=[in_vmem] * 11 + [in_hbm] * (out is not None),
-                out_specs=block,
+                out_specs=in_hbm,
+                scratch_shapes=[
+                    pltpu.VMEM((tokens, head_count * HEAD_DIM), jnp.float32),
+                    pltpu.SemaphoreType.DMA((4,)),
+                ],
             ),
             input_output_aliases={14: 0} if out is not None else {},
             compiler_params=params,

time: 51.8 us -> 51.6 us (level)
  no operation moved by 1% of the time
where the time goes in v15:
time: 51.6 us; the launch traced here: 51.2 us
  waiting for transfers between devices  22.5 us (44%)
  starting transfers between devices  16 us (31%)
  Pallas kernels  12.5 us (24%)
    pallas_call x10, Pallas kernels, local(): pl.pallas_call(kernel, out_shape=shapes, in_specs=specs or [in_vmem] * le...  7.04 us
    ppermute x1, waiting for transfers between devices, body(): right = lax.ppermute(minus, 'cols', backward)  6.32 us
    pallas_call x2, Pallas kernels, body(): pl.pallas_call(functools.partial(late_kernel, first_head), out_shape=jax....  5.43 us
    ppermute x2, waiting for transfers between devices, body(): near_parts = [lax.ppermute(text, 'cols', p) for p in (forward, backward)]  4.89 us
    ppermute x1, waiting for transfers between devices, body(): left = lax.ppermute(plus, 'cols', forward)  4.38 us
    ppermute x2, starting transfers between devices, body(): near_parts = [lax.ppermute(text, 'cols', p) for p in (forward, backward)]  3.88 us
    ppermute x2, starting transfers between devices, body(): far = [lax.ppermute(chunk, 'rows', swap) for chunk in packed]  2.93 us
    ppermute x1, waiting for transfers between devices, body(): lower = lax.ppermute(lower, 'cols', [(1, 0), (2, 1)])  2.9 us
  transfers between devices with their start and end apart: 18, of which 8 were waited for; matrix products, arithmetic and copies ran while one was open for 0% of the time, Pallas kernels for 17%

profile of v15, /device:TPU:0, one launch (start us, length us, event | category | flops | bytes accessed | tf_op | source)
XLA Modules:
  0.0 51.2 jit_solution(362967339453503562)
XLA Ops:
  0.0 1.6 %pack.1 = (bf16[512,1536]{1,0:T(8,128)(2,1)S(1)}, bf16[32,1536]{1,0:T(8,128)(2,1)S(1)}, bf16[32,1536]{1,0:T(8,128)(2,1)S(1)}, bf16[64,1536]{1,0:T(8,128)(2,1)S(1)}) custom-call(bf16[256,1536]{1,0:T(8,128)(2,1)} %bitcast.11, bf16[256,1536]{1,0:T(8,128)(2,1)} %bitcast.12, bf16[8,32,1536]{2,1,0:T(8,128)(2,1)} %cells.5, bf16[32,1536]{1,0:T(8,128)(2,1)} %text_k.1, ...), custom_call_target="tpu_custom_call" | custom-call | flops 1048576 | bytes 65536 | tf_op jit(solution)/shard_map/pack/pallas_call | solution.py:442
  1.6 0.5 %collective-permute-start.2 = (bf16[512,1536]{1,0:T(8,128)(2,1)S(1)}, bf16[512,1536]{1,0:T(8,128)(2,1)S(1)}, u32[]{:S(2)}, u32[]{:S(2)}) collective-permute-start(bf16[512,1536]{1,0:T(8,128)(2,1)S(1)} %get-tuple-element.28.stale), channel_id=1, source_target_pairs={{0,4},{4,0},{8,12},{12,8},{1,5},{5,1},{9,13},{13,9},{2,6},{6,2},{1... | collective-permute-start | bytes 4718600 | tf_op jit(solution)/shard_map/ppermute | solution.py:434
  2.1 0.6 %offer.1 = bf16[72,1536]{1,0:T(8,128)(2,1)S(1)} custom-call(s32[1,1,2]{2,1,0:T(1,128)S(1)} %copy-done.5, bf16[64,1536]{1,0:T(8,128)(2,1)S(1)} %get-tuple-element.25.text), custom_call_target="tpu_custom_call" | custom-call | flops 1048576 | bytes 65536 | tf_op jit(solution)/shard_map/offer/pallas_call | solution.py:442
  2.7 2.6 %collective-permute-start = (bf16[72,1536]{1,0:T(8,128)(2,1)S(1)}, bf16[72,1536]{1,0:T(8,128)(2,1)S(1)}, u32[]{:S(2)}, u32[]{:S(2)}) collective-permute-start(bf16[72,1536]{1,0:T(8,128)(2,1)S(1)} %offer.1), channel_id=1, source_target_pairs={{0,8},{4,12},{8,0},{12,4},{1,9},{5,13},{9,1},{13,5},{2,10},{6,14},... | collective-permute-start | bytes 663560 | tf_op jit(solution)/shard_map/ppermute | solution.py:482
  5.2 0.8 %collective-permute-start.1 = (bf16[32,1536]{1,0:T(8,128)(2,1)S(1)}, bf16[32,1536]{1,0:T(8,128)(2,1)S(1)}, u32[]{:S(2)}, u32[]{:S(2)}) collective-permute-start(bf16[32,1536]{1,0:T(8,128)(2,1)S(1)} %get-tuple-element.26), channel_id=1, source_target_pairs={{4,8},{8,4},{5,9},{9,5},{6,10},{10,6},{7,11},{11,7},{20,24},{24,20... | collective-permute-start | bytes 294920 | tf_op jit(solution)/shard_map/ppermute | solution.py:473
  6.0 1.6 %collective-permute-start.5 = (bf16[64,1536]{1,0:T(8,128)(2,1)S(1)}, bf16[64,1536]{1,0:T(8,128)(2,1)S(1)}, u32[]{:S(2)}, u32[]{:S(2)}) collective-permute-start(bf16[64,1536]{1,0:T(8,128)(2,1)S(1)} %get-tuple-element.25.text), channel_id=1, source_target_pairs={{0,1},{1,2},{2,3},{3,0},{4,5},{5,6},{6,7},{7,4},{8,9},{9,10},{10,1... | collective-permute-start | bytes 589832 | tf_op jit(solution)/shard_map/ppermute | solution.py:471
  7.7 2.2 %collective-permute-start.6 = (bf16[64,1536]{1,0:T(8,128)(2,1)S(1)}, bf16[64,1536]{1,0:T(8,128)(2,1)S(1)}, u32[]{:S(2)}, u32[]{:S(2)}) collective-permute-start(bf16[64,1536]{1,0:T(8,128)(2,1)S(1)} %get-tuple-element.25.text), channel_id=1, source_target_pairs={{0,3},{1,0},{2,1},{3,2},{4,7},{5,4},{6,5},{7,6},{8,11},{9,8},{10,9... | collective-permute-start | bytes 589832 | tf_op jit(solution)/shard_map/ppermute | solution.py:471
  9.9 1.4 %collective-permute-done.across = bf16[72,1536]{1,0:T(8,128)(2,1)S(1)} collective-permute-done((bf16[72,1536]{1,0:T(8,128)(2,1)S(1)}, bf16[72,1536]{1,0:T(8,128)(2,1)S(1)}, u32[]{:S(2)}, u32[]{:S(2)}) %collective-permute-start) | collective-permute-done | bytes 221216 | tf_op jit(solution)/shard_map/ppermute | solution.py:482
  11.6 2.9 %collective-permute-start.13 = (bf16[512,1152]{1,0:T(8,128)(2,1)S(1)}, bf16[512,1152]{1,0:T(8,128)(2,1)S(1)}, u32[]{:S(2)}, u32[]{:S(2)}) collective-permute-start(bf16[512,1152]{1,0:T(8,128)(2,1)S(1)} %get-tuple-element.29), channel_id=1, source_target_pairs={{0,8},{4,12},{8,0},{12,4},{1,9},{5,13},{9,1},{13,5},{2,10},{6,14},... | collective-permute-start | bytes 3538952 | tf_op jit(solution)/shard_map/ppermute | solution.py:487
  14.8 4.5 %collective-permute-done.6.refs_1_.refs_0_ = bf16[64,1536]{1,0:T(8,128)(2,1)S(1)} collective-permute-done((bf16[64,1536]{1,0:T(8,128)(2,1)S(1)}, bf16[64,1536]{1,0:T(8,128)(2,1)S(1)}, u32[]{:S(2)}, u32[]{:S(2)}) %collective-permute-start.6) | collective-permute-done | bytes 196640 | tf_op jit(solution)/shard_map/ppermute | solution.py:471
  19.4 0.5 collective-permute-start.7
  20.2 2.0 %collective-permute-start.10 = (bf16[80,1536]{1,0:T(8,128)(2,1)S(1)}, bf16[80,1536]{1,0:T(8,128)(2,1)S(1)}, u32[]{:S(2)}, u32[]{:S(2)}) collective-permute-start(bf16[80,1536]{1,0:T(8,128)(2,1)S(1)} %get-tuple-element.34), channel_id=1, source_target_pairs={{0,3},{1,0},{2,1},{3,2},{4,7},{5,4},{6,5},{7,6},{8,11},{9,8},{10,9... | collective-permute-start | bytes 737288 | tf_op jit(solution)/shard_map/ppermute | solution.py:500
  22.2 6.3 %collective-permute-done.10.right.refs_1_ = bf16[80,1536]{1,0:T(8,128)(2,1)S(1)} collective-permute-done((bf16[80,1536]{1,0:T(8,128)(2,1)S(1)}, bf16[80,1536]{1,0:T(8,128)(2,1)S(1)}, u32[]{:S(2)}, u32[]{:S(2)}) %collective-permute-start.10) | collective-permute-done | bytes 245792 | tf_op jit(solution)/shard_map/ppermute | solution.py:500
  28.6 1.3 %collective-permute-start.15 = (bf16[128,1536]{1,0:T(8,128)(2,1)S(1)}, bf16[128,1536]{1,0:T(8,128)(2,1)S(1)}, u32[]{:S(2)}, u32[]{:S(2)}) collective-permute-start(bf16[128,1536]{1,0:T(8,128)(2,1)S(1)} %pair.3), channel_id=1, source_target_pairs={{1,0},{2,1},{5,4},{6,5},{9,8},{10,9},{13,12},{14,13},{17,16},{18,1... | collective-permute-start | bytes 1179656 | tf_op jit(solution)/shard_map/ppermute | solution.py:509
  29.9 4.4 %collective-permute-done.8.left.refs_1_ = bf16[80,1536]{1,0:T(8,128)(2,1)S(1)} collective-permute-done((bf16[80,1536]{1,0:T(8,128)(2,1)S(1)}, bf16[80,1536]{1,0:T(8,128)(2,1)S(1)}, u32[]{:S(2)}, u32[]{:S(2)}) %collective-permute-start.8) | collective-permute-done | bytes 245792 | tf_op jit(solution)/shard_map/ppermute | solution.py:499
  34.3 0.7 %collective-permute-start.14 = (bf16[128,1536]{1,0:T(8,128)(2,1)S(1)}, bf16[128,1536]{1,0:T(8,128)(2,1)S(1)}, u32[]{:S(2)}, u32[]{:S(2)}) collective-permute-start(bf16[128,1536]{1,0:T(8,128)(2,1)S(1)} %pair.2), channel_id=1, source_target_pairs={{1,2},{2,3},{5,6},{6,7},{9,10},{10,11},{13,14},{14,15},{17,18},{18... | collective-permute-start | bytes 1179656 | tf_op jit(solution)/shard_map/ppermute | solution.py:508
  35.2 1.4 %collective-permute-done.9.left_mate = bf16[80,1536]{1,0:T(8,128)(2,1)S(1)} collective-permute-done((bf16[80,1536]{1,0:T(8,128)(2,1)S(1)}, bf16[80,1536]{1,0:T(8,128)(2,1)S(1)}, u32[]{:S(2)}, u32[]{:S(2)}) %collective-permute-start.9) | collective-permute-done | bytes 245792 | tf_op jit(solution)/shard_map/ppermute | solution.py:434
  36.6 3.1 %early.1 = (f32[256,1536]{1,0:T(8,128)S(1)}, f32[256,1536]{1,0:T(8,128)S(1)}, f32[256,1536]{1,0:T(8,128)S(1)}) custom-call(s32[2,1,2]{2,1,0:T(1,128)S(1)} %copy-done.4, bf16[256,1536]{1,0:T(8,128)(2,1)S(1)} %bitcast.7, bf16[256,1536]{1,0:T(8,128)(2,1)S(1)} %bitcast.10, bf16[256,1536]{1,0:T(8,128)(2,1)S(1)} %bitcast.6, ...), custom_call_target="tpu_custom_call" | custom-call | flops 1048576 | bytes 65536 | tf_op jit(solution)/shard_map/early/pallas_call | solution.py:442
  39.7 2.9 %collective-permute-done.15.lower = bf16[128,1536]{1,0:T(8,128)(2,1)S(1)} collective-permute-done((bf16[128,1536]{1,0:T(8,128)(2,1)S(1)}, bf16[128,1536]{1,0:T(8,128)(2,1)S(1)}, u32[]{:S(2)}, u32[]{:S(2)}) %collective-permute-start.15) | collective-permute-done | bytes 393248 | tf_op jit(solution)/shard_map/ppermute | solution.py:509
  42.8 0.4 collective-permute-start.17
  43.3 1.3 %term.1.refs_5_ = f32[256,1536]{1,0:T(8,128)S(1)} custom-call(bf16[8,32,1536]{2,1,0:T(8,128)(2,1)S(1)} %copy-done, bf16[32,1536]{1,0:T(8,128)(2,1)S(1)} %collective-permute-done.3.beside, bf16[32,1536]{1,0:T(8,128)(2,1)S(1)} %collective-permute-done.1.diagonal, bf16[80,1536]{1,0:T(8,128)(2,1)S(1)} %collective-permute-done.8.left.refs_1_, ...), custom_call_target="tpu_custom_call" | custom-call | flops 1048576 | bytes 65536 | tf_op jit(solution)/shard_map/term/pallas_call | solution.py:442
  44.6 3.4 %late0.1.refs_10_ = f32[256,1536]{1,0:T(8,128)} custom-call(s32[1,1,2]{2,1,0:T(1,128)S(1)} %copy-done.5, s32[2,1,2]{2,1,0:T(1,128)S(1)} %copy-done.6, s32[2,1,2]{2,1,0:T(1,128)S(1)} %copy-done.4, bf16[256,1536]{1,0:T(8,128)(2,1)S(1)} %bitcast.8, f32[256,1536]{1,0:T(8,128)S(1)} %get-tuple-element.35.refs_0_, f32[256,1536]{1,0:T(8,128)S(1)} %get-tuple-element.36.refs_1_, ...), custom_call_target="tpu_custom_call" | custom-call | flops 1048576 | bytes 65536 | tf_op jit(solution)/shard_map/late0/pallas_call | solution.py:534
  48.0 1.1 %collective-permute-done.12.refs_4_ = bf16[512,384]{1,0:T(8,128)(2,1)S(1)} collective-permute-done((bf16[512,384]{1,0:T(8,128)(2,1)S(1)}, bf16[512,384]{1,0:T(8,128)(2,1)S(1)}, u32[]{:S(2)}, u32[]{:S(2)}) %collective-permute-start.12) | collective-permute-done | bytes 393248 | tf_op jit(solution)/shard_map/ppermute | solution.py:487
  49.1 2.1 %late1.1 = f32[256,1536]{1,0:T(8,128)} custom-call(s32[1,1,2]{2,1,0:T(1,128)S(1)} %copy-done.5, s32[2,1,2]{2,1,0:T(1,128)S(1)} %copy-done.6, s32[2,1,2]{2,1,0:T(1,128)S(1)} %copy-done.4, bf16[256,1536]{1,0:T(8,128)(2,1)S(1)} %bitcast.9, f32[256,1536]{1,0:T(8,128)S(1)} %get-tuple-element.35.refs_0_, ...), custom_call_target="tpu_custom_call", output_to_operand_aliasing={{}: (14, {})} | custom-call | flops 1048576 | bytes 65536 | tf_op jit(solution)/shard_map/late1/pallas_call | solution.py:534
  (38 shorter events, 1.4 us)
Async XLA Ops:
  0.0 2.1 %copy-start.5 = (s32[1,1,2]{2,1,0:T(1,128)S(1)}, s32[1,1,2]{2,1,0:T(1,128)}, u32[]{:S(2)}) copy-start(s32[1,1,2]{2,1,0:T(1,128)} %reads_ref.5) | copy-start | bytes 28
  1.6 9.8 %collective-permute-start.2 = (bf16[512,1536]{1,0:T(8,128)(2,1)S(1)}, bf16[512,1536]{1,0:T(8,128)(2,1)S(1)}, u32[]{:S(2)}, u32[]{:S(2)}) collective-permute-start(bf16[512,1536]{1,0:T(8,128)(2,1)S(1)} %get-tuple-element.28.stale), channel_id=1, source_target_pairs={{0,4},{4,0},{8,12},{12,8},{1,5},{5,1},{9,13},{13,9},{2,6},{6,2},{1... | collective-permute-start | bytes 4718600 | tf_op jit(solution)/shard_map/ppermute | solution.py:434
  2.7 8.7 %collective-permute-start = (bf16[72,1536]{1,0:T(8,128)(2,1)S(1)}, bf16[72,1536]{1,0:T(8,128)(2,1)S(1)}, u32[]{:S(2)}, u32[]{:S(2)}) collective-permute-start(bf16[72,1536]{1,0:T(8,128)(2,1)S(1)} %offer.1), channel_id=1, source_target_pairs={{0,8},{4,12},{8,0},{12,4},{1,9},{5,13},{9,1},{13,5},{2,10},{6,14},... | collective-permute-start | bytes 663560 | tf_op jit(solution)/shard_map/ppermute | solution.py:482
  5.2 14.7 %copy-start = (bf16[8,32,1536]{2,1,0:T(8,128)(2,1)S(1)}, bf16[8,32,1536]{2,1,0:T(8,128)(2,1)}, u32[]{:S(2)}) copy-start(bf16[8,32,1536]{2,1,0:T(8,128)(2,1)} %cells.5) | copy-start | bytes 2359300
  5.2 4.7 %collective-permute-start.1 = (bf16[32,1536]{1,0:T(8,128)(2,1)S(1)}, bf16[32,1536]{1,0:T(8,128)(2,1)S(1)}, u32[]{:S(2)}, u32[]{:S(2)}) collective-permute-start(bf16[32,1536]{1,0:T(8,128)(2,1)S(1)} %get-tuple-element.26), channel_id=1, source_target_pairs={{4,8},{8,4},{5,9},{9,5},{6,10},{10,6},{7,11},{11,7},{20,24},{24,20... | collective-permute-start | bytes 294920 | tf_op jit(solution)/shard_map/ppermute | solution.py:473
  6.0 8.8 %collective-permute-start.5 = (bf16[64,1536]{1,0:T(8,128)(2,1)S(1)}, bf16[64,1536]{1,0:T(8,128)(2,1)S(1)}, u32[]{:S(2)}, u32[]{:S(2)}) collective-permute-start(bf16[64,1536]{1,0:T(8,128)(2,1)S(1)} %get-tuple-element.25.text), channel_id=1, source_target_pairs={{0,1},{1,2},{2,3},{3,0},{4,5},{5,6},{6,7},{7,4},{8,9},{9,10},{10,1... | collective-permute-start | bytes 589832 | tf_op jit(solution)/shard_map/ppermute | solution.py:471
  7.7 11.7 %collective-permute-start.6 = (bf16[64,1536]{1,0:T(8,128)(2,1)S(1)}, bf16[64,1536]{1,0:T(8,128)(2,1)S(1)}, u32[]{:S(2)}, u32[]{:S(2)}) collective-permute-start(bf16[64,1536]{1,0:T(8,128)(2,1)S(1)} %get-tuple-element.25.text), channel_id=1, source_target_pairs={{0,3},{1,0},{2,1},{3,2},{4,7},{5,4},{6,5},{7,6},{8,11},{9,8},{10,9... | collective-permute-start | bytes 589832 | tf_op jit(solution)/shard_map/ppermute | solution.py:471
  11.6 33.0 %collective-permute-start.13 = (bf16[512,1152]{1,0:T(8,128)(2,1)S(1)}, bf16[512,1152]{1,0:T(8,128)(2,1)S(1)}, u32[]{:S(2)}, u32[]{:S(2)}) collective-permute-start(bf16[512,1152]{1,0:T(8,128)(2,1)S(1)} %get-tuple-element.29), channel_id=1, source_target_pairs={{0,8},{4,12},{8,0},{12,4},{1,9},{5,13},{9,1},{13,5},{2,10},{6,14},... | collective-permute-start | bytes 3538952 | tf_op jit(solution)/shard_map/ppermute | solution.py:487
  14.4 5.5 %collective-permute-start.3 = (bf16[32,1536]{1,0:T(8,128)(2,1)S(1)}, bf16[32,1536]{1,0:T(8,128)(2,1)S(1)}, u32[]{:S(2)}, u32[]{:S(2)}) collective-permute-start(bf16[32,1536]{1,0:T(8,128)(2,1)S(1)} %get-tuple-element.31), channel_id=1, source_target_pairs={{0,4},{4,0},{8,12},{12,8},{1,5},{5,1},{9,13},{13,9},{2,6},{6,2},{1... | collective-permute-start | bytes 294920 | tf_op jit(solution)/shard_map/ppermute | solution.py:434
  19.4 17.2 %copy-start.1 = (bf16[8,32,1536]{2,1,0:T(8,128)(2,1)S(1)}, bf16[8,32,1536]{2,1,0:T(8,128)(2,1)}, u32[]{:S(2)}) copy-start(bf16[8,32,1536]{2,1,0:T(8,128)(2,1)} %param.11) | copy-start | bytes 2359300
  19.4 17.2 %copy-start.2 = (bf16[8,32,1536]{2,1,0:T(8,128)(2,1)S(1)}, bf16[8,32,1536]{2,1,0:T(8,128)(2,1)}, u32[]{:S(2)}) copy-start(bf16[8,32,1536]{2,1,0:T(8,128)(2,1)} %param.12) | copy-start | bytes 2359300
  19.4 17.2 %copy-start.4 = (s32[2,1,2]{2,1,0:T(1,128)S(1)}, s32[2,1,2]{2,1,0:T(1,128)}, u32[]{:S(2)}) copy-start(s32[2,1,2]{2,1,0:T(1,128)} %text_ref.5) | copy-start | bytes 52
  19.4 9.2 %collective-permute-start.7 = (bf16[128,1536]{1,0:T(8,128)(2,1)S(1)}, bf16[128,1536]{1,0:T(8,128)(2,1)S(1)}, u32[]{:S(2)}, u32[]{:S(2)}) collective-permute-start(bf16[128,1536]{1,0:T(8,128)(2,1)S(1)} %bundle.1.early), channel_id=1, source_target_pairs={{0,4},{4,0},{8,12},{12,8},{1,5},{5,1},{9,13},{13,9},{2,6},{6,2},{1... | collective-permute-start | bytes 1179656 | tf_op jit(solution)/shard_map/ppermute | solution.py:434
  20.1 9.8 %collective-permute-start.4 = (bf16[128,1536]{1,0:T(8,128)(2,1)S(1)}, bf16[128,1536]{1,0:T(8,128)(2,1)S(1)}, u32[]{:S(2)}, u32[]{:S(2)}) collective-permute-start(bf16[128,1536]{1,0:T(8,128)(2,1)S(1)} %get-tuple-element.32.both), channel_id=1, source_target_pairs={{0,4},{4,0},{8,12},{12,8},{1,5},{5,1},{9,13},{13,9},{2,6},{6,2},{1... | collective-permute-start | bytes 1179656 | tf_op jit(solution)/shard_map/ppermute | solution.py:434
  20.2 8.3 %collective-permute-start.10 = (bf16[80,1536]{1,0:T(8,128)(2,1)S(1)}, bf16[80,1536]{1,0:T(8,128)(2,1)S(1)}, u32[]{:S(2)}, u32[]{:S(2)}) collective-permute-start(bf16[80,1536]{1,0:T(8,128)(2,1)S(1)} %get-tuple-element.34), channel_id=1, source_target_pairs={{0,3},{1,0},{2,1},{3,2},{4,7},{5,4},{6,5},{7,6},{8,11},{9,8},{10,9... | collective-permute-start | bytes 737288 | tf_op jit(solution)/shard_map/ppermute | solution.py:500
  22.2 12.1 %collective-permute-start.8 = (bf16[80,1536]{1,0:T(8,128)(2,1)S(1)}, bf16[80,1536]{1,0:T(8,128)(2,1)S(1)}, u32[]{:S(2)}, u32[]{:S(2)}) collective-permute-start(bf16[80,1536]{1,0:T(8,128)(2,1)S(1)} %get-tuple-element.33), channel_id=1, source_target_pairs={{0,1},{1,2},{2,3},{3,0},{4,5},{5,6},{6,7},{7,4},{8,9},{9,10},{10,1... | collective-permute-start | bytes 737288 | tf_op jit(solution)/shard_map/ppermute | solution.py:499
  28.5 6.5 %collective-permute-start.11 = (bf16[80,1536]{1,0:T(8,128)(2,1)S(1)}, bf16[80,1536]{1,0:T(8,128)(2,1)S(1)}, u32[]{:S(2)}, u32[]{:S(2)}) collective-permute-start(bf16[80,1536]{1,0:T(8,128)(2,1)S(1)} %collective-permute-done.10.right.refs_1_), channel_id=1, source_target_pairs={{0,4},{4,0},{8,12},{12,8},{1,5},{5,1},{9,13},{13,9},{2,6},{6,2},{1... | collective-permute-start | bytes 737288 | tf_op jit(solution)/shard_map/ppermute | solution.py:434
  28.6 14.1 %collective-permute-start.15 = (bf16[128,1536]{1,0:T(8,128)(2,1)S(1)}, bf16[128,1536]{1,0:T(8,128)(2,1)S(1)}, u32[]{:S(2)}, u32[]{:S(2)}) collective-permute-start(bf16[128,1536]{1,0:T(8,128)(2,1)S(1)} %pair.3), channel_id=1, source_target_pairs={{1,0},{2,1},{5,4},{6,5},{9,8},{10,9},{13,12},{14,13},{17,16},{18,1... | collective-permute-start | bytes 1179656 | tf_op jit(solution)/shard_map/ppermute | solution.py:509
  34.3 8.3 %collective-permute-start.14 = (bf16[128,1536]{1,0:T(8,128)(2,1)S(1)}, bf16[128,1536]{1,0:T(8,128)(2,1)S(1)}, u32[]{:S(2)}, u32[]{:S(2)}) collective-permute-start(bf16[128,1536]{1,0:T(8,128)(2,1)S(1)} %pair.2), channel_id=1, source_target_pairs={{1,2},{2,3},{5,6},{6,7},{9,10},{10,11},{13,14},{14,15},{17,18},{18... | collective-permute-start | bytes 1179656 | tf_op jit(solution)/shard_map/ppermute | solution.py:508
  35.0 1.6 %collective-permute-start.9 = (bf16[80,1536]{1,0:T(8,128)(2,1)S(1)}, bf16[80,1536]{1,0:T(8,128)(2,1)S(1)}, u32[]{:S(2)}, u32[]{:S(2)}) collective-permute-start(bf16[80,1536]{1,0:T(8,128)(2,1)S(1)} %collective-permute-done.8.left.refs_1_), channel_id=1, source_target_pairs={{0,4},{4,0},{8,12},{12,8},{1,5},{5,1},{9,13},{13,9},{2,6},{6,2},{1... | collective-permute-start | bytes 737288 | tf_op jit(solution)/shard_map/ppermute | solution.py:434
  35.1 14.0 %collective-permute-start.12 = (bf16[512,384]{1,0:T(8,128)(2,1)S(1)}, bf16[512,384]{1,0:T(8,128)(2,1)S(1)}, u32[]{:S(2)}, u32[]{:S(2)}) collective-permute-start(bf16[512,384]{1,0:T(8,128)(2,1)S(1)} %get-tuple-element.38), channel_id=1, source_target_pairs={{0,8},{4,12},{8,0},{12,4},{1,9},{5,13},{9,1},{13,5},{2,10},{6,14},... | collective-permute-start | bytes 1179656 | tf_op jit(solution)/shard_map/ppermute | solution.py:487
  36.6 6.7 %copy-start.3 = (f32[3,3,1536]{2,1,0:T(4,128)S(1)}, f32[3,3,1536]{2,1,0:T(4,128)}, u32[]{:S(2)}) copy-start(f32[3,3,1536]{2,1,0:T(4,128)} %weights.1) | copy-start | bytes 165892
  42.7 1.9 %collective-permute-start.16 = (bf16[64,1536]{1,0:T(8,128)(2,1)S(1)}, bf16[64,1536]{1,0:T(8,128)(2,1)S(1)}, u32[]{:S(2)}, u32[]{:S(2)}) collective-permute-start(bf16[64,1536]{1,0:T(8,128)(2,1)S(1)} %get-tuple-element.42.refs_6_), channel_id=1, source_target_pairs={{0,4},{4,0},{8,12},{12,8},{1,5},{5,1},{9,13},{13,9},{2,6},{6,2},{1... | collective-permute-start | bytes 589832 | tf_op jit(solution)/shard_map/ppermute | solution.py:434
  42.8 1.7 %collective-permute-start.17 = (bf16[64,1536]{1,0:T(8,128)(2,1)S(1)}, bf16[64,1536]{1,0:T(8,128)(2,1)S(1)}, u32[]{:S(2)}, u32[]{:S(2)}) collective-permute-start(bf16[64,1536]{1,0:T(8,128)(2,1)S(1)} %get-tuple-element.43.refs_8_), channel_id=1, source_target_pairs={{0,4},{4,0},{8,12},{12,8},{1,5},{5,1},{9,13},{13,9},{2,6},{6,2},{1... | collective-permute-start | bytes 589832 | tf_op jit(solution)/shard_map/ppermute | solution.py:434
  (1 other events, 1.9 us)

commit v16 on v15

--- a/solution.py
+++ b/solution.py
@@ -15,7 +15,7 @@
 SCORE_SCALE = 1.0 / math.sqrt(HEAD_DIM)
 EXP2_SCALE = SCORE_SCALE * math.log2(math.e)
 CHUNK_HEADS = (9, 3)
-GROUP = 8
+GROUP = 20
 VMEM_LIMIT = 24 * 1024 * 1024
 
 

time: 51.6 us -> 51.9 us (level)
  transfers between devices with their start and end apart: 18 -> 18, of which waited for: 8 -> 8; matrix products, arithmetic and copies ran while one was open for 0% -> 0% of each run, Pallas kernels for 17% -> 18%
where the time goes in v16:
time: 51.9 us; the launch traced here: 51.2 us
  waiting for transfers between devices  22 us (42%)
  starting transfers between devices  16 us (31%)
  Pallas kernels  13 us (25%)
    pallas_call x10, Pallas kernels, local(): pl.pallas_call(kernel, out_shape=shapes, in_specs=specs or [in_vmem] * le...  7.24 us
    ppermute x1, waiting for transfers between devices, body(): right = lax.ppermute(minus, 'cols', backward)  6.32 us
    pallas_call x2, Pallas kernels, body(): pl.pallas_call(functools.partial(late_kernel, first_head), out_shape=jax....  5.73 us
    ppermute x2, waiting for transfers between devices, body(): near_parts = [lax.ppermute(text, 'cols', p) for p in (forward, backward)]  4.89 us
    ppermute x1, waiting for transfers between devices, body(): left = lax.ppermute(plus, 'cols', forward)  4.38 us
    ppermute x2, starting transfers between devices, body(): near_parts = [lax.ppermute(text, 'cols', p) for p in (forward, backward)]  3.88 us
    ppermute x2, starting transfers between devices, body(): far = [lax.ppermute(chunk, 'rows', swap) for chunk in packed]  2.93 us
    ppermute x1, waiting for transfers between devices, body(): lower = lax.ppermute(lower, 'cols', [(1, 0), (2, 1)])  2.71 us
  transfers between devices with their start and end apart: 18, of which 8 were waited for; matrix products, arithmetic and copies ran while one was open for 0% of the time, Pallas kernels for 18%

profile of v16, /device:TPU:0, one launch (start us, length us, event | category | flops | bytes accessed | tf_op | source)
XLA Modules:
  0.0 51.2 jit_solution(14383707367532273730)
XLA Ops:
  0.0 1.6 %pack.1 = (bf16[512,1536]{1,0:T(8,128)(2,1)S(1)}, bf16[32,1536]{1,0:T(8,128)(2,1)S(1)}, bf16[32,1536]{1,0:T(8,128)(2,1)S(1)}, bf16[64,1536]{1,0:T(8,128)(2,1)S(1)}) custom-call(bf16[256,1536]{1,0:T(8,128)(2,1)} %bitcast.11, bf16[256,1536]{1,0:T(8,128)(2,1)} %bitcast.12, bf16[8,32,1536]{2,1,0:T(8,128)(2,1)} %cells.5, bf16[32,1536]{1,0:T(8,128)(2,1)} %text_k.1, ...), custom_call_target="tpu_custom_call" | custom-call | flops 1048576 | bytes 65536 | tf_op jit(solution)/shard_map/pack/pallas_call | solution.py:442
  1.6 0.5 %collective-permute-start.2 = (bf16[512,1536]{1,0:T(8,128)(2,1)S(1)}, bf16[512,1536]{1,0:T(8,128)(2,1)S(1)}, u32[]{:S(2)}, u32[]{:S(2)}) collective-permute-start(bf16[512,1536]{1,0:T(8,128)(2,1)S(1)} %get-tuple-element.28.stale), channel_id=1, source_target_pairs={{0,4},{4,0},{8,12},{12,8},{1,5},{5,1},{9,13},{13,9},{2,6},{6,2},{1... | collective-permute-start | bytes 4718600 | tf_op jit(solution)/shard_map/ppermute | solution.py:434
  2.1 0.6 %offer.1 = bf16[72,1536]{1,0:T(8,128)(2,1)S(1)} custom-call(s32[1,1,2]{2,1,0:T(1,128)S(1)} %copy-done.5, bf16[64,1536]{1,0:T(8,128)(2,1)S(1)} %get-tuple-element.25.text), custom_call_target="tpu_custom_call" | custom-call | flops 1048576 | bytes 65536 | tf_op jit(solution)/shard_map/offer/pallas_call | solution.py:442
  2.7 2.6 %collective-permute-start = (bf16[72,1536]{1,0:T(8,128)(2,1)S(1)}, bf16[72,1536]{1,0:T(8,128)(2,1)S(1)}, u32[]{:S(2)}, u32[]{:S(2)}) collective-permute-start(bf16[72,1536]{1,0:T(8,128)(2,1)S(1)} %offer.1), channel_id=1, source_target_pairs={{0,8},{4,12},{8,0},{12,4},{1,9},{5,13},{9,1},{13,5},{2,10},{6,14},... | collective-permute-start | bytes 663560 | tf_op jit(solution)/shard_map/ppermute | solution.py:482
  5.2 0.8 %collective-permute-start.1 = (bf16[32,1536]{1,0:T(8,128)(2,1)S(1)}, bf16[32,1536]{1,0:T(8,128)(2,1)S(1)}, u32[]{:S(2)}, u32[]{:S(2)}) collective-permute-start(bf16[32,1536]{1,0:T(8,128)(2,1)S(1)} %get-tuple-element.26), channel_id=1, source_target_pairs={{4,8},{8,4},{5,9},{9,5},{6,10},{10,6},{7,11},{11,7},{20,24},{24,20... | collective-permute-start | bytes 294920 | tf_op jit(solution)/shard_map/ppermute | solution.py:473
  6.0 1.6 %collective-permute-start.5 = (bf16[64,1536]{1,0:T(8,128)(2,1)S(1)}, bf16[64,1536]{1,0:T(8,128)(2,1)S(1)}, u32[]{:S(2)}, u32[]{:S(2)}) collective-permute-start(bf16[64,1536]{1,0:T(8,128)(2,1)S(1)} %get-tuple-element.25.text), channel_id=1, source_target_pairs={{0,1},{1,2},{2,3},{3,0},{4,5},{5,6},{6,7},{7,4},{8,9},{9,10},{10,1... | collective-permute-start | bytes 589832 | tf_op jit(solution)/shard_map/ppermute | solution.py:471
  7.7 2.2 %collective-permute-start.6 = (bf16[64,1536]{1,0:T(8,128)(2,1)S(1)}, bf16[64,1536]{1,0:T(8,128)(2,1)S(1)}, u32[]{:S(2)}, u32[]{:S(2)}) collective-permute-start(bf16[64,1536]{1,0:T(8,128)(2,1)S(1)} %get-tuple-element.25.text), channel_id=1, source_target_pairs={{0,3},{1,0},{2,1},{3,2},{4,7},{5,4},{6,5},{7,6},{8,11},{9,8},{10,9... | collective-permute-start | bytes 589832 | tf_op jit(solution)/shard_map/ppermute | solution.py:471
  9.9 1.4 %collective-permute-done.across = bf16[72,1536]{1,0:T(8,128)(2,1)S(1)} collective-permute-done((bf16[72,1536]{1,0:T(8,128)(2,1)S(1)}, bf16[72,1536]{1,0:T(8,128)(2,1)S(1)}, u32[]{:S(2)}, u32[]{:S(2)}) %collective-permute-start) | collective-permute-done | bytes 221216 | tf_op jit(solution)/shard_map/ppermute | solution.py:482
  11.6 2.9 %collective-permute-start.13 = (bf16[512,1152]{1,0:T(8,128)(2,1)S(1)}, bf16[512,1152]{1,0:T(8,128)(2,1)S(1)}, u32[]{:S(2)}, u32[]{:S(2)}) collective-permute-start(bf16[512,1152]{1,0:T(8,128)(2,1)S(1)} %get-tuple-element.29), channel_id=1, source_target_pairs={{0,8},{4,12},{8,0},{12,4},{1,9},{5,13},{9,1},{13,5},{2,10},{6,14},... | collective-permute-start | bytes 3538952 | tf_op jit(solution)/shard_map/ppermute | solution.py:487
  14.8 4.5 %collective-permute-done.6.refs_1_.refs_0_ = bf16[64,1536]{1,0:T(8,128)(2,1)S(1)} collective-permute-done((bf16[64,1536]{1,0:T(8,128)(2,1)S(1)}, bf16[64,1536]{1,0:T(8,128)(2,1)S(1)}, u32[]{:S(2)}, u32[]{:S(2)}) %collective-permute-start.6) | collective-permute-done | bytes 196640 | tf_op jit(solution)/shard_map/ppermute | solution.py:471
  19.4 0.5 collective-permute-start.7
  20.2 2.0 %collective-permute-start.10 = (bf16[80,1536]{1,0:T(8,128)(2,1)S(1)}, bf16[80,1536]{1,0:T(8,128)(2,1)S(1)}, u32[]{:S(2)}, u32[]{:S(2)}) collective-permute-start(bf16[80,1536]{1,0:T(8,128)(2,1)S(1)} %get-tuple-element.34), channel_id=1, source_target_pairs={{0,3},{1,0},{2,1},{3,2},{4,7},{5,4},{6,5},{7,6},{8,11},{9,8},{10,9... | collective-permute-start | bytes 737288 | tf_op jit(solution)/shard_map/ppermute | solution.py:500
  22.2 6.3 %collective-permute-done.10.right.refs_1_ = bf16[80,1536]{1,0:T(8,128)(2,1)S(1)} collective-permute-done((bf16[80,1536]{1,0:T(8,128)(2,1)S(1)}, bf16[80,1536]{1,0:T(8,128)(2,1)S(1)}, u32[]{:S(2)}, u32[]{:S(2)}) %collective-permute-start.10) | collective-permute-done | bytes 245792 | tf_op jit(solution)/shard_map/ppermute | solution.py:500
  28.6 1.3 %collective-permute-start.15 = (bf16[128,1536]{1,0:T(8,128)(2,1)S(1)}, bf16[128,1536]{1,0:T(8,128)(2,1)S(1)}, u32[]{:S(2)}, u32[]{:S(2)}) collective-permute-start(bf16[128,1536]{1,0:T(8,128)(2,1)S(1)} %pair.3), channel_id=1, source_target_pairs={{1,0},{2,1},{5,4},{6,5},{9,8},{10,9},{13,12},{14,13},{17,16},{18,1... | collective-permute-start | bytes 1179656 | tf_op jit(solution)/shard_map/ppermute | solution.py:509
  29.9 4.4 %collective-permute-done.8.left.refs_1_ = bf16[80,1536]{1,0:T(8,128)(2,1)S(1)} collective-permute-done((bf16[80,1536]{1,0:T(8,128)(2,1)S(1)}, bf16[80,1536]{1,0:T(8,128)(2,1)S(1)}, u32[]{:S(2)}, u32[]{:S(2)}) %collective-permute-start.8) | collective-permute-done | bytes 245792 | tf_op jit(solution)/shard_map/ppermute | solution.py:499
  34.3 0.7 %collective-permute-start.14 = (bf16[128,1536]{1,0:T(8,128)(2,1)S(1)}, bf16[128,1536]{1,0:T(8,128)(2,1)S(1)}, u32[]{:S(2)}, u32[]{:S(2)}) collective-permute-start(bf16[128,1536]{1,0:T(8,128)(2,1)S(1)} %pair.2), channel_id=1, source_target_pairs={{1,2},{2,3},{5,6},{6,7},{9,10},{10,11},{13,14},{14,15},{17,18},{18... | collective-permute-start | bytes 1179656 | tf_op jit(solution)/shard_map/ppermute | solution.py:508
  35.2 1.4 %collective-permute-done.9.left_mate = bf16[80,1536]{1,0:T(8,128)(2,1)S(1)} collective-permute-done((bf16[80,1536]{1,0:T(8,128)(2,1)S(1)}, bf16[80,1536]{1,0:T(8,128)(2,1)S(1)}, u32[]{:S(2)}, u32[]{:S(2)}) %collective-permute-start.9) | collective-permute-done | bytes 245792 | tf_op jit(solution)/shard_map/ppermute | solution.py:434
  36.6 3.3 %early.1 = (f32[256,1536]{1,0:T(8,128)S(1)}, f32[256,1536]{1,0:T(8,128)S(1)}, f32[256,1536]{1,0:T(8,128)S(1)}) custom-call(s32[2,1,2]{2,1,0:T(1,128)S(1)} %copy-done.4, bf16[256,1536]{1,0:T(8,128)(2,1)S(1)} %bitcast.7, bf16[256,1536]{1,0:T(8,128)(2,1)S(1)} %bitcast.10, bf16[256,1536]{1,0:T(8,128)(2,1)S(1)} %bitcast.6, ...), custom_call_target="tpu_custom_call" | custom-call | flops 1048576 | bytes 65536 | tf_op jit(solution)/shard_map/early/pallas_call | solution.py:442
  39.9 2.7 %collective-permute-done.15.lower = bf16[128,1536]{1,0:T(8,128)(2,1)S(1)} collective-permute-done((bf16[128,1536]{1,0:T(8,128)(2,1)S(1)}, bf16[128,1536]{1,0:T(8,128)(2,1)S(1)}, u32[]{:S(2)}, u32[]{:S(2)}) %collective-permute-start.15) | collective-permute-done | bytes 393248 | tf_op jit(solution)/shard_map/ppermute | solution.py:509
  42.8 0.4 collective-permute-start.17
  43.3 1.3 %term.1.refs_5_ = f32[256,1536]{1,0:T(8,128)S(1)} custom-call(bf16[8,32,1536]{2,1,0:T(8,128)(2,1)S(1)} %copy-done, bf16[32,1536]{1,0:T(8,128)(2,1)S(1)} %collective-permute-done.3.beside, bf16[32,1536]{1,0:T(8,128)(2,1)S(1)} %collective-permute-done.1.diagonal, bf16[80,1536]{1,0:T(8,128)(2,1)S(1)} %collective-permute-done.8.left.refs_1_, ...), custom_call_target="tpu_custom_call" | custom-call | flops 1048576 | bytes 65536 | tf_op jit(solution)/shard_map/term/pallas_call | solution.py:442
  44.6 3.7 %late0.1.refs_10_ = f32[256,1536]{1,0:T(8,128)} custom-call(s32[1,1,2]{2,1,0:T(1,128)S(1)} %copy-done.5, s32[2,1,2]{2,1,0:T(1,128)S(1)} %copy-done.6, s32[2,1,2]{2,1,0:T(1,128)S(1)} %copy-done.4, bf16[256,1536]{1,0:T(8,128)(2,1)S(1)} %bitcast.8, f32[256,1536]{1,0:T(8,128)S(1)} %get-tuple-element.35.refs_0_, f32[256,1536]{1,0:T(8,128)S(1)} %get-tuple-element.36.refs_1_, ...), custom_call_target="tpu_custom_call" | custom-call | flops 1048576 | bytes 65536 | tf_op jit(solution)/shard_map/late0/pallas_call | solution.py:534
  48.3 0.8 %collective-permute-done.12.refs_4_ = bf16[512,384]{1,0:T(8,128)(2,1)S(1)} collective-permute-done((bf16[512,384]{1,0:T(8,128)(2,1)S(1)}, bf16[512,384]{1,0:T(8,128)(2,1)S(1)}, u32[]{:S(2)}, u32[]{:S(2)}) %collective-permute-start.12) | collective-permute-done | bytes 393248 | tf_op jit(solution)/shard_map/ppermute | solution.py:487
  49.1 2.1 %late1.1 = f32[256,1536]{1,0:T(8,128)} custom-call(s32[1,1,2]{2,1,0:T(1,128)S(1)} %copy-done.5, s32[2,1,2]{2,1,0:T(1,128)S(1)} %copy-done.6, s32[2,1,2]{2,1,0:T(1,128)S(1)} %copy-done.4, bf16[256,1536]{1,0:T(8,128)(2,1)S(1)} %bitcast.9, f32[256,1536]{1,0:T(8,128)S(1)} %get-tuple-element.35.refs_0_, ...), custom_call_target="tpu_custom_call", output_to_operand_aliasing={{}: (14, {})} | custom-call | flops 1048576 | bytes 65536 | tf_op jit(solution)/shard_map/late1/pallas_call | solution.py:534
  (38 shorter events, 1.4 us)
Async XLA Ops:
  0.0 2.1 %copy-start.5 = (s32[1,1,2]{2,1,0:T(1,128)S(1)}, s32[1,1,2]{2,1,0:T(1,128)}, u32[]{:S(2)}) copy-start(s32[1,1,2]{2,1,0:T(1,128)} %reads_ref.5) | copy-start | bytes 28
  1.6 9.8 %collective-permute-start.2 = (bf16[512,1536]{1,0:T(8,128)(2,1)S(1)}, bf16[512,1536]{1,0:T(8,128)(2,1)S(1)}, u32[]{:S(2)}, u32[]{:S(2)}) collective-permute-start(bf16[512,1536]{1,0:T(8,128)(2,1)S(1)} %get-tuple-element.28.stale), channel_id=1, source_target_pairs={{0,4},{4,0},{8,12},{12,8},{1,5},{5,1},{9,13},{13,9},{2,6},{6,2},{1... | collective-permute-start | bytes 4718600 | tf_op jit(solution)/shard_map/ppermute | solution.py:434
  2.7 8.7 %collective-permute-start = (bf16[72,1536]{1,0:T(8,128)(2,1)S(1)}, bf16[72,1536]{1,0:T(8,128)(2,1)S(1)}, u32[]{:S(2)}, u32[]{:S(2)}) collective-permute-start(bf16[72,1536]{1,0:T(8,128)(2,1)S(1)} %offer.1), channel_id=1, source_target_pairs={{0,8},{4,12},{8,0},{12,4},{1,9},{5,13},{9,1},{13,5},{2,10},{6,14},... | collective-permute-start | bytes 663560 | tf_op jit(solution)/shard_map/ppermute | solution.py:482
  5.2 14.7 %copy-start = (bf16[8,32,1536]{2,1,0:T(8,128)(2,1)S(1)}, bf16[8,32,1536]{2,1,0:T(8,128)(2,1)}, u32[]{:S(2)}) copy-start(bf16[8,32,1536]{2,1,0:T(8,128)(2,1)} %cells.5) | copy-start | bytes 2359300
  5.2 4.7 %collective-permute-start.1 = (bf16[32,1536]{1,0:T(8,128)(2,1)S(1)}, bf16[32,1536]{1,0:T(8,128)(2,1)S(1)}, u32[]{:S(2)}, u32[]{:S(2)}) collective-permute-start(bf16[32,1536]{1,0:T(8,128)(2,1)S(1)} %get-tuple-element.26), channel_id=1, source_target_pairs={{4,8},{8,4},{5,9},{9,5},{6,10},{10,6},{7,11},{11,7},{20,24},{24,20... | collective-permute-start | bytes 294920 | tf_op jit(solution)/shard_map/ppermute | solution.py:473
  6.0 8.8 %collective-permute-start.5 = (bf16[64,1536]{1,0:T(8,128)(2,1)S(1)}, bf16[64,1536]{1,0:T(8,128)(2,1)S(1)}, u32[]{:S(2)}, u32[]{:S(2)}) collective-permute-start(bf16[64,1536]{1,0:T(8,128)(2,1)S(1)} %get-tuple-element.25.text), channel_id=1, source_target_pairs={{0,1},{1,2},{2,3},{3,0},{4,5},{5,6},{6,7},{7,4},{8,9},{9,10},{10,1... | collective-permute-start | bytes 589832 | tf_op jit(solution)/shard_map/ppermute | solution.py:471
  7.7 11.7 %collective-permute-start.6 = (bf16[64,1536]{1,0:T(8,128)(2,1)S(1)}, bf16[64,1536]{1,0:T(8,128)(2,1)S(1)}, u32[]{:S(2)}, u32[]{:S(2)}) collective-permute-start(bf16[64,1536]{1,0:T(8,128)(2,1)S(1)} %get-tuple-element.25.text), channel_id=1, source_target_pairs={{0,3},{1,0},{2,1},{3,2},{4,7},{5,4},{6,5},{7,6},{8,11},{9,8},{10,9... | collective-permute-start | bytes 589832 | tf_op jit(solution)/shard_map/ppermute | solution.py:471
  11.6 33.0 %collective-permute-start.13 = (bf16[512,1152]{1,0:T(8,128)(2,1)S(1)}, bf16[512,1152]{1,0:T(8,128)(2,1)S(1)}, u32[]{:S(2)}, u32[]{:S(2)}) collective-permute-start(bf16[512,1152]{1,0:T(8,128)(2,1)S(1)} %get-tuple-element.29), channel_id=1, source_target_pairs={{0,8},{4,12},{8,0},{12,4},{1,9},{5,13},{9,1},{13,5},{2,10},{6,14},... | collective-permute-start | bytes 3538952 | tf_op jit(solution)/shard_map/ppermute | solution.py:487
  14.4 5.5 %collective-permute-start.3 = (bf16[32,1536]{1,0:T(8,128)(2,1)S(1)}, bf16[32,1536]{1,0:T(8,128)(2,1)S(1)}, u32[]{:S(2)}, u32[]{:S(2)}) collective-permute-start(bf16[32,1536]{1,0:T(8,128)(2,1)S(1)} %get-tuple-element.31), channel_id=1, source_target_pairs={{0,4},{4,0},{8,12},{12,8},{1,5},{5,1},{9,13},{13,9},{2,6},{6,2},{1... | collective-permute-start | bytes 294920 | tf_op jit(solution)/shard_map/ppermute | solution.py:434
  19.4 17.2 %copy-start.1 = (bf16[8,32,1536]{2,1,0:T(8,128)(2,1)S(1)}, bf16[8,32,1536]{2,1,0:T(8,128)(2,1)}, u32[]{:S(2)}) copy-start(bf16[8,32,1536]{2,1,0:T(8,128)(2,1)} %param.11) | copy-start | bytes 2359300
  19.4 17.2 %copy-start.2 = (bf16[8,32,1536]{2,1,0:T(8,128)(2,1)S(1)}, bf16[8,32,1536]{2,1,0:T(8,128)(2,1)}, u32[]{:S(2)}) copy-start(bf16[8,32,1536]{2,1,0:T(8,128)(2,1)} %param.12) | copy-start | bytes 2359300
  19.4 17.2 %copy-start.4 = (s32[2,1,2]{2,1,0:T(1,128)S(1)}, s32[2,1,2]{2,1,0:T(1,128)}, u32[]{:S(2)}) copy-start(s32[2,1,2]{2,1,0:T(1,128)} %text_ref.5) | copy-start | bytes 52
  19.4 9.2 %collective-permute-start.7 = (bf16[128,1536]{1,0:T(8,128)(2,1)S(1)}, bf16[128,1536]{1,0:T(8,128)(2,1)S(1)}, u32[]{:S(2)}, u32[]{:S(2)}) collective-permute-start(bf16[128,1536]{1,0:T(8,128)(2,1)S(1)} %bundle.1.early), channel_id=1, source_target_pairs={{0,4},{4,0},{8,12},{12,8},{1,5},{5,1},{9,13},{13,9},{2,6},{6,2},{1... | collective-permute-start | bytes 1179656 | tf_op jit(solution)/shard_map/ppermute | solution.py:434
  20.1 9.8 %collective-permute-start.4 = (bf16[128,1536]{1,0:T(8,128)(2,1)S(1)}, bf16[128,1536]{1,0:T(8,128)(2,1)S(1)}, u32[]{:S(2)}, u32[]{:S(2)}) collective-permute-start(bf16[128,1536]{1,0:T(8,128)(2,1)S(1)} %get-tuple-element.32.both), channel_id=1, source_target_pairs={{0,4},{4,0},{8,12},{12,8},{1,5},{5,1},{9,13},{13,9},{2,6},{6,2},{1... | collective-permute-start | bytes 1179656 | tf_op jit(solution)/shard_map/ppermute | solution.py:434
  20.2 8.3 %collective-permute-start.10 = (bf16[80,1536]{1,0:T(8,128)(2,1)S(1)}, bf16[80,1536]{1,0:T(8,128)(2,1)S(1)}, u32[]{:S(2)}, u32[]{:S(2)}) collective-permute-start(bf16[80,1536]{1,0:T(8,128)(2,1)S(1)} %get-tuple-element.34), channel_id=1, source_target_pairs={{0,3},{1,0},{2,1},{3,2},{4,7},{5,4},{6,5},{7,6},{8,11},{9,8},{10,9... | collective-permute-start | bytes 737288 | tf_op jit(solution)/shard_map/ppermute | solution.py:500
  22.2 12.1 %collective-permute-start.8 = (bf16[80,1536]{1,0:T(8,128)(2,1)S(1)}, bf16[80,1536]{1,0:T(8,128)(2,1)S(1)}, u32[]{:S(2)}, u32[]{:S(2)}) collective-permute-start(bf16[80,1536]{1,0:T(8,128)(2,1)S(1)} %get-tuple-element.33), channel_id=1, source_target_pairs={{0,1},{1,2},{2,3},{3,0},{4,5},{5,6},{6,7},{7,4},{8,9},{9,10},{10,1... | collective-permute-start | bytes 737288 | tf_op jit(solution)/shard_map/ppermute | solution.py:499
  28.5 6.5 %collective-permute-start.11 = (bf16[80,1536]{1,0:T(8,128)(2,1)S(1)}, bf16[80,1536]{1,0:T(8,128)(2,1)S(1)}, u32[]{:S(2)}, u32[]{:S(2)}) collective-permute-start(bf16[80,1536]{1,0:T(8,128)(2,1)S(1)} %collective-permute-done.10.right.refs_1_), channel_id=1, source_target_pairs={{0,4},{4,0},{8,12},{12,8},{1,5},{5,1},{9,13},{13,9},{2,6},{6,2},{1... | collective-permute-start | bytes 737288 | tf_op jit(solution)/shard_map/ppermute | solution.py:434
  28.6 14.1 %collective-permute-start.15 = (bf16[128,1536]{1,0:T(8,128)(2,1)S(1)}, bf16[128,1536]{1,0:T(8,128)(2,1)S(1)}, u32[]{:S(2)}, u32[]{:S(2)}) collective-permute-start(bf16[128,1536]{1,0:T(8,128)(2,1)S(1)} %pair.3), channel_id=1, source_target_pairs={{1,0},{2,1},{5,4},{6,5},{9,8},{10,9},{13,12},{14,13},{17,16},{18,1... | collective-permute-start | bytes 1179656 | tf_op jit(solution)/shard_map/ppermute | solution.py:509
  34.3 8.3 %collective-permute-start.14 = (bf16[128,1536]{1,0:T(8,128)(2,1)S(1)}, bf16[128,1536]{1,0:T(8,128)(2,1)S(1)}, u32[]{:S(2)}, u32[]{:S(2)}) collective-permute-start(bf16[128,1536]{1,0:T(8,128)(2,1)S(1)} %pair.2), channel_id=1, source_target_pairs={{1,2},{2,3},{5,6},{6,7},{9,10},{10,11},{13,14},{14,15},{17,18},{18... | collective-permute-start | bytes 1179656 | tf_op jit(solution)/shard_map/ppermute | solution.py:508
  35.0 1.6 %collective-permute-start.9 = (bf16[80,1536]{1,0:T(8,128)(2,1)S(1)}, bf16[80,1536]{1,0:T(8,128)(2,1)S(1)}, u32[]{:S(2)}, u32[]{:S(2)}) collective-permute-start(bf16[80,1536]{1,0:T(8,128)(2,1)S(1)} %collective-permute-done.8.left.refs_1_), channel_id=1, source_target_pairs={{0,4},{4,0},{8,12},{12,8},{1,5},{5,1},{9,13},{13,9},{2,6},{6,2},{1... | collective-permute-start | bytes 737288 | tf_op jit(solution)/shard_map/ppermute | solution.py:434
  35.1 14.0 %collective-permute-start.12 = (bf16[512,384]{1,0:T(8,128)(2,1)S(1)}, bf16[512,384]{1,0:T(8,128)(2,1)S(1)}, u32[]{:S(2)}, u32[]{:S(2)}) collective-permute-start(bf16[512,384]{1,0:T(8,128)(2,1)S(1)} %get-tuple-element.38), channel_id=1, source_target_pairs={{0,8},{4,12},{8,0},{12,4},{1,9},{5,13},{9,1},{13,5},{2,10},{6,14},... | collective-permute-start | bytes 1179656 | tf_op jit(solution)/shard_map/ppermute | solution.py:487
  36.6 6.7 %copy-start.3 = (f32[3,3,1536]{2,1,0:T(4,128)S(1)}, f32[3,3,1536]{2,1,0:T(4,128)}, u32[]{:S(2)}) copy-start(f32[3,3,1536]{2,1,0:T(4,128)} %weights.1) | copy-start | bytes 165892
  42.7 1.9 %collective-permute-start.16 = (bf16[64,1536]{1,0:T(8,128)(2,1)S(1)}, bf16[64,1536]{1,0:T(8,128)(2,1)S(1)}, u32[]{:S(2)}, u32[]{:S(2)}) collective-permute-start(bf16[64,1536]{1,0:T(8,128)(2,1)S(1)} %get-tuple-element.42.refs_6_), channel_id=1, source_target_pairs={{0,4},{4,0},{8,12},{12,8},{1,5},{5,1},{9,13},{13,9},{2,6},{6,2},{1... | collective-permute-start | bytes 589832 | tf_op jit(solution)/shard_map/ppermute | solution.py:434
  42.8 1.7 %collective-permute-start.17 = (bf16[64,1536]{1,0:T(8,128)(2,1)S(1)}, bf16[64,1536]{1,0:T(8,128)(2,1)S(1)}, u32[]{:S(2)}, u32[]{:S(2)}) collective-permute-start(bf16[64,1536]{1,0:T(8,128)(2,1)S(1)} %get-tuple-element.43.refs_8_), channel_id=1, source_target_pairs={{0,4},{4,0},{8,12},{12,8},{1,5},{5,1},{9,13},{13,9},{2,6},{6,2},{1... | collective-permute-start | bytes 589832 | tf_op jit(solution)/shard_map/ppermute | solution.py:434
  (1 other events, 1.9 us)

commit v17 on v15

--- a/solution.py
+++ b/solution.py
@@ -516,15 +516,15 @@
         both, both_mate, early, early_mate, left, left_mate, right, right_mate,
         specs=[pl.BlockSpec(memory_space=pltpu.SMEM)] + [in_vmem] * 11,
     )
-    upper, lower = after(upper, sums), after(lower, sums)
-    far_side = local(choose_kernel, "choose", rows_of(2 * shard, 2 * shard), upper, lower)
-    late = [part for side in far_side for part in (side, to_mate(side))]
     term = local(
         term_kernel,
         "term",
         jax.ShapeDtypeStruct((tokens, width), jnp.float32),
         v_fresh, beside, diagonal, left, right, conv_w,
     )
+    upper, lower = after(upper, sums, term), after(lower, sums, term)
+    far_side = local(choose_kernel, "choose", rows_of(2 * shard, 2 * shard), upper, lower)
+    late = [part for side in far_side for part in (side, to_mate(side))]
 
     out = None
     first_head = 0

time: 51.6 us -> 54.5 us (1.056)
  starting transfers between devices: 16 us -> 17.9 us
    ppermute x1, waiting for transfers between devices: 6.32 us -> 3.46 us  [body(): right = lax.ppermute(minus, 'cols', backward)]
    ppermute x1, waiting for transfers between devices: 4.38 us -> 6.78 us  [body(): left = lax.ppermute(plus, 'cols', forward)]
    ppermute x1, waiting for transfers between devices: 2.9 us -> 4.95 us  [body(): lower = lax.ppermute(lower, 'cols', [(1, 0), (2, 1)])]
    ppermute x2, waiting for transfers between devices: 1.15 us -> 0.01 us  [body(): far = [lax.ppermute(chunk, 'rows', swap) for chunk in packed]]
    ppermute x1, starting transfers between devices: 0.01 us -> 1.02 us  [body(): left = lax.ppermute(plus, 'cols', forward)]
    ppermute x1, starting transfers between devices: 2.02 us -> 2.8 us  [body(): right = lax.ppermute(minus, 'cols', backward)]
  transfers between devices with their start and end apart: 18 -> 18, of which waited for: 8 -> 9; matrix products, arithmetic and copies ran while one was open for 0% -> 0% of each run, Pallas kernels for 17% -> 16%
where the time goes in v17:
time: 54.5 us; the launch traced here: 53.5 us
  waiting for transfers between devices  22.8 us (42%)
  starting transfers between devices  17.9 us (33%)
  Pallas kernels  12.6 us (23%)
    pallas_call x10, Pallas kernels, local(): pl.pallas_call(kernel, out_shape=shapes, in_specs=specs or [in_vmem] * le...  7.13 us
    ppermute x1, waiting for transfers between devices, body(): left = lax.ppermute(plus, 'cols', forward)  6.78 us
    pallas_call x2, Pallas kernels, body(): pl.pallas_call(functools.partial(late_kernel, first_head), out_shape=jax....  5.43 us
    ppermute x1, waiting for transfers between devices, body(): lower = lax.ppermute(lower, 'cols', [(1, 0), (2, 1)])  4.95 us
    ppermute x2, waiting for transfers between devices, body(): near_parts = [lax.ppermute(text, 'cols', p) for p in (forward, backward)]  4.89 us
    ppermute x2, starting transfers between devices, body(): near_parts = [lax.ppermute(text, 'cols', p) for p in (forward, backward)]  3.88 us
    ppermute x1, waiting for transfers between devices, body(): right = lax.ppermute(minus, 'cols', backward)  3.46 us
    ppermute x2, starting transfers between devices, body(): far = [lax.ppermute(chunk, 'rows', swap) for chunk in packed]  2.93 us
  transfers between devices with their start and end apart: 18, of which 9 were waited for; matrix products, arithmetic and copies ran while one was open for 0% of the time, Pallas kernels for 16%

profile of v17, /device:TPU:0, one launch (start us, length us, event | category | flops | bytes accessed | tf_op | source)
XLA Modules:
  0.0 53.5 jit_solution(18263220448292657144)
XLA Ops:
  0.0 1.6 %pack.1 = (bf16[512,1536]{1,0:T(8,128)(2,1)S(1)}, bf16[32,1536]{1,0:T(8,128)(2,1)S(1)}, bf16[32,1536]{1,0:T(8,128)(2,1)S(1)}, bf16[64,1536]{1,0:T(8,128)(2,1)S(1)}) custom-call(bf16[256,1536]{1,0:T(8,128)(2,1)} %bitcast.11, bf16[256,1536]{1,0:T(8,128)(2,1)} %bitcast.12, bf16[8,32,1536]{2,1,0:T(8,128)(2,1)} %cells.5, bf16[32,1536]{1,0:T(8,128)(2,1)} %text_k.1, ...), custom_call_target="tpu_custom_call" | custom-call | flops 1048576 | bytes 65536 | tf_op jit(solution)/shard_map/pack/pallas_call | solution.py:442
  1.6 0.5 collective-permute-start.2
  2.1 0.6 %offer.1 = bf16[72,1536]{1,0:T(8,128)(2,1)S(1)} custom-call(s32[1,1,2]{2,1,0:T(1,128)S(1)} %copy-done.5, bf16[64,1536]{1,0:T(8,128)(2,1)S(1)} %get-tuple-element.25.text), custom_call_target="tpu_custom_call" | custom-call | flops 1048576 | bytes 65536 | tf_op jit(solution)/shard_map/offer/pallas_call | solution.py:442
  2.7 2.6 %collective-permute-start = (bf16[72,1536]{1,0:T(8,128)(2,1)S(1)}, bf16[72,1536]{1,0:T(8,128)(2,1)S(1)}, u32[]{:S(2)}, u32[]{:S(2)}) collective-permute-start(bf16[72,1536]{1,0:T(8,128)(2,1)S(1)} %offer.1), channel_id=1, source_target_pairs={{0,8},{4,12},{8,0},{12,4},{1,9},{5,13},{9,1},{13,5},{2,10},{6,14},... | collective-permute-start | bytes 663560 | tf_op jit(solution)/shard_map/ppermute | solution.py:482
  5.2 0.8 %collective-permute-start.1 = (bf16[32,1536]{1,0:T(8,128)(2,1)S(1)}, bf16[32,1536]{1,0:T(8,128)(2,1)S(1)}, u32[]{:S(2)}, u32[]{:S(2)}) collective-permute-start(bf16[32,1536]{1,0:T(8,128)(2,1)S(1)} %get-tuple-element.26), channel_id=1, source_target_pairs={{4,8},{8,4},{5,9},{9,5},{6,10},{10,6},{7,11},{11,7},{20,24},{24,20... | collective-permute-start | bytes 294920 | tf_op jit(solution)/shard_map/ppermute | solution.py:473
  6.0 1.6 %collective-permute-start.5 = (bf16[64,1536]{1,0:T(8,128)(2,1)S(1)}, bf16[64,1536]{1,0:T(8,128)(2,1)S(1)}, u32[]{:S(2)}, u32[]{:S(2)}) collective-permute-start(bf16[64,1536]{1,0:T(8,128)(2,1)S(1)} %get-tuple-element.25.text), channel_id=1, source_target_pairs={{0,1},{1,2},{2,3},{3,0},{4,5},{5,6},{6,7},{7,4},{8,9},{9,10},{10,1... | collective-permute-start | bytes 589832 | tf_op jit(solution)/shard_map/ppermute | solution.py:471
  7.7 2.2 %collective-permute-start.6 = (bf16[64,1536]{1,0:T(8,128)(2,1)S(1)}, bf16[64,1536]{1,0:T(8,128)(2,1)S(1)}, u32[]{:S(2)}, u32[]{:S(2)}) collective-permute-start(bf16[64,1536]{1,0:T(8,128)(2,1)S(1)} %get-tuple-element.25.text), channel_id=1, source_target_pairs={{0,3},{1,0},{2,1},{3,2},{4,7},{5,4},{6,5},{7,6},{8,11},{9,8},{10,9... | collective-permute-start | bytes 589832 | tf_op jit(solution)/shard_map/ppermute | solution.py:471
  9.9 1.4 %collective-permute-done.across = bf16[72,1536]{1,0:T(8,128)(2,1)S(1)} collective-permute-done((bf16[72,1536]{1,0:T(8,128)(2,1)S(1)}, bf16[72,1536]{1,0:T(8,128)(2,1)S(1)}, u32[]{:S(2)}, u32[]{:S(2)}) %collective-permute-start) | collective-permute-done | bytes 221216 | tf_op jit(solution)/shard_map/ppermute | solution.py:482
  11.6 2.9 %collective-permute-start.13 = (bf16[512,1152]{1,0:T(8,128)(2,1)S(1)}, bf16[512,1152]{1,0:T(8,128)(2,1)S(1)}, u32[]{:S(2)}, u32[]{:S(2)}) collective-permute-start(bf16[512,1152]{1,0:T(8,128)(2,1)S(1)} %get-tuple-element.29), channel_id=1, source_target_pairs={{0,8},{4,12},{8,0},{12,4},{1,9},{5,13},{9,1},{13,5},{2,10},{6,14},... | collective-permute-start | bytes 3538952 | tf_op jit(solution)/shard_map/ppermute | solution.py:487
  14.8 4.5 %collective-permute-done.6.refs_1_.refs_0_ = bf16[64,1536]{1,0:T(8,128)(2,1)S(1)} collective-permute-done((bf16[64,1536]{1,0:T(8,128)(2,1)S(1)}, bf16[64,1536]{1,0:T(8,128)(2,1)S(1)}, u32[]{:S(2)}, u32[]{:S(2)}) %collective-permute-start.6) | collective-permute-done | bytes 196640 | tf_op jit(solution)/shard_map/ppermute | solution.py:471
  19.4 0.5 collective-permute-start.7
  20.2 1.0 %collective-permute-start.8 = (bf16[80,1536]{1,0:T(8,128)(2,1)S(1)}, bf16[80,1536]{1,0:T(8,128)(2,1)S(1)}, u32[]{:S(2)}, u32[]{:S(2)}) collective-permute-start(bf16[80,1536]{1,0:T(8,128)(2,1)S(1)} %get-tuple-element.33), channel_id=1, source_target_pairs={{0,1},{1,2},{2,3},{3,0},{4,5},{5,6},{6,7},{7,4},{8,9},{9,10},{10,1... | collective-permute-start | bytes 737288 | tf_op jit(solution)/shard_map/ppermute | solution.py:499
  21.2 2.8 %collective-permute-start.10 = (bf16[80,1536]{1,0:T(8,128)(2,1)S(1)}, bf16[80,1536]{1,0:T(8,128)(2,1)S(1)}, u32[]{:S(2)}, u32[]{:S(2)}) collective-permute-start(bf16[80,1536]{1,0:T(8,128)(2,1)S(1)} %get-tuple-element.34), channel_id=1, source_target_pairs={{0,3},{1,0},{2,1},{3,2},{4,7},{5,4},{6,5},{7,6},{8,11},{9,8},{10,9... | collective-permute-start | bytes 737288 | tf_op jit(solution)/shard_map/ppermute | solution.py:500
  24.0 6.8 %collective-permute-done.8.left.refs_1_ = bf16[80,1536]{1,0:T(8,128)(2,1)S(1)} collective-permute-done((bf16[80,1536]{1,0:T(8,128)(2,1)S(1)}, bf16[80,1536]{1,0:T(8,128)(2,1)S(1)}, u32[]{:S(2)}, u32[]{:S(2)}) %collective-permute-start.8) | collective-permute-done | bytes 245792 | tf_op jit(solution)/shard_map/ppermute | solution.py:499
  30.8 3.5 %collective-permute-done.10.right.refs_1_ = bf16[80,1536]{1,0:T(8,128)(2,1)S(1)} collective-permute-done((bf16[80,1536]{1,0:T(8,128)(2,1)S(1)}, bf16[80,1536]{1,0:T(8,128)(2,1)S(1)}, u32[]{:S(2)}, u32[]{:S(2)}) %collective-permute-start.10) | collective-permute-done | bytes 245792 | tf_op jit(solution)/shard_map/ppermute | solution.py:500
  34.3 1.3 %collective-permute-start.15 = (bf16[128,1536]{1,0:T(8,128)(2,1)S(1)}, bf16[128,1536]{1,0:T(8,128)(2,1)S(1)}, u32[]{:S(2)}, u32[]{:S(2)}) collective-permute-start(bf16[128,1536]{1,0:T(8,128)(2,1)S(1)} %pair.3), channel_id=1, source_target_pairs={{1,0},{2,1},{5,4},{6,5},{9,8},{10,9},{13,12},{14,13},{17,16},{18,1... | collective-permute-start | bytes 1179656 | tf_op jit(solution)/shard_map/ppermute | solution.py:509
  35.7 0.8 %collective-permute-start.14 = (bf16[128,1536]{1,0:T(8,128)(2,1)S(1)}, bf16[128,1536]{1,0:T(8,128)(2,1)S(1)}, u32[]{:S(2)}, u32[]{:S(2)}) collective-permute-start(bf16[128,1536]{1,0:T(8,128)(2,1)S(1)} %pair.2), channel_id=1, source_target_pairs={{1,2},{2,3},{5,6},{6,7},{9,10},{10,11},{13,14},{14,15},{17,18},{18... | collective-permute-start | bytes 1179656 | tf_op jit(solution)/shard_map/ppermute | solution.py:508
  36.7 1.3 %term.1.refs_5_ = f32[256,1536]{1,0:T(8,128)S(1)} custom-call(bf16[8,32,1536]{2,1,0:T(8,128)(2,1)S(1)} %copy-done, bf16[32,1536]{1,0:T(8,128)(2,1)S(1)} %collective-permute-done.3.beside, bf16[32,1536]{1,0:T(8,128)(2,1)S(1)} %collective-permute-done.1.diagonal, bf16[80,1536]{1,0:T(8,128)(2,1)S(1)} %collective-permute-done.8.left.refs_1_, ...), custom_call_target="tpu_custom_call" | custom-call | flops 1048576 | bytes 65536 | tf_op jit(solution)/shard_map/term/pallas_call | solution.py:442
  38.1 3.2 %early.1 = (f32[256,1536]{1,0:T(8,128)S(1)}, f32[256,1536]{1,0:T(8,128)S(1)}, f32[256,1536]{1,0:T(8,128)S(1)}) custom-call(s32[2,1,2]{2,1,0:T(1,128)S(1)} %copy-done.4, bf16[256,1536]{1,0:T(8,128)(2,1)S(1)} %bitcast.7, bf16[256,1536]{1,0:T(8,128)(2,1)S(1)} %bitcast.10, bf16[256,1536]{1,0:T(8,128)(2,1)S(1)} %bitcast.6, ...), custom_call_target="tpu_custom_call" | custom-call | flops 1048576 | bytes 65536 | tf_op jit(solution)/shard_map/early/pallas_call | solution.py:442
  41.3 4.9 %collective-permute-done.15.lower = bf16[128,1536]{1,0:T(8,128)(2,1)S(1)} collective-permute-done((bf16[128,1536]{1,0:T(8,128)(2,1)S(1)}, bf16[128,1536]{1,0:T(8,128)(2,1)S(1)}, u32[]{:S(2)}, u32[]{:S(2)}) %collective-permute-start.15) | collective-permute-done | bytes 393248 | tf_op jit(solution)/shard_map/ppermute | solution.py:509
  46.4 0.5 collective-permute-start.17
  46.9 0.9 %collective-permute-done.16.refs_7_ = bf16[64,1536]{1,0:T(8,128)(2,1)S(1)} collective-permute-done((bf16[64,1536]{1,0:T(8,128)(2,1)S(1)}, bf16[64,1536]{1,0:T(8,128)(2,1)S(1)}, u32[]{:S(2)}, u32[]{:S(2)}) %collective-permute-start.16) | collective-permute-done | bytes 196640 | tf_op jit(solution)/shard_map/ppermute | solution.py:434
  48.1 3.3 %late0.1.refs_10_ = f32[256,1536]{1,0:T(8,128)} custom-call(s32[1,1,2]{2,1,0:T(1,128)S(1)} %copy-done.5, s32[2,1,2]{2,1,0:T(1,128)S(1)} %copy-done.6, s32[2,1,2]{2,1,0:T(1,128)S(1)} %copy-done.4, bf16[256,1536]{1,0:T(8,128)(2,1)S(1)} %bitcast.8, f32[256,1536]{1,0:T(8,128)S(1)} %get-tuple-element.35.refs_0_, f32[256,1536]{1,0:T(8,128)S(1)} %get-tuple-element.36.refs_1_, ...), custom_call_target="tpu_custom_call" | custom-call | flops 1048576 | bytes 65536 | tf_op jit(solution)/shard_map/late0/pallas_call | solution.py:534
  51.4 2.1 %late1.1 = f32[256,1536]{1,0:T(8,128)} custom-call(s32[1,1,2]{2,1,0:T(1,128)S(1)} %copy-done.5, s32[2,1,2]{2,1,0:T(1,128)S(1)} %copy-done.6, s32[2,1,2]{2,1,0:T(1,128)S(1)} %copy-done.4, bf16[256,1536]{1,0:T(8,128)(2,1)S(1)} %bitcast.9, f32[256,1536]{1,0:T(8,128)S(1)} %get-tuple-element.35.refs_0_, ...), custom_call_target="tpu_custom_call", output_to_operand_aliasing={{}: (14, {})} | custom-call | flops 1048576 | bytes 65536 | tf_op jit(solution)/shard_map/late1/pallas_call | solution.py:534
  (38 shorter events, 1.7 us)
Async XLA Ops:
  1.6 9.8 %collective-permute-start.2 = (bf16[512,1536]{1,0:T(8,128)(2,1)S(1)}, bf16[512,1536]{1,0:T(8,128)(2,1)S(1)}, u32[]{:S(2)}, u32[]{:S(2)}) collective-permute-start(bf16[512,1536]{1,0:T(8,128)(2,1)S(1)} %get-tuple-element.28.stale), channel_id=1, source_target_pairs={{0,4},{4,0},{8,12},{12,8},{1,5},{5,1},{9,13},{13,9},{2,6},{6,2},{1... | collective-permute-start | bytes 4718600 | tf_op jit(solution)/shard_map/ppermute | solution.py:434
  2.7 8.7 %collective-permute-start = (bf16[72,1536]{1,0:T(8,128)(2,1)S(1)}, bf16[72,1536]{1,0:T(8,128)(2,1)S(1)}, u32[]{:S(2)}, u32[]{:S(2)}) collective-permute-start(bf16[72,1536]{1,0:T(8,128)(2,1)S(1)} %offer.1), channel_id=1, source_target_pairs={{0,8},{4,12},{8,0},{12,4},{1,9},{5,13},{9,1},{13,5},{2,10},{6,14},... | collective-permute-start | bytes 663560 | tf_op jit(solution)/shard_map/ppermute | solution.py:482
  5.2 14.6 %copy-start = (bf16[8,32,1536]{2,1,0:T(8,128)(2,1)S(1)}, bf16[8,32,1536]{2,1,0:T(8,128)(2,1)}, u32[]{:S(2)}) copy-start(bf16[8,32,1536]{2,1,0:T(8,128)(2,1)} %cells.5) | copy-start | bytes 2359300
  5.2 4.7 %collective-permute-start.1 = (bf16[32,1536]{1,0:T(8,128)(2,1)S(1)}, bf16[32,1536]{1,0:T(8,128)(2,1)S(1)}, u32[]{:S(2)}, u32[]{:S(2)}) collective-permute-start(bf16[32,1536]{1,0:T(8,128)(2,1)S(1)} %get-tuple-element.26), channel_id=1, source_target_pairs={{4,8},{8,4},{5,9},{9,5},{6,10},{10,6},{7,11},{11,7},{20,24},{24,20... | collective-permute-start | bytes 294920 | tf_op jit(solution)/shard_map/ppermute | solution.py:473
  6.0 8.8 %collective-permute-start.5 = (bf16[64,1536]{1,0:T(8,128)(2,1)S(1)}, bf16[64,1536]{1,0:T(8,128)(2,1)S(1)}, u32[]{:S(2)}, u32[]{:S(2)}) collective-permute-start(bf16[64,1536]{1,0:T(8,128)(2,1)S(1)} %get-tuple-element.25.text), channel_id=1, source_target_pairs={{0,1},{1,2},{2,3},{3,0},{4,5},{5,6},{6,7},{7,4},{8,9},{9,10},{10,1... | collective-permute-start | bytes 589832 | tf_op jit(solution)/shard_map/ppermute | solution.py:471
  7.7 11.7 %collective-permute-start.6 = (bf16[64,1536]{1,0:T(8,128)(2,1)S(1)}, bf16[64,1536]{1,0:T(8,128)(2,1)S(1)}, u32[]{:S(2)}, u32[]{:S(2)}) collective-permute-start(bf16[64,1536]{1,0:T(8,128)(2,1)S(1)} %get-tuple-element.25.text), channel_id=1, source_target_pairs={{0,3},{1,0},{2,1},{3,2},{4,7},{5,4},{6,5},{7,6},{8,11},{9,8},{10,9... | collective-permute-start | bytes 589832 | tf_op jit(solution)/shard_map/ppermute | solution.py:471
  11.6 36.5 %collective-permute-start.13 = (bf16[512,1152]{1,0:T(8,128)(2,1)S(1)}, bf16[512,1152]{1,0:T(8,128)(2,1)S(1)}, u32[]{:S(2)}, u32[]{:S(2)}) collective-permute-start(bf16[512,1152]{1,0:T(8,128)(2,1)S(1)} %get-tuple-element.29), channel_id=1, source_target_pairs={{0,8},{4,12},{8,0},{12,4},{1,9},{5,13},{9,1},{13,5},{2,10},{6,14},... | collective-permute-start | bytes 3538952 | tf_op jit(solution)/shard_map/ppermute | solution.py:487
  14.4 5.4 %collective-permute-start.3 = (bf16[32,1536]{1,0:T(8,128)(2,1)S(1)}, bf16[32,1536]{1,0:T(8,128)(2,1)S(1)}, u32[]{:S(2)}, u32[]{:S(2)}) collective-permute-start(bf16[32,1536]{1,0:T(8,128)(2,1)S(1)} %get-tuple-element.31), channel_id=1, source_target_pairs={{0,4},{4,0},{8,12},{12,8},{1,5},{5,1},{9,13},{13,9},{2,6},{6,2},{1... | collective-permute-start | bytes 294920 | tf_op jit(solution)/shard_map/ppermute | solution.py:434
  19.4 17.3 %copy-start.3 = (f32[3,3,1536]{2,1,0:T(4,128)S(1)}, f32[3,3,1536]{2,1,0:T(4,128)}, u32[]{:S(2)}) copy-start(f32[3,3,1536]{2,1,0:T(4,128)} %weights.1) | copy-start | bytes 165892
  19.4 16.2 %collective-permute-start.7 = (bf16[128,1536]{1,0:T(8,128)(2,1)S(1)}, bf16[128,1536]{1,0:T(8,128)(2,1)S(1)}, u32[]{:S(2)}, u32[]{:S(2)}) collective-permute-start(bf16[128,1536]{1,0:T(8,128)(2,1)S(1)} %bundle.1.early), channel_id=1, source_target_pairs={{0,4},{4,0},{8,12},{12,8},{1,5},{5,1},{9,13},{13,9},{2,6},{6,2},{1... | collective-permute-start | bytes 1179656 | tf_op jit(solution)/shard_map/ppermute | solution.py:434
  20.0 15.6 %collective-permute-start.4 = (bf16[128,1536]{1,0:T(8,128)(2,1)S(1)}, bf16[128,1536]{1,0:T(8,128)(2,1)S(1)}, u32[]{:S(2)}, u32[]{:S(2)}) collective-permute-start(bf16[128,1536]{1,0:T(8,128)(2,1)S(1)} %get-tuple-element.32.both), channel_id=1, source_target_pairs={{0,4},{4,0},{8,12},{12,8},{1,5},{5,1},{9,13},{13,9},{2,6},{6,2},{1... | collective-permute-start | bytes 1179656 | tf_op jit(solution)/shard_map/ppermute | solution.py:434
  20.2 10.6 %collective-permute-start.8 = (bf16[80,1536]{1,0:T(8,128)(2,1)S(1)}, bf16[80,1536]{1,0:T(8,128)(2,1)S(1)}, u32[]{:S(2)}, u32[]{:S(2)}) collective-permute-start(bf16[80,1536]{1,0:T(8,128)(2,1)S(1)} %get-tuple-element.33), channel_id=1, source_target_pairs={{0,1},{1,2},{2,3},{3,0},{4,5},{5,6},{6,7},{7,4},{8,9},{9,10},{10,1... | collective-permute-start | bytes 737288 | tf_op jit(solution)/shard_map/ppermute | solution.py:499
  21.2 13.1 %collective-permute-start.10 = (bf16[80,1536]{1,0:T(8,128)(2,1)S(1)}, bf16[80,1536]{1,0:T(8,128)(2,1)S(1)}, u32[]{:S(2)}, u32[]{:S(2)}) collective-permute-start(bf16[80,1536]{1,0:T(8,128)(2,1)S(1)} %get-tuple-element.34), channel_id=1, source_target_pairs={{0,3},{1,0},{2,1},{3,2},{4,7},{5,4},{6,5},{7,6},{8,11},{9,8},{10,9... | collective-permute-start | bytes 737288 | tf_op jit(solution)/shard_map/ppermute | solution.py:500
  30.8 5.8 %collective-permute-start.9 = (bf16[80,1536]{1,0:T(8,128)(2,1)S(1)}, bf16[80,1536]{1,0:T(8,128)(2,1)S(1)}, u32[]{:S(2)}, u32[]{:S(2)}) collective-permute-start(bf16[80,1536]{1,0:T(8,128)(2,1)S(1)} %collective-permute-done.8.left.refs_1_), channel_id=1, source_target_pairs={{0,4},{4,0},{8,12},{12,8},{1,5},{5,1},{9,13},{13,9},{2,6},{6,2},{1... | collective-permute-start | bytes 737288 | tf_op jit(solution)/shard_map/ppermute | solution.py:434
  34.3 12.0 %collective-permute-start.15 = (bf16[128,1536]{1,0:T(8,128)(2,1)S(1)}, bf16[128,1536]{1,0:T(8,128)(2,1)S(1)}, u32[]{:S(2)}, u32[]{:S(2)}) collective-permute-start(bf16[128,1536]{1,0:T(8,128)(2,1)S(1)} %pair.3), channel_id=1, source_target_pairs={{1,0},{2,1},{5,4},{6,5},{9,8},{10,9},{13,12},{14,13},{17,16},{18,1... | collective-permute-start | bytes 1179656 | tf_op jit(solution)/shard_map/ppermute | solution.py:509
  35.6 2.4 %copy-start.1 = (bf16[8,32,1536]{2,1,0:T(8,128)(2,1)S(1)}, bf16[8,32,1536]{2,1,0:T(8,128)(2,1)}, u32[]{:S(2)}) copy-start(bf16[8,32,1536]{2,1,0:T(8,128)(2,1)} %param.11) | copy-start | bytes 2359300
  35.6 2.4 %copy-start.2 = (bf16[8,32,1536]{2,1,0:T(8,128)(2,1)S(1)}, bf16[8,32,1536]{2,1,0:T(8,128)(2,1)}, u32[]{:S(2)}) copy-start(bf16[8,32,1536]{2,1,0:T(8,128)(2,1)} %param.12) | copy-start | bytes 2359300
  35.6 2.4 %copy-start.4 = (s32[2,1,2]{2,1,0:T(1,128)S(1)}, s32[2,1,2]{2,1,0:T(1,128)}, u32[]{:S(2)}) copy-start(s32[2,1,2]{2,1,0:T(1,128)} %text_ref.5) | copy-start | bytes 52
  35.7 10.6 %collective-permute-start.14 = (bf16[128,1536]{1,0:T(8,128)(2,1)S(1)}, bf16[128,1536]{1,0:T(8,128)(2,1)S(1)}, u32[]{:S(2)}, u32[]{:S(2)}) collective-permute-start(bf16[128,1536]{1,0:T(8,128)(2,1)S(1)} %pair.2), channel_id=1, source_target_pairs={{1,2},{2,3},{5,6},{6,7},{9,10},{10,11},{13,14},{14,15},{17,18},{18... | collective-permute-start | bytes 1179656 | tf_op jit(solution)/shard_map/ppermute | solution.py:508
  36.5 1.6 %collective-permute-start.11 = (bf16[80,1536]{1,0:T(8,128)(2,1)S(1)}, bf16[80,1536]{1,0:T(8,128)(2,1)S(1)}, u32[]{:S(2)}, u32[]{:S(2)}) collective-permute-start(bf16[80,1536]{1,0:T(8,128)(2,1)S(1)} %collective-permute-done.10.right.refs_1_), channel_id=1, source_target_pairs={{0,4},{4,0},{8,12},{12,8},{1,5},{5,1},{9,13},{13,9},{2,6},{6,2},{1... | collective-permute-start | bytes 737288 | tf_op jit(solution)/shard_map/ppermute | solution.py:434
  36.6 14.9 %collective-permute-start.12 = (bf16[512,384]{1,0:T(8,128)(2,1)S(1)}, bf16[512,384]{1,0:T(8,128)(2,1)S(1)}, u32[]{:S(2)}, u32[]{:S(2)}) collective-permute-start(bf16[512,384]{1,0:T(8,128)(2,1)S(1)} %get-tuple-element.38), channel_id=1, source_target_pairs={{0,8},{4,12},{8,0},{12,4},{1,9},{5,13},{9,1},{13,5},{2,10},{6,14},... | collective-permute-start | bytes 1179656 | tf_op jit(solution)/shard_map/ppermute | solution.py:487
  38.1 10.0 %copy-start.6 = (s32[2,1,2]{2,1,0:T(1,128)S(1)}, s32[2,1,2]{2,1,0:T(1,128)}, u32[]{:S(2)}) copy-start(s32[2,1,2]{2,1,0:T(1,128)} %pattern_ref.3) | copy-start | bytes 52
  46.3 1.5 %collective-permute-start.16 = (bf16[64,1536]{1,0:T(8,128)(2,1)S(1)}, bf16[64,1536]{1,0:T(8,128)(2,1)S(1)}, u32[]{:S(2)}, u32[]{:S(2)}) collective-permute-start(bf16[64,1536]{1,0:T(8,128)(2,1)S(1)} %get-tuple-element.42.refs_6_), channel_id=1, source_target_pairs={{0,4},{4,0},{8,12},{12,8},{1,5},{5,1},{9,13},{13,9},{2,6},{6,2},{1... | collective-permute-start | bytes 589832 | tf_op jit(solution)/shard_map/ppermute | solution.py:434
  46.4 1.7 %collective-permute-start.17 = (bf16[64,1536]{1,0:T(8,128)(2,1)S(1)}, bf16[64,1536]{1,0:T(8,128)(2,1)S(1)}, u32[]{:S(2)}, u32[]{:S(2)}) collective-permute-start(bf16[64,1536]{1,0:T(8,128)(2,1)S(1)} %get-tuple-element.43.refs_8_), channel_id=1, source_target_pairs={{0,4},{4,0},{8,12},{12,8},{1,5},{5,1},{9,13},{13,9},{2,6},{6,2},{1... | collective-permute-start | bytes 589832 | tf_op jit(solution)/shard_map/ppermute | solution.py:434
  (1 other events, 2.1 us)
